TPU v7x, 512 devices: a whole 4x8x8 slice. The times are simulated.
512 devices in a mesh: sec: 32 (over z, y_lo), blk: 16 (over x, y_hi, core).
Axes of the slice: x: 4, y: 8 (y_hi: 2, y_lo: 4; y = y_hi * 4 + y_lo), z: 8, core: 2. Of those that a mesh axis runs over, the one named last changes fastest.
Arguments:
- wave: bfloat16 [32, 16, 256, 256], P('sec', 'blk'), may hold values from -6 to 6
- left_block_environment: bfloat16 [32, 16, 16, 256, 256], P('sec', 'blk'), may hold values from -0.375 to 0.375
- right_block_environment: bfloat16 [32, 16, 16, 256, 256], P('sec', 'blk'), may hold values from -0.09375 to 0.09375
- source_block: int32 [32, 16, 16], P('sec', 'blk'), may hold values from 0 to 15
- sector_size: int32 [32, 16], P('sec', 'blk'), may hold values from 1 to 256, 2560 in all within a row
Outputs:
- first_product: bfloat16 [32, 16, 256, 256], P('sec', 'blk')
- second_product: bfloat16 [32, 16, 256, 256], P('sec', 'blk')
All inputs are finite; a program needn't handle non-finite values. No bound on the sum of `sector_size` on one device may be relied on, other than what follows from the above.
Results may differ from a plain program's by a relative error of at most 0.015.
Values may be sent and summed in bfloat16 or wider, within the bound.
No kernel may reach another device: no remote copies, remote signals or barrier semaphores. Data moves between devices by JAX's collectives and lax.ppermute only.
A program may use at most 64 MiB of HBM per device.

v0:
```python
import math

import jax
import jax.numpy as jnp
from jax import lax
from jax.sharding import Mesh
from jax.sharding import PartitionSpec as P

BLK = ("blk_0", "blk_1", "blk_2")


def copy_for_each(value, axis):
    length = lax.axis_size(axis)
    return lax.all_to_all(
        jnp.broadcast_to(value[None], (length, *value.shape)), axis, 0, 0, tiled=True
    )


def in_order(blocks, dim):
    shape = list(blocks.shape[1:])
    shape[dim] *= blocks.shape[0]
    return jnp.moveaxis(blocks, 0, dim).reshape(shape)


def gather_axes(value, axes, dim):
    far, near = axes
    blocks = copy_for_each(copy_for_each(value, far), near)
    return in_order(blocks.swapaxes(0, 1).reshape(-1, *value.shape), dim)


def of_everyone(value, axis):
    return copy_for_each(value, axis).sum(axis=0)


def in_one(arrays, axis):
    ends = [0]
    for a in arrays:
        ends.append(ends[-1] + a.size)
    so_far = of_everyone(jnp.concatenate([a.ravel() for a in arrays]), axis)
    return tuple((so_far[b:e].reshape(a.shape) for a, b, e in zip(arrays, ends, ends[1:])))


def split_up(value, dim, length):
    before, after = (value.shape[:dim], value.shape[dim + 1 :])
    return jnp.moveaxis(value.reshape(*before, length, -1, *after), dim, 0)


def sum_at_owner(value, axis, dim):
    blocks = split_up(value, dim, lax.axis_size(axis))
    arrived = lax.all_to_all(blocks, axis, split_axis=0, concat_axis=0, tiled=True)
    return arrived.astype(jnp.float32).sum(axis=0)


def shifted(value, axis, steps):
    count = lax.axis_size(axis)
    initial, last = (max(0, -steps), min(count, count - steps))
    return lax.ppermute(value, axis, [(source, source + steps) for source in range(initial, last)])


def live_mask(sizes, width):
    rows = jnp.arange(width, dtype=jnp.int32)
    first = rows[None, :, None] < sizes[:, None, None]
    second_apply = rows[None, None, :] < sizes[:, None, None]
    return (first & second_apply).astype(jnp.bfloat16)


def apply_blocks(left, pool, picks, right):
    chosen = jnp.take(pool, picks, axis=0)
    inner = jnp.einsum("ktab,ktbc->ktac", left, chosen, preferred_element_type=jnp.float32).astype(
        jnp.bfloat16
    )
    return jnp.einsum("ktab,ktbc->kac", inner, right, preferred_element_type=jnp.float32)


def shards(wave, left_block_environment, right_block_environment, source_block, sector_size):
    left = left_block_environment[0]
    right = right_block_environment[0]
    picks = source_block[0]
    sizes = sector_size[0]
    blocks = wave.shape[1]
    width = wave.shape[2]
    mask = live_mask(sizes, width)
    mask_f = mask.astype(jnp.float32)
    live = wave[0] * mask
    pool = gather_axes(live, (("blk_0", "blk_1"), "blk_2"), 0)
    first = (apply_blocks(left, pool, picks, right) * mask_f).astype(jnp.bfloat16)
    first_f = first.astype(jnp.float32)
    squares = jnp.sum(first_f * first_f)
    count = jnp.sum((sizes * sizes).astype(jnp.float32))
    totals = in_one((squares, count), BLK)
    scale = lax.rsqrt(totals[0] / totals[1] + 1e-06)
    trial_vector = (first_f * scale).astype(jnp.bfloat16)
    second_pool_result = gather_axes(trial_vector, (("blk_0", "blk_1"), "blk_2"), 0)
    left_vector = jnp.einsum(
        "ktab,kbc->ktac", left, trial_vector, preferred_element_type=jnp.float32
    ).astype(jnp.bfloat16)
    partial_border_sum = jnp.einsum(
        "glj,gdls->djs", trial_vector, left_vector, preferred_element_type=jnp.float32
    )
    factor = 1.0 / (width * math.sqrt(blocks * lax.axis_size(BLK)))
    share = sum_at_owner(partial_border_sum.astype(jnp.bfloat16), BLK, 1)
    edge = (share * factor).astype(jnp.bfloat16)
    moved = shifted(edge, "sec", 1)
    incoming = gather_axes(moved, (("blk_0", "blk_1"), "blk_2"), 1)
    left_two = left + incoming[None]
    second_apply = (apply_blocks(left_two, second_pool_result, picks, right) * mask_f).astype(
        jnp.bfloat16
    )
    return (first[None], second_apply[None])


def solution(mesh):
    finer = Mesh(
        mesh.devices.reshape(mesh.shape["sec"], 4, 2, 2), ("sec", "blk_0", "blk_1", "blk_2")
    )
    return jax.shard_map(
        shards,
        mesh=finer,
        in_specs=(
            P("sec", BLK, None, None),
            P("sec", BLK, None, None, None),
            P("sec", BLK, None, None, None),
            P("sec", BLK, None),
            P("sec", BLK),
        ),
        out_specs=(P("sec", BLK, None, None), P("sec", BLK, None, None)),
        check_vma=False,
    )
```

profile of v0, /device:TPU:457, one launch (start us, length us, event | category | flops | bytes accessed | tf_op | source)
XLA Modules:
  0.0 217.7 jit_solution(11686539942867932500)
XLA Ops:
  3.5 8.4 %all-to-all-start = ((bf16[8,1,256,256]{3,2,1,0:T(8,128)(2,1)}), bf16[8,1,256,256]{3,2,1,0:T(8,128)(2,1)S(1)}, u32[]{:S(2)}, u32[]{:S(2)}) async-start(bf16[8,1,256,256]{3,2,1,0:T(8,128)(2,1)} %broadcast_in_dim.34), calls=%async_computation | async-start | bytes 2097152 | tf_op jit(solution)/shard_map/all_to_all | solution.py:14
  12.0 31.0 %all-to-all-done = bf16[8,1,256,256]{3,2,1,0:T(8,128)(2,1)S(1)} async-done(((bf16[8,1,256,256]{3,2,1,0:T(8,128)(2,1)}), bf16[8,1,256,256]{3,2,1,0:T(8,128)(2,1)S(1)}, u32[]{:S(2)}, u32[]{:S(2)}) %all-to-all-start) | async-done | bytes 1048608 | tf_op jit(solution)/shard_map/all_to_all | solution.py:14
  43.2 5.8 %all_to_all.41 = bf16[2,8,1,256,256]{4,3,1,2,0:T(8,128)(2,1)S(1)} all-to-all(bf16[2,8,1,256,256]{4,3,1,2,0:T(8,128)(2,1)S(1)} %broadcast_in_dim.36), channel_id=1, replica_groups=mesh['sec'=32,'blk_0'=4,'blk_1'=2,'blk_2'=2] {'blk_2'}, dimensions={0} | all-to-all | bytes 4194304 | tf_op jit(solution)/shard_map/all_to_all | solution.py:14
  49.0 1.5 copy.50
  50.4 3.6 %gather_fusion = bf16[16,256,256]{2,1,0:T(8,128)(2,1)} fusion(bf16[16,256,256]{2,1,0:T(8,128)(2,1)} %bitcast.189, s32[1024]{0:T(1024)S(1)} %pad_clamp_fusion), kind=kCustom, calls=%fused_computation.clone | custom fusion | bytes 4194368 | tf_op jit(solution)/shard_map/jit(_take)/gather | solution.py:68
  54.0 4.4 %fusion.99 = (f32[]{:T(128)}, bf16[256,256]{1,0:T(8,128)(2,1)S(1)}) fusion(pred[256]{0:T(512)(128)(4,1)S(1)} %iota_compare_fusion, bf16[1,1,16,256,256]{4,3,2,1,0:T(8,128)(2,1)S(1)} %copy-done, bf16[1,1,16,256,256]{4,3,2,1,0:T(8,128)(2,1)} %param.8, bf16[16,256,256]{2,1,0:T(8,128)(2,1)} %gather_fusion, pred[16]{0:T(512)(128)(4,1)S(1)} %and_bitcast_fusion), kind=kOutput, calls=%fused_computation.38 | convolution fusion | flops 1076363264 | bytes 6422804 | tf_op jit(solution)/shard_map/ktab,ktbc->kac/dot_general | solution.py:72
  59.2 12.3 %all_to_all.42 = f32[16,1,2]{2,1,0:T(1,128)S(1)} all-to-all(f32[16,1,2]{2,1,0:T(1,128)S(1)} %broadcast_in_dim.70), channel_id=1, replica_groups=mesh['sec'=32,'blk_0'=4,'blk_1'=2,'blk_2'=2] {'blk_0','blk_1','blk_2'}, dimensions={0} | all-to-all | bytes 256 | tf_op jit(solution)/shard_map/all_to_all | solution.py:14
  73.5 4.2 %fusion.23 = bf16[16,256,256]{1,2,0:T(8,128)(2,1)} fusion(bf16[1,1,16,256,256]{4,3,2,1,0:T(8,128)(2,1)} %param.8, bf16[256,256]{1,0:T(8,128)(2,1)S(1)} %fusion.100), kind=kOutput, calls=%fused_computation.26 | convolution fusion | flops 1075838976 | bytes 4325376 | tf_op jit(solution)/shard_map/glj,gdls->djs/dot_general | solution.py:97
  77.7 1.8 copy.73
  79.5 55.8 %all_to_all.43 = bf16[16,16,16,256]{3,2,1,0:T(8,128)(2,1)} all-to-all(bf16[16,16,16,256]{3,2,1,0:T(8,128)(2,1)S(1)} %bitcast.190), channel_id=1, replica_groups=mesh['sec'=32,'blk_0'=4,'blk_1'=2,'blk_2'=2] {'blk_0','blk_1','blk_2'}, dimensions={0} | all-to-all | bytes 4194304 | tf_op jit(solution)/shard_map/all_to_all | solution.py:50
  136.4 3.6 %all-to-all-start.6 = ((bf16[8,1,256,256]{3,2,1,0:T(8,128)(2,1)}), bf16[8,1,256,256]{3,2,1,0:T(8,128)(2,1)S(1)}, u32[]{:S(2)}, u32[]{:S(2)}) async-start(bf16[8,1,256,256]{3,2,1,0:T(8,128)(2,1)} %broadcast_in_dim.73), calls=%async_computation.6 | async-start | bytes 2097152 | tf_op jit(solution)/shard_map/all_to_all | solution.py:14
  139.9 1.9 convert_reduce_fusion
  141.9 2.2 %collective-permute-start = (bf16[16,16,256]{2,1,0:T(8,128)(2,1)S(1)}, bf16[16,16,256]{2,1,0:T(8,128)(2,1)S(1)}, u32[]{:S(2)}, u32[]{:S(2)}) collective-permute-start(bf16[16,16,256]{2,1,0:T(8,128)(2,1)S(1)} %multiply_convert_fusion), channel_id=1, source_target_pairs={{0,16},{16,32},{32,48},{48,64},{64,80},{80,96},{96,112},{112,128},... | collective-permute-start | bytes 393224 | tf_op jit(solution)/shard_map/ppermute | solution.py:57
  144.1 19.4 %all-to-all-done.6 = bf16[8,1,256,256]{3,2,1,0:T(8,128)(2,1)S(1)} async-done(((bf16[8,1,256,256]{3,2,1,0:T(8,128)(2,1)}), bf16[8,1,256,256]{3,2,1,0:T(8,128)(2,1)S(1)}, u32[]{:S(2)}, u32[]{:S(2)}) %all-to-all-start.6) | async-done | bytes 1048608 | tf_op jit(solution)/shard_map/all_to_all | solution.py:14
  163.7 6.4 %all_to_all.44 = bf16[2,8,1,256,256]{4,3,1,2,0:T(8,128)(2,1)} all-to-all(bf16[2,8,1,256,256]{4,3,1,2,0:T(8,128)(2,1)S(1)} %broadcast_in_dim.75), channel_id=1, replica_groups=mesh['sec'=32,'blk_0'=4,'blk_1'=2,'blk_2'=2] {'blk_2'}, dimensions={0} | all-to-all | bytes 4194304 | tf_op jit(solution)/shard_map/all_to_all | solution.py:14
  170.1 1.1 broadcast_in_dim.71
  171.2 3.6 %all-to-all-start.4 = ((bf16[8,16,16,256]{3,2,1,0:T(8,128)(2,1)}), bf16[8,16,16,256]{3,2,1,0:T(8,128)(2,1)S(1)}, u32[]{:S(2)}, u32[]{:S(2)}) async-start(bf16[8,16,16,256]{3,2,1,0:T(8,128)(2,1)} %broadcast_in_dim.71), calls=%async_computation.4 | async-start | bytes 2097152 | tf_op jit(solution)/shard_map/all_to_all | solution.py:14
  174.8 3.1 %copy.61 = bf16[2,8,1,256,256]{4,3,0,1,2:T(8,128)(2,1)} copy(bf16[2,8,1,256,256]{4,3,1,2,0:T(8,128)(2,1)} %all_to_all.44) | data formatting | bytes 4194304 | tf_op jit(solution)/shard_map/all_to_all | solution.py:14
  177.9 3.6 %gather_fusion.1 = bf16[16,256,256]{2,1,0:T(8,128)(2,1)} fusion(bf16[16,256,256]{2,1,0:T(8,128)(2,1)} %bitcast.188, s32[1024]{0:T(1024)S(1)} %pad_clamp_fusion), kind=kCustom, calls=%fused_computation.1.clone | custom fusion | bytes 4194368 | tf_op jit(solution)/shard_map/jit(_take)/gather | solution.py:68
  181.5 22.5 %all-to-all-done.4 = bf16[8,16,16,256]{3,2,1,0:T(8,128)(2,1)S(1)} async-done(((bf16[8,16,16,256]{3,2,1,0:T(8,128)(2,1)}), bf16[8,16,16,256]{3,2,1,0:T(8,128)(2,1)S(1)}, u32[]{:S(2)}, u32[]{:S(2)}) %all-to-all-start.4) | async-done | bytes 1048608 | tf_op jit(solution)/shard_map/all_to_all | solution.py:14
  204.4 5.5 %all_to_all.45 = bf16[2,8,16,16,256]{4,3,1,2,0:T(8,128)(2,1)S(1)} all-to-all(bf16[2,8,16,16,256]{4,3,1,2,0:T(8,128)(2,1)S(1)} %broadcast_in_dim.72), channel_id=1, replica_groups=mesh['sec'=32,'blk_0'=4,'blk_1'=2,'blk_2'=2] {'blk_2'}, dimensions={0} | all-to-all | bytes 4194304 | tf_op jit(solution)/shard_map/all_to_all | solution.py:14
  210.4 1.4 copy-done.1
  211.7 1.7 bitcast_add_fusion
  213.4 4.3 %fusion.88 = bf16[1,1,256,256]{3,2,1,0:T(8,128)(2,1)} fusion(bf16[1,1,16,256,256]{4,3,2,1,0:T(8,128)(2,1)S(1)} %copy-done, bf16[16,256,256]{2,1,0:T(8,128)(2,1)} %bitcast_add_fusion, bf16[16,256,256]{2,1,0:T(8,128)(2,1)} %gather_fusion.1, pred[16]{0:T(512)(128)(4,1)S(1)} %and_bitcast_fusion, pred[256]{0:T(512)(128)(4,1)S(1)} %iota_compare_fusion), kind=kOutput, calls=%fused_computation.33 | convolution fusion | flops 1076166656 | bytes 6422800 | tf_op jit(solution)/shard_map/ktab,ktbc->kac/dot_general | solution.py:72
  (27 shorter events, 5.8 us)
Async XLA Ops:
  0.6 53.4 %copy-start = (bf16[1,1,16,256,256]{4,3,2,1,0:T(8,128)(2,1)S(1)}, bf16[1,1,16,256,256]{4,3,2,1,0:T(8,128)(2,1)}, u32[]{:S(2)}) copy-start(bf16[1,1,16,256,256]{4,3,2,1,0:T(8,128)(2,1)} %param.9) | copy-start | bytes 6291460
  0.6 11.3 %copy-start.3 = (s32[1,1,16]{2,1,0:T(1,128)S(1)}, s32[1,1,16]{2,1,0:T(1,128)}, u32[]{:S(2)}) copy-start(s32[1,1,16]{2,1,0:T(1,128)} %param.10) | copy-start | bytes 196
  3.5 39.5 %all-to-all-start = ((bf16[8,1,256,256]{3,2,1,0:T(8,128)(2,1)}), bf16[8,1,256,256]{3,2,1,0:T(8,128)(2,1)S(1)}, u32[]{:S(2)}, u32[]{:S(2)}) async-start(bf16[8,1,256,256]{3,2,1,0:T(8,128)(2,1)} %broadcast_in_dim.34), calls=%async_computation | async-start | bytes 2097152 | tf_op jit(solution)/shard_map/all_to_all | solution.py:14
  58.5 19.2 %copy-start.2 = (bf16[256,256]{1,0:T(8,128)(2,1)}, bf16[256,256]{1,0:T(8,128)(2,1)S(1)}, u32[]{:S(2)}) copy-start(bf16[256,256]{1,0:T(8,128)(2,1)S(1)} %get-tuple-element.6) | copy-start | bytes 393220
  136.4 27.2 %all-to-all-start.6 = ((bf16[8,1,256,256]{3,2,1,0:T(8,128)(2,1)}), bf16[8,1,256,256]{3,2,1,0:T(8,128)(2,1)S(1)}, u32[]{:S(2)}, u32[]{:S(2)}) async-start(bf16[8,1,256,256]{3,2,1,0:T(8,128)(2,1)} %broadcast_in_dim.73), calls=%async_computation.6 | async-start | bytes 2097152 | tf_op jit(solution)/shard_map/all_to_all | solution.py:14
  141.9 28.3 %collective-permute-start = (bf16[16,16,256]{2,1,0:T(8,128)(2,1)S(1)}, bf16[16,16,256]{2,1,0:T(8,128)(2,1)S(1)}, u32[]{:S(2)}, u32[]{:S(2)}) collective-permute-start(bf16[16,16,256]{2,1,0:T(8,128)(2,1)S(1)} %multiply_convert_fusion), channel_id=1, source_target_pairs={{0,16},{16,32},{32,48},{48,64},{64,80},{80,96},{96,112},{112,128},... | collective-permute-start | bytes 393224 | tf_op jit(solution)/shard_map/ppermute | solution.py:57
  171.2 32.8 %all-to-all-start.4 = ((bf16[8,16,16,256]{3,2,1,0:T(8,128)(2,1)}), bf16[8,16,16,256]{3,2,1,0:T(8,128)(2,1)S(1)}, u32[]{:S(2)}, u32[]{:S(2)}) async-start(bf16[8,16,16,256]{3,2,1,0:T(8,128)(2,1)} %broadcast_in_dim.71), calls=%async_computation.4 | async-start | bytes 2097152 | tf_op jit(solution)/shard_map/all_to_all | solution.py:14
  210.1 1.6 copy-start.1
where the time goes:
time: 218 us
  blocking collectives  85.7 us (39%)
  waiting for transfers between devices  73 us (33%)
  local copies, waits for them, and re-layouts  19.9 us (9%)
  starting transfers between devices  17.7 us (8%)
  matrix products  13 us (6%)
  other arithmetic  5.39 us (2%)
  between operations  2.96 us (1%)
    all_to_all x3, waiting for transfers between devices, copy_for_each(): lax.all_to_all(jnp.broadcast_to(value[None], (length, *value.shape)), axi...  73 us
    all_to_all x1, blocking collectives, sum_at_owner(): lax.all_to_all(blocks, axis, split_axis=0, concat_axis=0, tiled=True)  55.8 us
    all_to_all x4, blocking collectives, copy_for_each(): lax.all_to_all(jnp.broadcast_to(value[None], (length, *value.shape)), axi...  30 us
    all_to_all x3, starting transfers between devices, copy_for_each(): lax.all_to_all(jnp.broadcast_to(value[None], (length, *value.shape)), axi...  15.5 us
    dot_general x2, matrix products, apply_blocks(): jnp.einsum('ktab,ktbc->kac', inner, right, preferred_element_type=jnp.flo...  8.75 us
    gather x2, local copies, waits for them, and re-layouts, apply_blocks(): chosen = jnp.take(pool, picks, axis=0)  7.17 us
    all_to_all x4, local copies, waits for them, and re-layouts, copy_for_each(): lax.all_to_all(jnp.broadcast_to(value[None], (length, *value.shape)), axi...  4.87 us
  transfers between devices with their start and end apart: 4, of which 3 were waited for; matrix products, arithmetic and copies ran while one was open for 4% of the time, Pallas kernels for 0%

commit v1 on v0

v1 whole, which is shorter than its diff:
```python
import math

import jax
import jax.numpy as jnp
from jax import lax
from jax.experimental import pallas as pl
from jax.experimental.pallas import tpu as pltpu
from jax.sharding import Mesh
from jax.sharding import PartitionSpec as P

BF = jnp.bfloat16
F32 = jnp.float32
TILE = 16
YROW = ("z", "yl", "yh")
SWAP = [(0, 1), (1, 0)]
VMEM = pl.BlockSpec(memory_space=pltpu.VMEM)
SMEM = pl.BlockSpec(memory_space=pltpu.SMEM)
ANY = pl.BlockSpec(memory_space=pl.ANY)
PARAMS = pltpu.CompilerParams(vmem_limit_bytes=24 << 20)


def dot(a, b):
    return jnp.dot(a, b, preferred_element_type=F32)


def pieces(value):
    high = value.astype(BF).astype(F32)
    mid = (value - high).astype(BF).astype(F32)
    return high, mid, value - high - mid


def pack(squares, count):
    width = squares.shape[-1]
    row = lax.broadcasted_iota(jnp.int32, (TILE, width), 0)
    tile = jnp.zeros((TILE, width), F32)
    for at, part in enumerate(pieces(squares) + pieces(count)):
        tile = jnp.where(row == at, jnp.broadcast_to(part, (TILE, width)), tile)
    return tile.astype(BF)


def unpack(tile):
    t = tile.astype(F32)
    return t[0:1] + t[1:2] + t[2:3], t[3:4] + t[4:5] + t[5:6]


def live(size, shape):
    rows = lax.broadcasted_iota(jnp.int32, shape, 0)
    columns = lax.broadcasted_iota(jnp.int32, shape, 1)
    return (rows < size) & (columns < size)


def place(source, meta, yh_known):
    x, yh, c = source // 4, (source // 2) % 2, source % 2
    other = lax.rem(c + meta[1], 2)
    if yh_known:
        yh = lax.rem(yh + meta[2], 2)
    return (other * 4 + x) * 2 + yh


def first_kernel(meta, picks, pool_own, pool_other, left_hbm, right_hbm,
                 first_out, message, stats, send, keep,
                 pool, left, right, inner, lv, pool_sem, left_sem, right_sem):
    channels, width = left.shape[0], left.shape[1]
    half = channels // 2
    pool_copies = [
        pltpu.make_async_copy(pool_own, pool.at[pl.ds(0, half)], pool_sem.at[0]),
        pltpu.make_async_copy(pool_other, pool.at[pl.ds(half, half)], pool_sem.at[1]),
    ]
    left_copies = [pltpu.make_async_copy(left_hbm.at[t], left.at[t], left_sem.at[t]) for t in range(channels)]
    right_copies = [pltpu.make_async_copy(right_hbm.at[t], right.at[t], right_sem.at[t]) for t in range(channels)]
    for copy in pool_copies + left_copies + right_copies:
        copy.start()
    for copy in pool_copies:
        copy.wait()
    for t in range(channels):
        left_copies[t].wait()
        block = pool[place(picks[t], meta, False)]
        inner[:, t * width:(t + 1) * width] = dot(left[t], block).astype(BF)
    for copy in right_copies:
        copy.wait()
    product = dot(inner[...], right[...].reshape(channels * width, width))
    size = meta[0]
    product = jnp.where(live(size, product.shape), product, 0.0).astype(BF)
    first_out[...] = product
    message[0:width, :] = product
    value = product.astype(F32)
    columns = jnp.sum(value * value, axis=0, keepdims=True)
    squares = jnp.broadcast_to(jnp.sum(columns, axis=1, keepdims=True), (1, width))
    count = jnp.full((1, width), size * size, jnp.int32).astype(F32)
    tile = pack(squares, count)
    message[width:width + TILE, :] = tile
    stats[...] = tile
    send[half * width:half * width + TILE, :] = tile
    turned = value.T.astype(BF)
    for t in range(channels):
        lv[t] = dot(left[t], product).astype(BF)
    mine = meta[1]
    for j in range(half):
        send[j * width:(j + 1) * width, :] = dot(turned, lv[(1 - mine) * half + j]).astype(BF)
    for j in range(half):
        keep[j * width:(j + 1) * width, :] = dot(turned, lv[mine * half + j]).astype(BF)


def core_sum_kernel(keep, stats, arrived, out):
    rows = keep.shape[0]
    quarter = rows // 4
    q0, c0 = unpack(stats[...])
    q1, c1 = unpack(arrived[rows:rows + TILE, :])
    tile = pack(q0 + q1, c0 + c1)
    for x in range(4):
        at = x * quarter
        out[x, 0:quarter, :] = (
            keep[at:at + quarter, :].astype(F32) + arrived[at:at + quarter, :].astype(F32)
        ).astype(BF)
        out[x, quarter:quarter + TILE, :] = tile


def row_sum_kernel(arrived, out):
    rows = out.shape[0] - TILE
    out[0:rows, :] = (
        (arrived[0, 0:rows, :].astype(F32) + arrived[1, 0:rows, :].astype(F32))
        + (arrived[2, 0:rows, :].astype(F32) + arrived[3, 0:rows, :].astype(F32))
    ).astype(BF)
    squares, count = unpack(arrived[0, rows:rows + TILE, :])
    for x in range(1, 4):
        q, c = unpack(arrived[x, rows:rows + TILE, :])
        squares, count = squares + q, count + c
    out[rows:rows + TILE, :] = pack(squares, count)


def edge_kernel(factor, near, far, out):
    rows = near.shape[0] - TILE
    q0, c0 = unpack(near[rows:rows + TILE, :])
    q1, c1 = unpack(far[rows:rows + TILE, :])
    weight = factor / ((q0 + q1) / jnp.maximum(c0 + c1, 1.0) + 1e-6)
    total = near[0:rows, :].astype(F32) + far[0:rows, :].astype(F32)
    edge = (total * weight).astype(BF)
    for x in range(4):
        out[x] = edge


def pool_two_kernel(meta, picks, own, other, left_hbm, right_hbm, g_out, base, pool, left, right, pool_sem, left_sem, right_sem):
    channels, width = left.shape[0], left.shape[1]
    pool_copies = [
        pltpu.make_async_copy(own, pool.at[pl.ds(0, 4)], pool_sem.at[0]),
        pltpu.make_async_copy(other, pool.at[pl.ds(4, 4)], pool_sem.at[1]),
    ]
    left_copies = [pltpu.make_async_copy(left_hbm.at[t], left.at[t], left_sem.at[t]) for t in range(channels)]
    right_copies = [pltpu.make_async_copy(right_hbm.at[t], right.at[t], right_sem.at[t]) for t in range(channels)]
    for copy in pool_copies + right_copies + left_copies:
        copy.start()
    for copy in pool_copies:
        copy.wait()
    squares = count = jnp.zeros((1, width), F32)
    span = width + TILE
    for at in range(8):
        for row in range(2):
            q, c = unpack(pool[at, row * span + width:(row + 1) * span, :])
            squares, count = squares + q, count + c
    scale = lax.rsqrt(squares / count + 1e-6)
    base[...] = jnp.zeros_like(base)
    for t in range(channels):
        right_copies[t].wait()
        left_copies[t].wait()
        slot = place(picks[t], meta, True)
        start = pl.multiple_of(lax.rem(slot, 2) * span, TILE)
        block = pool[slot // 2, pl.ds(start, width), :]
        g = (dot(block, right[t]) * scale).astype(BF)
        g_out[t] = g
        base[...] += dot(left[t], g)


def half_kernel(final, meta, edges, g, start, out):
    half, width = edges.shape[0] * 2, g.shape[1]
    side = meta[1] if not final else 1 - meta[1]
    total = start[...]
    for j in range(half):
        block = edges[j // 2, (j % 2) * width:(j % 2 + 1) * width, :]
        total = total + dot(block, g[side * half + j])
    if final:
        total = jnp.where(live(meta[0], total.shape), total, 0.0)
    out[...] = total.astype(out.dtype)


def call(kernel, shapes, specs, scratch, flops, moved):
    several = isinstance(shapes, (list, tuple))
    return pl.pallas_call(
        kernel,
        out_shape=[jax.ShapeDtypeStruct(*s) for s in shapes] if several else shapes,
        in_specs=specs,
        out_specs=[VMEM] * len(shapes) if several else VMEM,
        scratch_shapes=scratch,
        compiler_params=PARAMS,
        cost_estimate=pl.CostEstimate(flops=flops, bytes_accessed=moved, transcendentals=0),
    )


def one(shape, dtype):
    return jax.ShapeDtypeStruct(shape, dtype)


def for_each(value, count):
    return jnp.broadcast_to(value[None], (count, *value.shape))


def exchange(value, axes):
    return lax.all_to_all(value, axes, 0, 0, tiled=True)


def routes(z_count, y_count):
    def at(z, yl, yh):
        return (z * y_count + yl) * 2 + yh

    near, far = [], []
    for z in range(z_count):
        for yl in range(y_count):
            for yh in range(2):
                if yl + 1 < y_count:
                    following = (z, yl + 1, yh)
                elif z + 1 < z_count:
                    following = (z + 1, 0, 1 - yh)
                else:
                    continue
                near.append((at(z, yl, yh), at(*following)))
                far.append((at(z, yl, yh), at(following[0], following[1], 1 - following[2])))
    return near, far


def shards(wave, left_block_environment, right_block_environment, source_block, sector_size):
    left = left_block_environment[0, 0]
    right = right_block_environment[0, 0]
    picks = source_block[0, 0]
    size = sector_size[0, 0]
    channels, width = left.shape[0], left.shape[1]
    half = channels // 2
    span = width + TILE
    unit = 2 * channels * width**3
    block_bytes = width * width * 2
    meta = jnp.stack([size, lax.axis_index("c").astype(jnp.int32), lax.axis_index("yh").astype(jnp.int32)])

    masked = jnp.where(live(size, (width, width)), wave[0, 0], jnp.zeros((), BF))
    pool_own = exchange(for_each(masked, 8), ("x", "yh"))
    pool_other = lax.ppermute(pool_own, "c", SWAP)
    copies = [pltpu.SemaphoreType.DMA((2,)), pltpu.SemaphoreType.DMA((channels,)), pltpu.SemaphoreType.DMA((channels,))]
    stack = pltpu.VMEM((channels, width, width), BF)
    first, message, stats, send, keep = call(
        first_kernel,
        [((width, width), BF), ((span, width), BF), ((TILE, width), BF),
         ((half * width + TILE, width), BF), ((half * width, width), BF)],
        [SMEM, SMEM, ANY, ANY, ANY, ANY],
        [stack, stack, stack, pltpu.VMEM((width, channels * width), BF), stack, *copies],
        4 * unit, 5 * channels * block_bytes,
    )(meta, picks, pool_own, pool_other, left, right)

    arrived = lax.ppermute(send, "c", SWAP)
    message_other = lax.ppermute(message, "yh", SWAP)
    parts = call(
        core_sum_kernel, one((4, 2 * width + TILE, width), BF), [VMEM] * 3, [], 1 << 20, 3 * half * block_bytes
    )(keep, stats, arrived)
    parts = exchange(parts, "x")
    row = call(row_sum_kernel, one((2 * width + TILE, width), BF), [VMEM], [], 1 << 20, 10 * block_bytes)(parts)
    near, far = routes(lax.axis_size("z"), lax.axis_size("yl"))
    from_far = lax.ppermute(row, YROW, far)
    from_near = lax.ppermute(row, YROW, near)

    both = jnp.concatenate([message, message_other], axis=0)
    two_own = exchange(for_each(both, 4), "x")
    two_other = lax.ppermute(two_own, "c", SWAP)
    g, base = call(
        pool_two_kernel,
        [((channels, width, width), BF), ((width, width), F32)],
        [SMEM, SMEM, ANY, ANY, ANY, ANY],
        [pltpu.VMEM((8, 2 * span, width), BF), stack, stack, *copies],
        2 * unit, 5 * channels * block_bytes,
    )(meta, picks, two_own, two_other, left, right)

    factor = 1.0 / (width * math.sqrt(channels_of(sector_size)))
    edge = call(
        lambda *refs: edge_kernel(factor, *refs), one((4, 2 * width, width), BF), [VMEM] * 2, [], 1 << 20, 12 * block_bytes
    )(from_near, from_far)
    edges_own = exchange(edge, "x")
    edges_other = lax.ppermute(edges_own, "c", SWAP)
    partial = call(
        lambda *refs: half_kernel(False, *refs), one((width, width), F32), [SMEM, VMEM, VMEM, VMEM], [], unit // 2,
        3 * half * block_bytes,
    )(meta, edges_own, g, base)
    second = call(
        lambda *refs: half_kernel(True, *refs), one((width, width), BF), [SMEM, VMEM, VMEM, VMEM], [], unit // 2,
        3 * half * block_bytes,
    )(meta, edges_other, g, partial)
    return (first[None, None], second[None, None])


def channels_of(sector_size):
    return sector_size.shape[1] * lax.axis_size(("x", "yh", "c"))


def solution(mesh):
    finer = Mesh(mesh.devices.reshape(mesh.shape["sec"] // 4, 4, 4, 2, 2), ("z", "yl", "x", "yh", "c"))
    sec, blk = ("z", "yl"), ("x", "yh", "c")
    return jax.shard_map(
        shards,
        mesh=finer,
        in_specs=(
            P(sec, blk, None, None),
            P(sec, blk, None, None, None),
            P(sec, blk, None, None, None),
            P(sec, blk, None),
            P(sec, blk),
        ),
        out_specs=(P(sec, blk, None, None), P(sec, blk, None, None)),
        check_vma=False,
    )
```

time: 218 us -> 156 us (0.72)
  the two profiles are of different devices: /device:TPU:457 before, /device:TPU:9 now
where the time goes in v1:
time: 156 us
  waiting for transfers between devices  49.6 us (32%)
  blocking collectives  39.4 us (25%)
  Pallas kernels  29.5 us (19%)
  starting transfers between devices  28.9 us (19%)
  local copies, waits for them, and re-layouts  5.94 us (4%)
    all_to_all x1, blocking collectives, exchange(): return lax.all_to_all(value, axes, 0, 0, tiled=True)  39.4 us
    ppermute x1, waiting for transfers between devices, shards(): from_far = lax.ppermute(row, YROW, far)  20.4 us
    all_to_all x3, waiting for transfers between devices, exchange(): return lax.all_to_all(value, axes, 0, 0, tiled=True)  16 us
    pallas_call x1, Pallas kernels, shards(): call(first_kernel, [((width, width), BF), ((span, width), BF), ((TILE, wi...  13.1 us
    pallas_call x1, Pallas kernels, shards(): call(pool_two_kernel, [((channels, width, width), BF), ((width, width), F...  11.3 us
    all_to_all x3, starting transfers between devices, exchange(): return lax.all_to_all(value, axes, 0, 0, tiled=True)  11.2 us
    ppermute x1, waiting for transfers between devices, shards(): message_other = lax.ppermute(message, 'yh', SWAP)  8.55 us
    unnamed x10, local copies, waits for them, and re-layouts  4.78 us
  transfers between devices with their start and end apart: 10, of which 6 were waited for; matrix products, arithmetic and copies ran while one was open for 0% of the time, Pallas kernels for 9%

profile of v1, /device:TPU:9, one launch (start us, length us, event | category | flops | bytes accessed | tf_op | source)
XLA Modules:
  0.0 155.8 jit_solution(9868619496784392059)
XLA Ops:
  2.4 39.4 %all_to_all.20.pool_own = bf16[8,256,256]{2,1,0:T(8,128)(2,1)S(1)} all-to-all(bf16[8,256,256]{2,1,0:T(8,128)(2,1)S(1)} %broadcast_in_dim.23), channel_id=1, replica_groups=mesh['z'=8,'yl'=4,'x'=4,'yh'=2,'c'=2] {'x','yh'}, dimensions={0} | all-to-all | bytes 2097152 | tf_op jit(solution)/shard_map/all_to_all | solution.py:207
  41.8 2.6 %collective-permute-start = (bf16[8,256,256]{2,1,0:T(8,128)(2,1)S(1)}, bf16[8,256,256]{2,1,0:T(8,128)(2,1)}, u32[]{:S(2)}, u32[]{:S(2)}) collective-permute-start(bf16[8,256,256]{2,1,0:T(8,128)(2,1)S(1)} %all_to_all.20.pool_own), channel_id=1, source_target_pairs={{0,1},{1,0},{2,3},{3,2},{4,5},{5,4},{6,7},{7,6},{8,9},{9,8},{10,11... | collective-permute-start | bytes 3145736 | tf_op jit(solution)/shard_map/ppermute | solution.py:243
  44.5 2.3 %collective-permute-done.pool_other = bf16[8,256,256]{2,1,0:T(8,128)(2,1)} collective-permute-done((bf16[8,256,256]{2,1,0:T(8,128)(2,1)S(1)}, bf16[8,256,256]{2,1,0:T(8,128)(2,1)}, u32[]{:S(2)}, u32[]{:S(2)}) %collective-permute-start) | collective-permute-done | bytes 1048608 | tf_op jit(solution)/shard_map/ppermute | solution.py:243
  46.8 1.6 %copy-done.2 = bf16[1,1,16,256,256]{4,3,2,1,0:T(8,128)(2,1)S(1)} copy-done((bf16[1,1,16,256,256]{4,3,2,1,0:T(8,128)(2,1)S(1)}, bf16[1,1,16,256,256]{4,3,2,1,0:T(8,128)(2,1)}, u32[]{:S(2)}) %copy-start.2) | copy-done | bytes 2097176
  48.4 13.1 %shard_map.68 = (bf16[256,256]{1,0:T(8,128)(2,1)}, bf16[272,256]{1,0:T(8,128)(2,1)S(1)}, bf16[16,256]{1,0:T(8,128)(2,1)S(1)}, bf16[2064,256]{1,0:T(8,128)(2,1)S(1)}, bf16[2048,256]{1,0:T(8,128)(2,1)S(1)}) custom-call(s32[3]{0:T(128)S(1)} %pad_add_fusion.meta.refs_0_, s32[16]{0:T(128)S(1)} %bitcast.17, bf16[8,256,256]{2,1,0:T(8,128)(2,1)S(1)} %all_to_all.20.pool_own, ...), custom_call_target="tpu_custom_call" | custom-call | flops 2147483648 | bytes 10485760 | tf_op jit(solution)/shard_map/pallas_call | solution.py:246
  61.5 2.3 %collective-permute-start.1 = (bf16[2064,256]{1,0:T(8,128)(2,1)S(1)}, bf16[2064,256]{1,0:T(8,128)(2,1)S(1)}, u32[]{:S(2)}, u32[]{:S(2)}) collective-permute-start(bf16[2064,256]{1,0:T(8,128)(2,1)S(1)} %get-tuple-element.12), channel_id=1, source_target_pairs={{0,1},{1,0},{2,3},{3,2},{4,5},{5,4},{6,7},{7,6},{8,9},{9,8},{10,11... | collective-permute-start | bytes 3170312 | tf_op jit(solution)/shard_map/ppermute | solution.py:255
  63.8 2.3 %collective-permute-done.1.arrived = bf16[2064,256]{1,0:T(8,128)(2,1)S(1)} collective-permute-done((bf16[2064,256]{1,0:T(8,128)(2,1)S(1)}, bf16[2064,256]{1,0:T(8,128)(2,1)S(1)}, u32[]{:S(2)}, u32[]{:S(2)}) %collective-permute-start.1) | collective-permute-done | bytes 1056800 | tf_op jit(solution)/shard_map/ppermute | solution.py:255
  66.1 1.2 shard_map.69
  67.3 3.5 %all-to-all-start.1 = ((bf16[4,528,256]{2,1,0:T(8,128)(2,1)}), bf16[4,528,256]{2,1,0:T(8,128)(2,1)S(1)}, u32[]{:S(2)}, u32[]{:S(2)}) async-start(bf16[4,528,256]{2,1,0:T(8,128)(2,1)} %shard_map.69), calls=%async_computation.1 | async-start | bytes 2162688 | tf_op jit(solution)/shard_map/all_to_all | solution.py:207
  70.9 2.1 %collective-permute-start.5 = (bf16[272,256]{1,0:T(8,128)(2,1)S(1)}, bf16[272,256]{1,0:T(8,128)(2,1)S(1)}, u32[]{:S(2)}, u32[]{:S(2)}) collective-permute-start(bf16[272,256]{1,0:T(8,128)(2,1)S(1)} %get-tuple-element.13), channel_id=1, source_target_pairs={{0,2},{2,0},{1,3},{3,1},{4,6},{6,4},{5,7},{7,5},{8,10},{10,8},{9,1... | collective-permute-start | bytes 417800 | tf_op jit(solution)/shard_map/ppermute | solution.py:256
  73.0 8.5 %collective-permute-done.5 = bf16[272,256]{1,0:T(8,128)(2,1)S(1)} collective-permute-done((bf16[272,256]{1,0:T(8,128)(2,1)S(1)}, bf16[272,256]{1,0:T(8,128)(2,1)S(1)}, u32[]{:S(2)}, u32[]{:S(2)}) %collective-permute-start.5) | collective-permute-done | bytes 139296 | tf_op jit(solution)/shard_map/ppermute | solution.py:256
  81.5 4.5 %all-to-all-done.1.arrived = bf16[4,528,256]{2,1,0:T(8,128)(2,1)S(1)} async-done(((bf16[4,528,256]{2,1,0:T(8,128)(2,1)}), bf16[4,528,256]{2,1,0:T(8,128)(2,1)S(1)}, u32[]{:S(2)}, u32[]{:S(2)}) %all-to-all-start.1) | async-done | bytes 1081376 | tf_op jit(solution)/shard_map/all_to_all | solution.py:207
  87.1 3.5 %all-to-all-start.3 = ((bf16[4,544,256]{2,1,0:T(8,128)(2,1)}), bf16[4,544,256]{2,1,0:T(8,128)(2,1)S(1)}, u32[]{:S(2)}, u32[]{:S(2)}) async-start(bf16[4,544,256]{2,1,0:T(8,128)(2,1)} %broadcast_in_dim.25), calls=%async_computation.3 | async-start | bytes 2228224 | tf_op jit(solution)/shard_map/all_to_all | solution.py:207
  90.8 1.9 %collective-permute-start.3 = (bf16[528,256]{1,0:T(8,128)(2,1)S(1)}, bf16[528,256]{1,0:T(8,128)(2,1)S(1)}, u32[]{:S(2)}, u32[]{:S(2)}) collective-permute-start(bf16[528,256]{1,0:T(8,128)(2,1)S(1)} %shard_map.70), channel_id=1, source_target_pairs={{0,18},{2,16},{16,34},{18,32},{32,50},{34,48},{48,64},{50,66},{64,... | collective-permute-start | bytes 811016 | tf_op jit(solution)/shard_map/ppermute | solution.py:263
  92.7 2.3 %collective-permute-start.2 = (bf16[528,256]{1,0:T(8,128)(2,1)S(1)}, bf16[528,256]{1,0:T(8,128)(2,1)S(1)}, u32[]{:S(2)}, u32[]{:S(2)}) collective-permute-start(bf16[528,256]{1,0:T(8,128)(2,1)S(1)} %shard_map.70), channel_id=1, source_target_pairs={{0,16},{2,18},{16,32},{18,34},{32,48},{34,50},{48,66},{50,64},{64,... | collective-permute-start | bytes 811016 | tf_op jit(solution)/shard_map/ppermute | solution.py:264
  95.0 20.4 %collective-permute-done.3.refs_1_ = bf16[528,256]{1,0:T(8,128)(2,1)S(1)} collective-permute-done((bf16[528,256]{1,0:T(8,128)(2,1)S(1)}, bf16[528,256]{1,0:T(8,128)(2,1)S(1)}, u32[]{:S(2)}, u32[]{:S(2)}) %collective-permute-start.3) | collective-permute-done | bytes 270368 | tf_op jit(solution)/shard_map/ppermute | solution.py:263
  116.5 4.2 %all-to-all-start.2 = ((bf16[4,512,256]{2,1,0:T(8,128)(2,1)}), bf16[4,512,256]{2,1,0:T(8,128)(2,1)S(1)}, u32[]{:S(2)}, u32[]{:S(2)}) async-start(bf16[4,512,256]{2,1,0:T(8,128)(2,1)} %shard_map.71), calls=%async_computation.2 | async-start | bytes 2097152 | tf_op jit(solution)/shard_map/all_to_all | solution.py:207
  120.7 2.8 %collective-permute-start.6 = (bf16[4,544,256]{2,1,0:T(8,128)(2,1)S(1)}, bf16[4,544,256]{2,1,0:T(8,128)(2,1)S(1)}, u32[]{:S(2)}, u32[]{:S(2)}) collective-permute-start(bf16[4,544,256]{2,1,0:T(8,128)(2,1)S(1)} %all-to-all-done.3.own), channel_id=1, source_target_pairs={{0,1},{1,0},{2,3},{3,2},{4,5},{5,4},{6,7},{7,6},{8,9},{9,8},{10,11... | collective-permute-start | bytes 3342344 | tf_op jit(solution)/shard_map/ppermute | solution.py:268
  123.5 11.5 %all-to-all-done.2.refs_1_ = bf16[4,512,256]{2,1,0:T(8,128)(2,1)S(1)} async-done(((bf16[4,512,256]{2,1,0:T(8,128)(2,1)}), bf16[4,512,256]{2,1,0:T(8,128)(2,1)S(1)}, u32[]{:S(2)}, u32[]{:S(2)}) %all-to-all-start.2) | async-done | bytes 1048608 | tf_op jit(solution)/shard_map/all_to_all | solution.py:207
  135.0 3.6 %collective-permute-start.4 = (bf16[4,512,256]{2,1,0:T(8,128)(2,1)S(1)}, bf16[4,512,256]{2,1,0:T(8,128)(2,1)S(1)}, u32[]{:S(2)}, u32[]{:S(2)}) collective-permute-start(bf16[4,512,256]{2,1,0:T(8,128)(2,1)S(1)} %all-to-all-done.2.refs_1_), channel_id=1, source_target_pairs={{0,1},{1,0},{2,3},{3,2},{4,5},{5,4},{6,7},{7,6},{8,9},{9,8},{10,11... | collective-permute-start | bytes 3145736 | tf_op jit(solution)/shard_map/ppermute | solution.py:282
  138.7 1.6 %copy-done.1 = bf16[1,1,16,256,256]{4,3,2,1,0:T(8,128)(2,1)S(1)} copy-done((bf16[1,1,16,256,256]{4,3,2,1,0:T(8,128)(2,1)S(1)}, bf16[1,1,16,256,256]{4,3,2,1,0:T(8,128)(2,1)}, u32[]{:S(2)}) %copy-start.1) | copy-done | bytes 2097176
  140.3 1.6 %copy-done.3 = bf16[1,1,16,256,256]{4,3,2,1,0:T(8,128)(2,1)S(1)} copy-done((bf16[1,1,16,256,256]{4,3,2,1,0:T(8,128)(2,1)S(1)}, bf16[1,1,16,256,256]{4,3,2,1,0:T(8,128)(2,1)}, u32[]{:S(2)}) %copy-start.3) | copy-done | bytes 2097176
  141.9 11.3 %shard_map.72 = (bf16[16,256,256]{2,1,0:T(8,128)(2,1)S(1)}, f32[256,256]{1,0:T(8,128)S(1)}) custom-call(s32[3]{0:T(128)S(1)} %pad_add_fusion.meta.refs_0_, s32[16]{0:T(128)S(1)} %bitcast.18, bf16[4,544,256]{2,1,0:T(8,128)(2,1)S(1)} %all-to-all-done.3.own, bf16[4,544,256]{2,1,0:T(8,128)(2,1)S(1)} %collective-permute-done.6.other, ...), custom_call_target="tpu_custom_call" | custom-call | flops 1073741824 | bytes 10485760 | tf_op jit(solution)/shard_map/pallas_call | solution.py:269
  154.2 1.6 %shard_map.74 = bf16[256,256]{1,0:T(8,128)(2,1)} custom-call(s32[3]{0:T(128)S(1)} %pad_add_fusion.meta.refs_0_, bf16[4,512,256]{2,1,0:T(8,128)(2,1)S(1)} %collective-permute-done.4.refs_1_, bf16[16,256,256]{2,1,0:T(8,128)(2,1)S(1)} %get-tuple-element.14.refs_2_, f32[256,256]{1,0:T(8,128)S(1)} %shard_map.73.refs_3_), custom_call_target="tpu_custom_call" | custom-call | flops 268435456 | bytes 3145728 | tf_op jit(solution)/shard_map/pallas_call | solution.py:287
  (20 shorter events, 4.5 us)
Async XLA Ops:
  2.4 44.4 %copy-start = (bf16[1,1,16,256,256]{4,3,2,1,0:T(8,128)(2,1)S(1)}, bf16[1,1,16,256,256]{4,3,2,1,0:T(8,128)(2,1)}, u32[]{:S(2)}) copy-start(bf16[1,1,16,256,256]{4,3,2,1,0:T(8,128)(2,1)} %param.6) | copy-start | bytes 6291460
  2.4 44.4 %copy-start.4 = (s32[1,1,16]{2,1,0:T(1,128)S(1)}, s32[1,1,16]{2,1,0:T(1,128)}, u32[]{:S(2)}) copy-start(s32[1,1,16]{2,1,0:T(1,128)} %param.8) | copy-start | bytes 196
  41.8 5.0 %collective-permute-start = (bf16[8,256,256]{2,1,0:T(8,128)(2,1)S(1)}, bf16[8,256,256]{2,1,0:T(8,128)(2,1)}, u32[]{:S(2)}, u32[]{:S(2)}) collective-permute-start(bf16[8,256,256]{2,1,0:T(8,128)(2,1)S(1)} %all_to_all.20.pool_own), channel_id=1, source_target_pairs={{0,1},{1,0},{2,3},{3,2},{4,5},{5,4},{6,7},{7,6},{8,9},{9,8},{10,11... | collective-permute-start | bytes 3145736 | tf_op jit(solution)/shard_map/ppermute | solution.py:243
  46.8 1.6 %copy-start.2 = (bf16[1,1,16,256,256]{4,3,2,1,0:T(8,128)(2,1)S(1)}, bf16[1,1,16,256,256]{4,3,2,1,0:T(8,128)(2,1)}, u32[]{:S(2)}) copy-start(bf16[1,1,16,256,256]{4,3,2,1,0:T(8,128)(2,1)} %param.7) | copy-start | bytes 6291460
  61.5 4.6 %collective-permute-start.1 = (bf16[2064,256]{1,0:T(8,128)(2,1)S(1)}, bf16[2064,256]{1,0:T(8,128)(2,1)S(1)}, u32[]{:S(2)}, u32[]{:S(2)}) collective-permute-start(bf16[2064,256]{1,0:T(8,128)(2,1)S(1)} %get-tuple-element.12), channel_id=1, source_target_pairs={{0,1},{1,0},{2,3},{3,2},{4,5},{5,4},{6,7},{7,6},{8,9},{9,8},{10,11... | collective-permute-start | bytes 3170312 | tf_op jit(solution)/shard_map/ppermute | solution.py:255
  67.3 18.7 %all-to-all-start.1 = ((bf16[4,528,256]{2,1,0:T(8,128)(2,1)}), bf16[4,528,256]{2,1,0:T(8,128)(2,1)S(1)}, u32[]{:S(2)}, u32[]{:S(2)}) async-start(bf16[4,528,256]{2,1,0:T(8,128)(2,1)} %shard_map.69), calls=%async_computation.1 | async-start | bytes 2162688 | tf_op jit(solution)/shard_map/all_to_all | solution.py:207
  70.9 10.7 %collective-permute-start.5 = (bf16[272,256]{1,0:T(8,128)(2,1)S(1)}, bf16[272,256]{1,0:T(8,128)(2,1)S(1)}, u32[]{:S(2)}, u32[]{:S(2)}) collective-permute-start(bf16[272,256]{1,0:T(8,128)(2,1)S(1)} %get-tuple-element.13), channel_id=1, source_target_pairs={{0,2},{2,0},{1,3},{3,1},{4,6},{6,4},{5,7},{7,5},{8,10},{10,8},{9,1... | collective-permute-start | bytes 417800 | tf_op jit(solution)/shard_map/ppermute | solution.py:256
  87.1 29.4 %all-to-all-start.3 = ((bf16[4,544,256]{2,1,0:T(8,128)(2,1)}), bf16[4,544,256]{2,1,0:T(8,128)(2,1)S(1)}, u32[]{:S(2)}, u32[]{:S(2)}) async-start(bf16[4,544,256]{2,1,0:T(8,128)(2,1)} %broadcast_in_dim.25), calls=%async_computation.3 | async-start | bytes 2228224 | tf_op jit(solution)/shard_map/all_to_all | solution.py:207
  90.8 24.7 %collective-permute-start.3 = (bf16[528,256]{1,0:T(8,128)(2,1)S(1)}, bf16[528,256]{1,0:T(8,128)(2,1)S(1)}, u32[]{:S(2)}, u32[]{:S(2)}) collective-permute-start(bf16[528,256]{1,0:T(8,128)(2,1)S(1)} %shard_map.70), channel_id=1, source_target_pairs={{0,18},{2,16},{16,34},{18,32},{32,50},{34,48},{48,64},{50,66},{64,... | collective-permute-start | bytes 811016 | tf_op jit(solution)/shard_map/ppermute | solution.py:263
  92.7 22.8 %collective-permute-start.2 = (bf16[528,256]{1,0:T(8,128)(2,1)S(1)}, bf16[528,256]{1,0:T(8,128)(2,1)S(1)}, u32[]{:S(2)}, u32[]{:S(2)}) collective-permute-start(bf16[528,256]{1,0:T(8,128)(2,1)S(1)} %shard_map.70), channel_id=1, source_target_pairs={{0,16},{2,18},{16,32},{18,34},{32,48},{34,50},{48,66},{50,64},{64,... | collective-permute-start | bytes 811016 | tf_op jit(solution)/shard_map/ppermute | solution.py:264
  116.5 18.5 %all-to-all-start.2 = ((bf16[4,512,256]{2,1,0:T(8,128)(2,1)}), bf16[4,512,256]{2,1,0:T(8,128)(2,1)S(1)}, u32[]{:S(2)}, u32[]{:S(2)}) async-start(bf16[4,512,256]{2,1,0:T(8,128)(2,1)} %shard_map.71), calls=%async_computation.2 | async-start | bytes 2097152 | tf_op jit(solution)/shard_map/all_to_all | solution.py:207
  120.7 18.0 %collective-permute-start.6 = (bf16[4,544,256]{2,1,0:T(8,128)(2,1)S(1)}, bf16[4,544,256]{2,1,0:T(8,128)(2,1)S(1)}, u32[]{:S(2)}, u32[]{:S(2)}) collective-permute-start(bf16[4,544,256]{2,1,0:T(8,128)(2,1)S(1)} %all-to-all-done.3.own), channel_id=1, source_target_pairs={{0,1},{1,0},{2,3},{3,2},{4,5},{5,4},{6,7},{7,6},{8,9},{9,8},{10,11... | collective-permute-start | bytes 3342344 | tf_op jit(solution)/shard_map/ppermute | solution.py:268
  135.0 19.2 %collective-permute-start.4 = (bf16[4,512,256]{2,1,0:T(8,128)(2,1)S(1)}, bf16[4,512,256]{2,1,0:T(8,128)(2,1)S(1)}, u32[]{:S(2)}, u32[]{:S(2)}) collective-permute-start(bf16[4,512,256]{2,1,0:T(8,128)(2,1)S(1)} %all-to-all-done.2.refs_1_), channel_id=1, source_target_pairs={{0,1},{1,0},{2,3},{3,2},{4,5},{5,4},{6,7},{7,6},{8,9},{9,8},{10,11... | collective-permute-start | bytes 3145736 | tf_op jit(solution)/shard_map/ppermute | solution.py:282
  138.7 1.6 %copy-start.1 = (bf16[1,1,16,256,256]{4,3,2,1,0:T(8,128)(2,1)S(1)}, bf16[1,1,16,256,256]{4,3,2,1,0:T(8,128)(2,1)}, u32[]{:S(2)}) copy-start(bf16[1,1,16,256,256]{4,3,2,1,0:T(8,128)(2,1)} %param.6) | copy-start | bytes 6291460
  140.3 1.6 %copy-start.3 = (bf16[1,1,16,256,256]{4,3,2,1,0:T(8,128)(2,1)S(1)}, bf16[1,1,16,256,256]{4,3,2,1,0:T(8,128)(2,1)}, u32[]{:S(2)}) copy-start(bf16[1,1,16,256,256]{4,3,2,1,0:T(8,128)(2,1)} %param.7) | copy-start | bytes 6291460

commit v2 on v1

v2 whole, which is shorter than its diff:
```python
import math

import jax
import jax.numpy as jnp
from jax import lax
from jax.experimental import pallas as pl
from jax.experimental.pallas import tpu as pltpu
from jax.sharding import Mesh
from jax.sharding import PartitionSpec as P


BF = jnp.bfloat16
F32 = jnp.float32
TILE = 16
YROW = ("z", "yl", "yh")
SWAP = [(0, 1), (1, 0)]
VMEM = pl.BlockSpec(memory_space=pltpu.VMEM)
SMEM = pl.BlockSpec(memory_space=pltpu.SMEM)
ANY = pl.BlockSpec(memory_space=pl.ANY)
PARAMS = pltpu.CompilerParams(vmem_limit_bytes=16 << 20)


def dot(a, b):
    return jnp.dot(a, b, preferred_element_type=F32)


def pieces(value):
    high = value.astype(BF).astype(F32)
    mid = (value - high).astype(BF).astype(F32)
    return high, mid, value - high - mid


def pack(squares, count):
    width = squares.shape[-1]
    row = lax.broadcasted_iota(jnp.int32, (TILE, width), 0)
    tile = jnp.zeros((TILE, width), F32)
    for at, part in enumerate(pieces(squares) + pieces(count)):
        tile = jnp.where(row == at, jnp.broadcast_to(part, (TILE, width)), tile)
    return tile.astype(BF)


def unpack(tile):
    t = tile.astype(F32)
    return t[0:1] + t[1:2] + t[2:3], t[3:4] + t[4:5] + t[5:6]


def live(size, shape):
    rows = lax.broadcasted_iota(jnp.int32, shape, 0)
    columns = lax.broadcasted_iota(jnp.int32, shape, 1)
    return (rows < size) & (columns < size)


def place(source, meta):
    x, yh, c = source // 4, (source // 2) % 2, source % 2
    return lax.rem(c + meta[1], 2), lax.rem(yh + meta[2], 2), lax.rem(x + 4 - meta[3], 4)


def channel(meta, side, j):
    return side * 8 + lax.rem(meta[3] + j // 2, 4) * 2 + j % 2


def first_kernel(meta, picks, pool, left, right, first_out, message, stats, send, turned_out, inner, lv):
    channels, width = left.shape[0], left.shape[1]
    half = channels // 2
    for t in range(channels):
        c, yh, x = place(picks[t], meta)
        inner[:, t * width:(t + 1) * width] = dot(left[t], pool[(c * 2 + yh) * 4 + x]).astype(BF)
    product = dot(inner[...], right[...].reshape(channels * width, width))
    size = meta[0]
    product = jnp.where(live(size, product.shape), product, 0.0).astype(BF)
    first_out[...] = product
    message[0:width, :] = product
    value = product.astype(F32)
    columns = jnp.sum(value * value, axis=0, keepdims=True)
    squares = jnp.broadcast_to(jnp.sum(columns, axis=1, keepdims=True), (1, width))
    count = jnp.full((1, width), size * size, jnp.int32).astype(F32)
    tile = pack(squares, count)
    message[width:width + TILE, :] = tile
    stats[...] = tile
    send[half * width:half * width + TILE, :] = tile
    turned = value.T.astype(BF)
    turned_out[...] = turned
    for j in range(half):
        lv[j] = dot(left[channel(meta, 1 - meta[1], j)], product).astype(BF)
    for j in range(half):
        send[j * width:(j + 1) * width, :] = dot(turned, lv[j]).astype(BF)


def keep_kernel(meta, message, turned, left, keep, lv):
    half, width = left.shape[0] // 2, left.shape[1]
    first = message[0:width, :]
    for j in range(half):
        lv[j] = dot(left[channel(meta, meta[1], j)], first).astype(BF)
    for j in range(half):
        keep[j * width:(j + 1) * width, :] = dot(turned[...], lv[j]).astype(BF)


def core_sum_kernel(keep, stats, arrived, *outs):
    rows = keep.shape[0]
    quarter = rows // 4
    q0, c0 = unpack(stats[...])
    q1, c1 = unpack(arrived[rows:rows + TILE, :])
    tile = pack(q0 + q1, c0 + c1)
    for step, out in enumerate(outs):
        at = step * quarter
        out[0:quarter, :] = (
            keep[at:at + quarter, :].astype(F32) + arrived[at:at + quarter, :].astype(F32)
        ).astype(BF)
        out[quarter:quarter + TILE, :] = tile


def row_sum_kernel(a, b, c, d, out):
    rows = out.shape[0] - TILE
    out[0:rows, :] = (
        (a[0:rows, :].astype(F32) + b[0:rows, :].astype(F32)) + (c[0:rows, :].astype(F32) + d[0:rows, :].astype(F32))
    ).astype(BF)
    sums = [unpack(part[rows:rows + TILE, :]) for part in (a, b, c, d)]
    out[rows:rows + TILE, :] = pack(
        (sums[0][0] + sums[1][0]) + (sums[2][0] + sums[3][0]), (sums[0][1] + sums[1][1]) + (sums[2][1] + sums[3][1])
    )


def edge_kernel(factor, near, far, out):
    rows = near.shape[0] - TILE
    q0, c0 = unpack(near[rows:rows + TILE, :])
    q1, c1 = unpack(far[rows:rows + TILE, :])
    weight = factor / ((q0 + q1) / jnp.maximum(c0 + c1, 1.0) + 1e-6)
    total = near[0:rows, :].astype(F32) + far[0:rows, :].astype(F32)
    out[...] = (total * weight).astype(BF)


def pool_two_kernel(meta, picks, pool, left, right, g_out, base):
    channels, width = left.shape[0], left.shape[1]
    span = width + TILE
    squares = count = jnp.zeros((1, width), F32)
    for at in range(16):
        q, c = unpack(pool[at * span + width:(at + 1) * span, :])
        squares, count = squares + q, count + c
    scale = lax.rsqrt(squares / count + 1e-6)
    for t in range(channels):
        c, yh, x = place(picks[t], meta)
        start = pl.multiple_of(((c * 4 + x) * 2 + yh) * span, TILE)
        g_out[t] = (dot(pool[pl.ds(start, width), :], right[t]) * scale).astype(BF)
    total = dot(left[0], g_out[0])
    for t in range(1, channels):
        total = total + dot(left[t], g_out[t])
    base[...] = total


def half_kernel(final, meta, edges, g, start, out):
    width = g.shape[1]
    side = meta[1] if not final else 1 - meta[1]
    total = start[...]
    for j in range(edges.shape[0] // width):
        total = total + dot(edges[j * width:(j + 1) * width, :], g[channel(meta, side, j)])
    if final:
        total = jnp.where(live(meta[0], total.shape), total, 0.0)
    out[...] = total.astype(out.dtype)


def call(kernel, shapes, specs, scratch, flops, moved):
    several = isinstance(shapes, (list, tuple))
    return pl.pallas_call(
        kernel,
        out_shape=[jax.ShapeDtypeStruct(*s) for s in shapes] if several else shapes,
        in_specs=specs,
        out_specs=[VMEM] * len(shapes) if several else VMEM,
        scratch_shapes=scratch,
        compiler_params=PARAMS,
        cost_estimate=pl.CostEstimate(flops=flops, bytes_accessed=moved, transcendentals=0),
    )


def one(shape, dtype):
    return jax.ShapeDtypeStruct(shape, dtype)


def along_x(value, step):
    count = lax.axis_size("x")
    return lax.ppermute(value, "x", [(i, (i + step) % count) for i in range(count)])


def round_x(value):
    far = along_x(value, 2)
    return [value, along_x(value, 3), far, along_x(value, 1)]


def routes(z_count, y_count):
    def at(z, yl, yh):
        return (z * y_count + yl) * 2 + yh

    near, far = [], []
    for z in range(z_count):
        for yl in range(y_count):
            for yh in range(2):
                if yl + 1 < y_count:
                    following = (z, yl + 1, yh)
                elif z + 1 < z_count:
                    following = (z + 1, 0, 1 - yh)
                else:
                    continue
                near.append((at(z, yl, yh), at(*following)))
                far.append((at(z, yl, yh), at(following[0], following[1], 1 - following[2])))
    return near, far


def body(wave, left_block_environment, right_block_environment, source_block, sector_size):
    left = left_block_environment[0, 0]
    right = right_block_environment[0, 0]
    picks = source_block[0, 0]
    size = sector_size[0, 0]
    channels, width = left.shape[0], left.shape[1]
    half = channels // 2
    span = width + TILE
    unit = 2 * channels * width**3
    block_bytes = width * width * 2
    meta = jnp.stack([size, lax.axis_index("c").astype(jnp.int32), lax.axis_index("yh").astype(jnp.int32),
                      lax.axis_index("x").astype(jnp.int32)])

    masked = jnp.where(live(size, (width, width)), wave[0, 0], jnp.zeros((), BF))
    masked_other = lax.ppermute(masked, "yh", SWAP)
    own = jnp.stack(round_x(masked))
    across = lax.ppermute(own, "c", SWAP)
    own_other = jnp.stack(round_x(masked_other))
    across_other = lax.ppermute(own_other, "c", SWAP)
    pool = jnp.concatenate([own, own_other, across, across_other], axis=0)
    stack = pltpu.VMEM((half, width, width), BF)
    first, message, stats, send, turned = call(
        first_kernel,
        [((width, width), BF), ((span, width), BF), ((TILE, width), BF),
         ((half * width + TILE, width), BF), ((width, width), BF)],
        [SMEM, SMEM, VMEM, VMEM, VMEM],
        [pltpu.VMEM((width, channels * width), BF), stack],
        3 * unit, 4 * channels * block_bytes,
    )(meta, picks, pool, left, right)

    arrived = lax.ppermute(send, "c", SWAP)
    message_other = lax.ppermute(message, "yh", SWAP)
    keep = call(
        keep_kernel, one((half * width, width), BF), [SMEM, VMEM, VMEM, VMEM], [stack], unit, 2 * channels * block_bytes
    )(meta, message, turned, left)
    parts = call(
        core_sum_kernel, [((2 * width + TILE, width), BF)] * 4, [VMEM] * 3, [], 1 << 20, 3 * half * block_bytes
    )(keep, stats, arrived)
    arrived_x = [along_x(parts[2], 2), along_x(parts[1], 1), along_x(parts[3], 3)]
    row = call(
        row_sum_kernel, one((2 * width + TILE, width), BF), [VMEM] * 4, [], 1 << 20, 10 * block_bytes
    )(parts[0], *arrived_x)
    near, far = routes(lax.axis_size("z"), lax.axis_size("yl"))
    from_far = lax.ppermute(row, YROW, far)
    from_near = lax.ppermute(row, YROW, near)

    both = jnp.concatenate([message, message_other], axis=0)
    two_own = jnp.concatenate(round_x(both))
    two_other = lax.ppermute(two_own, "c", SWAP)
    pool_two = jnp.concatenate([two_own, two_other])
    g, base = call(
        pool_two_kernel,
        [((channels, width, width), BF), ((width, width), F32)],
        [SMEM, SMEM, VMEM, VMEM, VMEM],
        [],
        2 * unit, 4 * channels * block_bytes,
    )(meta, picks, pool_two, left, right)

    factor = 1.0 / (width * math.sqrt(channels_of(sector_size)))
    edge = call(
        lambda *refs: edge_kernel(factor, *refs), one((2 * width, width), BF), [VMEM] * 2, [], 1 << 20, 12 * block_bytes
    )(from_near, from_far)
    edges_own = jnp.concatenate(round_x(edge))
    edges_other = lax.ppermute(edges_own, "c", SWAP)
    partial = call(
        lambda *refs: half_kernel(False, *refs), one((width, width), F32), [SMEM, VMEM, VMEM, VMEM], [], unit // 2,
        3 * half * block_bytes,
    )(meta, edges_own, g, base)
    second = call(
        lambda *refs: half_kernel(True, *refs), one((width, width), BF), [SMEM, VMEM, VMEM, VMEM], [], unit // 2,
        3 * half * block_bytes,
    )(meta, edges_other, g, partial)
    return (first[None, None], second[None, None])


def channels_of(sector_size):
    return sector_size.shape[1] * lax.axis_size(("x", "yh", "c"))


def solution(mesh):
    finer = Mesh(mesh.devices.reshape(mesh.shape["sec"] // 4, 4, 4, 2, 2), ("z", "yl", "x", "yh", "c"))
    sec, blk = ("z", "yl"), ("x", "yh", "c")
    return jax.shard_map(
        body,
        mesh=finer,
        in_specs=(
            P(sec, blk, None, None),
            P(sec, blk, None, None, None),
            P(sec, blk, None, None, None),
            P(sec, blk, None),
            P(sec, blk),
        ),
        out_specs=(P(sec, blk, None, None), P(sec, blk, None, None)),
        check_vma=False,
    )
```

time: 156 us -> 152 us (0.974)
  the two profiles are of different devices: /device:TPU:9 before, /device:TPU:201 now
where the time goes in v2:
time: 152 us; the launch traced here: 151 us
  starting transfers between devices  83.6 us (55%)
  waiting for transfers between devices  52.8 us (35%)
  Pallas kernels  10 us (7%)
  other arithmetic  2.31 us (2%)
  between operations  1.8 us (1%)
    ppermute x15, starting transfers between devices, along_x(): lax.ppermute(value, 'x', [(i, (i + step) % count) for i in range(count)])  45.3 us
    ppermute x15, waiting for transfers between devices, along_x(): lax.ppermute(value, 'x', [(i, (i + step) % count) for i in range(count)])  27.1 us
    ppermute x1, waiting for transfers between devices, body(): from_far = lax.ppermute(row, YROW, far)  17.4 us
    ppermute x1, starting transfers between devices, body(): message_other = lax.ppermute(message, 'yh', SWAP)  6.93 us
    ppermute x1, waiting for transfers between devices, body(): message_other = lax.ppermute(message, 'yh', SWAP)  6.91 us
    ppermute x1, starting transfers between devices, body(): masked_other = lax.ppermute(masked, 'yh', SWAP)  6.55 us
    ppermute x1, starting transfers between devices, body(): across_other = lax.ppermute(own_other, 'c', SWAP)  5.1 us
    ppermute x1, starting transfers between devices, body(): from_near = lax.ppermute(row, YROW, near)  4.18 us
  transfers between devices with their start and end apart: 24, of which 9 were waited for; matrix products, arithmetic and copies ran while one was open for 1% of the time, Pallas kernels for 3%

profile of v2, /device:TPU:201, one launch (start us, length us, event | category | flops | bytes accessed | tf_op | source)
XLA Modules:
  0.0 150.9 jit_solution(15349935111065368200)
XLA Ops:
  2.3 4.4 %collective-permute-start = (bf16[256,256]{1,0:T(8,128)(2,1)S(1)}, bf16[256,256]{1,0:T(8,128)(2,1)S(1)}, u32[]{:S(2)}, u32[]{:S(2)}) collective-permute-start(bf16[256,256]{1,0:T(8,128)(2,1)S(1)} %and_select_fusion), channel_id=1, source_target_pairs={{0,12},{4,0},{8,4},{12,8},{1,13},{5,1},{9,5},{13,9},{2,14},{6,2},{... | collective-permute-start | bytes 393224 | tf_op jit(solution)/shard_map/ppermute | solution.py:180
  6.7 2.4 %collective-permute-start.1 = (bf16[256,256]{1,0:T(8,128)(2,1)S(1)}, bf16[256,256]{1,0:T(8,128)(2,1)S(1)}, u32[]{:S(2)}, u32[]{:S(2)}) collective-permute-start(bf16[256,256]{1,0:T(8,128)(2,1)S(1)} %and_select_fusion), channel_id=1, source_target_pairs={{0,8},{4,12},{8,0},{12,4},{1,9},{5,13},{9,1},{13,5},{2,10},{6,14},... | collective-permute-start | bytes 393224 | tf_op jit(solution)/shard_map/ppermute | solution.py:180
  9.1 2.5 %collective-permute-start.2 = (bf16[256,256]{1,0:T(8,128)(2,1)S(1)}, bf16[256,256]{1,0:T(8,128)(2,1)S(1)}, u32[]{:S(2)}, u32[]{:S(2)}) collective-permute-start(bf16[256,256]{1,0:T(8,128)(2,1)S(1)} %and_select_fusion), channel_id=1, source_target_pairs={{0,4},{4,8},{8,12},{12,0},{1,5},{5,9},{9,13},{13,1},{2,6},{6,10},{... | collective-permute-start | bytes 393224 | tf_op jit(solution)/shard_map/ppermute | solution.py:180
  11.7 6.6 %collective-permute-start.3 = (bf16[256,256]{1,0:T(8,128)(2,1)S(1)}, bf16[256,256]{1,0:T(8,128)(2,1)S(1)}, u32[]{:S(2)}, u32[]{:S(2)}) collective-permute-start(bf16[256,256]{1,0:T(8,128)(2,1)S(1)} %and_select_fusion), channel_id=1, source_target_pairs={{0,2},{2,0},{1,3},{3,1},{4,6},{6,4},{5,7},{7,5},{8,10},{10,8},{9,1... | collective-permute-start | bytes 393224 | tf_op jit(solution)/shard_map/ppermute | solution.py:221
  19.4 3.7 %collective-permute-start.7 = (bf16[4,256,256]{2,1,0:T(8,128)(2,1)S(1)}, bf16[4,256,256]{2,1,0:T(8,128)(2,1)S(1)}, u32[]{:S(2)}, u32[]{:S(2)}) collective-permute-start(bf16[4,256,256]{2,1,0:T(8,128)(2,1)S(1)} %pad_maximum_fusion.1), channel_id=1, source_target_pairs={{0,1},{1,0},{2,3},{3,2},{4,5},{5,4},{6,7},{7,6},{8,9},{9,8},{10,11... | collective-permute-start | bytes 1572872 | tf_op jit(solution)/shard_map/ppermute | solution.py:223
  23.1 4.0 %collective-permute-start.4 = (bf16[256,256]{1,0:T(8,128)(2,1)S(1)}, bf16[256,256]{1,0:T(8,128)(2,1)S(1)}, u32[]{:S(2)}, u32[]{:S(2)}) collective-permute-start(bf16[256,256]{1,0:T(8,128)(2,1)S(1)} %collective-permute-done.3), channel_id=1, source_target_pairs={{0,12},{4,0},{8,4},{12,8},{1,13},{5,1},{9,5},{13,9},{2,14},{6,2},{... | collective-permute-start | bytes 393224 | tf_op jit(solution)/shard_map/ppermute | solution.py:180
  27.1 3.1 %collective-permute-start.5 = (bf16[256,256]{1,0:T(8,128)(2,1)S(1)}, bf16[256,256]{1,0:T(8,128)(2,1)S(1)}, u32[]{:S(2)}, u32[]{:S(2)}) collective-permute-start(bf16[256,256]{1,0:T(8,128)(2,1)S(1)} %collective-permute-done.3), channel_id=1, source_target_pairs={{0,8},{4,12},{8,0},{12,4},{1,9},{5,13},{9,1},{13,5},{2,10},{6,14},... | collective-permute-start | bytes 393224 | tf_op jit(solution)/shard_map/ppermute | solution.py:180
  34.3 4.3 %collective-permute-done.6 = bf16[256,256]{1,0:T(8,128)(2,1)S(1)} collective-permute-done((bf16[256,256]{1,0:T(8,128)(2,1)S(1)}, bf16[256,256]{1,0:T(8,128)(2,1)S(1)}, u32[]{:S(2)}, u32[]{:S(2)}) %collective-permute-start.6) | collective-permute-done | bytes 131104 | tf_op jit(solution)/shard_map/ppermute | solution.py:180
  38.7 5.1 %collective-permute-start.8 = (bf16[4,256,256]{2,1,0:T(8,128)(2,1)S(1)}, bf16[4,256,256]{2,1,0:T(8,128)(2,1)S(1)}, u32[]{:S(2)}, u32[]{:S(2)}) collective-permute-start(bf16[4,256,256]{2,1,0:T(8,128)(2,1)S(1)} %pad_maximum_fusion.2), channel_id=1, source_target_pairs={{0,1},{1,0},{2,3},{3,2},{4,5},{5,4},{6,7},{7,6},{8,9},{9,8},{10,11... | collective-permute-start | bytes 1572872 | tf_op jit(solution)/shard_map/ppermute | solution.py:225
  45.4 3.6 %shard_map.68 = (bf16[256,256]{1,0:T(8,128)(2,1)}, bf16[272,256]{1,0:T(8,128)(2,1)S(1)}, bf16[16,256]{1,0:T(8,128)(2,1)S(1)}, bf16[2064,256]{1,0:T(8,128)(2,1)S(1)}, bf16[256,256]{1,0:T(8,128)(2,1)S(1)}) custom-call(s32[4]{0:T(128)S(1)} %pad_add_fusion.meta.refs_0_, s32[16]{0:T(128)S(1)} %bitcast.36, ...), custom_call_target="tpu_custom_call" | custom-call | flops 1610612736 | bytes 8388608 | tf_op jit(solution)/shard_map/pallas_call | solution.py:228
  51.2 6.9 %collective-permute-start.19 = (bf16[272,256]{1,0:T(8,128)(2,1)S(1)}, bf16[272,256]{1,0:T(8,128)(2,1)S(1)}, u32[]{:S(2)}, u32[]{:S(2)}) collective-permute-start(bf16[272,256]{1,0:T(8,128)(2,1)S(1)} %get-tuple-element.14.message), channel_id=1, source_target_pairs={{0,2},{2,0},{1,3},{3,1},{4,6},{6,4},{5,7},{7,5},{8,10},{10,8},{9,1... | collective-permute-start | bytes 417800 | tf_op jit(solution)/shard_map/ppermute | solution.py:238
  58.2 6.9 %collective-permute-done.19 = bf16[272,256]{1,0:T(8,128)(2,1)S(1)} collective-permute-done((bf16[272,256]{1,0:T(8,128)(2,1)S(1)}, bf16[272,256]{1,0:T(8,128)(2,1)S(1)}, u32[]{:S(2)}, u32[]{:S(2)}) %collective-permute-start.19) | collective-permute-done | bytes 139296 | tf_op jit(solution)/shard_map/ppermute | solution.py:238
  71.1 4.4 %collective-permute-start.10 = (bf16[528,256]{1,0:T(8,128)(2,1)S(1)}, bf16[528,256]{1,0:T(8,128)(2,1)S(1)}, u32[]{:S(2)}, u32[]{:S(2)}) collective-permute-start(bf16[528,256]{1,0:T(8,128)(2,1)S(1)} %get-tuple-element.19), channel_id=1, source_target_pairs={{0,8},{4,12},{8,0},{12,4},{1,9},{5,13},{9,1},{13,5},{2,10},{6,14},... | collective-permute-start | bytes 811016 | tf_op jit(solution)/shard_map/ppermute | solution.py:180
  75.4 3.4 %collective-permute-start.11 = (bf16[528,256]{1,0:T(8,128)(2,1)S(1)}, bf16[528,256]{1,0:T(8,128)(2,1)S(1)}, u32[]{:S(2)}, u32[]{:S(2)}) collective-permute-start(bf16[528,256]{1,0:T(8,128)(2,1)S(1)} %get-tuple-element.20), channel_id=1, source_target_pairs={{0,4},{4,8},{8,12},{12,0},{1,5},{5,9},{9,13},{13,1},{2,6},{6,10},{... | collective-permute-start | bytes 811016 | tf_op jit(solution)/shard_map/ppermute | solution.py:180
  78.8 3.1 %collective-permute-start.12 = (bf16[528,256]{1,0:T(8,128)(2,1)S(1)}, bf16[528,256]{1,0:T(8,128)(2,1)S(1)}, u32[]{:S(2)}, u32[]{:S(2)}) collective-permute-start(bf16[528,256]{1,0:T(8,128)(2,1)S(1)} %get-tuple-element.21), channel_id=1, source_target_pairs={{0,12},{4,0},{8,4},{12,8},{1,13},{5,1},{9,5},{13,9},{2,14},{6,2},{... | collective-permute-start | bytes 811016 | tf_op jit(solution)/shard_map/ppermute | solution.py:180
  84.2 6.5 %collective-permute-done.11.c = bf16[528,256]{1,0:T(8,128)(2,1)S(1)} collective-permute-done((bf16[528,256]{1,0:T(8,128)(2,1)S(1)}, bf16[528,256]{1,0:T(8,128)(2,1)S(1)}, u32[]{:S(2)}, u32[]{:S(2)}) %collective-permute-start.11) | collective-permute-done | bytes 270368 | tf_op jit(solution)/shard_map/ppermute | solution.py:180
  92.3 4.2 %collective-permute-start.13 = (bf16[528,256]{1,0:T(8,128)(2,1)S(1)}, bf16[528,256]{1,0:T(8,128)(2,1)S(1)}, u32[]{:S(2)}, u32[]{:S(2)}) collective-permute-start(bf16[528,256]{1,0:T(8,128)(2,1)S(1)} %shard_map.71), channel_id=1, source_target_pairs={{0,16},{2,18},{16,32},{18,34},{32,48},{34,50},{48,66},{50,64},{64,... | collective-permute-start | bytes 811016 | tf_op jit(solution)/shard_map/ppermute | solution.py:251
  96.5 3.4 %collective-permute-start.14 = (bf16[528,256]{1,0:T(8,128)(2,1)S(1)}, bf16[528,256]{1,0:T(8,128)(2,1)S(1)}, u32[]{:S(2)}, u32[]{:S(2)}) collective-permute-start(bf16[528,256]{1,0:T(8,128)(2,1)S(1)} %shard_map.71), channel_id=1, source_target_pairs={{0,18},{2,16},{16,34},{18,32},{32,50},{34,48},{48,64},{50,66},{64,... | collective-permute-start | bytes 811016 | tf_op jit(solution)/shard_map/ppermute | solution.py:250
  100.0 3.7 %collective-permute-start.23 = (bf16[2176,256]{1,0:T(8,128)(2,1)S(1)}, bf16[2176,256]{1,0:T(8,128)(2,1)S(1)}, u32[]{:S(2)}, u32[]{:S(2)}) collective-permute-start(bf16[2176,256]{1,0:T(8,128)(2,1)S(1)} %get-tuple-element.26), channel_id=1, source_target_pairs={{0,1},{1,0},{2,3},{3,2},{4,5},{5,4},{6,7},{7,6},{8,9},{9,8},{10,11... | collective-permute-start | bytes 3342344 | tf_op jit(solution)/shard_map/ppermute | solution.py:255
  103.8 17.4 %collective-permute-done.14.refs_1_ = bf16[528,256]{1,0:T(8,128)(2,1)S(1)} collective-permute-done((bf16[528,256]{1,0:T(8,128)(2,1)S(1)}, bf16[528,256]{1,0:T(8,128)(2,1)S(1)}, u32[]{:S(2)}, u32[]{:S(2)}) %collective-permute-start.14) | collective-permute-done | bytes 270368 | tf_op jit(solution)/shard_map/ppermute | solution.py:250
  121.2 5.2 %collective-permute-start.15 = (bf16[512,256]{1,0:T(8,128)(2,1)S(1)}, bf16[512,256]{1,0:T(8,128)(2,1)S(1)}, u32[]{:S(2)}, u32[]{:S(2)}) collective-permute-start(bf16[512,256]{1,0:T(8,128)(2,1)S(1)} %shard_map.72), channel_id=1, source_target_pairs={{0,12},{4,0},{8,4},{12,8},{1,13},{5,1},{9,5},{13,9},{2,14},{6,2},{... | collective-permute-start | bytes 786440 | tf_op jit(solution)/shard_map/ppermute | solution.py:180
  128.3 2.5 %collective-permute-start.17 = (bf16[512,256]{1,0:T(8,128)(2,1)S(1)}, bf16[512,256]{1,0:T(8,128)(2,1)S(1)}, u32[]{:S(2)}, u32[]{:S(2)}) collective-permute-start(bf16[512,256]{1,0:T(8,128)(2,1)S(1)} %shard_map.72), channel_id=1, source_target_pairs={{0,4},{4,8},{8,12},{12,0},{1,5},{5,9},{9,13},{13,1},{2,6},{6,10},{... | collective-permute-start | bytes 786440 | tf_op jit(solution)/shard_map/ppermute | solution.py:180
  130.8 6.2 %collective-permute-done.15 = bf16[512,256]{1,0:T(8,128)(2,1)S(1)} collective-permute-done((bf16[512,256]{1,0:T(8,128)(2,1)S(1)}, bf16[512,256]{1,0:T(8,128)(2,1)S(1)}, u32[]{:S(2)}, u32[]{:S(2)}) %collective-permute-start.15) | collective-permute-done | bytes 262176 | tf_op jit(solution)/shard_map/ppermute | solution.py:180
  137.0 6.6 %collective-permute-done.17 = bf16[512,256]{1,0:T(8,128)(2,1)S(1)} collective-permute-done((bf16[512,256]{1,0:T(8,128)(2,1)S(1)}, bf16[512,256]{1,0:T(8,128)(2,1)S(1)}, u32[]{:S(2)}, u32[]{:S(2)}) %collective-permute-start.17) | collective-permute-done | bytes 262176 | tf_op jit(solution)/shard_map/ppermute | solution.py:180
  (60 shorter events, 29.1 us)
Async XLA Ops:
  2.3 17.0 %collective-permute-start = (bf16[256,256]{1,0:T(8,128)(2,1)S(1)}, bf16[256,256]{1,0:T(8,128)(2,1)S(1)}, u32[]{:S(2)}, u32[]{:S(2)}) collective-permute-start(bf16[256,256]{1,0:T(8,128)(2,1)S(1)} %and_select_fusion), channel_id=1, source_target_pairs={{0,12},{4,0},{8,4},{12,8},{1,13},{5,1},{9,5},{13,9},{2,14},{6,2},{... | collective-permute-start | bytes 393224 | tf_op jit(solution)/shard_map/ppermute | solution.py:180
  6.7 12.6 %collective-permute-start.1 = (bf16[256,256]{1,0:T(8,128)(2,1)S(1)}, bf16[256,256]{1,0:T(8,128)(2,1)S(1)}, u32[]{:S(2)}, u32[]{:S(2)}) collective-permute-start(bf16[256,256]{1,0:T(8,128)(2,1)S(1)} %and_select_fusion), channel_id=1, source_target_pairs={{0,8},{4,12},{8,0},{12,4},{1,9},{5,13},{9,1},{13,5},{2,10},{6,14},... | collective-permute-start | bytes 393224 | tf_op jit(solution)/shard_map/ppermute | solution.py:180
  9.1 10.2 %collective-permute-start.2 = (bf16[256,256]{1,0:T(8,128)(2,1)S(1)}, bf16[256,256]{1,0:T(8,128)(2,1)S(1)}, u32[]{:S(2)}, u32[]{:S(2)}) collective-permute-start(bf16[256,256]{1,0:T(8,128)(2,1)S(1)} %and_select_fusion), channel_id=1, source_target_pairs={{0,4},{4,8},{8,12},{12,0},{1,5},{5,9},{9,13},{13,1},{2,6},{6,10},{... | collective-permute-start | bytes 393224 | tf_op jit(solution)/shard_map/ppermute | solution.py:180
  11.7 11.5 %collective-permute-start.3 = (bf16[256,256]{1,0:T(8,128)(2,1)S(1)}, bf16[256,256]{1,0:T(8,128)(2,1)S(1)}, u32[]{:S(2)}, u32[]{:S(2)}) collective-permute-start(bf16[256,256]{1,0:T(8,128)(2,1)S(1)} %and_select_fusion), channel_id=1, source_target_pairs={{0,2},{2,0},{1,3},{3,1},{4,6},{6,4},{5,7},{7,5},{8,10},{10,8},{9,1... | collective-permute-start | bytes 393224 | tf_op jit(solution)/shard_map/ppermute | solution.py:221
  19.4 24.4 %collective-permute-start.7 = (bf16[4,256,256]{2,1,0:T(8,128)(2,1)S(1)}, bf16[4,256,256]{2,1,0:T(8,128)(2,1)S(1)}, u32[]{:S(2)}, u32[]{:S(2)}) collective-permute-start(bf16[4,256,256]{2,1,0:T(8,128)(2,1)S(1)} %pad_maximum_fusion.1), channel_id=1, source_target_pairs={{0,1},{1,0},{2,3},{3,2},{4,5},{5,4},{6,7},{7,6},{8,9},{9,8},{10,11... | collective-permute-start | bytes 1572872 | tf_op jit(solution)/shard_map/ppermute | solution.py:223
  23.1 9.2 %collective-permute-start.4 = (bf16[256,256]{1,0:T(8,128)(2,1)S(1)}, bf16[256,256]{1,0:T(8,128)(2,1)S(1)}, u32[]{:S(2)}, u32[]{:S(2)}) collective-permute-start(bf16[256,256]{1,0:T(8,128)(2,1)S(1)} %collective-permute-done.3), channel_id=1, source_target_pairs={{0,12},{4,0},{8,4},{12,8},{1,13},{5,1},{9,5},{13,9},{2,14},{6,2},{... | collective-permute-start | bytes 393224 | tf_op jit(solution)/shard_map/ppermute | solution.py:180
  27.1 7.2 %collective-permute-start.5 = (bf16[256,256]{1,0:T(8,128)(2,1)S(1)}, bf16[256,256]{1,0:T(8,128)(2,1)S(1)}, u32[]{:S(2)}, u32[]{:S(2)}) collective-permute-start(bf16[256,256]{1,0:T(8,128)(2,1)S(1)} %collective-permute-done.3), channel_id=1, source_target_pairs={{0,8},{4,12},{8,0},{12,4},{1,9},{5,13},{9,1},{13,5},{2,10},{6,14},... | collective-permute-start | bytes 393224 | tf_op jit(solution)/shard_map/ppermute | solution.py:180
  30.3 8.3 %collective-permute-start.6 = (bf16[256,256]{1,0:T(8,128)(2,1)S(1)}, bf16[256,256]{1,0:T(8,128)(2,1)S(1)}, u32[]{:S(2)}, u32[]{:S(2)}) collective-permute-start(bf16[256,256]{1,0:T(8,128)(2,1)S(1)} %collective-permute-done.3), channel_id=1, source_target_pairs={{0,4},{4,8},{8,12},{12,0},{1,5},{5,9},{9,13},{13,1},{2,6},{6,10},{... | collective-permute-start | bytes 393224 | tf_op jit(solution)/shard_map/ppermute | solution.py:180
  38.7 6.6 %collective-permute-start.8 = (bf16[4,256,256]{2,1,0:T(8,128)(2,1)S(1)}, bf16[4,256,256]{2,1,0:T(8,128)(2,1)S(1)}, u32[]{:S(2)}, u32[]{:S(2)}) collective-permute-start(bf16[4,256,256]{2,1,0:T(8,128)(2,1)S(1)} %pad_maximum_fusion.2), channel_id=1, source_target_pairs={{0,1},{1,0},{2,3},{3,2},{4,5},{5,4},{6,7},{7,6},{8,9},{9,8},{10,11... | collective-permute-start | bytes 1572872 | tf_op jit(solution)/shard_map/ppermute | solution.py:225
  49.0 21.8 %collective-permute-start.9 = (bf16[2064,256]{1,0:T(8,128)(2,1)S(1)}, bf16[2064,256]{1,0:T(8,128)(2,1)S(1)}, u32[]{:S(2)}, u32[]{:S(2)}) collective-permute-start(bf16[2064,256]{1,0:T(8,128)(2,1)S(1)} %get-tuple-element.17), channel_id=1, source_target_pairs={{0,1},{1,0},{2,3},{3,2},{4,5},{5,4},{6,7},{7,6},{8,9},{9,8},{10,11... | collective-permute-start | bytes 3170312 | tf_op jit(solution)/shard_map/ppermute | solution.py:237
  51.2 13.9 %collective-permute-start.19 = (bf16[272,256]{1,0:T(8,128)(2,1)S(1)}, bf16[272,256]{1,0:T(8,128)(2,1)S(1)}, u32[]{:S(2)}, u32[]{:S(2)}) collective-permute-start(bf16[272,256]{1,0:T(8,128)(2,1)S(1)} %get-tuple-element.14.message), channel_id=1, source_target_pairs={{0,2},{2,0},{1,3},{3,1},{4,6},{6,4},{5,7},{7,5},{8,10},{10,8},{9,1... | collective-permute-start | bytes 417800 | tf_op jit(solution)/shard_map/ppermute | solution.py:238
  65.2 16.8 %collective-permute-start.20 = (bf16[544,256]{1,0:T(8,128)(2,1)S(1)}, bf16[544,256]{1,0:T(8,128)(2,1)S(1)}, u32[]{:S(2)}, u32[]{:S(2)}) collective-permute-start(bf16[544,256]{1,0:T(8,128)(2,1)S(1)} %get-tuple-element.34), channel_id=1, source_target_pairs={{0,12},{4,0},{8,4},{12,8},{1,13},{5,1},{9,5},{13,9},{2,14},{6,2},{... | collective-permute-start | bytes 835592 | tf_op jit(solution)/shard_map/ppermute | solution.py:180
  67.1 32.8 %collective-permute-start.21 = (bf16[544,256]{1,0:T(8,128)(2,1)S(1)}, bf16[544,256]{1,0:T(8,128)(2,1)S(1)}, u32[]{:S(2)}, u32[]{:S(2)}) collective-permute-start(bf16[544,256]{1,0:T(8,128)(2,1)S(1)} %get-tuple-element.34), channel_id=1, source_target_pairs={{0,8},{4,12},{8,0},{12,4},{1,9},{5,13},{9,1},{13,5},{2,10},{6,14},... | collective-permute-start | bytes 835592 | tf_op jit(solution)/shard_map/ppermute | solution.py:180
  71.1 13.1 %collective-permute-start.10 = (bf16[528,256]{1,0:T(8,128)(2,1)S(1)}, bf16[528,256]{1,0:T(8,128)(2,1)S(1)}, u32[]{:S(2)}, u32[]{:S(2)}) collective-permute-start(bf16[528,256]{1,0:T(8,128)(2,1)S(1)} %get-tuple-element.19), channel_id=1, source_target_pairs={{0,8},{4,12},{8,0},{12,4},{1,9},{5,13},{9,1},{13,5},{2,10},{6,14},... | collective-permute-start | bytes 811016 | tf_op jit(solution)/shard_map/ppermute | solution.py:180
  75.4 15.2 %collective-permute-start.11 = (bf16[528,256]{1,0:T(8,128)(2,1)S(1)}, bf16[528,256]{1,0:T(8,128)(2,1)S(1)}, u32[]{:S(2)}, u32[]{:S(2)}) collective-permute-start(bf16[528,256]{1,0:T(8,128)(2,1)S(1)} %get-tuple-element.20), channel_id=1, source_target_pairs={{0,4},{4,8},{8,12},{12,0},{1,5},{5,9},{9,13},{13,1},{2,6},{6,10},{... | collective-permute-start | bytes 811016 | tf_op jit(solution)/shard_map/ppermute | solution.py:180
  78.8 13.4 %collective-permute-start.12 = (bf16[528,256]{1,0:T(8,128)(2,1)S(1)}, bf16[528,256]{1,0:T(8,128)(2,1)S(1)}, u32[]{:S(2)}, u32[]{:S(2)}) collective-permute-start(bf16[528,256]{1,0:T(8,128)(2,1)S(1)} %get-tuple-element.21), channel_id=1, source_target_pairs={{0,12},{4,0},{8,4},{12,8},{1,13},{5,1},{9,5},{13,9},{2,14},{6,2},{... | collective-permute-start | bytes 811016 | tf_op jit(solution)/shard_map/ppermute | solution.py:180
  81.9 18.0 %collective-permute-start.22 = (bf16[544,256]{1,0:T(8,128)(2,1)S(1)}, bf16[544,256]{1,0:T(8,128)(2,1)S(1)}, u32[]{:S(2)}, u32[]{:S(2)}) collective-permute-start(bf16[544,256]{1,0:T(8,128)(2,1)S(1)} %get-tuple-element.34), channel_id=1, source_target_pairs={{0,4},{4,8},{8,12},{12,0},{1,5},{5,9},{9,13},{13,1},{2,6},{6,10},{... | collective-permute-start | bytes 835592 | tf_op jit(solution)/shard_map/ppermute | solution.py:180
  92.3 11.4 %collective-permute-start.13 = (bf16[528,256]{1,0:T(8,128)(2,1)S(1)}, bf16[528,256]{1,0:T(8,128)(2,1)S(1)}, u32[]{:S(2)}, u32[]{:S(2)}) collective-permute-start(bf16[528,256]{1,0:T(8,128)(2,1)S(1)} %shard_map.71), channel_id=1, source_target_pairs={{0,16},{2,18},{16,32},{18,34},{32,48},{34,50},{48,66},{50,64},{64,... | collective-permute-start | bytes 811016 | tf_op jit(solution)/shard_map/ppermute | solution.py:251
  96.5 24.6 %collective-permute-start.14 = (bf16[528,256]{1,0:T(8,128)(2,1)S(1)}, bf16[528,256]{1,0:T(8,128)(2,1)S(1)}, u32[]{:S(2)}, u32[]{:S(2)}) collective-permute-start(bf16[528,256]{1,0:T(8,128)(2,1)S(1)} %shard_map.71), channel_id=1, source_target_pairs={{0,18},{2,16},{16,34},{18,32},{32,50},{34,48},{48,64},{50,66},{64,... | collective-permute-start | bytes 811016 | tf_op jit(solution)/shard_map/ppermute | solution.py:250
  100.0 46.1 %collective-permute-start.23 = (bf16[2176,256]{1,0:T(8,128)(2,1)S(1)}, bf16[2176,256]{1,0:T(8,128)(2,1)S(1)}, u32[]{:S(2)}, u32[]{:S(2)}) collective-permute-start(bf16[2176,256]{1,0:T(8,128)(2,1)S(1)} %get-tuple-element.26), channel_id=1, source_target_pairs={{0,1},{1,0},{2,3},{3,2},{4,5},{5,4},{6,7},{7,6},{8,9},{9,8},{10,11... | collective-permute-start | bytes 3342344 | tf_op jit(solution)/shard_map/ppermute | solution.py:255
  121.2 15.8 %collective-permute-start.15 = (bf16[512,256]{1,0:T(8,128)(2,1)S(1)}, bf16[512,256]{1,0:T(8,128)(2,1)S(1)}, u32[]{:S(2)}, u32[]{:S(2)}) collective-permute-start(bf16[512,256]{1,0:T(8,128)(2,1)S(1)} %shard_map.72), channel_id=1, source_target_pairs={{0,12},{4,0},{8,4},{12,8},{1,13},{5,1},{9,5},{13,9},{2,14},{6,2},{... | collective-permute-start | bytes 786440 | tf_op jit(solution)/shard_map/ppermute | solution.py:180
  126.4 10.6 %collective-permute-start.16 = (bf16[512,256]{1,0:T(8,128)(2,1)S(1)}, bf16[512,256]{1,0:T(8,128)(2,1)S(1)}, u32[]{:S(2)}, u32[]{:S(2)}) collective-permute-start(bf16[512,256]{1,0:T(8,128)(2,1)S(1)} %shard_map.72), channel_id=1, source_target_pairs={{0,8},{4,12},{8,0},{12,4},{1,9},{5,13},{9,1},{13,5},{2,10},{6,14},... | collective-permute-start | bytes 786440 | tf_op jit(solution)/shard_map/ppermute | solution.py:180
  128.3 15.3 %collective-permute-start.17 = (bf16[512,256]{1,0:T(8,128)(2,1)S(1)}, bf16[512,256]{1,0:T(8,128)(2,1)S(1)}, u32[]{:S(2)}, u32[]{:S(2)}) collective-permute-start(bf16[512,256]{1,0:T(8,128)(2,1)S(1)} %shard_map.72), channel_id=1, source_target_pairs={{0,4},{4,8},{8,12},{12,0},{1,5},{5,9},{9,13},{13,1},{2,6},{6,10},{... | collective-permute-start | bytes 786440 | tf_op jit(solution)/shard_map/ppermute | solution.py:180
  143.7 5.5 %collective-permute-start.18 = (bf16[2048,256]{1,0:T(8,128)(2,1)S(1)}, bf16[2048,256]{1,0:T(8,128)(2,1)S(1)}, u32[]{:S(2)}, u32[]{:S(2)}) collective-permute-start(bf16[2048,256]{1,0:T(8,128)(2,1)S(1)} %pad_maximum_fusion.refs_1_), channel_id=1, source_target_pairs={{0,1},{1,0},{2,3},{3,2},{4,5},{5,4},{6,7},{7,6},{8,9},{9,8},{10,11... | collective-permute-start | bytes 3145736 | tf_op jit(solution)/shard_map/ppermute | solution.py:270
  (3 other events, 39.2 us)

commit v3 on v2

--- a/solution.py
+++ b/solution.py
@@ -12,6 +12,7 @@
 BF = jnp.bfloat16
 F32 = jnp.float32
 TILE = 16
+UP = 128
 YROW = ("z", "yl", "yh")
 SWAP = [(0, 1), (1, 0)]
 VMEM = pl.BlockSpec(memory_space=pltpu.VMEM)
@@ -120,13 +121,14 @@
     )
 
 
-def edge_kernel(factor, near, far, out):
+def edge_kernel(factor, near, far_up, far, out):
     rows = near.shape[0] - TILE
+    up = far_up.shape[0]
     q0, c0 = unpack(near[rows:rows + TILE, :])
-    q1, c1 = unpack(far[rows:rows + TILE, :])
+    q1, c1 = unpack(far[rows - up:rows - up + TILE, :])
     weight = factor / ((q0 + q1) / jnp.maximum(c0 + c1, 1.0) + 1e-6)
-    total = near[0:rows, :].astype(F32) + far[0:rows, :].astype(F32)
-    out[...] = (total * weight).astype(BF)
+    out[0:up, :] = ((near[0:up, :].astype(F32) + far_up[...].astype(F32)) * weight).astype(BF)
+    out[up:rows, :] = ((near[up:rows, :].astype(F32) + far[0:rows - up, :].astype(F32)) * weight).astype(BF)
 
 
 def pool_two_kernel(meta, picks, pool, left, right, g_out, base):
@@ -185,23 +187,21 @@
     return [value, along_x(value, 3), far, along_x(value, 1)]
 
 
-def routes(z_count, y_count):
-    def at(z, yl, yh):
-        return (z * y_count + yl) * 2 + yh
-
-    near, far = [], []
+def routes(z_count):
+    near, far, up_two, up_three = [], [], [], []
+
+    def at(z, y):
+        return (z * 4 + y % 4) * 2 + (y // 4) % 2
+
     for z in range(z_count):
-        for yl in range(y_count):
-            for yh in range(2):
-                if yl + 1 < y_count:
-                    following = (z, yl + 1, yh)
-                elif z + 1 < z_count:
-                    following = (z + 1, 0, 1 - yh)
-                else:
-                    continue
-                near.append((at(z, yl, yh), at(*following)))
-                far.append((at(z, yl, yh), at(following[0], following[1], 1 - following[2])))
-    return near, far
+        for y in range(8):
+            up_two.append((at(z, y), at(z, y + 2)))
+            next_z = z + (y % 4 == 3)
+            if next_z < z_count:
+                near.append((at(z, y), at(next_z, y + 1)))
+                far.append((at(z, y), at(next_z, y + 5)))
+                up_three.append((at(z, y + 2), at(next_z, y + 5)))
+    return near, far, up_two, up_three
 
 
 def body(wave, left_block_environment, right_block_environment, source_block, sector_size):
@@ -214,14 +214,14 @@
     span = width + TILE
     unit = 2 * channels * width**3
     block_bytes = width * width * 2
-    meta = jnp.stack([size, lax.axis_index("c").astype(jnp.int32), lax.axis_index("yh").astype(jnp.int32),
-                      lax.axis_index("x").astype(jnp.int32)])
+    meta = jnp.stack([size, *(lax.axis_index(axis).astype(jnp.int32) for axis in ("c", "yh", "x"))])
 
     masked = jnp.where(live(size, (width, width)), wave[0, 0], jnp.zeros((), BF))
     masked_other = lax.ppermute(masked, "yh", SWAP)
     own = jnp.stack(round_x(masked))
     across = lax.ppermute(own, "c", SWAP)
-    own_other = jnp.stack(round_x(masked_other))
+    diagonal = lax.ppermute(masked, ("x", "yh"), [(2 * x + y, 2 * ((x + 2) % 4) + 1 - y) for x in range(4) for y in range(2)])
+    own_other = jnp.stack([masked_other, along_x(masked_other, 3), diagonal, along_x(masked_other, 1)])
     across_other = lax.ppermute(own_other, "c", SWAP)
     pool = jnp.concatenate([own, own_other, across, across_other], axis=0)
     stack = pltpu.VMEM((half, width, width), BF)
@@ -246,9 +246,11 @@
     row = call(
         row_sum_kernel, one((2 * width + TILE, width), BF), [VMEM] * 4, [], 1 << 20, 10 * block_bytes
     )(parts[0], *arrived_x)
-    near, far = routes(lax.axis_size("z"), lax.axis_size("yl"))
-    from_far = lax.ppermute(row, YROW, far)
+    near, far, up_two, up_three = routes(lax.axis_size("z"))
+    passing = lax.ppermute(row[0:UP], YROW, up_two)
+    from_far = lax.ppermute(row[UP:], YROW, far)
     from_near = lax.ppermute(row, YROW, near)
+    from_far_up = lax.ppermute(passing, YROW, up_three)
 
     both = jnp.concatenate([message, message_other], axis=0)
     two_own = jnp.concatenate(round_x(both))
@@ -264,8 +266,8 @@
 
     factor = 1.0 / (width * math.sqrt(channels_of(sector_size)))
     edge = call(
-        lambda *refs: edge_kernel(factor, *refs), one((2 * width, width), BF), [VMEM] * 2, [], 1 << 20, 12 * block_bytes
-    )(from_near, from_far)
+        lambda *refs: edge_kernel(factor, *refs), one((2 * width, width), BF), [VMEM] * 3, [], 1 << 20, 12 * block_bytes
+    )(from_near, from_far_up, from_far)
     edges_own = jnp.concatenate(round_x(edge))
     edges_other = lax.ppermute(edges_own, "c", SWAP)
     partial = call(

time: 152 us -> 150 us (0.987)
  waiting for transfers between devices: 52.8 us -> 39.5 us
  starting transfers between devices: 83.6 us -> 95 us
    ppermute x1 -> x4, starting transfers between devices: 3.36 us -> 17.8 us  [the longest x1 5.1 us: body(): from_far_up = lax.ppermute(passing, YROW, up_three)]
    ppermute x1 -> x4, waiting for transfers between devices: 17.4 us -> 5.05 us  [the longest x1 4.79 us: body(): passing = lax.ppermute(row[0:UP], YROW, up_two)]
    ppermute x15 -> x14, starting transfers between devices: 45.3 us -> 42.8 us  [along_x(): lax.ppermute(value, 'x', [(i, (i + step) % count) for i in range(count)])]
    ppermute x1, starting transfers between devices: 5.1 us -> 3.06 us  [body(): across_other = lax.ppermute(own_other, 'c', SWAP)]
    ppermute x1, starting transfers between devices: 3.74 us -> 5.28 us  [body(): two_other = lax.ppermute(two_own, 'c', SWAP)]
    ppermute x15 -> x14, waiting for transfers between devices: 27.1 us -> 26.4 us  [along_x(): lax.ppermute(value, 'x', [(i, (i + step) % count) for i in range(count)])]
  transfers between devices with their start and end apart: 24 -> 26, of which waited for: 9 -> 10; matrix products, arithmetic and copies ran while one was open for 1% -> 1% of each run, Pallas kernels for 3% -> 3%
where the time goes in v3:
time: 150 us; the launch traced here: 149 us
  starting transfers between devices  95 us (63%)
  waiting for transfers between devices  39.5 us (26%)
  Pallas kernels  10 us (7%)
  other arithmetic  2.31 us (2%)
  between operations  1.85 us (1%)
    ppermute x14, starting transfers between devices, along_x(): lax.ppermute(value, 'x', [(i, (i + step) % count) for i in range(count)])  42.8 us
    ppermute x14, waiting for transfers between devices, along_x(): lax.ppermute(value, 'x', [(i, (i + step) % count) for i in range(count)])  26.4 us
    ppermute x1, starting transfers between devices, body(): message_other = lax.ppermute(message, 'yh', SWAP)  7.29 us
    ppermute x1, waiting for transfers between devices, body(): message_other = lax.ppermute(message, 'yh', SWAP)  6.58 us
    ppermute x1, starting transfers between devices, body(): masked_other = lax.ppermute(masked, 'yh', SWAP)  6.55 us
    ppermute x1, starting transfers between devices, body(): two_other = lax.ppermute(two_own, 'c', SWAP)  5.28 us
    ppermute x1, starting transfers between devices, body(): from_far_up = lax.ppermute(passing, YROW, up_three)  5.1 us
    ppermute x1, waiting for transfers between devices, body(): passing = lax.ppermute(row[0:UP], YROW, up_two)  4.79 us
  transfers between devices with their start and end apart: 26, of which 10 were waited for; matrix products, arithmetic and copies ran while one was open for 1% of the time, Pallas kernels for 3%

profile of v3, /device:TPU:201, one launch (start us, length us, event | category | flops | bytes accessed | tf_op | source)
XLA Modules:
  0.0 149.1 jit_solution(5521247590224849428)
XLA Ops:
  2.3 4.4 %collective-permute-start = (bf16[256,256]{1,0:T(8,128)(2,1)S(1)}, bf16[256,256]{1,0:T(8,128)(2,1)S(1)}, u32[]{:S(2)}, u32[]{:S(2)}) collective-permute-start(bf16[256,256]{1,0:T(8,128)(2,1)S(1)} %and_select_fusion), channel_id=1, source_target_pairs={{0,12},{4,0},{8,4},{12,8},{1,13},{5,1},{9,5},{13,9},{2,14},{6,2},{... | collective-permute-start | bytes 393224 | tf_op jit(solution)/shard_map/ppermute | solution.py:182
  11.7 6.6 %collective-permute-start.3 = (bf16[256,256]{1,0:T(8,128)(2,1)S(1)}, bf16[256,256]{1,0:T(8,128)(2,1)S(1)}, u32[]{:S(2)}, u32[]{:S(2)}) collective-permute-start(bf16[256,256]{1,0:T(8,128)(2,1)S(1)} %and_select_fusion), channel_id=1, source_target_pairs={{0,2},{2,0},{1,3},{3,1},{4,6},{6,4},{5,7},{7,5},{8,10},{10,8},{9,1... | collective-permute-start | bytes 393224 | tf_op jit(solution)/shard_map/ppermute | solution.py:220
  18.2 4.2 %collective-permute-start.5 = (bf16[256,256]{1,0:T(8,128)(2,1)S(1)}, bf16[256,256]{1,0:T(8,128)(2,1)S(1)}, u32[]{:S(2)}, u32[]{:S(2)}) collective-permute-start(bf16[256,256]{1,0:T(8,128)(2,1)S(1)} %and_select_fusion), channel_id=1, source_target_pairs={{0,10},{2,8},{4,14},{6,12},{8,2},{10,0},{12,6},{14,4},{1,11},{3,9}... | collective-permute-start | bytes 393224 | tf_op jit(solution)/shard_map/ppermute | solution.py:223
  23.6 3.7 %collective-permute-start.7 = (bf16[4,256,256]{2,1,0:T(8,128)(2,1)S(1)}, bf16[4,256,256]{2,1,0:T(8,128)(2,1)S(1)}, u32[]{:S(2)}, u32[]{:S(2)}) collective-permute-start(bf16[4,256,256]{2,1,0:T(8,128)(2,1)S(1)} %pad_maximum_fusion.1), channel_id=1, source_target_pairs={{0,1},{1,0},{2,3},{3,2},{4,5},{5,4},{6,7},{7,6},{8,9},{9,8},{10,11... | collective-permute-start | bytes 1572872 | tf_op jit(solution)/shard_map/ppermute | solution.py:222
  27.3 4.2 %collective-permute-start.4 = (bf16[256,256]{1,0:T(8,128)(2,1)S(1)}, bf16[256,256]{1,0:T(8,128)(2,1)S(1)}, u32[]{:S(2)}, u32[]{:S(2)}) collective-permute-start(bf16[256,256]{1,0:T(8,128)(2,1)S(1)} %collective-permute-done.3), channel_id=1, source_target_pairs={{0,12},{4,0},{8,4},{12,8},{1,13},{5,1},{9,5},{13,9},{2,14},{6,2},{... | collective-permute-start | bytes 393224 | tf_op jit(solution)/shard_map/ppermute | solution.py:182
  35.9 3.6 %collective-permute-done.6 = bf16[256,256]{1,0:T(8,128)(2,1)S(1)} collective-permute-done((bf16[256,256]{1,0:T(8,128)(2,1)S(1)}, bf16[256,256]{1,0:T(8,128)(2,1)S(1)}, u32[]{:S(2)}, u32[]{:S(2)}) %collective-permute-start.6) | collective-permute-done | bytes 131104 | tf_op jit(solution)/shard_map/ppermute | solution.py:182
  39.5 3.1 %collective-permute-start.8 = (bf16[4,256,256]{2,1,0:T(8,128)(2,1)S(1)}, bf16[4,256,256]{2,1,0:T(8,128)(2,1)S(1)}, u32[]{:S(2)}, u32[]{:S(2)}) collective-permute-start(bf16[4,256,256]{2,1,0:T(8,128)(2,1)S(1)} %pad_maximum_fusion.2), channel_id=1, source_target_pairs={{0,1},{1,0},{2,3},{3,2},{4,5},{5,4},{6,7},{7,6},{8,9},{9,8},{10,11... | collective-permute-start | bytes 1572872 | tf_op jit(solution)/shard_map/ppermute | solution.py:225
  44.2 3.6 %shard_map.68 = (bf16[256,256]{1,0:T(8,128)(2,1)}, bf16[272,256]{1,0:T(8,128)(2,1)S(1)}, bf16[16,256]{1,0:T(8,128)(2,1)S(1)}, bf16[2064,256]{1,0:T(8,128)(2,1)S(1)}, bf16[256,256]{1,0:T(8,128)(2,1)S(1)}) custom-call(s32[4]{0:T(128)S(1)} %pad_add_fusion.meta.refs_0_, s32[16]{0:T(128)S(1)} %bitcast.36, ...), custom_call_target="tpu_custom_call" | custom-call | flops 1610612736 | bytes 8388608 | tf_op jit(solution)/shard_map/pallas_call | solution.py:228
  50.1 7.3 %collective-permute-start.21 = (bf16[272,256]{1,0:T(8,128)(2,1)S(1)}, bf16[272,256]{1,0:T(8,128)(2,1)S(1)}, u32[]{:S(2)}, u32[]{:S(2)}) collective-permute-start(bf16[272,256]{1,0:T(8,128)(2,1)S(1)} %get-tuple-element.14.message), channel_id=1, source_target_pairs={{0,2},{2,0},{1,3},{3,1},{4,6},{6,4},{5,7},{7,5},{8,10},{10,8},{9,1... | collective-permute-start | bytes 417800 | tf_op jit(solution)/shard_map/ppermute | solution.py:238
  57.4 6.6 %collective-permute-done.21 = bf16[272,256]{1,0:T(8,128)(2,1)S(1)} collective-permute-done((bf16[272,256]{1,0:T(8,128)(2,1)S(1)}, bf16[272,256]{1,0:T(8,128)(2,1)S(1)}, u32[]{:S(2)}, u32[]{:S(2)}) %collective-permute-start.21) | collective-permute-done | bytes 139296 | tf_op jit(solution)/shard_map/ppermute | solution.py:238
  66.0 3.2 %collective-permute-start.23 = (bf16[544,256]{1,0:T(8,128)(2,1)S(1)}, bf16[544,256]{1,0:T(8,128)(2,1)S(1)}, u32[]{:S(2)}, u32[]{:S(2)}) collective-permute-start(bf16[544,256]{1,0:T(8,128)(2,1)S(1)} %get-tuple-element.34), channel_id=1, source_target_pairs={{0,8},{4,12},{8,0},{12,4},{1,9},{5,13},{9,1},{13,5},{2,10},{6,14},... | collective-permute-start | bytes 835592 | tf_op jit(solution)/shard_map/ppermute | solution.py:182
  70.7 3.5 %collective-permute-start.10 = (bf16[528,256]{1,0:T(8,128)(2,1)S(1)}, bf16[528,256]{1,0:T(8,128)(2,1)S(1)}, u32[]{:S(2)}, u32[]{:S(2)}) collective-permute-start(bf16[528,256]{1,0:T(8,128)(2,1)S(1)} %get-tuple-element.19), channel_id=1, source_target_pairs={{0,8},{4,12},{8,0},{12,4},{1,9},{5,13},{9,1},{13,5},{2,10},{6,14},... | collective-permute-start | bytes 811016 | tf_op jit(solution)/shard_map/ppermute | solution.py:182
  74.3 3.4 %collective-permute-start.11 = (bf16[528,256]{1,0:T(8,128)(2,1)S(1)}, bf16[528,256]{1,0:T(8,128)(2,1)S(1)}, u32[]{:S(2)}, u32[]{:S(2)}) collective-permute-start(bf16[528,256]{1,0:T(8,128)(2,1)S(1)} %get-tuple-element.20), channel_id=1, source_target_pairs={{0,4},{4,8},{8,12},{12,0},{1,5},{5,9},{9,13},{13,1},{2,6},{6,10},{... | collective-permute-start | bytes 811016 | tf_op jit(solution)/shard_map/ppermute | solution.py:182
  77.7 3.1 %collective-permute-start.12 = (bf16[528,256]{1,0:T(8,128)(2,1)S(1)}, bf16[528,256]{1,0:T(8,128)(2,1)S(1)}, u32[]{:S(2)}, u32[]{:S(2)}) collective-permute-start(bf16[528,256]{1,0:T(8,128)(2,1)S(1)} %get-tuple-element.21), channel_id=1, source_target_pairs={{0,12},{4,0},{8,4},{12,8},{1,13},{5,1},{9,5},{13,9},{2,14},{6,2},{... | collective-permute-start | bytes 811016 | tf_op jit(solution)/shard_map/ppermute | solution.py:182
  83.0 6.5 %collective-permute-done.11.c = bf16[528,256]{1,0:T(8,128)(2,1)S(1)} collective-permute-done((bf16[528,256]{1,0:T(8,128)(2,1)S(1)}, bf16[528,256]{1,0:T(8,128)(2,1)S(1)}, u32[]{:S(2)}, u32[]{:S(2)}) %collective-permute-start.11) | collective-permute-done | bytes 270368 | tf_op jit(solution)/shard_map/ppermute | solution.py:182
  91.2 3.8 %collective-permute-start.13 = (bf16[528,256]{1,0:T(8,128)(2,1)S(1)}, bf16[528,256]{1,0:T(8,128)(2,1)S(1)}, u32[]{:S(2)}, u32[]{:S(2)}) collective-permute-start(bf16[528,256]{1,0:T(8,128)(2,1)S(1)} %shard_map.71), channel_id=1, source_target_pairs={{0,16},{16,32},{32,48},{48,66},{2,18},{18,34},{34,50},{50,64},{64,... | collective-permute-start | bytes 811016 | tf_op jit(solution)/shard_map/ppermute | solution.py:252
  95.0 3.7 %collective-permute-start.16 = (bf16[400,256]{1,0:T(8,128)(2,1)S(1)}, bf16[400,256]{1,0:T(8,128)(2,1)S(1)}, u32[]{:S(2)}, u32[]{:S(2)}) collective-permute-start(bf16[400,256]{1,0:T(8,128)(2,1)S(1)} %slice.9), channel_id=1, source_target_pairs={{0,18},{16,34},{32,50},{48,64},{2,16},{18,32},{34,48},{50,66},{64,... | collective-permute-start | bytes 614408 | tf_op jit(solution)/shard_map/ppermute | solution.py:251
  98.7 4.8 %collective-permute-start.14 = (bf16[128,256]{1,0:T(8,128)(2,1)S(1)}, bf16[128,256]{1,0:T(8,128)(2,1)S(1)}, u32[]{:S(2)}, u32[]{:S(2)}) collective-permute-start(bf16[128,256]{1,0:T(8,128)(2,1)S(1)} %slice.8), channel_id=1, source_target_pairs={{0,32},{16,48},{32,2},{48,18},{2,34},{18,50},{34,0},{50,16},{64,96... | collective-permute-start | bytes 196616 | tf_op jit(solution)/shard_map/ppermute | solution.py:250
  103.6 4.8 %collective-permute-done.14 = bf16[128,256]{1,0:T(8,128)(2,1)S(1)} collective-permute-done((bf16[128,256]{1,0:T(8,128)(2,1)S(1)}, bf16[128,256]{1,0:T(8,128)(2,1)S(1)}, u32[]{:S(2)}, u32[]{:S(2)}) %collective-permute-start.14) | collective-permute-done | bytes 65568 | tf_op jit(solution)/shard_map/ppermute | solution.py:250
  108.4 5.1 %collective-permute-start.15 = (bf16[128,256]{1,0:T(8,128)(2,1)S(1)}, bf16[128,256]{1,0:T(8,128)(2,1)S(1)}, u32[]{:S(2)}, u32[]{:S(2)}) collective-permute-start(bf16[128,256]{1,0:T(8,128)(2,1)S(1)} %collective-permute-done.14), channel_id=1, source_target_pairs={{32,18},{48,34},{2,50},{18,64},{34,16},{50,32},{0,48},{16,66},{96,... | collective-permute-start | bytes 196616 | tf_op jit(solution)/shard_map/ppermute | solution.py:253
  113.6 5.3 %collective-permute-start.25 = (bf16[2176,256]{1,0:T(8,128)(2,1)S(1)}, bf16[2176,256]{1,0:T(8,128)(2,1)S(1)}, u32[]{:S(2)}, u32[]{:S(2)}) collective-permute-start(bf16[2176,256]{1,0:T(8,128)(2,1)S(1)} %get-tuple-element.26), channel_id=1, source_target_pairs={{0,1},{1,0},{2,3},{3,2},{4,5},{5,4},{6,7},{7,6},{8,9},{9,8},{10,11... | collective-permute-start | bytes 3342344 | tf_op jit(solution)/shard_map/ppermute | solution.py:257
  119.0 5.6 %collective-permute-start.17 = (bf16[512,256]{1,0:T(8,128)(2,1)S(1)}, bf16[512,256]{1,0:T(8,128)(2,1)S(1)}, u32[]{:S(2)}, u32[]{:S(2)}) collective-permute-start(bf16[512,256]{1,0:T(8,128)(2,1)S(1)} %shard_map.72), channel_id=1, source_target_pairs={{0,12},{4,0},{8,4},{12,8},{1,13},{5,1},{9,5},{13,9},{2,14},{6,2},{... | collective-permute-start | bytes 786440 | tf_op jit(solution)/shard_map/ppermute | solution.py:182
  129.0 5.5 %collective-permute-done.17 = bf16[512,256]{1,0:T(8,128)(2,1)S(1)} collective-permute-done((bf16[512,256]{1,0:T(8,128)(2,1)S(1)}, bf16[512,256]{1,0:T(8,128)(2,1)S(1)}, u32[]{:S(2)}, u32[]{:S(2)}) %collective-permute-start.17) | collective-permute-done | bytes 262176 | tf_op jit(solution)/shard_map/ppermute | solution.py:182
  134.5 7.3 %collective-permute-done.19 = bf16[512,256]{1,0:T(8,128)(2,1)S(1)} collective-permute-done((bf16[512,256]{1,0:T(8,128)(2,1)S(1)}, bf16[512,256]{1,0:T(8,128)(2,1)S(1)}, u32[]{:S(2)}, u32[]{:S(2)}) %collective-permute-start.19) | collective-permute-done | bytes 262176 | tf_op jit(solution)/shard_map/ppermute | solution.py:182
  (66 shorter events, 34.4 us)
Async XLA Ops:
  2.3 21.2 %collective-permute-start = (bf16[256,256]{1,0:T(8,128)(2,1)S(1)}, bf16[256,256]{1,0:T(8,128)(2,1)S(1)}, u32[]{:S(2)}, u32[]{:S(2)}) collective-permute-start(bf16[256,256]{1,0:T(8,128)(2,1)S(1)} %and_select_fusion), channel_id=1, source_target_pairs={{0,12},{4,0},{8,4},{12,8},{1,13},{5,1},{9,5},{13,9},{2,14},{6,2},{... | collective-permute-start | bytes 393224 | tf_op jit(solution)/shard_map/ppermute | solution.py:182
  6.7 16.8 %collective-permute-start.1 = (bf16[256,256]{1,0:T(8,128)(2,1)S(1)}, bf16[256,256]{1,0:T(8,128)(2,1)S(1)}, u32[]{:S(2)}, u32[]{:S(2)}) collective-permute-start(bf16[256,256]{1,0:T(8,128)(2,1)S(1)} %and_select_fusion), channel_id=1, source_target_pairs={{0,8},{4,12},{8,0},{12,4},{1,9},{5,13},{9,1},{13,5},{2,10},{6,14},... | collective-permute-start | bytes 393224 | tf_op jit(solution)/shard_map/ppermute | solution.py:182
  9.1 14.4 %collective-permute-start.2 = (bf16[256,256]{1,0:T(8,128)(2,1)S(1)}, bf16[256,256]{1,0:T(8,128)(2,1)S(1)}, u32[]{:S(2)}, u32[]{:S(2)}) collective-permute-start(bf16[256,256]{1,0:T(8,128)(2,1)S(1)} %and_select_fusion), channel_id=1, source_target_pairs={{0,4},{4,8},{8,12},{12,0},{1,5},{5,9},{9,13},{13,1},{2,6},{6,10},{... | collective-permute-start | bytes 393224 | tf_op jit(solution)/shard_map/ppermute | solution.py:182
  11.7 15.7 %collective-permute-start.3 = (bf16[256,256]{1,0:T(8,128)(2,1)S(1)}, bf16[256,256]{1,0:T(8,128)(2,1)S(1)}, u32[]{:S(2)}, u32[]{:S(2)}) collective-permute-start(bf16[256,256]{1,0:T(8,128)(2,1)S(1)} %and_select_fusion), channel_id=1, source_target_pairs={{0,2},{2,0},{1,3},{3,1},{4,6},{6,4},{5,7},{7,5},{8,10},{10,8},{9,1... | collective-permute-start | bytes 393224 | tf_op jit(solution)/shard_map/ppermute | solution.py:220
  18.2 15.7 %collective-permute-start.5 = (bf16[256,256]{1,0:T(8,128)(2,1)S(1)}, bf16[256,256]{1,0:T(8,128)(2,1)S(1)}, u32[]{:S(2)}, u32[]{:S(2)}) collective-permute-start(bf16[256,256]{1,0:T(8,128)(2,1)S(1)} %and_select_fusion), channel_id=1, source_target_pairs={{0,10},{2,8},{4,14},{6,12},{8,2},{10,0},{12,6},{14,4},{1,11},{3,9}... | collective-permute-start | bytes 393224 | tf_op jit(solution)/shard_map/ppermute | solution.py:223
  23.6 19.0 %collective-permute-start.7 = (bf16[4,256,256]{2,1,0:T(8,128)(2,1)S(1)}, bf16[4,256,256]{2,1,0:T(8,128)(2,1)S(1)}, u32[]{:S(2)}, u32[]{:S(2)}) collective-permute-start(bf16[4,256,256]{2,1,0:T(8,128)(2,1)S(1)} %pad_maximum_fusion.1), channel_id=1, source_target_pairs={{0,1},{1,0},{2,3},{3,2},{4,5},{5,4},{6,7},{7,6},{8,9},{9,8},{10,11... | collective-permute-start | bytes 1572872 | tf_op jit(solution)/shard_map/ppermute | solution.py:222
  27.3 8.5 %collective-permute-start.4 = (bf16[256,256]{1,0:T(8,128)(2,1)S(1)}, bf16[256,256]{1,0:T(8,128)(2,1)S(1)}, u32[]{:S(2)}, u32[]{:S(2)}) collective-permute-start(bf16[256,256]{1,0:T(8,128)(2,1)S(1)} %collective-permute-done.3), channel_id=1, source_target_pairs={{0,12},{4,0},{8,4},{12,8},{1,13},{5,1},{9,5},{13,9},{2,14},{6,2},{... | collective-permute-start | bytes 393224 | tf_op jit(solution)/shard_map/ppermute | solution.py:182
  31.6 7.9 %collective-permute-start.6 = (bf16[256,256]{1,0:T(8,128)(2,1)S(1)}, bf16[256,256]{1,0:T(8,128)(2,1)S(1)}, u32[]{:S(2)}, u32[]{:S(2)}) collective-permute-start(bf16[256,256]{1,0:T(8,128)(2,1)S(1)} %collective-permute-done.3), channel_id=1, source_target_pairs={{0,4},{4,8},{8,12},{12,0},{1,5},{5,9},{9,13},{13,1},{2,6},{6,10},{... | collective-permute-start | bytes 393224 | tf_op jit(solution)/shard_map/ppermute | solution.py:182
  47.8 22.7 %collective-permute-start.9 = (bf16[2064,256]{1,0:T(8,128)(2,1)S(1)}, bf16[2064,256]{1,0:T(8,128)(2,1)S(1)}, u32[]{:S(2)}, u32[]{:S(2)}) collective-permute-start(bf16[2064,256]{1,0:T(8,128)(2,1)S(1)} %get-tuple-element.17), channel_id=1, source_target_pairs={{0,1},{1,0},{2,3},{3,2},{4,5},{5,4},{6,7},{7,6},{8,9},{9,8},{10,11... | collective-permute-start | bytes 3170312 | tf_op jit(solution)/shard_map/ppermute | solution.py:237
  50.1 13.9 %collective-permute-start.21 = (bf16[272,256]{1,0:T(8,128)(2,1)S(1)}, bf16[272,256]{1,0:T(8,128)(2,1)S(1)}, u32[]{:S(2)}, u32[]{:S(2)}) collective-permute-start(bf16[272,256]{1,0:T(8,128)(2,1)S(1)} %get-tuple-element.14.message), channel_id=1, source_target_pairs={{0,2},{2,0},{1,3},{3,1},{4,6},{6,4},{5,7},{7,5},{8,10},{10,8},{9,1... | collective-permute-start | bytes 417800 | tf_op jit(solution)/shard_map/ppermute | solution.py:238
  64.0 16.8 %collective-permute-start.22 = (bf16[544,256]{1,0:T(8,128)(2,1)S(1)}, bf16[544,256]{1,0:T(8,128)(2,1)S(1)}, u32[]{:S(2)}, u32[]{:S(2)}) collective-permute-start(bf16[544,256]{1,0:T(8,128)(2,1)S(1)} %get-tuple-element.34), channel_id=1, source_target_pairs={{0,12},{4,0},{8,4},{12,8},{1,13},{5,1},{9,5},{13,9},{2,14},{6,2},{... | collective-permute-start | bytes 835592 | tf_op jit(solution)/shard_map/ppermute | solution.py:182
  66.0 37.6 %collective-permute-start.23 = (bf16[544,256]{1,0:T(8,128)(2,1)S(1)}, bf16[544,256]{1,0:T(8,128)(2,1)S(1)}, u32[]{:S(2)}, u32[]{:S(2)}) collective-permute-start(bf16[544,256]{1,0:T(8,128)(2,1)S(1)} %get-tuple-element.34), channel_id=1, source_target_pairs={{0,8},{4,12},{8,0},{12,4},{1,9},{5,13},{9,1},{13,5},{2,10},{6,14},... | collective-permute-start | bytes 835592 | tf_op jit(solution)/shard_map/ppermute | solution.py:182
  70.7 12.3 %collective-permute-start.10 = (bf16[528,256]{1,0:T(8,128)(2,1)S(1)}, bf16[528,256]{1,0:T(8,128)(2,1)S(1)}, u32[]{:S(2)}, u32[]{:S(2)}) collective-permute-start(bf16[528,256]{1,0:T(8,128)(2,1)S(1)} %get-tuple-element.19), channel_id=1, source_target_pairs={{0,8},{4,12},{8,0},{12,4},{1,9},{5,13},{9,1},{13,5},{2,10},{6,14},... | collective-permute-start | bytes 811016 | tf_op jit(solution)/shard_map/ppermute | solution.py:182
  74.3 15.2 %collective-permute-start.11 = (bf16[528,256]{1,0:T(8,128)(2,1)S(1)}, bf16[528,256]{1,0:T(8,128)(2,1)S(1)}, u32[]{:S(2)}, u32[]{:S(2)}) collective-permute-start(bf16[528,256]{1,0:T(8,128)(2,1)S(1)} %get-tuple-element.20), channel_id=1, source_target_pairs={{0,4},{4,8},{8,12},{12,0},{1,5},{5,9},{9,13},{13,1},{2,6},{6,10},{... | collective-permute-start | bytes 811016 | tf_op jit(solution)/shard_map/ppermute | solution.py:182
  77.7 13.4 %collective-permute-start.12 = (bf16[528,256]{1,0:T(8,128)(2,1)S(1)}, bf16[528,256]{1,0:T(8,128)(2,1)S(1)}, u32[]{:S(2)}, u32[]{:S(2)}) collective-permute-start(bf16[528,256]{1,0:T(8,128)(2,1)S(1)} %get-tuple-element.21), channel_id=1, source_target_pairs={{0,12},{4,0},{8,4},{12,8},{1,13},{5,1},{9,5},{13,9},{2,14},{6,2},{... | collective-permute-start | bytes 811016 | tf_op jit(solution)/shard_map/ppermute | solution.py:182
  80.8 32.7 %collective-permute-start.24 = (bf16[544,256]{1,0:T(8,128)(2,1)S(1)}, bf16[544,256]{1,0:T(8,128)(2,1)S(1)}, u32[]{:S(2)}, u32[]{:S(2)}) collective-permute-start(bf16[544,256]{1,0:T(8,128)(2,1)S(1)} %get-tuple-element.34), channel_id=1, source_target_pairs={{0,4},{4,8},{8,12},{12,0},{1,5},{5,9},{9,13},{13,1},{2,6},{6,10},{... | collective-permute-start | bytes 835592 | tf_op jit(solution)/shard_map/ppermute | solution.py:182
  91.2 27.7 %collective-permute-start.13 = (bf16[528,256]{1,0:T(8,128)(2,1)S(1)}, bf16[528,256]{1,0:T(8,128)(2,1)S(1)}, u32[]{:S(2)}, u32[]{:S(2)}) collective-permute-start(bf16[528,256]{1,0:T(8,128)(2,1)S(1)} %shard_map.71), channel_id=1, source_target_pairs={{0,16},{16,32},{32,48},{48,66},{2,18},{18,34},{34,50},{50,64},{64,... | collective-permute-start | bytes 811016 | tf_op jit(solution)/shard_map/ppermute | solution.py:252
  95.0 23.8 %collective-permute-start.16 = (bf16[400,256]{1,0:T(8,128)(2,1)S(1)}, bf16[400,256]{1,0:T(8,128)(2,1)S(1)}, u32[]{:S(2)}, u32[]{:S(2)}) collective-permute-start(bf16[400,256]{1,0:T(8,128)(2,1)S(1)} %slice.9), channel_id=1, source_target_pairs={{0,18},{16,34},{32,50},{48,64},{2,16},{18,32},{34,48},{50,66},{64,... | collective-permute-start | bytes 614408 | tf_op jit(solution)/shard_map/ppermute | solution.py:251
  98.7 9.7 %collective-permute-start.14 = (bf16[128,256]{1,0:T(8,128)(2,1)S(1)}, bf16[128,256]{1,0:T(8,128)(2,1)S(1)}, u32[]{:S(2)}, u32[]{:S(2)}) collective-permute-start(bf16[128,256]{1,0:T(8,128)(2,1)S(1)} %slice.8), channel_id=1, source_target_pairs={{0,32},{16,48},{32,2},{48,18},{2,34},{18,50},{34,0},{50,16},{64,96... | collective-permute-start | bytes 196616 | tf_op jit(solution)/shard_map/ppermute | solution.py:250
  108.4 10.5 %collective-permute-start.15 = (bf16[128,256]{1,0:T(8,128)(2,1)S(1)}, bf16[128,256]{1,0:T(8,128)(2,1)S(1)}, u32[]{:S(2)}, u32[]{:S(2)}) collective-permute-start(bf16[128,256]{1,0:T(8,128)(2,1)S(1)} %collective-permute-done.14), channel_id=1, source_target_pairs={{32,18},{48,34},{2,50},{18,64},{34,16},{50,32},{0,48},{16,66},{96,... | collective-permute-start | bytes 196616 | tf_op jit(solution)/shard_map/ppermute | solution.py:253
  113.6 30.7 %collective-permute-start.25 = (bf16[2176,256]{1,0:T(8,128)(2,1)S(1)}, bf16[2176,256]{1,0:T(8,128)(2,1)S(1)}, u32[]{:S(2)}, u32[]{:S(2)}) collective-permute-start(bf16[2176,256]{1,0:T(8,128)(2,1)S(1)} %get-tuple-element.26), channel_id=1, source_target_pairs={{0,1},{1,0},{2,3},{3,2},{4,5},{5,4},{6,7},{7,6},{8,9},{9,8},{10,11... | collective-permute-start | bytes 3342344 | tf_op jit(solution)/shard_map/ppermute | solution.py:257
  119.0 15.5 %collective-permute-start.17 = (bf16[512,256]{1,0:T(8,128)(2,1)S(1)}, bf16[512,256]{1,0:T(8,128)(2,1)S(1)}, u32[]{:S(2)}, u32[]{:S(2)}) collective-permute-start(bf16[512,256]{1,0:T(8,128)(2,1)S(1)} %shard_map.72), channel_id=1, source_target_pairs={{0,12},{4,0},{8,4},{12,8},{1,13},{5,1},{9,5},{13,9},{2,14},{6,2},{... | collective-permute-start | bytes 786440 | tf_op jit(solution)/shard_map/ppermute | solution.py:182
  124.5 10.0 %collective-permute-start.18 = (bf16[512,256]{1,0:T(8,128)(2,1)S(1)}, bf16[512,256]{1,0:T(8,128)(2,1)S(1)}, u32[]{:S(2)}, u32[]{:S(2)}) collective-permute-start(bf16[512,256]{1,0:T(8,128)(2,1)S(1)} %shard_map.72), channel_id=1, source_target_pairs={{0,8},{4,12},{8,0},{12,4},{1,9},{5,13},{9,1},{13,5},{2,10},{6,14},... | collective-permute-start | bytes 786440 | tf_op jit(solution)/shard_map/ppermute | solution.py:182
  126.5 15.3 %collective-permute-start.19 = (bf16[512,256]{1,0:T(8,128)(2,1)S(1)}, bf16[512,256]{1,0:T(8,128)(2,1)S(1)}, u32[]{:S(2)}, u32[]{:S(2)}) collective-permute-start(bf16[512,256]{1,0:T(8,128)(2,1)S(1)} %shard_map.72), channel_id=1, source_target_pairs={{0,4},{4,8},{8,12},{12,0},{1,5},{5,9},{9,13},{13,1},{2,6},{6,10},{... | collective-permute-start | bytes 786440 | tf_op jit(solution)/shard_map/ppermute | solution.py:182
  (5 other events, 41.8 us)

commit v4 on v2

--- a/solution.py
+++ b/solution.py
@@ -59,54 +59,47 @@
     return side * 8 + lax.rem(meta[3] + j // 2, 4) * 2 + j % 2
 
 
-def first_kernel(meta, picks, pool, left, right, first_out, message, stats, send, turned_out, inner, lv):
+def first_kernel(meta, picks, pool, left, right, message, inner):
     channels, width = left.shape[0], left.shape[1]
-    half = channels // 2
     for t in range(channels):
-        c, yh, x = place(picks[t], meta)
-        inner[:, t * width:(t + 1) * width] = dot(left[t], pool[(c * 2 + yh) * 4 + x]).astype(BF)
+        c, yh, step = place(picks[t], meta)
+        inner[:, t * width:(t + 1) * width] = dot(left[t], pool[(c * 2 + yh) * 4 + step]).astype(BF)
     product = dot(inner[...], right[...].reshape(channels * width, width))
     size = meta[0]
     product = jnp.where(live(size, product.shape), product, 0.0).astype(BF)
-    first_out[...] = product
     message[0:width, :] = product
     value = product.astype(F32)
     columns = jnp.sum(value * value, axis=0, keepdims=True)
     squares = jnp.broadcast_to(jnp.sum(columns, axis=1, keepdims=True), (1, width))
     count = jnp.full((1, width), size * size, jnp.int32).astype(F32)
-    tile = pack(squares, count)
-    message[width:width + TILE, :] = tile
-    stats[...] = tile
-    send[half * width:half * width + TILE, :] = tile
-    turned = value.T.astype(BF)
-    turned_out[...] = turned
-    for j in range(half):
-        lv[j] = dot(left[channel(meta, 1 - meta[1], j)], product).astype(BF)
-    for j in range(half):
-        send[j * width:(j + 1) * width, :] = dot(turned, lv[j]).astype(BF)
-
-
-def keep_kernel(meta, message, turned, left, keep, lv):
-    half, width = left.shape[0] // 2, left.shape[1]
+    message[width:width + TILE, :] = pack(squares, count)
+
+
+def terms(message, left_of, lv, count):
+    width = message.shape[1]
     first = message[0:width, :]
-    for j in range(half):
-        lv[j] = dot(left[channel(meta, meta[1], j)], first).astype(BF)
-    for j in range(half):
-        keep[j * width:(j + 1) * width, :] = dot(turned[...], lv[j]).astype(BF)
-
-
-def core_sum_kernel(keep, stats, arrived, *outs):
-    rows = keep.shape[0]
-    quarter = rows // 4
-    q0, c0 = unpack(stats[...])
-    q1, c1 = unpack(arrived[rows:rows + TILE, :])
+    turned = first.astype(F32).T.astype(BF)
+    for j in range(count):
+        lv[j] = dot(left_of(j), first).astype(BF)
+    return [lambda j=j: dot(turned, lv[j]) for j in range(count)]
+
+
+def keep_kernel(meta, message, left, keep, lv):
+    half = left.shape[0] // 2
+    for j, term in enumerate(terms(message, lambda j: left[channel(meta, meta[1], j)], lv, half)):
+        keep[j] = term()
+
+
+def core_sum_kernel(meta, message, keep, left, *refs):
+    own, lv, outs = refs[0], refs[-1], refs[1:-1]
+    half, width = left.shape[0], left.shape[1]
+    q0, c0 = unpack(own[width:width + TILE, :])
+    q1, c1 = unpack(message[width:width + TILE, :])
     tile = pack(q0 + q1, c0 + c1)
-    for step, out in enumerate(outs):
-        at = step * quarter
-        out[0:quarter, :] = (
-            keep[at:at + quarter, :].astype(F32) + arrived[at:at + quarter, :].astype(F32)
-        ).astype(BF)
-        out[quarter:quarter + TILE, :] = tile
+    for out in outs:
+        out[2 * width:2 * width + TILE, :] = tile
+    for j, term in enumerate(terms(message, lambda j: left[channel(meta, 0, j)], lv, half)):
+        outs[j // 2][(j % 2) * width:(j % 2 + 1) * width, :] = (keep[j] + term()).astype(BF)
 
 
 def row_sum_kernel(a, b, c, d, out):
@@ -129,33 +122,49 @@
     out[...] = (total * weight).astype(BF)
 
 
-def pool_two_kernel(meta, picks, pool, left, right, g_out, base):
+def pool_two_kernel(meta, picks, pool, left, right, g_own, g_send, base, g):
     channels, width = left.shape[0], left.shape[1]
+    half = channels // 2
     span = width + TILE
     squares = count = jnp.zeros((1, width), F32)
     for at in range(16):
         q, c = unpack(pool[at * span + width:(at + 1) * span, :])
         squares, count = squares + q, count + c
     scale = lax.rsqrt(squares / count + 1e-6)
-    for t in range(channels):
-        c, yh, x = place(picks[t], meta)
-        start = pl.multiple_of(((c * 4 + x) * 2 + yh) * span, TILE)
-        g_out[t] = (dot(pool[pl.ds(start, width), :], right[t]) * scale).astype(BF)
-    total = dot(left[0], g_out[0])
-    for t in range(1, channels):
-        total = total + dot(left[t], g_out[t])
+    for j in range(channels):
+        t = channel(meta, lax.rem(meta[1] + j // half, 2), j % half)
+        c, yh, step = place(picks[t], meta)
+        start = pl.multiple_of(((c * 4 + step) * 2 + yh) * span, TILE)
+        block = (dot(pool[pl.ds(start, width), :], right[t]) * scale).astype(BF)
+        (g_own if j < half else g_send)[j % half] = block
+        g[j] = left[t]
+    total = dot(g[0], g_own[0])
+    for j in range(1, half):
+        total = total + dot(g[j], g_own[j])
+    for j in range(half):
+        total = total + dot(g[half + j], g_send[j])
     base[...] = total
 
 
-def half_kernel(final, meta, edges, g, start, out):
+def other_kernel(edges, g, out):
     width = g.shape[1]
-    side = meta[1] if not final else 1 - meta[1]
-    total = start[...]
-    for j in range(edges.shape[0] // width):
-        total = total + dot(edges[j * width:(j + 1) * width, :], g[channel(meta, side, j)])
-    if final:
-        total = jnp.where(live(meta[0], total.shape), total, 0.0)
-    out[...] = total.astype(out.dtype)
+    total = dot(edges[0:width, :], g[0])
+    for j in range(1, g.shape[0]):
+        total = total + dot(edges[j * width:(j + 1) * width, :], g[j])
+    out[...] = total
+
+
+def own_kernel(edges, g, base, out):
+    width = g.shape[1]
+    total = base[...]
+    for j in range(g.shape[0]):
+        total = total + dot(edges[j * width:(j + 1) * width, :], g[j])
+    out[...] = total
+
+
+def second_kernel(meta, own, other, out):
+    total = own[...] + other[...]
+    out[...] = jnp.where(live(meta[0], total.shape), total, 0.0).astype(out.dtype)
 
 
 def call(kernel, shapes, specs, scratch, flops, moved):
@@ -214,34 +223,32 @@
     span = width + TILE
     unit = 2 * channels * width**3
     block_bytes = width * width * 2
-    meta = jnp.stack([size, lax.axis_index("c").astype(jnp.int32), lax.axis_index("yh").astype(jnp.int32),
-                      lax.axis_index("x").astype(jnp.int32)])
+    meta = jnp.stack([size, *(lax.axis_index(axis).astype(jnp.int32) for axis in ("c", "yh", "x"))])
 
     masked = jnp.where(live(size, (width, width)), wave[0, 0], jnp.zeros((), BF))
     masked_other = lax.ppermute(masked, "yh", SWAP)
     own = jnp.stack(round_x(masked))
+    left_send = lax.dynamic_slice_in_dim(left, (1 - lax.axis_index("c")) * half, half)
+    left_other = lax.ppermute(left_send, "c", SWAP)
     across = lax.ppermute(own, "c", SWAP)
     own_other = jnp.stack(round_x(masked_other))
     across_other = lax.ppermute(own_other, "c", SWAP)
     pool = jnp.concatenate([own, own_other, across, across_other], axis=0)
     stack = pltpu.VMEM((half, width, width), BF)
-    first, message, stats, send, turned = call(
-        first_kernel,
-        [((width, width), BF), ((span, width), BF), ((TILE, width), BF),
-         ((half * width + TILE, width), BF), ((width, width), BF)],
-        [SMEM, SMEM, VMEM, VMEM, VMEM],
-        [pltpu.VMEM((width, channels * width), BF), stack],
-        3 * unit, 4 * channels * block_bytes,
+    message = call(
+        first_kernel, one((span, width), BF), [SMEM, SMEM, VMEM, VMEM, VMEM],
+        [pltpu.VMEM((width, channels * width), BF)], 2 * unit, 4 * channels * block_bytes,
     )(meta, picks, pool, left, right)
-
-    arrived = lax.ppermute(send, "c", SWAP)
+    first = message[0:width]
+
+    message_core = lax.ppermute(message, "c", SWAP)
     message_other = lax.ppermute(message, "yh", SWAP)
     keep = call(
-        keep_kernel, one((half * width, width), BF), [SMEM, VMEM, VMEM, VMEM], [stack], unit, 2 * channels * block_bytes
-    )(meta, message, turned, left)
+        keep_kernel, one((half, width, width), F32), [SMEM, VMEM, VMEM], [stack], unit, 2 * channels * block_bytes
+    )(meta, message, left)
     parts = call(
-        core_sum_kernel, [((2 * width + TILE, width), BF)] * 4, [VMEM] * 3, [], 1 << 20, 3 * half * block_bytes
-    )(keep, stats, arrived)
+        core_sum_kernel, [((2 * width + TILE, width), BF)] * 4, [SMEM] + [VMEM] * 4, [stack], unit, 3 * half * block_bytes
+    )(meta, message_core, keep, left_other, message)
     arrived_x = [along_x(parts[2], 2), along_x(parts[1], 1), along_x(parts[3], 3)]
     row = call(
         row_sum_kernel, one((2 * width + TILE, width), BF), [VMEM] * 4, [], 1 << 20, 10 * block_bytes
@@ -254,28 +261,30 @@
     two_own = jnp.concatenate(round_x(both))
     two_other = lax.ppermute(two_own, "c", SWAP)
     pool_two = jnp.concatenate([two_own, two_other])
-    g, base = call(
+    g_own, g_send, base = call(
         pool_two_kernel,
-        [((channels, width, width), BF), ((width, width), F32)],
+        [((half, width, width), BF), ((half, width, width), BF), ((width, width), F32)],
         [SMEM, SMEM, VMEM, VMEM, VMEM],
-        [],
+        [pltpu.VMEM((channels, width, width), BF)],
         2 * unit, 4 * channels * block_bytes,
     )(meta, picks, pool_two, left, right)
+    g_other = lax.ppermute(g_send, "c", SWAP)
 
     factor = 1.0 / (width * math.sqrt(channels_of(sector_size)))
     edge = call(
         lambda *refs: edge_kernel(factor, *refs), one((2 * width, width), BF), [VMEM] * 2, [], 1 << 20, 12 * block_bytes
     )(from_near, from_far)
     edges_own = jnp.concatenate(round_x(edge))
-    edges_other = lax.ppermute(edges_own, "c", SWAP)
-    partial = call(
-        lambda *refs: half_kernel(False, *refs), one((width, width), F32), [SMEM, VMEM, VMEM, VMEM], [], unit // 2,
-        3 * half * block_bytes,
-    )(meta, edges_own, g, base)
-    second = call(
-        lambda *refs: half_kernel(True, *refs), one((width, width), BF), [SMEM, VMEM, VMEM, VMEM], [], unit // 2,
-        3 * half * block_bytes,
-    )(meta, edges_other, g, partial)
+    for_other = call(other_kernel, one((width, width), F32), [VMEM] * 2, [], unit // 2, 3 * half * block_bytes)(
+        edges_own, g_other
+    )
+    from_other = lax.ppermute(for_other, "c", SWAP)
+    from_own = call(own_kernel, one((width, width), F32), [VMEM] * 3, [], unit // 2, 3 * half * block_bytes)(
+        edges_own, g_own, base
+    )
+    second = call(second_kernel, one((width, width), BF), [SMEM, VMEM, VMEM], [], 1 << 18, 3 * block_bytes)(
+        meta, from_own, from_other
+    )
     return (first[None, None], second[None, None])
 
 

time: 152 us -> 166 us (1.092)
  waiting for transfers between devices: 52.8 us -> 60.1 us
  local copies, waits for them, and re-layouts: 0.42 us -> 7.23 us
    unnamed x18 -> x20, local copies, waits for them, and re-layouts: 0.27 us -> 5.55 us
    ppermute x2 -> x4, starting transfers between devices: 4.68 us -> 9.52 us  [the longest x1 2.8 us: body(): g_other = lax.ppermute(g_send, 'c', SWAP)]
    ppermute x15, waiting for transfers between devices: 27.1 us -> 31.9 us  [along_x(): lax.ppermute(value, 'x', [(i, (i + step) % count) for i in range(count)])]
    ppermute x15, starting transfers between devices: 45.3 us -> 41.7 us  [along_x(): lax.ppermute(value, 'x', [(i, (i + step) % count) for i in range(count)])]
    ppermute x1, waiting for transfers between devices: 0.01 us -> 1.9 us  [body(): from_near = lax.ppermute(row, YROW, near)]
    ppermute x1, waiting for transfers between devices: 17.4 us -> 19.1 us  [body(): from_far = lax.ppermute(row, YROW, far)]
    pallas_call x6 -> x7, Pallas kernels: 9.77 us -> 9.78 us  [the longest x1 3.09 us: body(): call(first_kernel, one((span, width), BF), [SMEM, SMEM, VMEM, VMEM, VMEM]...]
  transfers between devices with their start and end apart: 24 -> 26, of which waited for: 9 -> 11; matrix products, arithmetic and copies ran while one was open for 1% -> 5% of each run, Pallas kernels for 3% -> 3%
where the time goes in v4:
time: 166 us; the launch traced here: 165 us
  starting transfers between devices  82.8 us (50%)
  waiting for transfers between devices  60.1 us (36%)
  Pallas kernels  10 us (6%)
  local copies, waits for them, and re-layouts  7.23 us (4%)
  other arithmetic  2.97 us (2%)
  between operations  1.69 us (1%)
    ppermute x15, starting transfers between devices, along_x(): lax.ppermute(value, 'x', [(i, (i + step) % count) for i in range(count)])  41.7 us
    ppermute x15, waiting for transfers between devices, along_x(): lax.ppermute(value, 'x', [(i, (i + step) % count) for i in range(count)])  31.9 us
    ppermute x1, waiting for transfers between devices, body(): from_far = lax.ppermute(row, YROW, far)  19.1 us
    ppermute x1, waiting for transfers between devices, body(): message_other = lax.ppermute(message, 'yh', SWAP)  7.06 us
    ppermute x1, starting transfers between devices, body(): message_other = lax.ppermute(message, 'yh', SWAP)  6.92 us
    ppermute x1, starting transfers between devices, body(): masked_other = lax.ppermute(masked, 'yh', SWAP)  6.55 us
    unnamed x20, local copies, waits for them, and re-layouts  5.55 us
    ppermute x1, starting transfers between devices, body(): across_other = lax.ppermute(own_other, 'c', SWAP)  4.47 us
  transfers between devices with their start and end apart: 26, of which 11 were waited for; matrix products, arithmetic and copies ran while one was open for 5% of the time, Pallas kernels for 3%

profile of v4, /device:TPU:201, one launch (start us, length us, event | category | flops | bytes accessed | tf_op | source)
XLA Modules:
  0.0 164.8 jit_solution(7808812724587880120)
XLA Ops:
  2.3 4.4 %collective-permute-start = (bf16[256,256]{1,0:T(8,128)(2,1)S(1)}, bf16[256,256]{1,0:T(8,128)(2,1)S(1)}, u32[]{:S(2)}, u32[]{:S(2)}) collective-permute-start(bf16[256,256]{1,0:T(8,128)(2,1)S(1)} %and_select_fusion), channel_id=1, source_target_pairs={{0,12},{4,0},{8,4},{12,8},{1,13},{5,1},{9,5},{13,9},{2,14},{6,2},{... | collective-permute-start | bytes 393224 | tf_op jit(solution)/shard_map/ppermute | solution.py:189
  9.1 2.5 %collective-permute-start.2 = (bf16[256,256]{1,0:T(8,128)(2,1)S(1)}, bf16[256,256]{1,0:T(8,128)(2,1)S(1)}, u32[]{:S(2)}, u32[]{:S(2)}) collective-permute-start(bf16[256,256]{1,0:T(8,128)(2,1)S(1)} %and_select_fusion), channel_id=1, source_target_pairs={{0,4},{4,8},{8,12},{12,0},{1,5},{5,9},{9,13},{13,1},{2,6},{6,10},{... | collective-permute-start | bytes 393224 | tf_op jit(solution)/shard_map/ppermute | solution.py:189
  11.7 6.6 %collective-permute-start.3 = (bf16[256,256]{1,0:T(8,128)(2,1)S(1)}, bf16[256,256]{1,0:T(8,128)(2,1)S(1)}, u32[]{:S(2)}, u32[]{:S(2)}) collective-permute-start(bf16[256,256]{1,0:T(8,128)(2,1)S(1)} %and_select_fusion), channel_id=1, source_target_pairs={{0,2},{2,0},{1,3},{3,1},{4,6},{6,4},{5,7},{7,5},{8,10},{10,8},{9,1... | collective-permute-start | bytes 393224 | tf_op jit(solution)/shard_map/ppermute | solution.py:229
  20.0 3.7 %collective-permute-start.7 = (bf16[4,256,256]{2,1,0:T(8,128)(2,1)S(1)}, bf16[4,256,256]{2,1,0:T(8,128)(2,1)S(1)}, u32[]{:S(2)}, u32[]{:S(2)}) collective-permute-start(bf16[4,256,256]{2,1,0:T(8,128)(2,1)S(1)} %pad_maximum_fusion.1), channel_id=1, source_target_pairs={{0,1},{1,0},{2,3},{3,2},{4,5},{5,4},{6,7},{7,6},{8,9},{9,8},{10,11... | collective-permute-start | bytes 1572872 | tf_op jit(solution)/shard_map/ppermute | solution.py:233
  23.8 4.0 %collective-permute-start.4 = (bf16[256,256]{1,0:T(8,128)(2,1)S(1)}, bf16[256,256]{1,0:T(8,128)(2,1)S(1)}, u32[]{:S(2)}, u32[]{:S(2)}) collective-permute-start(bf16[256,256]{1,0:T(8,128)(2,1)S(1)} %collective-permute-done.3), channel_id=1, source_target_pairs={{0,12},{4,0},{8,4},{12,8},{1,13},{5,1},{9,5},{13,9},{2,14},{6,2},{... | collective-permute-start | bytes 393224 | tf_op jit(solution)/shard_map/ppermute | solution.py:189
  27.8 3.1 %collective-permute-start.5 = (bf16[256,256]{1,0:T(8,128)(2,1)S(1)}, bf16[256,256]{1,0:T(8,128)(2,1)S(1)}, u32[]{:S(2)}, u32[]{:S(2)}) collective-permute-start(bf16[256,256]{1,0:T(8,128)(2,1)S(1)} %collective-permute-done.3), channel_id=1, source_target_pairs={{0,8},{4,12},{8,0},{12,4},{1,9},{5,13},{9,1},{13,5},{2,10},{6,14},... | collective-permute-start | bytes 393224 | tf_op jit(solution)/shard_map/ppermute | solution.py:189
  35.5 3.8 %collective-permute-done.6 = bf16[256,256]{1,0:T(8,128)(2,1)S(1)} collective-permute-done((bf16[256,256]{1,0:T(8,128)(2,1)S(1)}, bf16[256,256]{1,0:T(8,128)(2,1)S(1)}, u32[]{:S(2)}, u32[]{:S(2)}) %collective-permute-start.6) | collective-permute-done | bytes 131104 | tf_op jit(solution)/shard_map/ppermute | solution.py:189
  39.3 4.5 %collective-permute-start.8 = (bf16[4,256,256]{2,1,0:T(8,128)(2,1)S(1)}, bf16[4,256,256]{2,1,0:T(8,128)(2,1)S(1)}, u32[]{:S(2)}, u32[]{:S(2)}) collective-permute-start(bf16[4,256,256]{2,1,0:T(8,128)(2,1)S(1)} %pad_maximum_fusion.2), channel_id=1, source_target_pairs={{0,1},{1,0},{2,3},{3,2},{4,5},{5,4},{6,7},{7,6},{8,9},{9,8},{10,11... | collective-permute-start | bytes 1572872 | tf_op jit(solution)/shard_map/ppermute | solution.py:235
  47.4 3.1 %shard_map.68.message.refs_0_ = bf16[272,256]{1,0:T(8,128)(2,1)S(1)} custom-call(s32[4]{0:T(128)S(1)} %pad_add_fusion.meta, s32[16]{0:T(128)S(1)} %bitcast.39, bf16[16,256,256]{2,1,0:T(8,128)(2,1)} %constant_dynamic-update-slice_fusion.pool, bf16[16,256,256]{2,1,0:T(8,128)(2,1)S(1)} %bitcast.34, bf16[16,256,256]{2,1,0:T(8,128)(2,1)S(1)} %bitcast.37), custom_call_target="tpu_custom_call" | custom-call | flops 1073741824 | bytes 8388608 | tf_op jit(solution)/shard_map/pallas_call | solution.py:238
  50.5 6.9 %collective-permute-start.19 = (bf16[272,256]{1,0:T(8,128)(2,1)S(1)}, bf16[272,256]{1,0:T(8,128)(2,1)S(1)}, u32[]{:S(2)}, u32[]{:S(2)}) collective-permute-start(bf16[272,256]{1,0:T(8,128)(2,1)S(1)} %shard_map.68.message.refs_0_), channel_id=1, source_target_pairs={{0,2},{2,0},{1,3},{3,1},{4,6},{6,4},{5,7},{7,5},{8,10},{10,8},{9,1... | collective-permute-start | bytes 417800 | tf_op jit(solution)/shard_map/ppermute | solution.py:245
  57.4 7.1 %collective-permute-done.19 = bf16[272,256]{1,0:T(8,128)(2,1)S(1)} collective-permute-done((bf16[272,256]{1,0:T(8,128)(2,1)S(1)}, bf16[272,256]{1,0:T(8,128)(2,1)S(1)}, u32[]{:S(2)}, u32[]{:S(2)}) %collective-permute-start.19) | collective-permute-done | bytes 139296 | tf_op jit(solution)/shard_map/ppermute | solution.py:245
  68.9 2.9 %collective-permute-start.22 = (bf16[544,256]{1,0:T(8,128)(2,1)S(1)}, bf16[544,256]{1,0:T(8,128)(2,1)S(1)}, u32[]{:S(2)}, u32[]{:S(2)}) collective-permute-start(bf16[544,256]{1,0:T(8,128)(2,1)S(1)} %pad_maximum_fusion.3), channel_id=1, source_target_pairs={{0,4},{4,8},{8,12},{12,0},{1,5},{5,9},{9,13},{13,1},{2,6},{6,10},{... | collective-permute-start | bytes 835592 | tf_op jit(solution)/shard_map/ppermute | solution.py:189
  73.8 3.4 %collective-permute-done.21 = bf16[544,256]{1,0:T(8,128)(2,1)S(1)} collective-permute-done((bf16[544,256]{1,0:T(8,128)(2,1)S(1)}, bf16[544,256]{1,0:T(8,128)(2,1)S(1)}, u32[]{:S(2)}, u32[]{:S(2)}) %collective-permute-start.21) | collective-permute-done | bytes 278560 | tf_op jit(solution)/shard_map/ppermute | solution.py:189
  77.3 7.1 %collective-permute-done.22 = bf16[544,256]{1,0:T(8,128)(2,1)S(1)} collective-permute-done((bf16[544,256]{1,0:T(8,128)(2,1)S(1)}, bf16[544,256]{1,0:T(8,128)(2,1)S(1)}, u32[]{:S(2)}, u32[]{:S(2)}) %collective-permute-start.22) | collective-permute-done | bytes 278560 | tf_op jit(solution)/shard_map/ppermute | solution.py:189
  93.8 2.4 %collective-permute-start.11 = (bf16[528,256]{1,0:T(8,128)(2,1)S(1)}, bf16[528,256]{1,0:T(8,128)(2,1)S(1)}, u32[]{:S(2)}, u32[]{:S(2)}) collective-permute-start(bf16[528,256]{1,0:T(8,128)(2,1)S(1)} %get-tuple-element.10), channel_id=1, source_target_pairs={{0,8},{4,12},{8,0},{12,4},{1,9},{5,13},{9,1},{13,5},{2,10},{6,14},... | collective-permute-start | bytes 811016 | tf_op jit(solution)/shard_map/ppermute | solution.py:189
  98.6 4.2 %collective-permute-start.13 = (bf16[528,256]{1,0:T(8,128)(2,1)S(1)}, bf16[528,256]{1,0:T(8,128)(2,1)S(1)}, u32[]{:S(2)}, u32[]{:S(2)}) collective-permute-start(bf16[528,256]{1,0:T(8,128)(2,1)S(1)} %get-tuple-element.12), channel_id=1, source_target_pairs={{0,12},{4,0},{8,4},{12,8},{1,13},{5,1},{9,5},{13,9},{2,14},{6,2},{... | collective-permute-start | bytes 811016 | tf_op jit(solution)/shard_map/ppermute | solution.py:189
  104.9 2.8 %collective-permute-start.24 = (bf16[8,256,256]{2,1,0:T(8,128)(2,1)S(1)}, bf16[8,256,256]{2,1,0:T(8,128)(2,1)S(1)}, u32[]{:S(2)}, u32[]{:S(2)}) collective-permute-start(bf16[8,256,256]{2,1,0:T(8,128)(2,1)S(1)} %get-tuple-element.15), channel_id=1, source_target_pairs={{0,1},{1,0},{2,3},{3,2},{4,5},{5,4},{6,7},{7,6},{8,9},{9,8},{10,11... | collective-permute-start | bytes 3145736 | tf_op jit(solution)/shard_map/ppermute | solution.py:271
  107.8 3.7 %collective-permute-done.12.c = bf16[528,256]{1,0:T(8,128)(2,1)S(1)} collective-permute-done((bf16[528,256]{1,0:T(8,128)(2,1)S(1)}, bf16[528,256]{1,0:T(8,128)(2,1)S(1)}, u32[]{:S(2)}, u32[]{:S(2)}) %collective-permute-start.12) | collective-permute-done | bytes 270368 | tf_op jit(solution)/shard_map/ppermute | solution.py:189
  111.6 3.9 %collective-permute-start.14 = (bf16[528,256]{1,0:T(8,128)(2,1)S(1)}, bf16[528,256]{1,0:T(8,128)(2,1)S(1)}, u32[]{:S(2)}, u32[]{:S(2)}) collective-permute-start(bf16[528,256]{1,0:T(8,128)(2,1)S(1)} %shard_map.71), channel_id=1, source_target_pairs={{0,16},{2,18},{16,32},{18,34},{32,48},{34,50},{48,66},{50,64},{64,... | collective-permute-start | bytes 811016 | tf_op jit(solution)/shard_map/ppermute | solution.py:258
  115.5 3.6 %collective-permute-start.15 = (bf16[528,256]{1,0:T(8,128)(2,1)S(1)}, bf16[528,256]{1,0:T(8,128)(2,1)S(1)}, u32[]{:S(2)}, u32[]{:S(2)}) collective-permute-start(bf16[528,256]{1,0:T(8,128)(2,1)S(1)} %shard_map.71), channel_id=1, source_target_pairs={{0,18},{2,16},{16,34},{18,32},{32,50},{34,48},{48,64},{50,66},{64,... | collective-permute-start | bytes 811016 | tf_op jit(solution)/shard_map/ppermute | solution.py:257
  121.1 19.1 %collective-permute-done.15.refs_1_ = bf16[528,256]{1,0:T(8,128)(2,1)S(1)} collective-permute-done((bf16[528,256]{1,0:T(8,128)(2,1)S(1)}, bf16[528,256]{1,0:T(8,128)(2,1)S(1)}, u32[]{:S(2)}, u32[]{:S(2)}) %collective-permute-start.15) | collective-permute-done | bytes 270368 | tf_op jit(solution)/shard_map/ppermute | solution.py:257
  144.7 2.9 %collective-permute-start.18 = (bf16[512,256]{1,0:T(8,128)(2,1)S(1)}, bf16[512,256]{1,0:T(8,128)(2,1)S(1)}, u32[]{:S(2)}, u32[]{:S(2)}) collective-permute-start(bf16[512,256]{1,0:T(8,128)(2,1)S(1)} %shard_map.72), channel_id=1, source_target_pairs={{0,4},{4,8},{8,12},{12,0},{1,5},{5,9},{9,13},{13,1},{2,6},{6,10},{... | collective-permute-start | bytes 786440 | tf_op jit(solution)/shard_map/ppermute | solution.py:189
  149.6 3.3 %collective-permute-done.17 = bf16[512,256]{1,0:T(8,128)(2,1)S(1)} collective-permute-done((bf16[512,256]{1,0:T(8,128)(2,1)S(1)}, bf16[512,256]{1,0:T(8,128)(2,1)S(1)}, u32[]{:S(2)}, u32[]{:S(2)}) %collective-permute-start.17) | collective-permute-done | bytes 262176 | tf_op jit(solution)/shard_map/ppermute | solution.py:189
  152.9 6.6 %collective-permute-done.18 = bf16[512,256]{1,0:T(8,128)(2,1)S(1)} collective-permute-done((bf16[512,256]{1,0:T(8,128)(2,1)S(1)}, bf16[512,256]{1,0:T(8,128)(2,1)S(1)}, u32[]{:S(2)}, u32[]{:S(2)}) %collective-permute-start.18) | collective-permute-done | bytes 262176 | tf_op jit(solution)/shard_map/ppermute | solution.py:189
  (70 shorter events, 47.5 us)
Async XLA Ops:
  2.3 17.7 %collective-permute-start = (bf16[256,256]{1,0:T(8,128)(2,1)S(1)}, bf16[256,256]{1,0:T(8,128)(2,1)S(1)}, u32[]{:S(2)}, u32[]{:S(2)}) collective-permute-start(bf16[256,256]{1,0:T(8,128)(2,1)S(1)} %and_select_fusion), channel_id=1, source_target_pairs={{0,12},{4,0},{8,4},{12,8},{1,13},{5,1},{9,5},{13,9},{2,14},{6,2},{... | collective-permute-start | bytes 393224 | tf_op jit(solution)/shard_map/ppermute | solution.py:189
  6.7 13.3 %collective-permute-start.1 = (bf16[256,256]{1,0:T(8,128)(2,1)S(1)}, bf16[256,256]{1,0:T(8,128)(2,1)S(1)}, u32[]{:S(2)}, u32[]{:S(2)}) collective-permute-start(bf16[256,256]{1,0:T(8,128)(2,1)S(1)} %and_select_fusion), channel_id=1, source_target_pairs={{0,8},{4,12},{8,0},{12,4},{1,9},{5,13},{9,1},{13,5},{2,10},{6,14},... | collective-permute-start | bytes 393224 | tf_op jit(solution)/shard_map/ppermute | solution.py:189
  9.1 10.8 %collective-permute-start.2 = (bf16[256,256]{1,0:T(8,128)(2,1)S(1)}, bf16[256,256]{1,0:T(8,128)(2,1)S(1)}, u32[]{:S(2)}, u32[]{:S(2)}) collective-permute-start(bf16[256,256]{1,0:T(8,128)(2,1)S(1)} %and_select_fusion), channel_id=1, source_target_pairs={{0,4},{4,8},{8,12},{12,0},{1,5},{5,9},{9,13},{13,1},{2,6},{6,10},{... | collective-permute-start | bytes 393224 | tf_op jit(solution)/shard_map/ppermute | solution.py:189
  11.7 12.1 %collective-permute-start.3 = (bf16[256,256]{1,0:T(8,128)(2,1)S(1)}, bf16[256,256]{1,0:T(8,128)(2,1)S(1)}, u32[]{:S(2)}, u32[]{:S(2)}) collective-permute-start(bf16[256,256]{1,0:T(8,128)(2,1)S(1)} %and_select_fusion), channel_id=1, source_target_pairs={{0,2},{2,0},{1,3},{3,1},{4,6},{6,4},{5,7},{7,5},{8,10},{10,8},{9,1... | collective-permute-start | bytes 393224 | tf_op jit(solution)/shard_map/ppermute | solution.py:229
  20.0 25.7 %collective-permute-start.7 = (bf16[4,256,256]{2,1,0:T(8,128)(2,1)S(1)}, bf16[4,256,256]{2,1,0:T(8,128)(2,1)S(1)}, u32[]{:S(2)}, u32[]{:S(2)}) collective-permute-start(bf16[4,256,256]{2,1,0:T(8,128)(2,1)S(1)} %pad_maximum_fusion.1), channel_id=1, source_target_pairs={{0,1},{1,0},{2,3},{3,2},{4,5},{5,4},{6,7},{7,6},{8,9},{9,8},{10,11... | collective-permute-start | bytes 1572872 | tf_op jit(solution)/shard_map/ppermute | solution.py:233
  23.8 11.7 %collective-permute-start.4 = (bf16[256,256]{1,0:T(8,128)(2,1)S(1)}, bf16[256,256]{1,0:T(8,128)(2,1)S(1)}, u32[]{:S(2)}, u32[]{:S(2)}) collective-permute-start(bf16[256,256]{1,0:T(8,128)(2,1)S(1)} %collective-permute-done.3), channel_id=1, source_target_pairs={{0,12},{4,0},{8,4},{12,8},{1,13},{5,1},{9,5},{13,9},{2,14},{6,2},{... | collective-permute-start | bytes 393224 | tf_op jit(solution)/shard_map/ppermute | solution.py:189
  27.8 7.7 %collective-permute-start.5 = (bf16[256,256]{1,0:T(8,128)(2,1)S(1)}, bf16[256,256]{1,0:T(8,128)(2,1)S(1)}, u32[]{:S(2)}, u32[]{:S(2)}) collective-permute-start(bf16[256,256]{1,0:T(8,128)(2,1)S(1)} %collective-permute-done.3), channel_id=1, source_target_pairs={{0,8},{4,12},{8,0},{12,4},{1,9},{5,13},{9,1},{13,5},{2,10},{6,14},... | collective-permute-start | bytes 393224 | tf_op jit(solution)/shard_map/ppermute | solution.py:189
  30.9 8.3 %collective-permute-start.6 = (bf16[256,256]{1,0:T(8,128)(2,1)S(1)}, bf16[256,256]{1,0:T(8,128)(2,1)S(1)}, u32[]{:S(2)}, u32[]{:S(2)}) collective-permute-start(bf16[256,256]{1,0:T(8,128)(2,1)S(1)} %collective-permute-done.3), channel_id=1, source_target_pairs={{0,4},{4,8},{8,12},{12,0},{1,5},{5,9},{9,13},{13,1},{2,6},{6,10},{... | collective-permute-start | bytes 393224 | tf_op jit(solution)/shard_map/ppermute | solution.py:189
  39.3 7.3 %collective-permute-start.8 = (bf16[4,256,256]{2,1,0:T(8,128)(2,1)S(1)}, bf16[4,256,256]{2,1,0:T(8,128)(2,1)S(1)}, u32[]{:S(2)}, u32[]{:S(2)}) collective-permute-start(bf16[4,256,256]{2,1,0:T(8,128)(2,1)S(1)} %pad_maximum_fusion.2), channel_id=1, source_target_pairs={{0,1},{1,0},{2,3},{3,2},{4,5},{5,4},{6,7},{7,6},{8,9},{9,8},{10,11... | collective-permute-start | bytes 1572872 | tf_op jit(solution)/shard_map/ppermute | solution.py:235
  50.5 14.0 %collective-permute-start.19 = (bf16[272,256]{1,0:T(8,128)(2,1)S(1)}, bf16[272,256]{1,0:T(8,128)(2,1)S(1)}, u32[]{:S(2)}, u32[]{:S(2)}) collective-permute-start(bf16[272,256]{1,0:T(8,128)(2,1)S(1)} %shard_map.68.message.refs_0_), channel_id=1, source_target_pairs={{0,2},{2,0},{1,3},{3,1},{4,6},{6,4},{5,7},{7,5},{8,10},{10,8},{9,1... | collective-permute-start | bytes 417800 | tf_op jit(solution)/shard_map/ppermute | solution.py:245
  64.5 9.2 %collective-permute-start.20 = (bf16[544,256]{1,0:T(8,128)(2,1)S(1)}, bf16[544,256]{1,0:T(8,128)(2,1)S(1)}, u32[]{:S(2)}, u32[]{:S(2)}) collective-permute-start(bf16[544,256]{1,0:T(8,128)(2,1)S(1)} %pad_maximum_fusion.3), channel_id=1, source_target_pairs={{0,12},{4,0},{8,4},{12,8},{1,13},{5,1},{9,5},{13,9},{2,14},{6,2},{... | collective-permute-start | bytes 835592 | tf_op jit(solution)/shard_map/ppermute | solution.py:189
  66.4 10.8 %collective-permute-start.21 = (bf16[544,256]{1,0:T(8,128)(2,1)S(1)}, bf16[544,256]{1,0:T(8,128)(2,1)S(1)}, u32[]{:S(2)}, u32[]{:S(2)}) collective-permute-start(bf16[544,256]{1,0:T(8,128)(2,1)S(1)} %pad_maximum_fusion.3), channel_id=1, source_target_pairs={{0,8},{4,12},{8,0},{12,4},{1,9},{5,13},{9,1},{13,5},{2,10},{6,14},... | collective-permute-start | bytes 835592 | tf_op jit(solution)/shard_map/ppermute | solution.py:189
  68.9 15.5 %collective-permute-start.22 = (bf16[544,256]{1,0:T(8,128)(2,1)S(1)}, bf16[544,256]{1,0:T(8,128)(2,1)S(1)}, u32[]{:S(2)}, u32[]{:S(2)}) collective-permute-start(bf16[544,256]{1,0:T(8,128)(2,1)S(1)} %pad_maximum_fusion.3), channel_id=1, source_target_pairs={{0,4},{4,8},{8,12},{12,0},{1,5},{5,9},{9,13},{13,1},{2,6},{6,10},{... | collective-permute-start | bytes 835592 | tf_op jit(solution)/shard_map/ppermute | solution.py:189
  84.4 18.4 %collective-permute-start.23 = (bf16[2176,256]{1,0:T(8,128)(2,1)S(1)}, bf16[2176,256]{1,0:T(8,128)(2,1)S(1)}, u32[]{:S(2)}, u32[]{:S(2)}) collective-permute-start(bf16[2176,256]{1,0:T(8,128)(2,1)S(1)} %get-tuple-element.18), channel_id=1, source_target_pairs={{0,1},{1,0},{2,3},{3,2},{4,5},{5,4},{6,7},{7,6},{8,9},{9,8},{10,11... | collective-permute-start | bytes 3342344 | tf_op jit(solution)/shard_map/ppermute | solution.py:262
  86.9 5.6 %collective-permute-start.10 = (bf16[8,256,256]{2,1,0:T(8,128)(2,1)S(1)}, bf16[8,256,256]{2,1,0:T(8,128)(2,1)S(1)}, u32[]{:S(2)}, u32[]{:S(2)}) collective-permute-start(bf16[8,256,256]{2,1,0:T(8,128)(2,1)S(1)} %dynamic-slice_bitcast_fusion), channel_id=1, source_target_pairs={{0,1},{1,0},{2,3},{3,2},{4,5},{5,4},{6,7},{7,6},{8,9},{9,8},{10,11... | collective-permute-start | bytes 3145736 | tf_op jit(solution)/shard_map/ppermute | solution.py:232
  93.8 13.9 %collective-permute-start.11 = (bf16[528,256]{1,0:T(8,128)(2,1)S(1)}, bf16[528,256]{1,0:T(8,128)(2,1)S(1)}, u32[]{:S(2)}, u32[]{:S(2)}) collective-permute-start(bf16[528,256]{1,0:T(8,128)(2,1)S(1)} %get-tuple-element.10), channel_id=1, source_target_pairs={{0,8},{4,12},{8,0},{12,4},{1,9},{5,13},{9,1},{13,5},{2,10},{6,14},... | collective-permute-start | bytes 811016 | tf_op jit(solution)/shard_map/ppermute | solution.py:189
  96.3 15.2 %collective-permute-start.12 = (bf16[528,256]{1,0:T(8,128)(2,1)S(1)}, bf16[528,256]{1,0:T(8,128)(2,1)S(1)}, u32[]{:S(2)}, u32[]{:S(2)}) collective-permute-start(bf16[528,256]{1,0:T(8,128)(2,1)S(1)} %get-tuple-element.11), channel_id=1, source_target_pairs={{0,4},{4,8},{8,12},{12,0},{1,5},{5,9},{9,13},{13,1},{2,6},{6,10},{... | collective-permute-start | bytes 811016 | tf_op jit(solution)/shard_map/ppermute | solution.py:189
  98.6 12.9 %collective-permute-start.13 = (bf16[528,256]{1,0:T(8,128)(2,1)S(1)}, bf16[528,256]{1,0:T(8,128)(2,1)S(1)}, u32[]{:S(2)}, u32[]{:S(2)}) collective-permute-start(bf16[528,256]{1,0:T(8,128)(2,1)S(1)} %get-tuple-element.12), channel_id=1, source_target_pairs={{0,12},{4,0},{8,4},{12,8},{1,13},{5,1},{9,5},{13,9},{2,14},{6,2},{... | collective-permute-start | bytes 811016 | tf_op jit(solution)/shard_map/ppermute | solution.py:189
  104.9 54.6 %collective-permute-start.24 = (bf16[8,256,256]{2,1,0:T(8,128)(2,1)S(1)}, bf16[8,256,256]{2,1,0:T(8,128)(2,1)S(1)}, u32[]{:S(2)}, u32[]{:S(2)}) collective-permute-start(bf16[8,256,256]{2,1,0:T(8,128)(2,1)S(1)} %get-tuple-element.15), channel_id=1, source_target_pairs={{0,1},{1,0},{2,3},{3,2},{4,5},{5,4},{6,7},{7,6},{8,9},{9,8},{10,11... | collective-permute-start | bytes 3145736 | tf_op jit(solution)/shard_map/ppermute | solution.py:271
  111.6 9.5 %collective-permute-start.14 = (bf16[528,256]{1,0:T(8,128)(2,1)S(1)}, bf16[528,256]{1,0:T(8,128)(2,1)S(1)}, u32[]{:S(2)}, u32[]{:S(2)}) collective-permute-start(bf16[528,256]{1,0:T(8,128)(2,1)S(1)} %shard_map.71), channel_id=1, source_target_pairs={{0,16},{2,18},{16,32},{18,34},{32,48},{34,50},{48,66},{50,64},{64,... | collective-permute-start | bytes 811016 | tf_op jit(solution)/shard_map/ppermute | solution.py:258
  115.5 24.7 %collective-permute-start.15 = (bf16[528,256]{1,0:T(8,128)(2,1)S(1)}, bf16[528,256]{1,0:T(8,128)(2,1)S(1)}, u32[]{:S(2)}, u32[]{:S(2)}) collective-permute-start(bf16[528,256]{1,0:T(8,128)(2,1)S(1)} %shard_map.71), channel_id=1, source_target_pairs={{0,18},{2,16},{16,34},{18,32},{32,50},{34,48},{48,64},{50,66},{64,... | collective-permute-start | bytes 811016 | tf_op jit(solution)/shard_map/ppermute | solution.py:257
  140.3 9.3 %collective-permute-start.16 = (bf16[512,256]{1,0:T(8,128)(2,1)S(1)}, bf16[512,256]{1,0:T(8,128)(2,1)S(1)}, u32[]{:S(2)}, u32[]{:S(2)}) collective-permute-start(bf16[512,256]{1,0:T(8,128)(2,1)S(1)} %shard_map.72), channel_id=1, source_target_pairs={{0,12},{4,0},{8,4},{12,8},{1,13},{5,1},{9,5},{13,9},{2,14},{6,2},{... | collective-permute-start | bytes 786440 | tf_op jit(solution)/shard_map/ppermute | solution.py:189
  142.2 10.6 %collective-permute-start.17 = (bf16[512,256]{1,0:T(8,128)(2,1)S(1)}, bf16[512,256]{1,0:T(8,128)(2,1)S(1)}, u32[]{:S(2)}, u32[]{:S(2)}) collective-permute-start(bf16[512,256]{1,0:T(8,128)(2,1)S(1)} %shard_map.72), channel_id=1, source_target_pairs={{0,8},{4,12},{8,0},{12,4},{1,9},{5,13},{9,1},{13,5},{2,10},{6,14},... | collective-permute-start | bytes 786440 | tf_op jit(solution)/shard_map/ppermute | solution.py:189
  144.7 14.8 %collective-permute-start.18 = (bf16[512,256]{1,0:T(8,128)(2,1)S(1)}, bf16[512,256]{1,0:T(8,128)(2,1)S(1)}, u32[]{:S(2)}, u32[]{:S(2)}) collective-permute-start(bf16[512,256]{1,0:T(8,128)(2,1)S(1)} %shard_map.72), channel_id=1, source_target_pairs={{0,4},{4,8},{8,12},{12,0},{1,5},{5,9},{9,13},{13,1},{2,6},{6,10},{... | collective-permute-start | bytes 786440 | tf_op jit(solution)/shard_map/ppermute | solution.py:189
  (6 other events, 55.3 us)

commit v5 on v2

--- a/solution.py
+++ b/solution.py
@@ -11,7 +11,7 @@
 
 BF = jnp.bfloat16
 F32 = jnp.float32
-TILE = 16
+TILE = 8
 YROW = ("z", "yl", "yh")
 SWAP = [(0, 1), (1, 0)]
 VMEM = pl.BlockSpec(memory_space=pltpu.VMEM)
@@ -214,8 +214,7 @@
     span = width + TILE
     unit = 2 * channels * width**3
     block_bytes = width * width * 2
-    meta = jnp.stack([size, lax.axis_index("c").astype(jnp.int32), lax.axis_index("yh").astype(jnp.int32),
-                      lax.axis_index("x").astype(jnp.int32)])
+    meta = jnp.stack([size, *(lax.axis_index(axis).astype(jnp.int32) for axis in ("c", "yh", "x"))])
 
     masked = jnp.where(live(size, (width, width)), wave[0, 0], jnp.zeros((), BF))
     masked_other = lax.ppermute(masked, "yh", SWAP)

time: 152 us -> 151 us (level)
  no operation moved by 1% of the time
where the time goes in v5:
time: 151 us; the launch traced here: 150 us
  starting transfers between devices  83.6 us (55%)
  waiting for transfers between devices  51.8 us (34%)
  Pallas kernels  10.1 us (7%)
  other arithmetic  2.31 us (2%)
  between operations  1.8 us (1%)
    ppermute x15, starting transfers between devices, along_x(): lax.ppermute(value, 'x', [(i, (i + step) % count) for i in range(count)])  45.3 us
    ppermute x15, waiting for transfers between devices, along_x(): lax.ppermute(value, 'x', [(i, (i + step) % count) for i in range(count)])  26.5 us
    ppermute x1, waiting for transfers between devices, body(): from_far = lax.ppermute(row, YROW, far)  17.1 us
    ppermute x1, starting transfers between devices, body(): message_other = lax.ppermute(message, 'yh', SWAP)  6.93 us
    ppermute x1, waiting for transfers between devices, body(): message_other = lax.ppermute(message, 'yh', SWAP)  6.73 us
    ppermute x1, starting transfers between devices, body(): masked_other = lax.ppermute(masked, 'yh', SWAP)  6.55 us
    ppermute x1, starting transfers between devices, body(): across_other = lax.ppermute(own_other, 'c', SWAP)  5.1 us
    ppermute x1, starting transfers between devices, body(): from_near = lax.ppermute(row, YROW, near)  4.19 us
  transfers between devices with their start and end apart: 24, of which 9 were waited for; matrix products, arithmetic and copies ran while one was open for 1% of the time, Pallas kernels for 3%

profile of v5, /device:TPU:201, one launch (start us, length us, event | category | flops | bytes accessed | tf_op | source)
XLA Modules:
  0.0 150.0 jit_solution(2396372371570667109)
XLA Ops:
  2.3 4.4 %collective-permute-start = (bf16[256,256]{1,0:T(8,128)(2,1)S(1)}, bf16[256,256]{1,0:T(8,128)(2,1)S(1)}, u32[]{:S(2)}, u32[]{:S(2)}) collective-permute-start(bf16[256,256]{1,0:T(8,128)(2,1)S(1)} %and_select_fusion), channel_id=1, source_target_pairs={{0,12},{4,0},{8,4},{12,8},{1,13},{5,1},{9,5},{13,9},{2,14},{6,2},{... | collective-permute-start | bytes 393224 | tf_op jit(solution)/shard_map/ppermute | solution.py:180
  6.7 2.4 %collective-permute-start.1 = (bf16[256,256]{1,0:T(8,128)(2,1)S(1)}, bf16[256,256]{1,0:T(8,128)(2,1)S(1)}, u32[]{:S(2)}, u32[]{:S(2)}) collective-permute-start(bf16[256,256]{1,0:T(8,128)(2,1)S(1)} %and_select_fusion), channel_id=1, source_target_pairs={{0,8},{4,12},{8,0},{12,4},{1,9},{5,13},{9,1},{13,5},{2,10},{6,14},... | collective-permute-start | bytes 393224 | tf_op jit(solution)/shard_map/ppermute | solution.py:180
  9.1 2.5 %collective-permute-start.2 = (bf16[256,256]{1,0:T(8,128)(2,1)S(1)}, bf16[256,256]{1,0:T(8,128)(2,1)S(1)}, u32[]{:S(2)}, u32[]{:S(2)}) collective-permute-start(bf16[256,256]{1,0:T(8,128)(2,1)S(1)} %and_select_fusion), channel_id=1, source_target_pairs={{0,4},{4,8},{8,12},{12,0},{1,5},{5,9},{9,13},{13,1},{2,6},{6,10},{... | collective-permute-start | bytes 393224 | tf_op jit(solution)/shard_map/ppermute | solution.py:180
  11.7 6.6 %collective-permute-start.3 = (bf16[256,256]{1,0:T(8,128)(2,1)S(1)}, bf16[256,256]{1,0:T(8,128)(2,1)S(1)}, u32[]{:S(2)}, u32[]{:S(2)}) collective-permute-start(bf16[256,256]{1,0:T(8,128)(2,1)S(1)} %and_select_fusion), channel_id=1, source_target_pairs={{0,2},{2,0},{1,3},{3,1},{4,6},{6,4},{5,7},{7,5},{8,10},{10,8},{9,1... | collective-permute-start | bytes 393224 | tf_op jit(solution)/shard_map/ppermute | solution.py:220
  19.4 3.7 %collective-permute-start.7 = (bf16[4,256,256]{2,1,0:T(8,128)(2,1)S(1)}, bf16[4,256,256]{2,1,0:T(8,128)(2,1)S(1)}, u32[]{:S(2)}, u32[]{:S(2)}) collective-permute-start(bf16[4,256,256]{2,1,0:T(8,128)(2,1)S(1)} %pad_maximum_fusion.1), channel_id=1, source_target_pairs={{0,1},{1,0},{2,3},{3,2},{4,5},{5,4},{6,7},{7,6},{8,9},{9,8},{10,11... | collective-permute-start | bytes 1572872 | tf_op jit(solution)/shard_map/ppermute | solution.py:222
  23.1 4.0 %collective-permute-start.4 = (bf16[256,256]{1,0:T(8,128)(2,1)S(1)}, bf16[256,256]{1,0:T(8,128)(2,1)S(1)}, u32[]{:S(2)}, u32[]{:S(2)}) collective-permute-start(bf16[256,256]{1,0:T(8,128)(2,1)S(1)} %collective-permute-done.3), channel_id=1, source_target_pairs={{0,12},{4,0},{8,4},{12,8},{1,13},{5,1},{9,5},{13,9},{2,14},{6,2},{... | collective-permute-start | bytes 393224 | tf_op jit(solution)/shard_map/ppermute | solution.py:180
  27.1 3.1 %collective-permute-start.5 = (bf16[256,256]{1,0:T(8,128)(2,1)S(1)}, bf16[256,256]{1,0:T(8,128)(2,1)S(1)}, u32[]{:S(2)}, u32[]{:S(2)}) collective-permute-start(bf16[256,256]{1,0:T(8,128)(2,1)S(1)} %collective-permute-done.3), channel_id=1, source_target_pairs={{0,8},{4,12},{8,0},{12,4},{1,9},{5,13},{9,1},{13,5},{2,10},{6,14},... | collective-permute-start | bytes 393224 | tf_op jit(solution)/shard_map/ppermute | solution.py:180
  34.3 4.3 %collective-permute-done.6 = bf16[256,256]{1,0:T(8,128)(2,1)S(1)} collective-permute-done((bf16[256,256]{1,0:T(8,128)(2,1)S(1)}, bf16[256,256]{1,0:T(8,128)(2,1)S(1)}, u32[]{:S(2)}, u32[]{:S(2)}) %collective-permute-start.6) | collective-permute-done | bytes 131104 | tf_op jit(solution)/shard_map/ppermute | solution.py:180
  38.7 5.1 %collective-permute-start.8 = (bf16[4,256,256]{2,1,0:T(8,128)(2,1)S(1)}, bf16[4,256,256]{2,1,0:T(8,128)(2,1)S(1)}, u32[]{:S(2)}, u32[]{:S(2)}) collective-permute-start(bf16[4,256,256]{2,1,0:T(8,128)(2,1)S(1)} %pad_maximum_fusion.2), channel_id=1, source_target_pairs={{0,1},{1,0},{2,3},{3,2},{4,5},{5,4},{6,7},{7,6},{8,9},{9,8},{10,11... | collective-permute-start | bytes 1572872 | tf_op jit(solution)/shard_map/ppermute | solution.py:224
  45.4 3.6 %shard_map.68 = (bf16[256,256]{1,0:T(8,128)(2,1)}, bf16[264,256]{1,0:T(8,128)(2,1)S(1)}, bf16[8,256]{1,0:T(8,128)(2,1)S(1)}, bf16[2056,256]{1,0:T(8,128)(2,1)S(1)}, bf16[256,256]{1,0:T(8,128)(2,1)S(1)}) custom-call(s32[4]{0:T(128)S(1)} %pad_add_fusion.meta.refs_0_, s32[16]{0:T(128)S(1)} %bitcast.36, ...), custom_call_target="tpu_custom_call" | custom-call | flops 1610612736 | bytes 8388608 | tf_op jit(solution)/shard_map/pallas_call | solution.py:227
  51.2 6.9 %collective-permute-start.19 = (bf16[264,256]{1,0:T(8,128)(2,1)S(1)}, bf16[264,256]{1,0:T(8,128)(2,1)S(1)}, u32[]{:S(2)}, u32[]{:S(2)}) collective-permute-start(bf16[264,256]{1,0:T(8,128)(2,1)S(1)} %get-tuple-element.14.message), channel_id=1, source_target_pairs={{0,2},{2,0},{1,3},{3,1},{4,6},{6,4},{5,7},{7,5},{8,10},{10,8},{9,1... | collective-permute-start | bytes 405512 | tf_op jit(solution)/shard_map/ppermute | solution.py:237
  58.2 6.7 %collective-permute-done.19 = bf16[264,256]{1,0:T(8,128)(2,1)S(1)} collective-permute-done((bf16[264,256]{1,0:T(8,128)(2,1)S(1)}, bf16[264,256]{1,0:T(8,128)(2,1)S(1)}, u32[]{:S(2)}, u32[]{:S(2)}) %collective-permute-start.19) | collective-permute-done | bytes 135200 | tf_op jit(solution)/shard_map/ppermute | solution.py:237
  70.9 4.4 %collective-permute-start.10 = (bf16[520,256]{1,0:T(8,128)(2,1)S(1)}, bf16[520,256]{1,0:T(8,128)(2,1)S(1)}, u32[]{:S(2)}, u32[]{:S(2)}) collective-permute-start(bf16[520,256]{1,0:T(8,128)(2,1)S(1)} %get-tuple-element.19), channel_id=1, source_target_pairs={{0,8},{4,12},{8,0},{12,4},{1,9},{5,13},{9,1},{13,5},{2,10},{6,14},... | collective-permute-start | bytes 798728 | tf_op jit(solution)/shard_map/ppermute | solution.py:180
  75.3 3.4 %collective-permute-start.11 = (bf16[520,256]{1,0:T(8,128)(2,1)S(1)}, bf16[520,256]{1,0:T(8,128)(2,1)S(1)}, u32[]{:S(2)}, u32[]{:S(2)}) collective-permute-start(bf16[520,256]{1,0:T(8,128)(2,1)S(1)} %get-tuple-element.20), channel_id=1, source_target_pairs={{0,4},{4,8},{8,12},{12,0},{1,5},{5,9},{9,13},{13,1},{2,6},{6,10},{... | collective-permute-start | bytes 798728 | tf_op jit(solution)/shard_map/ppermute | solution.py:180
  78.7 3.1 %collective-permute-start.12 = (bf16[520,256]{1,0:T(8,128)(2,1)S(1)}, bf16[520,256]{1,0:T(8,128)(2,1)S(1)}, u32[]{:S(2)}, u32[]{:S(2)}) collective-permute-start(bf16[520,256]{1,0:T(8,128)(2,1)S(1)} %get-tuple-element.21), channel_id=1, source_target_pairs={{0,12},{4,0},{8,4},{12,8},{1,13},{5,1},{9,5},{13,9},{2,14},{6,2},{... | collective-permute-start | bytes 798728 | tf_op jit(solution)/shard_map/ppermute | solution.py:180
  84.0 6.1 %collective-permute-done.11.c = bf16[520,256]{1,0:T(8,128)(2,1)S(1)} collective-permute-done((bf16[520,256]{1,0:T(8,128)(2,1)S(1)}, bf16[520,256]{1,0:T(8,128)(2,1)S(1)}, u32[]{:S(2)}, u32[]{:S(2)}) %collective-permute-start.11) | collective-permute-done | bytes 266272 | tf_op jit(solution)/shard_map/ppermute | solution.py:180
  91.6 4.2 %collective-permute-start.13 = (bf16[520,256]{1,0:T(8,128)(2,1)S(1)}, bf16[520,256]{1,0:T(8,128)(2,1)S(1)}, u32[]{:S(2)}, u32[]{:S(2)}) collective-permute-start(bf16[520,256]{1,0:T(8,128)(2,1)S(1)} %shard_map.71), channel_id=1, source_target_pairs={{0,16},{2,18},{16,32},{18,34},{32,48},{34,50},{48,66},{50,64},{64,... | collective-permute-start | bytes 798728 | tf_op jit(solution)/shard_map/ppermute | solution.py:250
  95.8 3.4 %collective-permute-start.14 = (bf16[520,256]{1,0:T(8,128)(2,1)S(1)}, bf16[520,256]{1,0:T(8,128)(2,1)S(1)}, u32[]{:S(2)}, u32[]{:S(2)}) collective-permute-start(bf16[520,256]{1,0:T(8,128)(2,1)S(1)} %shard_map.71), channel_id=1, source_target_pairs={{0,18},{2,16},{16,34},{18,32},{32,50},{34,48},{48,64},{50,66},{64,... | collective-permute-start | bytes 798728 | tf_op jit(solution)/shard_map/ppermute | solution.py:249
  99.3 3.8 %collective-permute-start.23 = (bf16[2112,256]{1,0:T(8,128)(2,1)S(1)}, bf16[2112,256]{1,0:T(8,128)(2,1)S(1)}, u32[]{:S(2)}, u32[]{:S(2)}) collective-permute-start(bf16[2112,256]{1,0:T(8,128)(2,1)S(1)} %get-tuple-element.26), channel_id=1, source_target_pairs={{0,1},{1,0},{2,3},{3,2},{4,5},{5,4},{6,7},{7,6},{8,9},{9,8},{10,11... | collective-permute-start | bytes 3244040 | tf_op jit(solution)/shard_map/ppermute | solution.py:254
  103.1 17.1 %collective-permute-done.14.refs_1_ = bf16[520,256]{1,0:T(8,128)(2,1)S(1)} collective-permute-done((bf16[520,256]{1,0:T(8,128)(2,1)S(1)}, bf16[520,256]{1,0:T(8,128)(2,1)S(1)}, u32[]{:S(2)}, u32[]{:S(2)}) %collective-permute-start.14) | collective-permute-done | bytes 266272 | tf_op jit(solution)/shard_map/ppermute | solution.py:249
  120.3 5.2 %collective-permute-start.15 = (bf16[512,256]{1,0:T(8,128)(2,1)S(1)}, bf16[512,256]{1,0:T(8,128)(2,1)S(1)}, u32[]{:S(2)}, u32[]{:S(2)}) collective-permute-start(bf16[512,256]{1,0:T(8,128)(2,1)S(1)} %shard_map.72), channel_id=1, source_target_pairs={{0,12},{4,0},{8,4},{12,8},{1,13},{5,1},{9,5},{13,9},{2,14},{6,2},{... | collective-permute-start | bytes 786440 | tf_op jit(solution)/shard_map/ppermute | solution.py:180
  127.4 2.5 %collective-permute-start.17 = (bf16[512,256]{1,0:T(8,128)(2,1)S(1)}, bf16[512,256]{1,0:T(8,128)(2,1)S(1)}, u32[]{:S(2)}, u32[]{:S(2)}) collective-permute-start(bf16[512,256]{1,0:T(8,128)(2,1)S(1)} %shard_map.72), channel_id=1, source_target_pairs={{0,4},{4,8},{8,12},{12,0},{1,5},{5,9},{9,13},{13,1},{2,6},{6,10},{... | collective-permute-start | bytes 786440 | tf_op jit(solution)/shard_map/ppermute | solution.py:180
  129.9 6.2 %collective-permute-done.15 = bf16[512,256]{1,0:T(8,128)(2,1)S(1)} collective-permute-done((bf16[512,256]{1,0:T(8,128)(2,1)S(1)}, bf16[512,256]{1,0:T(8,128)(2,1)S(1)}, u32[]{:S(2)}, u32[]{:S(2)}) %collective-permute-start.15) | collective-permute-done | bytes 262176 | tf_op jit(solution)/shard_map/ppermute | solution.py:180
  136.1 6.6 %collective-permute-done.17 = bf16[512,256]{1,0:T(8,128)(2,1)S(1)} collective-permute-done((bf16[512,256]{1,0:T(8,128)(2,1)S(1)}, bf16[512,256]{1,0:T(8,128)(2,1)S(1)}, u32[]{:S(2)}, u32[]{:S(2)}) %collective-permute-start.17) | collective-permute-done | bytes 262176 | tf_op jit(solution)/shard_map/ppermute | solution.py:180
  (60 shorter events, 29.0 us)
Async XLA Ops:
  2.3 17.0 %collective-permute-start = (bf16[256,256]{1,0:T(8,128)(2,1)S(1)}, bf16[256,256]{1,0:T(8,128)(2,1)S(1)}, u32[]{:S(2)}, u32[]{:S(2)}) collective-permute-start(bf16[256,256]{1,0:T(8,128)(2,1)S(1)} %and_select_fusion), channel_id=1, source_target_pairs={{0,12},{4,0},{8,4},{12,8},{1,13},{5,1},{9,5},{13,9},{2,14},{6,2},{... | collective-permute-start | bytes 393224 | tf_op jit(solution)/shard_map/ppermute | solution.py:180
  6.7 12.6 %collective-permute-start.1 = (bf16[256,256]{1,0:T(8,128)(2,1)S(1)}, bf16[256,256]{1,0:T(8,128)(2,1)S(1)}, u32[]{:S(2)}, u32[]{:S(2)}) collective-permute-start(bf16[256,256]{1,0:T(8,128)(2,1)S(1)} %and_select_fusion), channel_id=1, source_target_pairs={{0,8},{4,12},{8,0},{12,4},{1,9},{5,13},{9,1},{13,5},{2,10},{6,14},... | collective-permute-start | bytes 393224 | tf_op jit(solution)/shard_map/ppermute | solution.py:180
  9.1 10.2 %collective-permute-start.2 = (bf16[256,256]{1,0:T(8,128)(2,1)S(1)}, bf16[256,256]{1,0:T(8,128)(2,1)S(1)}, u32[]{:S(2)}, u32[]{:S(2)}) collective-permute-start(bf16[256,256]{1,0:T(8,128)(2,1)S(1)} %and_select_fusion), channel_id=1, source_target_pairs={{0,4},{4,8},{8,12},{12,0},{1,5},{5,9},{9,13},{13,1},{2,6},{6,10},{... | collective-permute-start | bytes 393224 | tf_op jit(solution)/shard_map/ppermute | solution.py:180
  11.7 11.5 %collective-permute-start.3 = (bf16[256,256]{1,0:T(8,128)(2,1)S(1)}, bf16[256,256]{1,0:T(8,128)(2,1)S(1)}, u32[]{:S(2)}, u32[]{:S(2)}) collective-permute-start(bf16[256,256]{1,0:T(8,128)(2,1)S(1)} %and_select_fusion), channel_id=1, source_target_pairs={{0,2},{2,0},{1,3},{3,1},{4,6},{6,4},{5,7},{7,5},{8,10},{10,8},{9,1... | collective-permute-start | bytes 393224 | tf_op jit(solution)/shard_map/ppermute | solution.py:220
  19.4 24.4 %collective-permute-start.7 = (bf16[4,256,256]{2,1,0:T(8,128)(2,1)S(1)}, bf16[4,256,256]{2,1,0:T(8,128)(2,1)S(1)}, u32[]{:S(2)}, u32[]{:S(2)}) collective-permute-start(bf16[4,256,256]{2,1,0:T(8,128)(2,1)S(1)} %pad_maximum_fusion.1), channel_id=1, source_target_pairs={{0,1},{1,0},{2,3},{3,2},{4,5},{5,4},{6,7},{7,6},{8,9},{9,8},{10,11... | collective-permute-start | bytes 1572872 | tf_op jit(solution)/shard_map/ppermute | solution.py:222
  23.1 9.2 %collective-permute-start.4 = (bf16[256,256]{1,0:T(8,128)(2,1)S(1)}, bf16[256,256]{1,0:T(8,128)(2,1)S(1)}, u32[]{:S(2)}, u32[]{:S(2)}) collective-permute-start(bf16[256,256]{1,0:T(8,128)(2,1)S(1)} %collective-permute-done.3), channel_id=1, source_target_pairs={{0,12},{4,0},{8,4},{12,8},{1,13},{5,1},{9,5},{13,9},{2,14},{6,2},{... | collective-permute-start | bytes 393224 | tf_op jit(solution)/shard_map/ppermute | solution.py:180
  27.1 7.2 %collective-permute-start.5 = (bf16[256,256]{1,0:T(8,128)(2,1)S(1)}, bf16[256,256]{1,0:T(8,128)(2,1)S(1)}, u32[]{:S(2)}, u32[]{:S(2)}) collective-permute-start(bf16[256,256]{1,0:T(8,128)(2,1)S(1)} %collective-permute-done.3), channel_id=1, source_target_pairs={{0,8},{4,12},{8,0},{12,4},{1,9},{5,13},{9,1},{13,5},{2,10},{6,14},... | collective-permute-start | bytes 393224 | tf_op jit(solution)/shard_map/ppermute | solution.py:180
  30.3 8.3 %collective-permute-start.6 = (bf16[256,256]{1,0:T(8,128)(2,1)S(1)}, bf16[256,256]{1,0:T(8,128)(2,1)S(1)}, u32[]{:S(2)}, u32[]{:S(2)}) collective-permute-start(bf16[256,256]{1,0:T(8,128)(2,1)S(1)} %collective-permute-done.3), channel_id=1, source_target_pairs={{0,4},{4,8},{8,12},{12,0},{1,5},{5,9},{9,13},{13,1},{2,6},{6,10},{... | collective-permute-start | bytes 393224 | tf_op jit(solution)/shard_map/ppermute | solution.py:180
  38.7 6.6 %collective-permute-start.8 = (bf16[4,256,256]{2,1,0:T(8,128)(2,1)S(1)}, bf16[4,256,256]{2,1,0:T(8,128)(2,1)S(1)}, u32[]{:S(2)}, u32[]{:S(2)}) collective-permute-start(bf16[4,256,256]{2,1,0:T(8,128)(2,1)S(1)} %pad_maximum_fusion.2), channel_id=1, source_target_pairs={{0,1},{1,0},{2,3},{3,2},{4,5},{5,4},{6,7},{7,6},{8,9},{9,8},{10,11... | collective-permute-start | bytes 1572872 | tf_op jit(solution)/shard_map/ppermute | solution.py:224
  49.0 21.7 %collective-permute-start.9 = (bf16[2056,256]{1,0:T(8,128)(2,1)S(1)}, bf16[2056,256]{1,0:T(8,128)(2,1)S(1)}, u32[]{:S(2)}, u32[]{:S(2)}) collective-permute-start(bf16[2056,256]{1,0:T(8,128)(2,1)S(1)} %get-tuple-element.17), channel_id=1, source_target_pairs={{0,1},{1,0},{2,3},{3,2},{4,5},{5,4},{6,7},{7,6},{8,9},{9,8},{10,11... | collective-permute-start | bytes 3158024 | tf_op jit(solution)/shard_map/ppermute | solution.py:236
  51.2 13.7 %collective-permute-start.19 = (bf16[264,256]{1,0:T(8,128)(2,1)S(1)}, bf16[264,256]{1,0:T(8,128)(2,1)S(1)}, u32[]{:S(2)}, u32[]{:S(2)}) collective-permute-start(bf16[264,256]{1,0:T(8,128)(2,1)S(1)} %get-tuple-element.14.message), channel_id=1, source_target_pairs={{0,2},{2,0},{1,3},{3,1},{4,6},{6,4},{5,7},{7,5},{8,10},{10,8},{9,1... | collective-permute-start | bytes 405512 | tf_op jit(solution)/shard_map/ppermute | solution.py:237
  65.0 16.8 %collective-permute-start.20 = (bf16[528,256]{1,0:T(8,128)(2,1)S(1)}, bf16[528,256]{1,0:T(8,128)(2,1)S(1)}, u32[]{:S(2)}, u32[]{:S(2)}) collective-permute-start(bf16[528,256]{1,0:T(8,128)(2,1)S(1)} %get-tuple-element.34), channel_id=1, source_target_pairs={{0,12},{4,0},{8,4},{12,8},{1,13},{5,1},{9,5},{13,9},{2,14},{6,2},{... | collective-permute-start | bytes 811016 | tf_op jit(solution)/shard_map/ppermute | solution.py:180
  66.9 32.3 %collective-permute-start.21 = (bf16[528,256]{1,0:T(8,128)(2,1)S(1)}, bf16[528,256]{1,0:T(8,128)(2,1)S(1)}, u32[]{:S(2)}, u32[]{:S(2)}) collective-permute-start(bf16[528,256]{1,0:T(8,128)(2,1)S(1)} %get-tuple-element.34), channel_id=1, source_target_pairs={{0,8},{4,12},{8,0},{12,4},{1,9},{5,13},{9,1},{13,5},{2,10},{6,14},... | collective-permute-start | bytes 811016 | tf_op jit(solution)/shard_map/ppermute | solution.py:180
  70.9 13.1 %collective-permute-start.10 = (bf16[520,256]{1,0:T(8,128)(2,1)S(1)}, bf16[520,256]{1,0:T(8,128)(2,1)S(1)}, u32[]{:S(2)}, u32[]{:S(2)}) collective-permute-start(bf16[520,256]{1,0:T(8,128)(2,1)S(1)} %get-tuple-element.19), channel_id=1, source_target_pairs={{0,8},{4,12},{8,0},{12,4},{1,9},{5,13},{9,1},{13,5},{2,10},{6,14},... | collective-permute-start | bytes 798728 | tf_op jit(solution)/shard_map/ppermute | solution.py:180
  75.3 14.8 %collective-permute-start.11 = (bf16[520,256]{1,0:T(8,128)(2,1)S(1)}, bf16[520,256]{1,0:T(8,128)(2,1)S(1)}, u32[]{:S(2)}, u32[]{:S(2)}) collective-permute-start(bf16[520,256]{1,0:T(8,128)(2,1)S(1)} %get-tuple-element.20), channel_id=1, source_target_pairs={{0,4},{4,8},{8,12},{12,0},{1,5},{5,9},{9,13},{13,1},{2,6},{6,10},{... | collective-permute-start | bytes 798728 | tf_op jit(solution)/shard_map/ppermute | solution.py:180
  78.7 12.8 %collective-permute-start.12 = (bf16[520,256]{1,0:T(8,128)(2,1)S(1)}, bf16[520,256]{1,0:T(8,128)(2,1)S(1)}, u32[]{:S(2)}, u32[]{:S(2)}) collective-permute-start(bf16[520,256]{1,0:T(8,128)(2,1)S(1)} %get-tuple-element.21), channel_id=1, source_target_pairs={{0,12},{4,0},{8,4},{12,8},{1,13},{5,1},{9,5},{13,9},{2,14},{6,2},{... | collective-permute-start | bytes 798728 | tf_op jit(solution)/shard_map/ppermute | solution.py:180
  81.8 17.4 %collective-permute-start.22 = (bf16[528,256]{1,0:T(8,128)(2,1)S(1)}, bf16[528,256]{1,0:T(8,128)(2,1)S(1)}, u32[]{:S(2)}, u32[]{:S(2)}) collective-permute-start(bf16[528,256]{1,0:T(8,128)(2,1)S(1)} %get-tuple-element.34), channel_id=1, source_target_pairs={{0,4},{4,8},{8,12},{12,0},{1,5},{5,9},{9,13},{13,1},{2,6},{6,10},{... | collective-permute-start | bytes 811016 | tf_op jit(solution)/shard_map/ppermute | solution.py:180
  91.6 11.4 %collective-permute-start.13 = (bf16[520,256]{1,0:T(8,128)(2,1)S(1)}, bf16[520,256]{1,0:T(8,128)(2,1)S(1)}, u32[]{:S(2)}, u32[]{:S(2)}) collective-permute-start(bf16[520,256]{1,0:T(8,128)(2,1)S(1)} %shard_map.71), channel_id=1, source_target_pairs={{0,16},{2,18},{16,32},{18,34},{32,48},{34,50},{48,66},{50,64},{64,... | collective-permute-start | bytes 798728 | tf_op jit(solution)/shard_map/ppermute | solution.py:250
  95.8 24.4 %collective-permute-start.14 = (bf16[520,256]{1,0:T(8,128)(2,1)S(1)}, bf16[520,256]{1,0:T(8,128)(2,1)S(1)}, u32[]{:S(2)}, u32[]{:S(2)}) collective-permute-start(bf16[520,256]{1,0:T(8,128)(2,1)S(1)} %shard_map.71), channel_id=1, source_target_pairs={{0,18},{2,16},{16,34},{18,32},{32,50},{34,48},{48,64},{50,66},{64,... | collective-permute-start | bytes 798728 | tf_op jit(solution)/shard_map/ppermute | solution.py:249
  99.3 45.9 %collective-permute-start.23 = (bf16[2112,256]{1,0:T(8,128)(2,1)S(1)}, bf16[2112,256]{1,0:T(8,128)(2,1)S(1)}, u32[]{:S(2)}, u32[]{:S(2)}) collective-permute-start(bf16[2112,256]{1,0:T(8,128)(2,1)S(1)} %get-tuple-element.26), channel_id=1, source_target_pairs={{0,1},{1,0},{2,3},{3,2},{4,5},{5,4},{6,7},{7,6},{8,9},{9,8},{10,11... | collective-permute-start | bytes 3244040 | tf_op jit(solution)/shard_map/ppermute | solution.py:254
  120.3 15.8 %collective-permute-start.15 = (bf16[512,256]{1,0:T(8,128)(2,1)S(1)}, bf16[512,256]{1,0:T(8,128)(2,1)S(1)}, u32[]{:S(2)}, u32[]{:S(2)}) collective-permute-start(bf16[512,256]{1,0:T(8,128)(2,1)S(1)} %shard_map.72), channel_id=1, source_target_pairs={{0,12},{4,0},{8,4},{12,8},{1,13},{5,1},{9,5},{13,9},{2,14},{6,2},{... | collective-permute-start | bytes 786440 | tf_op jit(solution)/shard_map/ppermute | solution.py:180
  125.4 10.6 %collective-permute-start.16 = (bf16[512,256]{1,0:T(8,128)(2,1)S(1)}, bf16[512,256]{1,0:T(8,128)(2,1)S(1)}, u32[]{:S(2)}, u32[]{:S(2)}) collective-permute-start(bf16[512,256]{1,0:T(8,128)(2,1)S(1)} %shard_map.72), channel_id=1, source_target_pairs={{0,8},{4,12},{8,0},{12,4},{1,9},{5,13},{9,1},{13,5},{2,10},{6,14},... | collective-permute-start | bytes 786440 | tf_op jit(solution)/shard_map/ppermute | solution.py:180
  127.4 15.3 %collective-permute-start.17 = (bf16[512,256]{1,0:T(8,128)(2,1)S(1)}, bf16[512,256]{1,0:T(8,128)(2,1)S(1)}, u32[]{:S(2)}, u32[]{:S(2)}) collective-permute-start(bf16[512,256]{1,0:T(8,128)(2,1)S(1)} %shard_map.72), channel_id=1, source_target_pairs={{0,4},{4,8},{8,12},{12,0},{1,5},{5,9},{9,13},{13,1},{2,6},{6,10},{... | collective-permute-start | bytes 786440 | tf_op jit(solution)/shard_map/ppermute | solution.py:180
  142.8 5.5 %collective-permute-start.18 = (bf16[2048,256]{1,0:T(8,128)(2,1)S(1)}, bf16[2048,256]{1,0:T(8,128)(2,1)S(1)}, u32[]{:S(2)}, u32[]{:S(2)}) collective-permute-start(bf16[2048,256]{1,0:T(8,128)(2,1)S(1)} %pad_maximum_fusion.refs_1_), channel_id=1, source_target_pairs={{0,1},{1,0},{2,3},{3,2},{4,5},{5,4},{6,7},{7,6},{8,9},{9,8},{10,11... | collective-permute-start | bytes 3145736 | tf_op jit(solution)/shard_map/ppermute | solution.py:269
  (3 other events, 39.2 us)

commit v6 on v2

--- a/solution.py
+++ b/solution.py
@@ -59,12 +59,19 @@
     return side * 8 + lax.rem(meta[3] + j // 2, 4) * 2 + j % 2
 
 
-def first_kernel(meta, picks, pool, left, right, first_out, message, stats, send, turned_out, inner, lv):
+def load_kernel(source, out):
+    out[...] = source[...]
+
+
+def first_kernel(meta, picks, own, across, left, right, first_out, message, stats, send, turned_out, pool, inner, lv):
     channels, width = left.shape[0], left.shape[1]
     half = channels // 2
+    pool[0:half] = own[...]
+    pool[half:channels] = across[...]
     for t in range(channels):
-        c, yh, x = place(picks[t], meta)
-        inner[:, t * width:(t + 1) * width] = dot(left[t], pool[(c * 2 + yh) * 4 + x]).astype(BF)
+        c, yh, step = place(picks[t], meta)
+        at = (c * 2 + yh) * 4 + step * (1 - yh) + (picks[t] // 4) * yh
+        inner[:, t * width:(t + 1) * width] = dot(left[t], pool[at]).astype(BF)
     product = dot(inner[...], right[...].reshape(channels * width, width))
     size = meta[0]
     product = jnp.where(live(size, product.shape), product, 0.0).astype(BF)
@@ -185,6 +192,11 @@
     return [value, along_x(value, 3), far, along_x(value, 1)]
 
 
+def to_everyone_on_x(value):
+    count = lax.axis_size("x")
+    return lax.all_to_all(jnp.broadcast_to(value[None], (count, *value.shape)), "x", 0, 0, tiled=True)
+
+
 def routes(z_count, y_count):
     def at(z, yl, yh):
         return (z * y_count + yl) * 2 + yh
@@ -214,25 +226,24 @@
     span = width + TILE
     unit = 2 * channels * width**3
     block_bytes = width * width * 2
-    meta = jnp.stack([size, lax.axis_index("c").astype(jnp.int32), lax.axis_index("yh").astype(jnp.int32),
-                      lax.axis_index("x").astype(jnp.int32)])
 
     masked = jnp.where(live(size, (width, width)), wave[0, 0], jnp.zeros((), BF))
     masked_other = lax.ppermute(masked, "yh", SWAP)
     own = jnp.stack(round_x(masked))
+    meta = jnp.stack([size, *(lax.axis_index(axis).astype(jnp.int32) for axis in ("c", "yh", "x"))])
+    own_other = to_everyone_on_x(masked_other)
+    own = jnp.concatenate(lax.optimization_barrier((own, own_other)))
     across = lax.ppermute(own, "c", SWAP)
-    own_other = jnp.stack(round_x(masked_other))
-    across_other = lax.ppermute(own_other, "c", SWAP)
-    pool = jnp.concatenate([own, own_other, across, across_other], axis=0)
+    right_here = call(load_kernel, one(right.shape, BF), [VMEM], [], 1 << 20, 2 * channels * block_bytes)(right)
     stack = pltpu.VMEM((half, width, width), BF)
     first, message, stats, send, turned = call(
         first_kernel,
         [((width, width), BF), ((span, width), BF), ((TILE, width), BF),
          ((half * width + TILE, width), BF), ((width, width), BF)],
-        [SMEM, SMEM, VMEM, VMEM, VMEM],
-        [pltpu.VMEM((width, channels * width), BF), stack],
+        [SMEM, SMEM] + [VMEM] * 4,
+        [pltpu.VMEM((channels, width, width), BF), pltpu.VMEM((width, channels * width), BF), stack],
         3 * unit, 4 * channels * block_bytes,
-    )(meta, picks, pool, left, right)
+    )(meta, picks, own, across, left, right_here)
 
     arrived = lax.ppermute(send, "c", SWAP)
     message_other = lax.ppermute(message, "yh", SWAP)
@@ -260,7 +271,7 @@
         [SMEM, SMEM, VMEM, VMEM, VMEM],
         [],
         2 * unit, 4 * channels * block_bytes,
-    )(meta, picks, pool_two, left, right)
+    )(meta, picks, pool_two, left, right_here)
 
     factor = 1.0 / (width * math.sqrt(channels_of(sector_size)))
     edge = call(

time: 152 us -> 148 us (0.974)
  the two profiles are of different devices: /device:TPU:201 before, /device:TPU:297 now
where the time goes in v6:
time: 148 us
  starting transfers between devices  68.5 us (46%)
  waiting for transfers between devices  60.2 us (41%)
  Pallas kernels  11 us (7%)
  local copies, waits for them, and re-layouts  3.27 us (2%)
  other arithmetic  3.05 us (2%)
  between operations  1.68 us (1%)
    ppermute x12, starting transfers between devices, along_x(): lax.ppermute(value, 'x', [(i, (i + step) % count) for i in range(count)])  38.9 us
    ppermute x12, waiting for transfers between devices, along_x(): lax.ppermute(value, 'x', [(i, (i + step) % count) for i in range(count)])  22.5 us
    ppermute x1, waiting for transfers between devices, body(): from_far = lax.ppermute(row, YROW, far)  15.8 us
    ppermute x1, waiting for transfers between devices, body(): message_other = lax.ppermute(message, 'yh', SWAP)  11.6 us
    ppermute x1, waiting for transfers between devices, body(): masked_other = lax.ppermute(masked, 'yh', SWAP)  8.18 us
    ppermute x1, starting transfers between devices, body(): across = lax.ppermute(own, 'c', SWAP)  7.09 us
    pallas_call x1, Pallas kernels, body(): call(first_kernel, [((width, width), BF), ((span, width), BF), ((TILE, wi...  4.4 us
    all_to_all x1, starting transfers between devices, to_everyone_on_x(): lax.all_to_all(jnp.broadcast_to(value[None], (count, *value.shape)), 'x',...  4.27 us
  transfers between devices with their start and end apart: 21, of which 9 were waited for; matrix products, arithmetic and copies ran while one was open for 2% of the time, Pallas kernels for 3%

profile of v6, /device:TPU:297, one launch (start us, length us, event | category | flops | bytes accessed | tf_op | source)
XLA Modules:
  0.0 147.6 jit_solution(2886349301067852245)
XLA Ops:
  2.3 2.6 %collective-permute-start.3 = (bf16[256,256]{1,0:T(8,128)(2,1)S(1)}, bf16[256,256]{1,0:T(8,128)(2,1)S(1)}, u32[]{:S(2)}, u32[]{:S(2)}) collective-permute-start(bf16[256,256]{1,0:T(8,128)(2,1)S(1)} %and_select_fusion), channel_id=1, source_target_pairs={{0,2},{2,0},{1,3},{3,1},{4,6},{6,4},{5,7},{7,5},{8,10},{10,8},{9,1... | collective-permute-start | bytes 393224 | tf_op jit(solution)/shard_map/ppermute | solution.py:231
  4.9 8.2 %collective-permute-done.3 = bf16[256,256]{1,0:T(8,128)(2,1)S(1)} collective-permute-done((bf16[256,256]{1,0:T(8,128)(2,1)S(1)}, bf16[256,256]{1,0:T(8,128)(2,1)S(1)}, u32[]{:S(2)}, u32[]{:S(2)}) %collective-permute-start.3) | collective-permute-done | bytes 131104 | tf_op jit(solution)/shard_map/ppermute | solution.py:231
  14.0 4.3 %all-to-all-start = ((bf16[4,256,256]{2,1,0:T(8,128)(2,1)}), bf16[4,256,256]{2,1,0:T(8,128)(2,1)}, u32[]{:S(2)}, u32[]{:S(2)}) async-start(bf16[4,256,256]{2,1,0:T(8,128)(2,1)} %broadcast_in_dim.20), calls=%async_computation | async-start | bytes 1048576 | tf_op jit(solution)/shard_map/all_to_all | solution.py:197
  18.3 3.3 %collective-permute-start.2 = (bf16[256,256]{1,0:T(8,128)(2,1)S(1)}, bf16[256,256]{1,0:T(8,128)(2,1)S(1)}, u32[]{:S(2)}, u32[]{:S(2)}) collective-permute-start(bf16[256,256]{1,0:T(8,128)(2,1)S(1)} %and_select_fusion), channel_id=1, source_target_pairs={{0,4},{4,8},{8,12},{12,0},{1,5},{5,9},{9,13},{13,1},{2,6},{6,10},{... | collective-permute-start | bytes 393224 | tf_op jit(solution)/shard_map/ppermute | solution.py:187
  21.6 3.2 %collective-permute-start = (bf16[256,256]{1,0:T(8,128)(2,1)S(1)}, bf16[256,256]{1,0:T(8,128)(2,1)S(1)}, u32[]{:S(2)}, u32[]{:S(2)}) collective-permute-start(bf16[256,256]{1,0:T(8,128)(2,1)S(1)} %and_select_fusion), channel_id=1, source_target_pairs={{0,12},{4,0},{8,4},{12,8},{1,13},{5,1},{9,5},{13,9},{2,14},{6,2},{... | collective-permute-start | bytes 393224 | tf_op jit(solution)/shard_map/ppermute | solution.py:187
  24.8 3.6 %collective-permute-start.1 = (bf16[256,256]{1,0:T(8,128)(2,1)S(1)}, bf16[256,256]{1,0:T(8,128)(2,1)S(1)}, u32[]{:S(2)}, u32[]{:S(2)}) collective-permute-start(bf16[256,256]{1,0:T(8,128)(2,1)S(1)} %and_select_fusion), channel_id=1, source_target_pairs={{0,8},{4,12},{8,0},{12,4},{1,9},{5,13},{9,1},{13,5},{2,10},{6,14},... | collective-permute-start | bytes 393224 | tf_op jit(solution)/shard_map/ppermute | solution.py:187
  29.4 2.9 %collective-permute-done.1 = bf16[256,256]{1,0:T(8,128)(2,1)S(1)} collective-permute-done((bf16[256,256]{1,0:T(8,128)(2,1)S(1)}, bf16[256,256]{1,0:T(8,128)(2,1)S(1)}, u32[]{:S(2)}, u32[]{:S(2)}) %collective-permute-start.1) | collective-permute-done | bytes 131104 | tf_op jit(solution)/shard_map/ppermute | solution.py:187
  35.4 7.1 %collective-permute-start.4 = (bf16[8,256,256]{2,1,0:T(8,128)(2,1)S(1)}, bf16[8,256,256]{2,1,0:T(8,128)(2,1)}, u32[]{:S(2)}, u32[]{:S(2)}) collective-permute-start(bf16[8,256,256]{2,1,0:T(8,128)(2,1)S(1)} %constant_dynamic-update-slice_fusion.own), channel_id=1, source_target_pairs={{0,1},{1,0},{2,3},{3,2},{4,5},{5,4},{6,7},{7,6},{8,9},{9,8},{10,11... | collective-permute-start | bytes 3145736 | tf_op jit(solution)/shard_map/ppermute | solution.py:236
  44.9 4.4 %shard_map.69 = (bf16[256,256]{1,0:T(8,128)(2,1)}, bf16[272,256]{1,0:T(8,128)(2,1)S(1)}, bf16[16,256]{1,0:T(8,128)(2,1)S(1)}, bf16[2064,256]{1,0:T(8,128)(2,1)S(1)}, bf16[256,256]{1,0:T(8,128)(2,1)S(1)}) custom-call(s32[4]{0:T(128)S(1)} %pad_add_fusion.meta.refs_0_, s32[16]{0:T(128)S(1)} %bitcast.23, ...), custom_call_target="tpu_custom_call" | custom-call | flops 1610612736 | bytes 8388608 | tf_op jit(solution)/shard_map/pallas_call | solution.py:239
  51.6 2.5 %collective-permute-start.15 = (bf16[272,256]{1,0:T(8,128)(2,1)S(1)}, bf16[272,256]{1,0:T(8,128)(2,1)S(1)}, u32[]{:S(2)}, u32[]{:S(2)}) collective-permute-start(bf16[272,256]{1,0:T(8,128)(2,1)S(1)} %get-tuple-element.18.message), channel_id=1, source_target_pairs={{0,2},{2,0},{1,3},{3,1},{4,6},{6,4},{5,7},{7,5},{8,10},{10,8},{9,1... | collective-permute-start | bytes 417800 | tf_op jit(solution)/shard_map/ppermute | solution.py:249
  54.1 11.6 %collective-permute-done.15 = bf16[272,256]{1,0:T(8,128)(2,1)S(1)} collective-permute-done((bf16[272,256]{1,0:T(8,128)(2,1)S(1)}, bf16[272,256]{1,0:T(8,128)(2,1)S(1)}, u32[]{:S(2)}, u32[]{:S(2)}) %collective-permute-start.15) | collective-permute-done | bytes 139296 | tf_op jit(solution)/shard_map/ppermute | solution.py:249
  65.8 3.6 %collective-permute-start.16 = (bf16[544,256]{1,0:T(8,128)(2,1)S(1)}, bf16[544,256]{1,0:T(8,128)(2,1)S(1)}, u32[]{:S(2)}, u32[]{:S(2)}) collective-permute-start(bf16[544,256]{1,0:T(8,128)(2,1)S(1)} %get-tuple-element.36), channel_id=1, source_target_pairs={{0,12},{4,0},{8,4},{12,8},{1,13},{5,1},{9,5},{13,9},{2,14},{6,2},{... | collective-permute-start | bytes 835592 | tf_op jit(solution)/shard_map/ppermute | solution.py:187
  69.4 2.5 %collective-permute-start.17 = (bf16[544,256]{1,0:T(8,128)(2,1)S(1)}, bf16[544,256]{1,0:T(8,128)(2,1)S(1)}, u32[]{:S(2)}, u32[]{:S(2)}) collective-permute-start(bf16[544,256]{1,0:T(8,128)(2,1)S(1)} %get-tuple-element.36), channel_id=1, source_target_pairs={{0,8},{4,12},{8,0},{12,4},{1,9},{5,13},{9,1},{13,5},{2,10},{6,14},... | collective-permute-start | bytes 835592 | tf_op jit(solution)/shard_map/ppermute | solution.py:187
  73.4 4.3 %collective-permute-start.6 = (bf16[528,256]{1,0:T(8,128)(2,1)S(1)}, bf16[528,256]{1,0:T(8,128)(2,1)S(1)}, u32[]{:S(2)}, u32[]{:S(2)}) collective-permute-start(bf16[528,256]{1,0:T(8,128)(2,1)S(1)} %get-tuple-element.23), channel_id=1, source_target_pairs={{0,8},{4,12},{8,0},{12,4},{1,9},{5,13},{9,1},{13,5},{2,10},{6,14},... | collective-permute-start | bytes 811016 | tf_op jit(solution)/shard_map/ppermute | solution.py:187
  79.7 4.6 %collective-permute-start.8 = (bf16[528,256]{1,0:T(8,128)(2,1)S(1)}, bf16[528,256]{1,0:T(8,128)(2,1)S(1)}, u32[]{:S(2)}, u32[]{:S(2)}) collective-permute-start(bf16[528,256]{1,0:T(8,128)(2,1)S(1)} %get-tuple-element.25), channel_id=1, source_target_pairs={{0,12},{4,0},{8,4},{12,8},{1,13},{5,1},{9,5},{13,9},{2,14},{6,2},{... | collective-permute-start | bytes 811016 | tf_op jit(solution)/shard_map/ppermute | solution.py:187
  86.3 6.7 %collective-permute-done.7.c = bf16[528,256]{1,0:T(8,128)(2,1)S(1)} collective-permute-done((bf16[528,256]{1,0:T(8,128)(2,1)S(1)}, bf16[528,256]{1,0:T(8,128)(2,1)S(1)}, u32[]{:S(2)}, u32[]{:S(2)}) %collective-permute-start.7) | collective-permute-done | bytes 270368 | tf_op jit(solution)/shard_map/ppermute | solution.py:187
  93.1 3.0 %collective-permute-start.10 = (bf16[528,256]{1,0:T(8,128)(2,1)S(1)}, bf16[528,256]{1,0:T(8,128)(2,1)S(1)}, u32[]{:S(2)}, u32[]{:S(2)}) collective-permute-start(bf16[528,256]{1,0:T(8,128)(2,1)S(1)} %shard_map.72), channel_id=1, source_target_pairs={{0,18},{2,16},{16,34},{18,32},{32,50},{34,48},{48,64},{50,66},{64,... | collective-permute-start | bytes 811016 | tf_op jit(solution)/shard_map/ppermute | solution.py:261
  98.2 3.5 %collective-permute-start.19 = (bf16[2176,256]{1,0:T(8,128)(2,1)S(1)}, bf16[2176,256]{1,0:T(8,128)(2,1)S(1)}, u32[]{:S(2)}, u32[]{:S(2)}) collective-permute-start(bf16[2176,256]{1,0:T(8,128)(2,1)S(1)} %get-tuple-element.28), channel_id=1, source_target_pairs={{0,1},{1,0},{2,3},{3,2},{4,5},{5,4},{6,7},{7,6},{8,9},{9,8},{10,11... | collective-permute-start | bytes 3342344 | tf_op jit(solution)/shard_map/ppermute | solution.py:266
  101.7 15.8 %collective-permute-done.10.refs_1_ = bf16[528,256]{1,0:T(8,128)(2,1)S(1)} collective-permute-done((bf16[528,256]{1,0:T(8,128)(2,1)S(1)}, bf16[528,256]{1,0:T(8,128)(2,1)S(1)}, u32[]{:S(2)}, u32[]{:S(2)}) %collective-permute-start.10) | collective-permute-done | bytes 270368 | tf_op jit(solution)/shard_map/ppermute | solution.py:261
  117.6 5.5 %collective-permute-start.11 = (bf16[512,256]{1,0:T(8,128)(2,1)S(1)}, bf16[512,256]{1,0:T(8,128)(2,1)S(1)}, u32[]{:S(2)}, u32[]{:S(2)}) collective-permute-start(bf16[512,256]{1,0:T(8,128)(2,1)S(1)} %shard_map.73), channel_id=1, source_target_pairs={{0,12},{4,0},{8,4},{12,8},{1,13},{5,1},{9,5},{13,9},{2,14},{6,2},{... | collective-permute-start | bytes 786440 | tf_op jit(solution)/shard_map/ppermute | solution.py:187
  123.1 2.5 %collective-permute-start.12 = (bf16[512,256]{1,0:T(8,128)(2,1)S(1)}, bf16[512,256]{1,0:T(8,128)(2,1)S(1)}, u32[]{:S(2)}, u32[]{:S(2)}) collective-permute-start(bf16[512,256]{1,0:T(8,128)(2,1)S(1)} %shard_map.73), channel_id=1, source_target_pairs={{0,8},{4,12},{8,0},{12,4},{1,9},{5,13},{9,1},{13,5},{2,10},{6,14},... | collective-permute-start | bytes 786440 | tf_op jit(solution)/shard_map/ppermute | solution.py:187
  128.7 4.7 %collective-permute-done.12 = bf16[512,256]{1,0:T(8,128)(2,1)S(1)} collective-permute-done((bf16[512,256]{1,0:T(8,128)(2,1)S(1)}, bf16[512,256]{1,0:T(8,128)(2,1)S(1)}, u32[]{:S(2)}, u32[]{:S(2)}) %collective-permute-start.12) | collective-permute-done | bytes 262176 | tf_op jit(solution)/shard_map/ppermute | solution.py:187
  133.3 7.0 %collective-permute-done.13 = bf16[512,256]{1,0:T(8,128)(2,1)S(1)} collective-permute-done((bf16[512,256]{1,0:T(8,128)(2,1)S(1)}, bf16[512,256]{1,0:T(8,128)(2,1)S(1)}, u32[]{:S(2)}, u32[]{:S(2)}) %collective-permute-start.13) | collective-permute-done | bytes 262176 | tf_op jit(solution)/shard_map/ppermute | solution.py:187
  140.4 2.4 %collective-permute-start.14 = (bf16[2048,256]{1,0:T(8,128)(2,1)S(1)}, bf16[2048,256]{1,0:T(8,128)(2,1)S(1)}, u32[]{:S(2)}, u32[]{:S(2)}) collective-permute-start(bf16[2048,256]{1,0:T(8,128)(2,1)S(1)} %pad_maximum_fusion.refs_1_), channel_id=1, source_target_pairs={{0,1},{1,0},{2,3},{3,2},{4,5},{5,4},{6,7},{7,6},{8,9},{9,8},{10,11... | collective-permute-start | bytes 3145736 | tf_op jit(solution)/shard_map/ppermute | solution.py:281
  (48 shorter events, 26.2 us)
Async XLA Ops:
  2.3 10.8 %collective-permute-start.3 = (bf16[256,256]{1,0:T(8,128)(2,1)S(1)}, bf16[256,256]{1,0:T(8,128)(2,1)S(1)}, u32[]{:S(2)}, u32[]{:S(2)}) collective-permute-start(bf16[256,256]{1,0:T(8,128)(2,1)S(1)} %and_select_fusion), channel_id=1, source_target_pairs={{0,2},{2,0},{1,3},{3,1},{4,6},{6,4},{5,7},{7,5},{8,10},{10,8},{9,1... | collective-permute-start | bytes 393224 | tf_op jit(solution)/shard_map/ppermute | solution.py:231
  14.0 28.5 %copy-start.1 = (bf16[1,1,16,256,256]{4,3,2,1,0:T(8,128)(2,1)S(1)}, bf16[1,1,16,256,256]{4,3,2,1,0:T(8,128)(2,1)}, u32[]{:S(2)}) copy-start(bf16[1,1,16,256,256]{4,3,2,1,0:T(8,128)(2,1)} %param.7) | copy-start | bytes 6291460
  14.0 19.3 %all-to-all-start = ((bf16[4,256,256]{2,1,0:T(8,128)(2,1)}), bf16[4,256,256]{2,1,0:T(8,128)(2,1)}, u32[]{:S(2)}, u32[]{:S(2)}) async-start(bf16[4,256,256]{2,1,0:T(8,128)(2,1)} %broadcast_in_dim.20), calls=%async_computation | async-start | bytes 1048576 | tf_op jit(solution)/shard_map/all_to_all | solution.py:197
  18.3 11.1 %collective-permute-start.2 = (bf16[256,256]{1,0:T(8,128)(2,1)S(1)}, bf16[256,256]{1,0:T(8,128)(2,1)S(1)}, u32[]{:S(2)}, u32[]{:S(2)}) collective-permute-start(bf16[256,256]{1,0:T(8,128)(2,1)S(1)} %and_select_fusion), channel_id=1, source_target_pairs={{0,4},{4,8},{8,12},{12,0},{1,5},{5,9},{9,13},{13,1},{2,6},{6,10},{... | collective-permute-start | bytes 393224 | tf_op jit(solution)/shard_map/ppermute | solution.py:187
  21.6 7.8 %collective-permute-start = (bf16[256,256]{1,0:T(8,128)(2,1)S(1)}, bf16[256,256]{1,0:T(8,128)(2,1)S(1)}, u32[]{:S(2)}, u32[]{:S(2)}) collective-permute-start(bf16[256,256]{1,0:T(8,128)(2,1)S(1)} %and_select_fusion), channel_id=1, source_target_pairs={{0,12},{4,0},{8,4},{12,8},{1,13},{5,1},{9,5},{13,9},{2,14},{6,2},{... | collective-permute-start | bytes 393224 | tf_op jit(solution)/shard_map/ppermute | solution.py:187
  24.8 7.6 %collective-permute-start.1 = (bf16[256,256]{1,0:T(8,128)(2,1)S(1)}, bf16[256,256]{1,0:T(8,128)(2,1)S(1)}, u32[]{:S(2)}, u32[]{:S(2)}) collective-permute-start(bf16[256,256]{1,0:T(8,128)(2,1)S(1)} %and_select_fusion), channel_id=1, source_target_pairs={{0,8},{4,12},{8,0},{12,4},{1,9},{5,13},{9,1},{13,5},{2,10},{6,14},... | collective-permute-start | bytes 393224 | tf_op jit(solution)/shard_map/ppermute | solution.py:187
  35.4 9.5 %collective-permute-start.4 = (bf16[8,256,256]{2,1,0:T(8,128)(2,1)S(1)}, bf16[8,256,256]{2,1,0:T(8,128)(2,1)}, u32[]{:S(2)}, u32[]{:S(2)}) collective-permute-start(bf16[8,256,256]{2,1,0:T(8,128)(2,1)S(1)} %constant_dynamic-update-slice_fusion.own), channel_id=1, source_target_pairs={{0,1},{1,0},{2,3},{3,2},{4,5},{5,4},{6,7},{7,6},{8,9},{9,8},{10,11... | collective-permute-start | bytes 3145736 | tf_op jit(solution)/shard_map/ppermute | solution.py:236
  42.5 2.4 %copy-start = (bf16[1,1,16,256,256]{4,3,2,1,0:T(8,128)(2,1)S(1)}, bf16[1,1,16,256,256]{4,3,2,1,0:T(8,128)(2,1)}, u32[]{:S(2)}) copy-start(bf16[1,1,16,256,256]{4,3,2,1,0:T(8,128)(2,1)} %param.6) | copy-start | bytes 6291460
  42.5 2.4 %copy-start.2 = (s32[1,1,16]{2,1,0:T(1,128)S(1)}, s32[1,1,16]{2,1,0:T(1,128)}, u32[]{:S(2)}) copy-start(s32[1,1,16]{2,1,0:T(1,128)} %param.8) | copy-start | bytes 196
  49.3 23.9 %collective-permute-start.5 = (bf16[2064,256]{1,0:T(8,128)(2,1)S(1)}, bf16[2064,256]{1,0:T(8,128)(2,1)S(1)}, u32[]{:S(2)}, u32[]{:S(2)}) collective-permute-start(bf16[2064,256]{1,0:T(8,128)(2,1)S(1)} %get-tuple-element.21), channel_id=1, source_target_pairs={{0,1},{1,0},{2,3},{3,2},{4,5},{5,4},{6,7},{7,6},{8,9},{9,8},{10,11... | collective-permute-start | bytes 3170312 | tf_op jit(solution)/shard_map/ppermute | solution.py:248
  51.6 14.1 %collective-permute-start.15 = (bf16[272,256]{1,0:T(8,128)(2,1)S(1)}, bf16[272,256]{1,0:T(8,128)(2,1)S(1)}, u32[]{:S(2)}, u32[]{:S(2)}) collective-permute-start(bf16[272,256]{1,0:T(8,128)(2,1)S(1)} %get-tuple-element.18.message), channel_id=1, source_target_pairs={{0,2},{2,0},{1,3},{3,1},{4,6},{6,4},{5,7},{7,5},{8,10},{10,8},{9,1... | collective-permute-start | bytes 417800 | tf_op jit(solution)/shard_map/ppermute | solution.py:249
  65.8 18.5 %collective-permute-start.16 = (bf16[544,256]{1,0:T(8,128)(2,1)S(1)}, bf16[544,256]{1,0:T(8,128)(2,1)S(1)}, u32[]{:S(2)}, u32[]{:S(2)}) collective-permute-start(bf16[544,256]{1,0:T(8,128)(2,1)S(1)} %get-tuple-element.36), channel_id=1, source_target_pairs={{0,12},{4,0},{8,4},{12,8},{1,13},{5,1},{9,5},{13,9},{2,14},{6,2},{... | collective-permute-start | bytes 835592 | tf_op jit(solution)/shard_map/ppermute | solution.py:187
  69.4 28.6 %collective-permute-start.17 = (bf16[544,256]{1,0:T(8,128)(2,1)S(1)}, bf16[544,256]{1,0:T(8,128)(2,1)S(1)}, u32[]{:S(2)}, u32[]{:S(2)}) collective-permute-start(bf16[544,256]{1,0:T(8,128)(2,1)S(1)} %get-tuple-element.36), channel_id=1, source_target_pairs={{0,8},{4,12},{8,0},{12,4},{1,9},{5,13},{9,1},{13,5},{2,10},{6,14},... | collective-permute-start | bytes 835592 | tf_op jit(solution)/shard_map/ppermute | solution.py:187
  73.4 12.8 %collective-permute-start.6 = (bf16[528,256]{1,0:T(8,128)(2,1)S(1)}, bf16[528,256]{1,0:T(8,128)(2,1)S(1)}, u32[]{:S(2)}, u32[]{:S(2)}) collective-permute-start(bf16[528,256]{1,0:T(8,128)(2,1)S(1)} %get-tuple-element.23), channel_id=1, source_target_pairs={{0,8},{4,12},{8,0},{12,4},{1,9},{5,13},{9,1},{13,5},{2,10},{6,14},... | collective-permute-start | bytes 811016 | tf_op jit(solution)/shard_map/ppermute | solution.py:187
  77.8 15.2 %collective-permute-start.7 = (bf16[528,256]{1,0:T(8,128)(2,1)S(1)}, bf16[528,256]{1,0:T(8,128)(2,1)S(1)}, u32[]{:S(2)}, u32[]{:S(2)}) collective-permute-start(bf16[528,256]{1,0:T(8,128)(2,1)S(1)} %get-tuple-element.24), channel_id=1, source_target_pairs={{0,4},{4,8},{8,12},{12,0},{1,5},{5,9},{9,13},{13,1},{2,6},{6,10},{... | collective-permute-start | bytes 811016 | tf_op jit(solution)/shard_map/ppermute | solution.py:187
  79.7 13.3 %collective-permute-start.8 = (bf16[528,256]{1,0:T(8,128)(2,1)S(1)}, bf16[528,256]{1,0:T(8,128)(2,1)S(1)}, u32[]{:S(2)}, u32[]{:S(2)}) collective-permute-start(bf16[528,256]{1,0:T(8,128)(2,1)S(1)} %get-tuple-element.25), channel_id=1, source_target_pairs={{0,12},{4,0},{8,4},{12,8},{1,13},{5,1},{9,5},{13,9},{2,14},{6,2},{... | collective-permute-start | bytes 811016 | tf_op jit(solution)/shard_map/ppermute | solution.py:187
  84.3 13.8 %collective-permute-start.18 = (bf16[544,256]{1,0:T(8,128)(2,1)S(1)}, bf16[544,256]{1,0:T(8,128)(2,1)S(1)}, u32[]{:S(2)}, u32[]{:S(2)}) collective-permute-start(bf16[544,256]{1,0:T(8,128)(2,1)S(1)} %get-tuple-element.36), channel_id=1, source_target_pairs={{0,4},{4,8},{8,12},{12,0},{1,5},{5,9},{9,13},{13,1},{2,6},{6,10},{... | collective-permute-start | bytes 835592 | tf_op jit(solution)/shard_map/ppermute | solution.py:187
  93.1 24.3 %collective-permute-start.10 = (bf16[528,256]{1,0:T(8,128)(2,1)S(1)}, bf16[528,256]{1,0:T(8,128)(2,1)S(1)}, u32[]{:S(2)}, u32[]{:S(2)}) collective-permute-start(bf16[528,256]{1,0:T(8,128)(2,1)S(1)} %shard_map.72), channel_id=1, source_target_pairs={{0,18},{2,16},{16,34},{18,32},{32,50},{34,48},{48,64},{50,66},{64,... | collective-permute-start | bytes 811016 | tf_op jit(solution)/shard_map/ppermute | solution.py:261
  96.1 21.4 %collective-permute-start.9 = (bf16[528,256]{1,0:T(8,128)(2,1)S(1)}, bf16[528,256]{1,0:T(8,128)(2,1)S(1)}, u32[]{:S(2)}, u32[]{:S(2)}) collective-permute-start(bf16[528,256]{1,0:T(8,128)(2,1)S(1)} %shard_map.72), channel_id=1, source_target_pairs={{0,16},{2,18},{16,32},{18,34},{32,48},{34,50},{48,66},{50,64},{64,... | collective-permute-start | bytes 811016 | tf_op jit(solution)/shard_map/ppermute | solution.py:262
  98.2 44.7 %collective-permute-start.19 = (bf16[2176,256]{1,0:T(8,128)(2,1)S(1)}, bf16[2176,256]{1,0:T(8,128)(2,1)S(1)}, u32[]{:S(2)}, u32[]{:S(2)}) collective-permute-start(bf16[2176,256]{1,0:T(8,128)(2,1)S(1)} %get-tuple-element.28), channel_id=1, source_target_pairs={{0,1},{1,0},{2,3},{3,2},{4,5},{5,4},{6,7},{7,6},{8,9},{9,8},{10,11... | collective-permute-start | bytes 3342344 | tf_op jit(solution)/shard_map/ppermute | solution.py:266
  117.6 11.1 %collective-permute-start.11 = (bf16[512,256]{1,0:T(8,128)(2,1)S(1)}, bf16[512,256]{1,0:T(8,128)(2,1)S(1)}, u32[]{:S(2)}, u32[]{:S(2)}) collective-permute-start(bf16[512,256]{1,0:T(8,128)(2,1)S(1)} %shard_map.73), channel_id=1, source_target_pairs={{0,12},{4,0},{8,4},{12,8},{1,13},{5,1},{9,5},{13,9},{2,14},{6,2},{... | collective-permute-start | bytes 786440 | tf_op jit(solution)/shard_map/ppermute | solution.py:187
  123.1 10.3 %collective-permute-start.12 = (bf16[512,256]{1,0:T(8,128)(2,1)S(1)}, bf16[512,256]{1,0:T(8,128)(2,1)S(1)}, u32[]{:S(2)}, u32[]{:S(2)}) collective-permute-start(bf16[512,256]{1,0:T(8,128)(2,1)S(1)} %shard_map.73), channel_id=1, source_target_pairs={{0,8},{4,12},{8,0},{12,4},{1,9},{5,13},{9,1},{13,5},{2,10},{6,14},... | collective-permute-start | bytes 786440 | tf_op jit(solution)/shard_map/ppermute | solution.py:187
  125.6 14.8 %collective-permute-start.13 = (bf16[512,256]{1,0:T(8,128)(2,1)S(1)}, bf16[512,256]{1,0:T(8,128)(2,1)S(1)}, u32[]{:S(2)}, u32[]{:S(2)}) collective-permute-start(bf16[512,256]{1,0:T(8,128)(2,1)S(1)} %shard_map.73), channel_id=1, source_target_pairs={{0,4},{4,8},{8,12},{12,0},{1,5},{5,9},{9,13},{13,1},{2,6},{6,10},{... | collective-permute-start | bytes 786440 | tf_op jit(solution)/shard_map/ppermute | solution.py:187
  140.4 5.5 %collective-permute-start.14 = (bf16[2048,256]{1,0:T(8,128)(2,1)S(1)}, bf16[2048,256]{1,0:T(8,128)(2,1)S(1)}, u32[]{:S(2)}, u32[]{:S(2)}) collective-permute-start(bf16[2048,256]{1,0:T(8,128)(2,1)S(1)} %pad_maximum_fusion.refs_1_), channel_id=1, source_target_pairs={{0,1},{1,0},{2,3},{3,2},{4,5},{5,4},{6,7},{7,6},{8,9},{9,8},{10,11... | collective-permute-start | bytes 3145736 | tf_op jit(solution)/shard_map/ppermute | solution.py:281

commit v7 on v6

--- a/solution.py
+++ b/solution.py
@@ -154,12 +154,23 @@
     base[...] = total
 
 
-def half_kernel(final, meta, edges, g, start, out):
+def early_kernel(meta, own, other, g, start, out):
+    width = g.shape[1]
+    total = start[...]
+    for edges, side in ((own, meta[1]), (other, 1 - meta[1])):
+        for at, step in enumerate((0, 1, 3)):
+            for i in range(2):
+                row = (at * 2 + i) * width
+                total = total + dot(edges[row:row + width, :], g[channel(meta, side, step * 2 + i)])
+    out[...] = total
+
+
+def late_kernel(final, meta, edges, g, start, out):
     width = g.shape[1]
     side = meta[1] if not final else 1 - meta[1]
     total = start[...]
-    for j in range(edges.shape[0] // width):
-        total = total + dot(edges[j * width:(j + 1) * width, :], g[channel(meta, side, j)])
+    for i in range(2):
+        total = total + dot(edges[i * width:(i + 1) * width, :], g[channel(meta, side, 4 + i)])
     if final:
         total = jnp.where(live(meta[0], total.shape), total, 0.0)
     out[...] = total.astype(out.dtype)
@@ -277,16 +288,21 @@
     edge = call(
         lambda *refs: edge_kernel(factor, *refs), one((2 * width, width), BF), [VMEM] * 2, [], 1 << 20, 12 * block_bytes
     )(from_near, from_far)
-    edges_own = jnp.concatenate(round_x(edge))
-    edges_other = lax.ppermute(edges_own, "c", SWAP)
+    edges_near = jnp.concatenate([edge, along_x(edge, 3), along_x(edge, 1)])
+    edges_far = along_x(edge, 2)
+    other_near = lax.ppermute(edges_near, "c", SWAP)
+    other_far = lax.ppermute(edges_far, "c", SWAP)
+    partial = call(early_kernel, one((width, width), F32), [SMEM] + [VMEM] * 4, [], unit, 4 * half * block_bytes)(
+        meta, edges_near, other_near, g, base
+    )
     partial = call(
-        lambda *refs: half_kernel(False, *refs), one((width, width), F32), [SMEM, VMEM, VMEM, VMEM], [], unit // 2,
-        3 * half * block_bytes,
-    )(meta, edges_own, g, base)
+        lambda *refs: late_kernel(False, *refs), one((width, width), F32), [SMEM] + [VMEM] * 3, [], unit // 8,
+        half * block_bytes,
+    )(meta, edges_far, g, partial)
     second = call(
-        lambda *refs: half_kernel(True, *refs), one((width, width), BF), [SMEM, VMEM, VMEM, VMEM], [], unit // 2,
-        3 * half * block_bytes,
-    )(meta, edges_other, g, partial)
+        lambda *refs: late_kernel(True, *refs), one((width, width), BF), [SMEM] + [VMEM] * 3, [], unit // 8,
+        half * block_bytes,
+    )(meta, other_far, g, partial)
     return (first[None, None], second[None, None])
 
 

time: 148 us -> 165 us (1.11)
  the two profiles are of different devices: /device:TPU:297 before, /device:TPU:217 now
where the time goes in v7:
time: 165 us; the launch traced here: 164 us
  starting transfers between devices  91.9 us (56%)
  waiting for transfers between devices  53.1 us (32%)
  Pallas kernels  11.6 us (7%)
  local copies, waits for them, and re-layouts  3.25 us (2%)
  other arithmetic  2.12 us (1%)
  between operations  1.72 us (1%)
    ppermute x12, starting transfers between devices, along_x(): lax.ppermute(value, 'x', [(i, (i + step) % count) for i in range(count)])  43.8 us
    ppermute x12, waiting for transfers between devices, along_x(): lax.ppermute(value, 'x', [(i, (i + step) % count) for i in range(count)])  24.8 us
    ppermute x1, waiting for transfers between devices, body(): from_far = lax.ppermute(row, YROW, far)  14.3 us
    ppermute x1, starting transfers between devices, body(): across = lax.ppermute(own, 'c', SWAP)  7.43 us
    ppermute x1, starting transfers between devices, body(): from_near = lax.ppermute(row, YROW, near)  7.05 us
    ppermute x1, starting transfers between devices, body(): two_other = lax.ppermute(two_own, 'c', SWAP)  6.45 us
    ppermute x1, waiting for transfers between devices, body(): message_other = lax.ppermute(message, 'yh', SWAP)  6.14 us
    ppermute x1, waiting for transfers between devices, body(): masked_other = lax.ppermute(masked, 'yh', SWAP)  5.42 us
  transfers between devices with their start and end apart: 22, of which 12 were waited for; matrix products, arithmetic and copies ran while one was open for 1% of the time, Pallas kernels for 4%

profile of v7, /device:TPU:217, one launch (start us, length us, event | category | flops | bytes accessed | tf_op | source)
XLA Modules:
  0.0 163.7 jit_solution(11149297857252325462)
XLA Ops:
  2.4 4.8 %collective-permute-start.3 = (bf16[256,256]{1,0:T(8,128)(2,1)S(1)}, bf16[256,256]{1,0:T(8,128)(2,1)S(1)}, u32[]{:S(2)}, u32[]{:S(2)}) collective-permute-start(bf16[256,256]{1,0:T(8,128)(2,1)S(1)} %and_select_fusion), channel_id=1, source_target_pairs={{0,2},{2,0},{1,3},{3,1},{4,6},{6,4},{5,7},{7,5},{8,10},{10,8},{9,1... | collective-permute-start | bytes 393224 | tf_op jit(solution)/shard_map/ppermute | solution.py:242
  7.1 5.4 %collective-permute-done.3 = bf16[256,256]{1,0:T(8,128)(2,1)S(1)} collective-permute-done((bf16[256,256]{1,0:T(8,128)(2,1)S(1)}, bf16[256,256]{1,0:T(8,128)(2,1)S(1)}, u32[]{:S(2)}, u32[]{:S(2)}) %collective-permute-start.3) | collective-permute-done | bytes 131104 | tf_op jit(solution)/shard_map/ppermute | solution.py:242
  13.4 4.1 %all-to-all-start = ((bf16[4,256,256]{2,1,0:T(8,128)(2,1)}), bf16[4,256,256]{2,1,0:T(8,128)(2,1)}, u32[]{:S(2)}, u32[]{:S(2)}) async-start(bf16[4,256,256]{2,1,0:T(8,128)(2,1)} %broadcast_in_dim.20), calls=%async_computation | async-start | bytes 1048576 | tf_op jit(solution)/shard_map/all_to_all | solution.py:208
  17.5 3.3 %collective-permute-start.2 = (bf16[256,256]{1,0:T(8,128)(2,1)S(1)}, bf16[256,256]{1,0:T(8,128)(2,1)S(1)}, u32[]{:S(2)}, u32[]{:S(2)}) collective-permute-start(bf16[256,256]{1,0:T(8,128)(2,1)S(1)} %and_select_fusion), channel_id=1, source_target_pairs={{0,4},{4,8},{8,12},{12,0},{1,5},{5,9},{9,13},{13,1},{2,6},{6,10},{... | collective-permute-start | bytes 393224 | tf_op jit(solution)/shard_map/ppermute | solution.py:198
  20.8 4.3 %collective-permute-start.1 = (bf16[256,256]{1,0:T(8,128)(2,1)S(1)}, bf16[256,256]{1,0:T(8,128)(2,1)S(1)}, u32[]{:S(2)}, u32[]{:S(2)}) collective-permute-start(bf16[256,256]{1,0:T(8,128)(2,1)S(1)} %and_select_fusion), channel_id=1, source_target_pairs={{0,8},{4,12},{8,0},{12,4},{1,9},{5,13},{9,1},{13,5},{2,10},{6,14},... | collective-permute-start | bytes 393224 | tf_op jit(solution)/shard_map/ppermute | solution.py:198
  25.1 3.1 %collective-permute-start = (bf16[256,256]{1,0:T(8,128)(2,1)S(1)}, bf16[256,256]{1,0:T(8,128)(2,1)S(1)}, u32[]{:S(2)}, u32[]{:S(2)}) collective-permute-start(bf16[256,256]{1,0:T(8,128)(2,1)S(1)} %and_select_fusion), channel_id=1, source_target_pairs={{0,12},{4,0},{8,4},{12,8},{1,13},{5,1},{9,5},{13,9},{2,14},{6,2},{... | collective-permute-start | bytes 393224 | tf_op jit(solution)/shard_map/ppermute | solution.py:198
  34.6 7.4 %collective-permute-start.4 = (bf16[8,256,256]{2,1,0:T(8,128)(2,1)S(1)}, bf16[8,256,256]{2,1,0:T(8,128)(2,1)}, u32[]{:S(2)}, u32[]{:S(2)}) collective-permute-start(bf16[8,256,256]{2,1,0:T(8,128)(2,1)S(1)} %constant_dynamic-update-slice_fusion.own), channel_id=1, source_target_pairs={{0,1},{1,0},{2,3},{3,2},{4,5},{5,4},{6,7},{7,6},{8,9},{9,8},{10,11... | collective-permute-start | bytes 3145736 | tf_op jit(solution)/shard_map/ppermute | solution.py:247
  44.4 4.4 %shard_map.69 = (bf16[256,256]{1,0:T(8,128)(2,1)}, bf16[272,256]{1,0:T(8,128)(2,1)S(1)}, bf16[16,256]{1,0:T(8,128)(2,1)S(1)}, bf16[2064,256]{1,0:T(8,128)(2,1)S(1)}, bf16[256,256]{1,0:T(8,128)(2,1)S(1)}) custom-call(s32[4]{0:T(128)S(1)} %pad_add_fusion.meta.refs_0_, s32[16]{0:T(128)S(1)} %bitcast.23, ...), custom_call_target="tpu_custom_call" | custom-call | flops 1610612736 | bytes 8388608 | tf_op jit(solution)/shard_map/pallas_call | solution.py:250
  51.1 4.7 %collective-permute-start.13 = (bf16[272,256]{1,0:T(8,128)(2,1)S(1)}, bf16[272,256]{1,0:T(8,128)(2,1)S(1)}, u32[]{:S(2)}, u32[]{:S(2)}) collective-permute-start(bf16[272,256]{1,0:T(8,128)(2,1)S(1)} %get-tuple-element.18.message), channel_id=1, source_target_pairs={{0,2},{2,0},{1,3},{3,1},{4,6},{6,4},{5,7},{7,5},{8,10},{10,8},{9,1... | collective-permute-start | bytes 417800 | tf_op jit(solution)/shard_map/ppermute | solution.py:260
  55.9 6.1 %collective-permute-done.13 = bf16[272,256]{1,0:T(8,128)(2,1)S(1)} collective-permute-done((bf16[272,256]{1,0:T(8,128)(2,1)S(1)}, bf16[272,256]{1,0:T(8,128)(2,1)S(1)}, u32[]{:S(2)}, u32[]{:S(2)}) %collective-permute-start.13) | collective-permute-done | bytes 139296 | tf_op jit(solution)/shard_map/ppermute | solution.py:260
  62.0 4.3 %collective-permute-start.14 = (bf16[544,256]{1,0:T(8,128)(2,1)S(1)}, bf16[544,256]{1,0:T(8,128)(2,1)S(1)}, u32[]{:S(2)}, u32[]{:S(2)}) collective-permute-start(bf16[544,256]{1,0:T(8,128)(2,1)S(1)} %get-tuple-element.36), channel_id=1, source_target_pairs={{0,12},{4,0},{8,4},{12,8},{1,13},{5,1},{9,5},{13,9},{2,14},{6,2},{... | collective-permute-start | bytes 835592 | tf_op jit(solution)/shard_map/ppermute | solution.py:198
  72.4 4.3 %collective-permute-start.6 = (bf16[528,256]{1,0:T(8,128)(2,1)S(1)}, bf16[528,256]{1,0:T(8,128)(2,1)S(1)}, u32[]{:S(2)}, u32[]{:S(2)}) collective-permute-start(bf16[528,256]{1,0:T(8,128)(2,1)S(1)} %get-tuple-element.23), channel_id=1, source_target_pairs={{0,8},{4,12},{8,0},{12,4},{1,9},{5,13},{9,1},{13,5},{2,10},{6,14},... | collective-permute-start | bytes 811016 | tf_op jit(solution)/shard_map/ppermute | solution.py:198
  76.7 4.0 %collective-permute-start.7 = (bf16[528,256]{1,0:T(8,128)(2,1)S(1)}, bf16[528,256]{1,0:T(8,128)(2,1)S(1)}, u32[]{:S(2)}, u32[]{:S(2)}) collective-permute-start(bf16[528,256]{1,0:T(8,128)(2,1)S(1)} %get-tuple-element.24), channel_id=1, source_target_pairs={{0,4},{4,8},{8,12},{12,0},{1,5},{5,9},{9,13},{13,1},{2,6},{6,10},{... | collective-permute-start | bytes 811016 | tf_op jit(solution)/shard_map/ppermute | solution.py:198
  85.4 6.5 %collective-permute-start.17 = (bf16[2176,256]{1,0:T(8,128)(2,1)S(1)}, bf16[2176,256]{1,0:T(8,128)(2,1)S(1)}, u32[]{:S(2)}, u32[]{:S(2)}) collective-permute-start(bf16[2176,256]{1,0:T(8,128)(2,1)S(1)} %get-tuple-element.28), channel_id=1, source_target_pairs={{0,1},{1,0},{2,3},{3,2},{4,5},{5,4},{6,7},{7,6},{8,9},{9,8},{10,11... | collective-permute-start | bytes 3342344 | tf_op jit(solution)/shard_map/ppermute | solution.py:277
  91.8 3.7 %collective-permute-done.7.c = bf16[528,256]{1,0:T(8,128)(2,1)S(1)} collective-permute-done((bf16[528,256]{1,0:T(8,128)(2,1)S(1)}, bf16[528,256]{1,0:T(8,128)(2,1)S(1)}, u32[]{:S(2)}, u32[]{:S(2)}) %collective-permute-start.7) | collective-permute-done | bytes 270368 | tf_op jit(solution)/shard_map/ppermute | solution.py:198
  95.7 7.1 %collective-permute-start.9 = (bf16[528,256]{1,0:T(8,128)(2,1)S(1)}, bf16[528,256]{1,0:T(8,128)(2,1)S(1)}, u32[]{:S(2)}, u32[]{:S(2)}) collective-permute-start(bf16[528,256]{1,0:T(8,128)(2,1)S(1)} %shard_map.72), channel_id=1, source_target_pairs={{0,16},{2,18},{16,32},{18,34},{32,48},{34,50},{48,66},{50,64},{64,... | collective-permute-start | bytes 811016 | tf_op jit(solution)/shard_map/ppermute | solution.py:273
  102.8 4.4 %collective-permute-start.10 = (bf16[528,256]{1,0:T(8,128)(2,1)S(1)}, bf16[528,256]{1,0:T(8,128)(2,1)S(1)}, u32[]{:S(2)}, u32[]{:S(2)}) collective-permute-start(bf16[528,256]{1,0:T(8,128)(2,1)S(1)} %shard_map.72), channel_id=1, source_target_pairs={{0,18},{2,16},{16,34},{18,32},{32,50},{34,48},{48,64},{50,66},{64,... | collective-permute-start | bytes 811016 | tf_op jit(solution)/shard_map/ppermute | solution.py:272
  107.5 14.3 %collective-permute-done.10.refs_1_ = bf16[528,256]{1,0:T(8,128)(2,1)S(1)} collective-permute-done((bf16[528,256]{1,0:T(8,128)(2,1)S(1)}, bf16[528,256]{1,0:T(8,128)(2,1)S(1)}, u32[]{:S(2)}, u32[]{:S(2)}) %collective-permute-start.10) | collective-permute-done | bytes 270368 | tf_op jit(solution)/shard_map/ppermute | solution.py:272
  121.9 9.7 %collective-permute-start.19 = (bf16[512,256]{1,0:T(8,128)(2,1)S(1)}, bf16[512,256]{1,0:T(8,128)(2,1)S(1)}, u32[]{:S(2)}, u32[]{:S(2)}) collective-permute-start(bf16[512,256]{1,0:T(8,128)(2,1)S(1)} %shard_map.73), channel_id=1, source_target_pairs={{0,4},{4,8},{8,12},{12,0},{1,5},{5,9},{9,13},{13,1},{2,6},{6,10},{... | collective-permute-start | bytes 786440 | tf_op jit(solution)/shard_map/ppermute | solution.py:198
  133.6 2.6 %collective-permute-done.19 = bf16[512,256]{1,0:T(8,128)(2,1)S(1)} collective-permute-done((bf16[512,256]{1,0:T(8,128)(2,1)S(1)}, bf16[512,256]{1,0:T(8,128)(2,1)S(1)}, u32[]{:S(2)}, u32[]{:S(2)}) %collective-permute-start.19) | collective-permute-done | bytes 262176 | tf_op jit(solution)/shard_map/ppermute | solution.py:198
  136.2 3.8 %collective-permute-done.18 = bf16[512,256]{1,0:T(8,128)(2,1)S(1)} collective-permute-done((bf16[512,256]{1,0:T(8,128)(2,1)S(1)}, bf16[512,256]{1,0:T(8,128)(2,1)S(1)}, u32[]{:S(2)}, u32[]{:S(2)}) %collective-permute-start.18) | collective-permute-done | bytes 262176 | tf_op jit(solution)/shard_map/ppermute | solution.py:198
  140.1 4.2 %collective-permute-start.20 = (bf16[1536,256]{1,0:T(8,128)(2,1)S(1)}, bf16[1536,256]{1,0:T(8,128)(2,1)S(1)}, u32[]{:S(2)}, u32[]{:S(2)}) collective-permute-start(bf16[1536,256]{1,0:T(8,128)(2,1)S(1)} %pad_maximum_fusion.own), channel_id=1, source_target_pairs={{0,1},{1,0},{2,3},{3,2},{4,5},{5,4},{6,7},{7,6},{8,9},{9,8},{10,11... | collective-permute-start | bytes 2359304 | tf_op jit(solution)/shard_map/ppermute | solution.py:293
  146.1 9.3 %collective-permute-done.11.refs_1_ = bf16[512,256]{1,0:T(8,128)(2,1)S(1)} collective-permute-done((bf16[512,256]{1,0:T(8,128)(2,1)S(1)}, bf16[512,256]{1,0:T(8,128)(2,1)S(1)}, u32[]{:S(2)}, u32[]{:S(2)}) %collective-permute-start.11) | collective-permute-done | bytes 262176 | tf_op jit(solution)/shard_map/ppermute | solution.py:198
  155.5 2.8 %collective-permute-start.12 = (bf16[512,256]{1,0:T(8,128)(2,1)S(1)}, bf16[512,256]{1,0:T(8,128)(2,1)S(1)}, u32[]{:S(2)}, u32[]{:S(2)}) collective-permute-start(bf16[512,256]{1,0:T(8,128)(2,1)S(1)} %collective-permute-done.11.refs_1_), channel_id=1, source_target_pairs={{0,1},{1,0},{2,3},{3,2},{4,5},{5,4},{6,7},{7,6},{8,9},{9,8},{10,11... | collective-permute-start | bytes 786440 | tf_op jit(solution)/shard_map/ppermute | solution.py:294
  (53 shorter events, 33.4 us)
Async XLA Ops:
  0.6 27.6 %copy-start.3 = (bf16[1,1,256,256]{3,2,1,0:T(8,128)(2,1)S(1)}, bf16[1,1,256,256]{3,2,1,0:T(8,128)(2,1)}, u32[]{:S(2)}) copy-start(bf16[1,1,256,256]{3,2,1,0:T(8,128)(2,1)} %param.5) | copy-start | bytes 393220
  2.4 10.2 %collective-permute-start.3 = (bf16[256,256]{1,0:T(8,128)(2,1)S(1)}, bf16[256,256]{1,0:T(8,128)(2,1)S(1)}, u32[]{:S(2)}, u32[]{:S(2)}) collective-permute-start(bf16[256,256]{1,0:T(8,128)(2,1)S(1)} %and_select_fusion), channel_id=1, source_target_pairs={{0,2},{2,0},{1,3},{3,1},{4,6},{6,4},{5,7},{7,5},{8,10},{10,8},{9,1... | collective-permute-start | bytes 393224 | tf_op jit(solution)/shard_map/ppermute | solution.py:242
  13.4 19.1 %all-to-all-start = ((bf16[4,256,256]{2,1,0:T(8,128)(2,1)}), bf16[4,256,256]{2,1,0:T(8,128)(2,1)}, u32[]{:S(2)}, u32[]{:S(2)}) async-start(bf16[4,256,256]{2,1,0:T(8,128)(2,1)} %broadcast_in_dim.20), calls=%async_computation | async-start | bytes 1048576 | tf_op jit(solution)/shard_map/all_to_all | solution.py:208
  17.5 10.9 %collective-permute-start.2 = (bf16[256,256]{1,0:T(8,128)(2,1)S(1)}, bf16[256,256]{1,0:T(8,128)(2,1)S(1)}, u32[]{:S(2)}, u32[]{:S(2)}) collective-permute-start(bf16[256,256]{1,0:T(8,128)(2,1)S(1)} %and_select_fusion), channel_id=1, source_target_pairs={{0,4},{4,8},{8,12},{12,0},{1,5},{5,9},{9,13},{13,1},{2,6},{6,10},{... | collective-permute-start | bytes 393224 | tf_op jit(solution)/shard_map/ppermute | solution.py:198
  20.8 9.0 %collective-permute-start.1 = (bf16[256,256]{1,0:T(8,128)(2,1)S(1)}, bf16[256,256]{1,0:T(8,128)(2,1)S(1)}, u32[]{:S(2)}, u32[]{:S(2)}) collective-permute-start(bf16[256,256]{1,0:T(8,128)(2,1)S(1)} %and_select_fusion), channel_id=1, source_target_pairs={{0,8},{4,12},{8,0},{12,4},{1,9},{5,13},{9,1},{13,5},{2,10},{6,14},... | collective-permute-start | bytes 393224 | tf_op jit(solution)/shard_map/ppermute | solution.py:198
  25.1 6.4 %collective-permute-start = (bf16[256,256]{1,0:T(8,128)(2,1)S(1)}, bf16[256,256]{1,0:T(8,128)(2,1)S(1)}, u32[]{:S(2)}, u32[]{:S(2)}) collective-permute-start(bf16[256,256]{1,0:T(8,128)(2,1)S(1)} %and_select_fusion), channel_id=1, source_target_pairs={{0,12},{4,0},{8,4},{12,8},{1,13},{5,1},{9,5},{13,9},{2,14},{6,2},{... | collective-permute-start | bytes 393224 | tf_op jit(solution)/shard_map/ppermute | solution.py:198
  31.6 10.5 %copy-start.1 = (bf16[1,1,16,256,256]{4,3,2,1,0:T(8,128)(2,1)S(1)}, bf16[1,1,16,256,256]{4,3,2,1,0:T(8,128)(2,1)}, u32[]{:S(2)}) copy-start(bf16[1,1,16,256,256]{4,3,2,1,0:T(8,128)(2,1)} %param.7) | copy-start | bytes 6291460
  34.6 9.8 %collective-permute-start.4 = (bf16[8,256,256]{2,1,0:T(8,128)(2,1)S(1)}, bf16[8,256,256]{2,1,0:T(8,128)(2,1)}, u32[]{:S(2)}, u32[]{:S(2)}) collective-permute-start(bf16[8,256,256]{2,1,0:T(8,128)(2,1)S(1)} %constant_dynamic-update-slice_fusion.own), channel_id=1, source_target_pairs={{0,1},{1,0},{2,3},{3,2},{4,5},{5,4},{6,7},{7,6},{8,9},{9,8},{10,11... | collective-permute-start | bytes 3145736 | tf_op jit(solution)/shard_map/ppermute | solution.py:247
  48.8 23.3 %collective-permute-start.5 = (bf16[2064,256]{1,0:T(8,128)(2,1)S(1)}, bf16[2064,256]{1,0:T(8,128)(2,1)S(1)}, u32[]{:S(2)}, u32[]{:S(2)}) collective-permute-start(bf16[2064,256]{1,0:T(8,128)(2,1)S(1)} %get-tuple-element.21), channel_id=1, source_target_pairs={{0,1},{1,0},{2,3},{3,2},{4,5},{5,4},{6,7},{7,6},{8,9},{9,8},{10,11... | collective-permute-start | bytes 3170312 | tf_op jit(solution)/shard_map/ppermute | solution.py:259
  51.1 10.9 %collective-permute-start.13 = (bf16[272,256]{1,0:T(8,128)(2,1)S(1)}, bf16[272,256]{1,0:T(8,128)(2,1)S(1)}, u32[]{:S(2)}, u32[]{:S(2)}) collective-permute-start(bf16[272,256]{1,0:T(8,128)(2,1)S(1)} %get-tuple-element.18.message), channel_id=1, source_target_pairs={{0,2},{2,0},{1,3},{3,1},{4,6},{6,4},{5,7},{7,5},{8,10},{10,8},{9,1... | collective-permute-start | bytes 417800 | tf_op jit(solution)/shard_map/ppermute | solution.py:260
  62.0 10.0 %collective-permute-start.14 = (bf16[544,256]{1,0:T(8,128)(2,1)S(1)}, bf16[544,256]{1,0:T(8,128)(2,1)S(1)}, u32[]{:S(2)}, u32[]{:S(2)}) collective-permute-start(bf16[544,256]{1,0:T(8,128)(2,1)S(1)} %get-tuple-element.36), channel_id=1, source_target_pairs={{0,12},{4,0},{8,4},{12,8},{1,13},{5,1},{9,5},{13,9},{2,14},{6,2},{... | collective-permute-start | bytes 835592 | tf_op jit(solution)/shard_map/ppermute | solution.py:198
  66.4 16.8 %collective-permute-start.15 = (bf16[544,256]{1,0:T(8,128)(2,1)S(1)}, bf16[544,256]{1,0:T(8,128)(2,1)S(1)}, u32[]{:S(2)}, u32[]{:S(2)}) collective-permute-start(bf16[544,256]{1,0:T(8,128)(2,1)S(1)} %get-tuple-element.36), channel_id=1, source_target_pairs={{0,8},{4,12},{8,0},{12,4},{1,9},{5,13},{9,1},{13,5},{2,10},{6,14},... | collective-permute-start | bytes 835592 | tf_op jit(solution)/shard_map/ppermute | solution.py:198
  68.3 17.0 %collective-permute-start.16 = (bf16[544,256]{1,0:T(8,128)(2,1)S(1)}, bf16[544,256]{1,0:T(8,128)(2,1)S(1)}, u32[]{:S(2)}, u32[]{:S(2)}) collective-permute-start(bf16[544,256]{1,0:T(8,128)(2,1)S(1)} %get-tuple-element.36), channel_id=1, source_target_pairs={{0,4},{4,8},{8,12},{12,0},{1,5},{5,9},{9,13},{13,1},{2,6},{6,10},{... | collective-permute-start | bytes 835592 | tf_op jit(solution)/shard_map/ppermute | solution.py:198
  72.4 19.4 %collective-permute-start.6 = (bf16[528,256]{1,0:T(8,128)(2,1)S(1)}, bf16[528,256]{1,0:T(8,128)(2,1)S(1)}, u32[]{:S(2)}, u32[]{:S(2)}) collective-permute-start(bf16[528,256]{1,0:T(8,128)(2,1)S(1)} %get-tuple-element.23), channel_id=1, source_target_pairs={{0,8},{4,12},{8,0},{12,4},{1,9},{5,13},{9,1},{13,5},{2,10},{6,14},... | collective-permute-start | bytes 811016 | tf_op jit(solution)/shard_map/ppermute | solution.py:198
  76.7 18.9 %collective-permute-start.7 = (bf16[528,256]{1,0:T(8,128)(2,1)S(1)}, bf16[528,256]{1,0:T(8,128)(2,1)S(1)}, u32[]{:S(2)}, u32[]{:S(2)}) collective-permute-start(bf16[528,256]{1,0:T(8,128)(2,1)S(1)} %get-tuple-element.24), channel_id=1, source_target_pairs={{0,4},{4,8},{8,12},{12,0},{1,5},{5,9},{9,13},{13,1},{2,6},{6,10},{... | collective-permute-start | bytes 811016 | tf_op jit(solution)/shard_map/ppermute | solution.py:198
  80.7 14.9 %collective-permute-start.8 = (bf16[528,256]{1,0:T(8,128)(2,1)S(1)}, bf16[528,256]{1,0:T(8,128)(2,1)S(1)}, u32[]{:S(2)}, u32[]{:S(2)}) collective-permute-start(bf16[528,256]{1,0:T(8,128)(2,1)S(1)} %get-tuple-element.25), channel_id=1, source_target_pairs={{0,12},{4,0},{8,4},{12,8},{1,13},{5,1},{9,5},{13,9},{2,14},{6,2},{... | collective-permute-start | bytes 811016 | tf_op jit(solution)/shard_map/ppermute | solution.py:198
  85.4 72.9 %collective-permute-start.17 = (bf16[2176,256]{1,0:T(8,128)(2,1)S(1)}, bf16[2176,256]{1,0:T(8,128)(2,1)S(1)}, u32[]{:S(2)}, u32[]{:S(2)}) collective-permute-start(bf16[2176,256]{1,0:T(8,128)(2,1)S(1)} %get-tuple-element.28), channel_id=1, source_target_pairs={{0,1},{1,0},{2,3},{3,2},{4,5},{5,4},{6,7},{7,6},{8,9},{9,8},{10,11... | collective-permute-start | bytes 3342344 | tf_op jit(solution)/shard_map/ppermute | solution.py:277
  95.7 11.8 %collective-permute-start.9 = (bf16[528,256]{1,0:T(8,128)(2,1)S(1)}, bf16[528,256]{1,0:T(8,128)(2,1)S(1)}, u32[]{:S(2)}, u32[]{:S(2)}) collective-permute-start(bf16[528,256]{1,0:T(8,128)(2,1)S(1)} %shard_map.72), channel_id=1, source_target_pairs={{0,16},{2,18},{16,32},{18,34},{32,48},{34,50},{48,66},{50,64},{64,... | collective-permute-start | bytes 811016 | tf_op jit(solution)/shard_map/ppermute | solution.py:273
  102.8 19.0 %collective-permute-start.10 = (bf16[528,256]{1,0:T(8,128)(2,1)S(1)}, bf16[528,256]{1,0:T(8,128)(2,1)S(1)}, u32[]{:S(2)}, u32[]{:S(2)}) collective-permute-start(bf16[528,256]{1,0:T(8,128)(2,1)S(1)} %shard_map.72), channel_id=1, source_target_pairs={{0,18},{2,16},{16,34},{18,32},{32,50},{34,48},{48,64},{50,66},{64,... | collective-permute-start | bytes 811016 | tf_op jit(solution)/shard_map/ppermute | solution.py:272
  121.9 14.3 %collective-permute-start.19 = (bf16[512,256]{1,0:T(8,128)(2,1)S(1)}, bf16[512,256]{1,0:T(8,128)(2,1)S(1)}, u32[]{:S(2)}, u32[]{:S(2)}) collective-permute-start(bf16[512,256]{1,0:T(8,128)(2,1)S(1)} %shard_map.73), channel_id=1, source_target_pairs={{0,4},{4,8},{8,12},{12,0},{1,5},{5,9},{9,13},{13,1},{2,6},{6,10},{... | collective-permute-start | bytes 786440 | tf_op jit(solution)/shard_map/ppermute | solution.py:198
  131.6 8.4 %collective-permute-start.18 = (bf16[512,256]{1,0:T(8,128)(2,1)S(1)}, bf16[512,256]{1,0:T(8,128)(2,1)S(1)}, u32[]{:S(2)}, u32[]{:S(2)}) collective-permute-start(bf16[512,256]{1,0:T(8,128)(2,1)S(1)} %shard_map.73), channel_id=1, source_target_pairs={{0,12},{4,0},{8,4},{12,8},{1,13},{5,1},{9,5},{13,9},{2,14},{6,2},{... | collective-permute-start | bytes 786440 | tf_op jit(solution)/shard_map/ppermute | solution.py:198
  140.1 20.3 %collective-permute-start.20 = (bf16[1536,256]{1,0:T(8,128)(2,1)S(1)}, bf16[1536,256]{1,0:T(8,128)(2,1)S(1)}, u32[]{:S(2)}, u32[]{:S(2)}) collective-permute-start(bf16[1536,256]{1,0:T(8,128)(2,1)S(1)} %pad_maximum_fusion.own), channel_id=1, source_target_pairs={{0,1},{1,0},{2,3},{3,2},{4,5},{5,4},{6,7},{7,6},{8,9},{9,8},{10,11... | collective-permute-start | bytes 2359304 | tf_op jit(solution)/shard_map/ppermute | solution.py:293
  144.2 11.2 %collective-permute-start.11 = (bf16[512,256]{1,0:T(8,128)(2,1)S(1)}, bf16[512,256]{1,0:T(8,128)(2,1)S(1)}, u32[]{:S(2)}, u32[]{:S(2)}) collective-permute-start(bf16[512,256]{1,0:T(8,128)(2,1)S(1)} %shard_map.73), channel_id=1, source_target_pairs={{0,8},{4,12},{8,0},{12,4},{1,9},{5,13},{9,1},{13,5},{2,10},{6,14},... | collective-permute-start | bytes 786440 | tf_op jit(solution)/shard_map/ppermute | solution.py:198
  155.5 6.8 %collective-permute-start.12 = (bf16[512,256]{1,0:T(8,128)(2,1)S(1)}, bf16[512,256]{1,0:T(8,128)(2,1)S(1)}, u32[]{:S(2)}, u32[]{:S(2)}) collective-permute-start(bf16[512,256]{1,0:T(8,128)(2,1)S(1)} %collective-permute-done.11.refs_1_), channel_id=1, source_target_pairs={{0,1},{1,0},{2,3},{3,2},{4,5},{5,4},{6,7},{7,6},{8,9},{9,8},{10,11... | collective-permute-start | bytes 786440 | tf_op jit(solution)/shard_map/ppermute | solution.py:294
  (2 other events, 4.8 us)

commit v8 on v6

--- a/solution.py
+++ b/solution.py
@@ -11,7 +11,7 @@
 
 BF = jnp.bfloat16
 F32 = jnp.float32
-TILE = 16
+TILE = 8
 YROW = ("z", "yl", "yh")
 SWAP = [(0, 1), (1, 0)]
 VMEM = pl.BlockSpec(memory_space=pltpu.VMEM)
@@ -63,7 +63,7 @@
     out[...] = source[...]
 
 
-def first_kernel(meta, picks, own, across, left, right, first_out, message, stats, send, turned_out, pool, inner, lv):
+def first_kernel(meta, picks, own, across, left, right, first_out, message, pool, inner):
     channels, width = left.shape[0], left.shape[1]
     half = channels // 2
     pool[0:half] = own[...]
@@ -81,39 +81,34 @@
     columns = jnp.sum(value * value, axis=0, keepdims=True)
     squares = jnp.broadcast_to(jnp.sum(columns, axis=1, keepdims=True), (1, width))
     count = jnp.full((1, width), size * size, jnp.int32).astype(F32)
-    tile = pack(squares, count)
-    message[width:width + TILE, :] = tile
-    stats[...] = tile
-    send[half * width:half * width + TILE, :] = tile
-    turned = value.T.astype(BF)
-    turned_out[...] = turned
-    for j in range(half):
-        lv[j] = dot(left[channel(meta, 1 - meta[1], j)], product).astype(BF)
-    for j in range(half):
-        send[j * width:(j + 1) * width, :] = dot(turned, lv[j]).astype(BF)
-
-
-def keep_kernel(meta, message, turned, left, keep, lv):
+    message[width:width + TILE, :] = pack(squares, count)
+
+
+def terms(message, left_of, lv, count):
+    width = message.shape[1]
+    first = message[0:width, :]
+    turned = first.astype(F32).T.astype(BF)
+    for j in range(count):
+        lv[j] = dot(left_of(j), first).astype(BF)
+    return [lambda j=j: dot(turned, lv[j]) for j in range(count)]
+
+
+def keep_kernel(meta, message, left, keep, lv):
+    half = left.shape[0] // 2
+    for j, term in enumerate(terms(message, lambda j: left[channel(meta, meta[1], j)], lv, half)):
+        keep[j] = term()
+
+
+def core_sum_kernel(meta, message, keep, left, *refs):
+    own, lv, outs = refs[0], refs[-1], refs[1:-1]
     half, width = left.shape[0] // 2, left.shape[1]
-    first = message[0:width, :]
-    for j in range(half):
-        lv[j] = dot(left[channel(meta, meta[1], j)], first).astype(BF)
-    for j in range(half):
-        keep[j * width:(j + 1) * width, :] = dot(turned[...], lv[j]).astype(BF)
-
-
-def core_sum_kernel(keep, stats, arrived, *outs):
-    rows = keep.shape[0]
-    quarter = rows // 4
-    q0, c0 = unpack(stats[...])
-    q1, c1 = unpack(arrived[rows:rows + TILE, :])
+    q0, c0 = unpack(own[width:width + TILE, :])
+    q1, c1 = unpack(message[width:width + TILE, :])
     tile = pack(q0 + q1, c0 + c1)
-    for step, out in enumerate(outs):
-        at = step * quarter
-        out[0:quarter, :] = (
-            keep[at:at + quarter, :].astype(F32) + arrived[at:at + quarter, :].astype(F32)
-        ).astype(BF)
-        out[quarter:quarter + TILE, :] = tile
+    for out in outs:
+        out[2 * width:2 * width + TILE, :] = tile
+    for j, term in enumerate(terms(message, lambda j: left[channel(meta, meta[1], j)], lv, half)):
+        outs[j // 2][(j % 2) * width:(j % 2 + 1) * width, :] = (keep[j] + term()).astype(BF)
 
 
 def row_sum_kernel(a, b, c, d, out):
@@ -235,24 +230,22 @@
     own = jnp.concatenate(lax.optimization_barrier((own, own_other)))
     across = lax.ppermute(own, "c", SWAP)
     right_here = call(load_kernel, one(right.shape, BF), [VMEM], [], 1 << 20, 2 * channels * block_bytes)(right)
+    left_other = lax.ppermute(left, "c", SWAP)
     stack = pltpu.VMEM((half, width, width), BF)
-    first, message, stats, send, turned = call(
-        first_kernel,
-        [((width, width), BF), ((span, width), BF), ((TILE, width), BF),
-         ((half * width + TILE, width), BF), ((width, width), BF)],
-        [SMEM, SMEM] + [VMEM] * 4,
-        [pltpu.VMEM((channels, width, width), BF), pltpu.VMEM((width, channels * width), BF), stack],
-        3 * unit, 4 * channels * block_bytes,
+    first, message = call(
+        first_kernel, [((width, width), BF), ((span, width), BF)], [SMEM, SMEM] + [VMEM] * 4,
+        [pltpu.VMEM((channels, width, width), BF), pltpu.VMEM((width, channels * width), BF)],
+        2 * unit, 4 * channels * block_bytes,
     )(meta, picks, own, across, left, right_here)
 
-    arrived = lax.ppermute(send, "c", SWAP)
+    message_core = lax.ppermute(message, "c", SWAP)
     message_other = lax.ppermute(message, "yh", SWAP)
     keep = call(
-        keep_kernel, one((half * width, width), BF), [SMEM, VMEM, VMEM, VMEM], [stack], unit, 2 * channels * block_bytes
-    )(meta, message, turned, left)
+        keep_kernel, one((half, width, width), F32), [SMEM, VMEM, VMEM], [stack], unit, 2 * channels * block_bytes
+    )(meta, message, left)
     parts = call(
-        core_sum_kernel, [((2 * width + TILE, width), BF)] * 4, [VMEM] * 3, [], 1 << 20, 3 * half * block_bytes
-    )(keep, stats, arrived)
+        core_sum_kernel, [((2 * width + TILE, width), BF)] * 4, [SMEM] + [VMEM] * 4, [stack], unit, 3 * half * block_bytes
+    )(meta, message_core, keep, left_other, message)
     arrived_x = [along_x(parts[2], 2), along_x(parts[1], 1), along_x(parts[3], 3)]
     row = call(
         row_sum_kernel, one((2 * width + TILE, width), BF), [VMEM] * 4, [], 1 << 20, 10 * block_bytes

time: 148 us -> 148 us (level)
  the two profiles are of different devices: /device:TPU:297 before, /device:TPU:329 now
where the time goes in v8:
time: 148 us; the launch traced here: 147 us
  starting transfers between devices  80.1 us (54%)
  waiting for transfers between devices  45.9 us (31%)
  Pallas kernels  11 us (7%)
  local copies, waits for them, and re-layouts  5.63 us (4%)
  other arithmetic  3.04 us (2%)
  between operations  1.68 us (1%)
    ppermute x12, starting transfers between devices, along_x(): lax.ppermute(value, 'x', [(i, (i + step) % count) for i in range(count)])  37.3 us
    ppermute x12, waiting for transfers between devices, along_x(): lax.ppermute(value, 'x', [(i, (i + step) % count) for i in range(count)])  19.2 us
    ppermute x1, waiting for transfers between devices, body(): from_far = lax.ppermute(row, YROW, far)  17.6 us
    ppermute x1, starting transfers between devices, body(): left_other = lax.ppermute(left, 'c', SWAP)  7.41 us
    ppermute x1, starting transfers between devices, body(): message_other = lax.ppermute(message, 'yh', SWAP)  6.69 us
    ppermute x1, starting transfers between devices, body(): masked_other = lax.ppermute(masked, 'yh', SWAP)  6.55 us
    ppermute x1, waiting for transfers between devices, body(): message_other = lax.ppermute(message, 'yh', SWAP)  4.87 us
    all_to_all x1, starting transfers between devices, to_everyone_on_x(): lax.all_to_all(jnp.broadcast_to(value[None], (count, *value.shape)), 'x',...  4.14 us
  transfers between devices with their start and end apart: 22, of which 8 were waited for; matrix products, arithmetic and copies ran while one was open for 3% of the time, Pallas kernels for 6%

profile of v8, /device:TPU:329, one launch (start us, length us, event | category | flops | bytes accessed | tf_op | source)
XLA Modules:
  0.0 147.3 jit_solution(7981147475599953196)
XLA Ops:
  2.3 6.6 %collective-permute-start.3 = (bf16[256,256]{1,0:T(8,128)(2,1)S(1)}, bf16[256,256]{1,0:T(8,128)(2,1)S(1)}, u32[]{:S(2)}, u32[]{:S(2)}) collective-permute-start(bf16[256,256]{1,0:T(8,128)(2,1)S(1)} %and_select_fusion), channel_id=1, source_target_pairs={{0,2},{2,0},{1,3},{3,1},{4,6},{6,4},{5,7},{7,5},{8,10},{10,8},{9,1... | collective-permute-start | bytes 393224 | tf_op jit(solution)/shard_map/ppermute | solution.py:226
  8.9 3.6 %collective-permute-done.3 = bf16[256,256]{1,0:T(8,128)(2,1)S(1)} collective-permute-done((bf16[256,256]{1,0:T(8,128)(2,1)S(1)}, bf16[256,256]{1,0:T(8,128)(2,1)S(1)}, u32[]{:S(2)}, u32[]{:S(2)}) %collective-permute-start.3) | collective-permute-done | bytes 131104 | tf_op jit(solution)/shard_map/ppermute | solution.py:226
  13.3 4.1 %all-to-all-start = ((bf16[4,256,256]{2,1,0:T(8,128)(2,1)}), bf16[4,256,256]{2,1,0:T(8,128)(2,1)}, u32[]{:S(2)}, u32[]{:S(2)}) async-start(bf16[4,256,256]{2,1,0:T(8,128)(2,1)} %broadcast_in_dim.20), calls=%async_computation | async-start | bytes 1048576 | tf_op jit(solution)/shard_map/all_to_all | solution.py:192
  17.5 3.3 %collective-permute-start.2 = (bf16[256,256]{1,0:T(8,128)(2,1)S(1)}, bf16[256,256]{1,0:T(8,128)(2,1)S(1)}, u32[]{:S(2)}, u32[]{:S(2)}) collective-permute-start(bf16[256,256]{1,0:T(8,128)(2,1)S(1)} %and_select_fusion), channel_id=1, source_target_pairs={{0,4},{4,8},{8,12},{12,0},{1,5},{5,9},{9,13},{13,1},{2,6},{6,10},{... | collective-permute-start | bytes 393224 | tf_op jit(solution)/shard_map/ppermute | solution.py:182
  20.8 3.2 %collective-permute-start = (bf16[256,256]{1,0:T(8,128)(2,1)S(1)}, bf16[256,256]{1,0:T(8,128)(2,1)S(1)}, u32[]{:S(2)}, u32[]{:S(2)}) collective-permute-start(bf16[256,256]{1,0:T(8,128)(2,1)S(1)} %and_select_fusion), channel_id=1, source_target_pairs={{0,12},{4,0},{8,4},{12,8},{1,13},{5,1},{9,5},{13,9},{2,14},{6,2},{... | collective-permute-start | bytes 393224 | tf_op jit(solution)/shard_map/ppermute | solution.py:182
  24.0 3.6 %collective-permute-start.1 = (bf16[256,256]{1,0:T(8,128)(2,1)S(1)}, bf16[256,256]{1,0:T(8,128)(2,1)S(1)}, u32[]{:S(2)}, u32[]{:S(2)}) collective-permute-start(bf16[256,256]{1,0:T(8,128)(2,1)S(1)} %and_select_fusion), channel_id=1, source_target_pairs={{0,8},{4,12},{8,0},{12,4},{1,9},{5,13},{9,1},{13,5},{2,10},{6,14},... | collective-permute-start | bytes 393224 | tf_op jit(solution)/shard_map/ppermute | solution.py:182
  27.6 7.4 %collective-permute-start.6 = (bf16[16,256,256]{2,1,0:T(8,128)(2,1)}, bf16[16,256,256]{2,1,0:T(8,128)(2,1)S(1)}, u32[]{:S(2)}, u32[]{:S(2)}) collective-permute-start(bf16[16,256,256]{2,1,0:T(8,128)(2,1)} %bitcast.19), channel_id=1, source_target_pairs={{0,1},{1,0},{2,3},{3,2},{4,5},{5,4},{6,7},{7,6},{8,9},{9,8},{10,11... | collective-permute-start | bytes 6291464 | tf_op jit(solution)/shard_map/ppermute | solution.py:233
  39.1 3.1 %collective-permute-start.4 = (bf16[8,256,256]{2,1,0:T(8,128)(2,1)S(1)}, bf16[8,256,256]{2,1,0:T(8,128)(2,1)}, u32[]{:S(2)}, u32[]{:S(2)}) collective-permute-start(bf16[8,256,256]{2,1,0:T(8,128)(2,1)S(1)} %constant_dynamic-update-slice_fusion.own), channel_id=1, source_target_pairs={{0,1},{1,0},{2,3},{3,2},{4,5},{5,4},{6,7},{7,6},{8,9},{9,8},{10,11... | collective-permute-start | bytes 3145736 | tf_op jit(solution)/shard_map/ppermute | solution.py:231
  45.4 3.4 %shard_map.69 = (bf16[256,256]{1,0:T(8,128)(2,1)}, bf16[264,256]{1,0:T(8,128)(2,1)S(1)}) custom-call(s32[4]{0:T(128)S(1)} %pad_add_fusion.meta.refs_0_, s32[16]{0:T(128)S(1)} %bitcast.24, bf16[8,256,256]{2,1,0:T(8,128)(2,1)S(1)} %constant_dynamic-update-slice_fusion.own, bf16[8,256,256]{2,1,0:T(8,128)(2,1)} %collective-permute-done.4.across, ...), custom_call_target="tpu_custom_call" | custom-call | flops 1073741824 | bytes 8388608 | tf_op jit(solution)/shard_map/pallas_call | solution.py:235
  48.8 6.7 %collective-permute-start.16 = (bf16[264,256]{1,0:T(8,128)(2,1)S(1)}, bf16[264,256]{1,0:T(8,128)(2,1)S(1)}, u32[]{:S(2)}, u32[]{:S(2)}) collective-permute-start(bf16[264,256]{1,0:T(8,128)(2,1)S(1)} %get-tuple-element.15.message.refs_0_), channel_id=1, source_target_pairs={{0,2},{2,0},{1,3},{3,1},{4,6},{6,4},{5,7},{7,5},{8,10},{10,8},{9,1... | collective-permute-start | bytes 405512 | tf_op jit(solution)/shard_map/ppermute | solution.py:242
  57.7 4.9 %collective-permute-done.16 = bf16[264,256]{1,0:T(8,128)(2,1)S(1)} collective-permute-done((bf16[264,256]{1,0:T(8,128)(2,1)S(1)}, bf16[264,256]{1,0:T(8,128)(2,1)S(1)}, u32[]{:S(2)}, u32[]{:S(2)}) %collective-permute-start.16) | collective-permute-done | bytes 135200 | tf_op jit(solution)/shard_map/ppermute | solution.py:242
  62.6 3.6 %collective-permute-start.17 = (bf16[528,256]{1,0:T(8,128)(2,1)S(1)}, bf16[528,256]{1,0:T(8,128)(2,1)S(1)}, u32[]{:S(2)}, u32[]{:S(2)}) collective-permute-start(bf16[528,256]{1,0:T(8,128)(2,1)S(1)} %get-tuple-element.30), channel_id=1, source_target_pairs={{0,12},{4,0},{8,4},{12,8},{1,13},{5,1},{9,5},{13,9},{2,14},{6,2},{... | collective-permute-start | bytes 811016 | tf_op jit(solution)/shard_map/ppermute | solution.py:182
  67.6 2.5 %collective-permute-start.18 = (bf16[528,256]{1,0:T(8,128)(2,1)S(1)}, bf16[528,256]{1,0:T(8,128)(2,1)S(1)}, u32[]{:S(2)}, u32[]{:S(2)}) collective-permute-start(bf16[528,256]{1,0:T(8,128)(2,1)S(1)} %get-tuple-element.30), channel_id=1, source_target_pairs={{0,8},{4,12},{8,0},{12,4},{1,9},{5,13},{9,1},{13,5},{2,10},{6,14},... | collective-permute-start | bytes 811016 | tf_op jit(solution)/shard_map/ppermute | solution.py:182
  71.4 4.3 %collective-permute-start.7 = (bf16[520,256]{1,0:T(8,128)(2,1)S(1)}, bf16[520,256]{1,0:T(8,128)(2,1)S(1)}, u32[]{:S(2)}, u32[]{:S(2)}) collective-permute-start(bf16[520,256]{1,0:T(8,128)(2,1)S(1)} %get-tuple-element.17), channel_id=1, source_target_pairs={{0,8},{4,12},{8,0},{12,4},{1,9},{5,13},{9,1},{13,5},{2,10},{6,14},... | collective-permute-start | bytes 798728 | tf_op jit(solution)/shard_map/ppermute | solution.py:182
  77.6 4.6 %collective-permute-start.9 = (bf16[520,256]{1,0:T(8,128)(2,1)S(1)}, bf16[520,256]{1,0:T(8,128)(2,1)S(1)}, u32[]{:S(2)}, u32[]{:S(2)}) collective-permute-start(bf16[520,256]{1,0:T(8,128)(2,1)S(1)} %get-tuple-element.19), channel_id=1, source_target_pairs={{0,12},{4,0},{8,4},{12,8},{1,13},{5,1},{9,5},{13,9},{2,14},{6,2},{... | collective-permute-start | bytes 798728 | tf_op jit(solution)/shard_map/ppermute | solution.py:182
  84.2 6.6 %collective-permute-done.8.c = bf16[520,256]{1,0:T(8,128)(2,1)S(1)} collective-permute-done((bf16[520,256]{1,0:T(8,128)(2,1)S(1)}, bf16[520,256]{1,0:T(8,128)(2,1)S(1)}, u32[]{:S(2)}, u32[]{:S(2)}) %collective-permute-start.8) | collective-permute-done | bytes 266272 | tf_op jit(solution)/shard_map/ppermute | solution.py:182
  90.9 3.7 %collective-permute-start.10 = (bf16[520,256]{1,0:T(8,128)(2,1)S(1)}, bf16[520,256]{1,0:T(8,128)(2,1)S(1)}, u32[]{:S(2)}, u32[]{:S(2)}) collective-permute-start(bf16[520,256]{1,0:T(8,128)(2,1)S(1)} %shard_map.72), channel_id=1, source_target_pairs={{0,16},{2,18},{16,32},{18,34},{32,48},{34,50},{48,66},{50,64},{64,... | collective-permute-start | bytes 798728 | tf_op jit(solution)/shard_map/ppermute | solution.py:255
  94.7 3.8 %collective-permute-start.11 = (bf16[520,256]{1,0:T(8,128)(2,1)S(1)}, bf16[520,256]{1,0:T(8,128)(2,1)S(1)}, u32[]{:S(2)}, u32[]{:S(2)}) collective-permute-start(bf16[520,256]{1,0:T(8,128)(2,1)S(1)} %shard_map.72), channel_id=1, source_target_pairs={{0,18},{2,16},{16,34},{18,32},{32,50},{34,48},{48,64},{50,66},{64,... | collective-permute-start | bytes 798728 | tf_op jit(solution)/shard_map/ppermute | solution.py:254
  98.6 2.8 %collective-permute-start.20 = (bf16[2112,256]{1,0:T(8,128)(2,1)S(1)}, bf16[2112,256]{1,0:T(8,128)(2,1)S(1)}, u32[]{:S(2)}, u32[]{:S(2)}) collective-permute-start(bf16[2112,256]{1,0:T(8,128)(2,1)S(1)} %get-tuple-element.22), channel_id=1, source_target_pairs={{0,1},{1,0},{2,3},{3,2},{4,5},{5,4},{6,7},{7,6},{8,9},{9,8},{10,11... | collective-permute-start | bytes 3244040 | tf_op jit(solution)/shard_map/ppermute | solution.py:259
  101.4 17.6 %collective-permute-done.11.refs_1_ = bf16[520,256]{1,0:T(8,128)(2,1)S(1)} collective-permute-done((bf16[520,256]{1,0:T(8,128)(2,1)S(1)}, bf16[520,256]{1,0:T(8,128)(2,1)S(1)}, u32[]{:S(2)}, u32[]{:S(2)}) %collective-permute-start.11) | collective-permute-done | bytes 266272 | tf_op jit(solution)/shard_map/ppermute | solution.py:254
  119.1 3.6 %collective-permute-start.12 = (bf16[512,256]{1,0:T(8,128)(2,1)S(1)}, bf16[512,256]{1,0:T(8,128)(2,1)S(1)}, u32[]{:S(2)}, u32[]{:S(2)}) collective-permute-start(bf16[512,256]{1,0:T(8,128)(2,1)S(1)} %shard_map.73), channel_id=1, source_target_pairs={{0,12},{4,0},{8,4},{12,8},{1,13},{5,1},{9,5},{13,9},{2,14},{6,2},{... | collective-permute-start | bytes 786440 | tf_op jit(solution)/shard_map/ppermute | solution.py:182
  122.7 2.8 %collective-permute-start.13 = (bf16[512,256]{1,0:T(8,128)(2,1)S(1)}, bf16[512,256]{1,0:T(8,128)(2,1)S(1)}, u32[]{:S(2)}, u32[]{:S(2)}) collective-permute-start(bf16[512,256]{1,0:T(8,128)(2,1)S(1)} %shard_map.73), channel_id=1, source_target_pairs={{0,8},{4,12},{8,0},{12,4},{1,9},{5,13},{9,1},{13,5},{2,10},{6,14},... | collective-permute-start | bytes 786440 | tf_op jit(solution)/shard_map/ppermute | solution.py:182
  128.4 4.9 %collective-permute-done.13 = bf16[512,256]{1,0:T(8,128)(2,1)S(1)} collective-permute-done((bf16[512,256]{1,0:T(8,128)(2,1)S(1)}, bf16[512,256]{1,0:T(8,128)(2,1)S(1)}, u32[]{:S(2)}, u32[]{:S(2)}) %collective-permute-start.13) | collective-permute-done | bytes 262176 | tf_op jit(solution)/shard_map/ppermute | solution.py:182
  133.3 6.7 %collective-permute-done.14 = bf16[512,256]{1,0:T(8,128)(2,1)S(1)} collective-permute-done((bf16[512,256]{1,0:T(8,128)(2,1)S(1)}, bf16[512,256]{1,0:T(8,128)(2,1)S(1)}, u32[]{:S(2)}, u32[]{:S(2)}) %collective-permute-start.14) | collective-permute-done | bytes 262176 | tf_op jit(solution)/shard_map/ppermute | solution.py:182
  (50 shorter events, 28.2 us)
Async XLA Ops:
  2.3 10.2 %collective-permute-start.3 = (bf16[256,256]{1,0:T(8,128)(2,1)S(1)}, bf16[256,256]{1,0:T(8,128)(2,1)S(1)}, u32[]{:S(2)}, u32[]{:S(2)}) collective-permute-start(bf16[256,256]{1,0:T(8,128)(2,1)S(1)} %and_select_fusion), channel_id=1, source_target_pairs={{0,2},{2,0},{1,3},{3,1},{4,6},{6,4},{5,7},{7,5},{8,10},{10,8},{9,1... | collective-permute-start | bytes 393224 | tf_op jit(solution)/shard_map/ppermute | solution.py:226
  13.3 23.6 %all-to-all-start = ((bf16[4,256,256]{2,1,0:T(8,128)(2,1)}), bf16[4,256,256]{2,1,0:T(8,128)(2,1)}, u32[]{:S(2)}, u32[]{:S(2)}) async-start(bf16[4,256,256]{2,1,0:T(8,128)(2,1)} %broadcast_in_dim.20), calls=%async_computation | async-start | bytes 1048576 | tf_op jit(solution)/shard_map/all_to_all | solution.py:192
  17.5 18.6 %collective-permute-start.2 = (bf16[256,256]{1,0:T(8,128)(2,1)S(1)}, bf16[256,256]{1,0:T(8,128)(2,1)S(1)}, u32[]{:S(2)}, u32[]{:S(2)}) collective-permute-start(bf16[256,256]{1,0:T(8,128)(2,1)S(1)} %and_select_fusion), channel_id=1, source_target_pairs={{0,4},{4,8},{8,12},{12,0},{1,5},{5,9},{9,13},{13,1},{2,6},{6,10},{... | collective-permute-start | bytes 393224 | tf_op jit(solution)/shard_map/ppermute | solution.py:182
  20.8 15.3 %collective-permute-start = (bf16[256,256]{1,0:T(8,128)(2,1)S(1)}, bf16[256,256]{1,0:T(8,128)(2,1)S(1)}, u32[]{:S(2)}, u32[]{:S(2)}) collective-permute-start(bf16[256,256]{1,0:T(8,128)(2,1)S(1)} %and_select_fusion), channel_id=1, source_target_pairs={{0,12},{4,0},{8,4},{12,8},{1,13},{5,1},{9,5},{13,9},{2,14},{6,2},{... | collective-permute-start | bytes 393224 | tf_op jit(solution)/shard_map/ppermute | solution.py:182
  24.0 12.1 %collective-permute-start.1 = (bf16[256,256]{1,0:T(8,128)(2,1)S(1)}, bf16[256,256]{1,0:T(8,128)(2,1)S(1)}, u32[]{:S(2)}, u32[]{:S(2)}) collective-permute-start(bf16[256,256]{1,0:T(8,128)(2,1)S(1)} %and_select_fusion), channel_id=1, source_target_pairs={{0,8},{4,12},{8,0},{12,4},{1,9},{5,13},{9,1},{13,5},{2,10},{6,14},... | collective-permute-start | bytes 393224 | tf_op jit(solution)/shard_map/ppermute | solution.py:182
  27.6 42.5 %collective-permute-start.6 = (bf16[16,256,256]{2,1,0:T(8,128)(2,1)}, bf16[16,256,256]{2,1,0:T(8,128)(2,1)S(1)}, u32[]{:S(2)}, u32[]{:S(2)}) collective-permute-start(bf16[16,256,256]{2,1,0:T(8,128)(2,1)} %bitcast.19), channel_id=1, source_target_pairs={{0,1},{1,0},{2,3},{3,2},{4,5},{5,4},{6,7},{7,6},{8,9},{9,8},{10,11... | collective-permute-start | bytes 6291464 | tf_op jit(solution)/shard_map/ppermute | solution.py:233
  39.1 5.5 %collective-permute-start.4 = (bf16[8,256,256]{2,1,0:T(8,128)(2,1)S(1)}, bf16[8,256,256]{2,1,0:T(8,128)(2,1)}, u32[]{:S(2)}, u32[]{:S(2)}) collective-permute-start(bf16[8,256,256]{2,1,0:T(8,128)(2,1)S(1)} %constant_dynamic-update-slice_fusion.own), channel_id=1, source_target_pairs={{0,1},{1,0},{2,3},{3,2},{4,5},{5,4},{6,7},{7,6},{8,9},{9,8},{10,11... | collective-permute-start | bytes 3145736 | tf_op jit(solution)/shard_map/ppermute | solution.py:231
  42.2 1.6 %copy-start.1 = (bf16[1,1,16,256,256]{4,3,2,1,0:T(8,128)(2,1)S(1)}, bf16[1,1,16,256,256]{4,3,2,1,0:T(8,128)(2,1)}, u32[]{:S(2)}) copy-start(bf16[1,1,16,256,256]{4,3,2,1,0:T(8,128)(2,1)} %param.7) | copy-start | bytes 6291460
  43.8 1.6 %copy-start.2 = (s32[1,1,16]{2,1,0:T(1,128)S(1)}, s32[1,1,16]{2,1,0:T(1,128)}, u32[]{:S(2)}) copy-start(s32[1,1,16]{2,1,0:T(1,128)} %param.8) | copy-start | bytes 196
  48.8 13.8 %collective-permute-start.16 = (bf16[264,256]{1,0:T(8,128)(2,1)S(1)}, bf16[264,256]{1,0:T(8,128)(2,1)S(1)}, u32[]{:S(2)}, u32[]{:S(2)}) collective-permute-start(bf16[264,256]{1,0:T(8,128)(2,1)S(1)} %get-tuple-element.15.message.refs_0_), channel_id=1, source_target_pairs={{0,2},{2,0},{1,3},{3,1},{4,6},{6,4},{5,7},{7,5},{8,10},{10,8},{9,1... | collective-permute-start | bytes 405512 | tf_op jit(solution)/shard_map/ppermute | solution.py:242
  55.5 14.6 %collective-permute-start.5 = (bf16[264,256]{1,0:T(8,128)(2,1)S(1)}, bf16[264,256]{1,0:T(8,128)(2,1)S(1)}, u32[]{:S(2)}, u32[]{:S(2)}) collective-permute-start(bf16[264,256]{1,0:T(8,128)(2,1)S(1)} %get-tuple-element.15.message.refs_0_), channel_id=1, source_target_pairs={{0,1},{1,0},{2,3},{3,2},{4,5},{5,4},{6,7},{7,6},{8,9},{9,8},{10,11... | collective-permute-start | bytes 405512 | tf_op jit(solution)/shard_map/ppermute | solution.py:241
  62.6 19.5 %collective-permute-start.17 = (bf16[528,256]{1,0:T(8,128)(2,1)S(1)}, bf16[528,256]{1,0:T(8,128)(2,1)S(1)}, u32[]{:S(2)}, u32[]{:S(2)}) collective-permute-start(bf16[528,256]{1,0:T(8,128)(2,1)S(1)} %get-tuple-element.30), channel_id=1, source_target_pairs={{0,12},{4,0},{8,4},{12,8},{1,13},{5,1},{9,5},{13,9},{2,14},{6,2},{... | collective-permute-start | bytes 811016 | tf_op jit(solution)/shard_map/ppermute | solution.py:182
  67.6 30.9 %collective-permute-start.18 = (bf16[528,256]{1,0:T(8,128)(2,1)S(1)}, bf16[528,256]{1,0:T(8,128)(2,1)S(1)}, u32[]{:S(2)}, u32[]{:S(2)}) collective-permute-start(bf16[528,256]{1,0:T(8,128)(2,1)S(1)} %get-tuple-element.30), channel_id=1, source_target_pairs={{0,8},{4,12},{8,0},{12,4},{1,9},{5,13},{9,1},{13,5},{2,10},{6,14},... | collective-permute-start | bytes 811016 | tf_op jit(solution)/shard_map/ppermute | solution.py:182
  71.4 12.8 %collective-permute-start.7 = (bf16[520,256]{1,0:T(8,128)(2,1)S(1)}, bf16[520,256]{1,0:T(8,128)(2,1)S(1)}, u32[]{:S(2)}, u32[]{:S(2)}) collective-permute-start(bf16[520,256]{1,0:T(8,128)(2,1)S(1)} %get-tuple-element.17), channel_id=1, source_target_pairs={{0,8},{4,12},{8,0},{12,4},{1,9},{5,13},{9,1},{13,5},{2,10},{6,14},... | collective-permute-start | bytes 798728 | tf_op jit(solution)/shard_map/ppermute | solution.py:182
  75.7 15.1 %collective-permute-start.8 = (bf16[520,256]{1,0:T(8,128)(2,1)S(1)}, bf16[520,256]{1,0:T(8,128)(2,1)S(1)}, u32[]{:S(2)}, u32[]{:S(2)}) collective-permute-start(bf16[520,256]{1,0:T(8,128)(2,1)S(1)} %get-tuple-element.18), channel_id=1, source_target_pairs={{0,4},{4,8},{8,12},{12,0},{1,5},{5,9},{9,13},{13,1},{2,6},{6,10},{... | collective-permute-start | bytes 798728 | tf_op jit(solution)/shard_map/ppermute | solution.py:182
  77.6 13.2 %collective-permute-start.9 = (bf16[520,256]{1,0:T(8,128)(2,1)S(1)}, bf16[520,256]{1,0:T(8,128)(2,1)S(1)}, u32[]{:S(2)}, u32[]{:S(2)}) collective-permute-start(bf16[520,256]{1,0:T(8,128)(2,1)S(1)} %get-tuple-element.19), channel_id=1, source_target_pairs={{0,12},{4,0},{8,4},{12,8},{1,13},{5,1},{9,5},{13,9},{2,14},{6,2},{... | collective-permute-start | bytes 798728 | tf_op jit(solution)/shard_map/ppermute | solution.py:182
  82.2 16.4 %collective-permute-start.19 = (bf16[528,256]{1,0:T(8,128)(2,1)S(1)}, bf16[528,256]{1,0:T(8,128)(2,1)S(1)}, u32[]{:S(2)}, u32[]{:S(2)}) collective-permute-start(bf16[528,256]{1,0:T(8,128)(2,1)S(1)} %get-tuple-element.30), channel_id=1, source_target_pairs={{0,4},{4,8},{8,12},{12,0},{1,5},{5,9},{9,13},{13,1},{2,6},{6,10},{... | collective-permute-start | bytes 811016 | tf_op jit(solution)/shard_map/ppermute | solution.py:182
  90.9 10.4 %collective-permute-start.10 = (bf16[520,256]{1,0:T(8,128)(2,1)S(1)}, bf16[520,256]{1,0:T(8,128)(2,1)S(1)}, u32[]{:S(2)}, u32[]{:S(2)}) collective-permute-start(bf16[520,256]{1,0:T(8,128)(2,1)S(1)} %shard_map.72), channel_id=1, source_target_pairs={{0,16},{2,18},{16,32},{18,34},{32,48},{34,50},{48,66},{50,64},{64,... | collective-permute-start | bytes 798728 | tf_op jit(solution)/shard_map/ppermute | solution.py:255
  94.7 24.4 %collective-permute-start.11 = (bf16[520,256]{1,0:T(8,128)(2,1)S(1)}, bf16[520,256]{1,0:T(8,128)(2,1)S(1)}, u32[]{:S(2)}, u32[]{:S(2)}) collective-permute-start(bf16[520,256]{1,0:T(8,128)(2,1)S(1)} %shard_map.72), channel_id=1, source_target_pairs={{0,18},{2,16},{16,34},{18,32},{32,50},{34,48},{48,64},{50,66},{64,... | collective-permute-start | bytes 798728 | tf_op jit(solution)/shard_map/ppermute | solution.py:254
  98.6 43.9 %collective-permute-start.20 = (bf16[2112,256]{1,0:T(8,128)(2,1)S(1)}, bf16[2112,256]{1,0:T(8,128)(2,1)S(1)}, u32[]{:S(2)}, u32[]{:S(2)}) collective-permute-start(bf16[2112,256]{1,0:T(8,128)(2,1)S(1)} %get-tuple-element.22), channel_id=1, source_target_pairs={{0,1},{1,0},{2,3},{3,2},{4,5},{5,4},{6,7},{7,6},{8,9},{9,8},{10,11... | collective-permute-start | bytes 3244040 | tf_op jit(solution)/shard_map/ppermute | solution.py:259
  119.1 9.3 %collective-permute-start.12 = (bf16[512,256]{1,0:T(8,128)(2,1)S(1)}, bf16[512,256]{1,0:T(8,128)(2,1)S(1)}, u32[]{:S(2)}, u32[]{:S(2)}) collective-permute-start(bf16[512,256]{1,0:T(8,128)(2,1)S(1)} %shard_map.73), channel_id=1, source_target_pairs={{0,12},{4,0},{8,4},{12,8},{1,13},{5,1},{9,5},{13,9},{2,14},{6,2},{... | collective-permute-start | bytes 786440 | tf_op jit(solution)/shard_map/ppermute | solution.py:182
  122.7 10.5 %collective-permute-start.13 = (bf16[512,256]{1,0:T(8,128)(2,1)S(1)}, bf16[512,256]{1,0:T(8,128)(2,1)S(1)}, u32[]{:S(2)}, u32[]{:S(2)}) collective-permute-start(bf16[512,256]{1,0:T(8,128)(2,1)S(1)} %shard_map.73), channel_id=1, source_target_pairs={{0,8},{4,12},{8,0},{12,4},{1,9},{5,13},{9,1},{13,5},{2,10},{6,14},... | collective-permute-start | bytes 786440 | tf_op jit(solution)/shard_map/ppermute | solution.py:182
  125.5 14.5 %collective-permute-start.14 = (bf16[512,256]{1,0:T(8,128)(2,1)S(1)}, bf16[512,256]{1,0:T(8,128)(2,1)S(1)}, u32[]{:S(2)}, u32[]{:S(2)}) collective-permute-start(bf16[512,256]{1,0:T(8,128)(2,1)S(1)} %shard_map.73), channel_id=1, source_target_pairs={{0,4},{4,8},{8,12},{12,0},{1,5},{5,9},{9,13},{13,1},{2,6},{6,10},{... | collective-permute-start | bytes 786440 | tf_op jit(solution)/shard_map/ppermute | solution.py:182
  140.0 5.5 %collective-permute-start.15 = (bf16[2048,256]{1,0:T(8,128)(2,1)S(1)}, bf16[2048,256]{1,0:T(8,128)(2,1)S(1)}, u32[]{:S(2)}, u32[]{:S(2)}) collective-permute-start(bf16[2048,256]{1,0:T(8,128)(2,1)S(1)} %pad_maximum_fusion.refs_1_), channel_id=1, source_target_pairs={{0,1},{1,0},{2,3},{3,2},{4,5},{5,4},{6,7},{7,6},{8,9},{9,8},{10,11... | collective-permute-start | bytes 3145736 | tf_op jit(solution)/shard_map/ppermute | solution.py:274
  (1 other events, 1.6 us)

commit v9 on v4

--- a/solution.py
+++ b/solution.py
@@ -11,7 +11,7 @@
 
 BF = jnp.bfloat16
 F32 = jnp.float32
-TILE = 16
+TILE = 8
 YROW = ("z", "yl", "yh")
 SWAP = [(0, 1), (1, 0)]
 VMEM = pl.BlockSpec(memory_space=pltpu.VMEM)
@@ -59,14 +59,23 @@
     return side * 8 + lax.rem(meta[3] + j // 2, 4) * 2 + j % 2
 
 
-def first_kernel(meta, picks, pool, left, right, message, inner):
+def load_kernel(source, out):
+    out[...] = source[...]
+
+
+def first_kernel(meta, picks, own, across, left, right, first_out, message, pool, inner):
     channels, width = left.shape[0], left.shape[1]
+    half = channels // 2
+    pool[0:half] = own[...]
+    pool[half:channels] = across[...]
     for t in range(channels):
         c, yh, step = place(picks[t], meta)
-        inner[:, t * width:(t + 1) * width] = dot(left[t], pool[(c * 2 + yh) * 4 + step]).astype(BF)
+        at = (c * 2 + yh) * 4 + step * (1 - yh) + (picks[t] // 4) * yh
+        inner[:, t * width:(t + 1) * width] = dot(left[t], pool[at]).astype(BF)
     product = dot(inner[...], right[...].reshape(channels * width, width))
     size = meta[0]
     product = jnp.where(live(size, product.shape), product, 0.0).astype(BF)
+    first_out[...] = product
     message[0:width, :] = product
     value = product.astype(F32)
     columns = jnp.sum(value * value, axis=0, keepdims=True)
@@ -92,13 +101,13 @@
 
 def core_sum_kernel(meta, message, keep, left, *refs):
     own, lv, outs = refs[0], refs[-1], refs[1:-1]
-    half, width = left.shape[0], left.shape[1]
+    half, width = left.shape[0] // 2, left.shape[1]
     q0, c0 = unpack(own[width:width + TILE, :])
     q1, c1 = unpack(message[width:width + TILE, :])
     tile = pack(q0 + q1, c0 + c1)
     for out in outs:
         out[2 * width:2 * width + TILE, :] = tile
-    for j, term in enumerate(terms(message, lambda j: left[channel(meta, 0, j)], lv, half)):
+    for j, term in enumerate(terms(message, lambda j: left[channel(meta, meta[1], j)], lv, half)):
         outs[j // 2][(j % 2) * width:(j % 2 + 1) * width, :] = (keep[j] + term()).astype(BF)
 
 
@@ -194,6 +203,11 @@
     return [value, along_x(value, 3), far, along_x(value, 1)]
 
 
+def to_everyone_on_x(value):
+    count = lax.axis_size("x")
+    return lax.all_to_all(jnp.broadcast_to(value[None], (count, *value.shape)), "x", 0, 0, tiled=True)
+
+
 def routes(z_count, y_count):
     def at(z, yl, yh):
         return (z * y_count + yl) * 2 + yh
@@ -223,23 +237,22 @@
     span = width + TILE
     unit = 2 * channels * width**3
     block_bytes = width * width * 2
-    meta = jnp.stack([size, *(lax.axis_index(axis).astype(jnp.int32) for axis in ("c", "yh", "x"))])
 
     masked = jnp.where(live(size, (width, width)), wave[0, 0], jnp.zeros((), BF))
     masked_other = lax.ppermute(masked, "yh", SWAP)
     own = jnp.stack(round_x(masked))
-    left_send = lax.dynamic_slice_in_dim(left, (1 - lax.axis_index("c")) * half, half)
-    left_other = lax.ppermute(left_send, "c", SWAP)
+    meta = jnp.stack([size, *(lax.axis_index(axis).astype(jnp.int32) for axis in ("c", "yh", "x"))])
+    own_other = to_everyone_on_x(masked_other)
+    own = jnp.concatenate(lax.optimization_barrier((own, own_other)))
     across = lax.ppermute(own, "c", SWAP)
-    own_other = jnp.stack(round_x(masked_other))
-    across_other = lax.ppermute(own_other, "c", SWAP)
-    pool = jnp.concatenate([own, own_other, across, across_other], axis=0)
+    right_here = call(load_kernel, one(right.shape, BF), [VMEM], [], 1 << 20, 2 * channels * block_bytes)(right)
+    left_other = lax.ppermute(left, "c", SWAP)
     stack = pltpu.VMEM((half, width, width), BF)
-    message = call(
-        first_kernel, one((span, width), BF), [SMEM, SMEM, VMEM, VMEM, VMEM],
-        [pltpu.VMEM((width, channels * width), BF)], 2 * unit, 4 * channels * block_bytes,
-    )(meta, picks, pool, left, right)
-    first = message[0:width]
+    first, message = call(
+        first_kernel, [((width, width), BF), ((span, width), BF)], [SMEM, SMEM] + [VMEM] * 4,
+        [pltpu.VMEM((channels, width, width), BF), pltpu.VMEM((width, channels * width), BF)],
+        2 * unit, 4 * channels * block_bytes,
+    )(meta, picks, own, across, left, right_here)
 
     message_core = lax.ppermute(message, "c", SWAP)
     message_other = lax.ppermute(message, "yh", SWAP)
@@ -267,7 +280,7 @@
         [SMEM, SMEM, VMEM, VMEM, VMEM],
         [pltpu.VMEM((channels, width, width), BF)],
         2 * unit, 4 * channels * block_bytes,
-    )(meta, picks, pool_two, left, right)
+    )(meta, picks, pool_two, left, right_here)
     g_other = lax.ppermute(g_send, "c", SWAP)
 
     factor = 1.0 / (width * math.sqrt(channels_of(sector_size)))

time: 166 us -> 175 us (1.054)
  the two profiles are of different devices: /device:TPU:201 before, /device:TPU:217 now
where the time goes in v9:
time: 175 us; the launch traced here: 174 us
  starting transfers between devices  80.7 us (46%)
  waiting for transfers between devices  74.4 us (43%)
  Pallas kernels  10.5 us (6%)
  local copies, waits for them, and re-layouts  3.24 us (2%)
  other arithmetic  3.04 us (2%)
    ppermute x12, waiting for transfers between devices, along_x(): lax.ppermute(value, 'x', [(i, (i + step) % count) for i in range(count)])  36.3 us
    ppermute x12, starting transfers between devices, along_x(): lax.ppermute(value, 'x', [(i, (i + step) % count) for i in range(count)])  34.9 us
    ppermute x1, waiting for transfers between devices, body(): from_far = lax.ppermute(row, YROW, far)  20.7 us
    ppermute x1, starting transfers between devices, body(): from_near = lax.ppermute(row, YROW, near)  10.5 us
    ppermute x1, starting transfers between devices, body(): across = lax.ppermute(own, 'c', SWAP)  7.09 us
    ppermute x1, waiting for transfers between devices, body(): message_other = lax.ppermute(message, 'yh', SWAP)  5.83 us
    ppermute x1, waiting for transfers between devices, body(): masked_other = lax.ppermute(masked, 'yh', SWAP)  5.42 us
    ppermute x1, starting transfers between devices, body(): masked_other = lax.ppermute(masked, 'yh', SWAP)  4.76 us
  transfers between devices with their start and end apart: 23, of which 14 were waited for; matrix products, arithmetic and copies ran while one was open for 1% of the time, Pallas kernels for 3%

profile of v9, /device:TPU:217, one launch (start us, length us, event | category | flops | bytes accessed | tf_op | source)
XLA Modules:
  0.0 173.6 jit_solution(11036337505002011706)
XLA Ops:
  2.3 4.8 %collective-permute-start.3 = (bf16[256,256]{1,0:T(8,128)(2,1)S(1)}, bf16[256,256]{1,0:T(8,128)(2,1)S(1)}, u32[]{:S(2)}, u32[]{:S(2)}) collective-permute-start(bf16[256,256]{1,0:T(8,128)(2,1)S(1)} %and_select_fusion), channel_id=1, source_target_pairs={{0,2},{2,0},{1,3},{3,1},{4,6},{6,4},{5,7},{7,5},{8,10},{10,8},{9,1... | collective-permute-start | bytes 393224 | tf_op jit(solution)/shard_map/ppermute | solution.py:242
  7.1 5.4 %collective-permute-done.3 = bf16[256,256]{1,0:T(8,128)(2,1)S(1)} collective-permute-done((bf16[256,256]{1,0:T(8,128)(2,1)S(1)}, bf16[256,256]{1,0:T(8,128)(2,1)S(1)}, u32[]{:S(2)}, u32[]{:S(2)}) %collective-permute-start.3) | collective-permute-done | bytes 131104 | tf_op jit(solution)/shard_map/ppermute | solution.py:242
  13.3 4.3 %all-to-all-start = ((bf16[4,256,256]{2,1,0:T(8,128)(2,1)}), bf16[4,256,256]{2,1,0:T(8,128)(2,1)}, u32[]{:S(2)}, u32[]{:S(2)}) async-start(bf16[4,256,256]{2,1,0:T(8,128)(2,1)} %broadcast_in_dim.20), calls=%async_computation | async-start | bytes 1048576 | tf_op jit(solution)/shard_map/all_to_all | solution.py:208
  17.6 3.3 %collective-permute-start.2 = (bf16[256,256]{1,0:T(8,128)(2,1)S(1)}, bf16[256,256]{1,0:T(8,128)(2,1)S(1)}, u32[]{:S(2)}, u32[]{:S(2)}) collective-permute-start(bf16[256,256]{1,0:T(8,128)(2,1)S(1)} %and_select_fusion), channel_id=1, source_target_pairs={{0,4},{4,8},{8,12},{12,0},{1,5},{5,9},{9,13},{13,1},{2,6},{6,10},{... | collective-permute-start | bytes 393224 | tf_op jit(solution)/shard_map/ppermute | solution.py:198
  20.9 3.2 %collective-permute-start = (bf16[256,256]{1,0:T(8,128)(2,1)S(1)}, bf16[256,256]{1,0:T(8,128)(2,1)S(1)}, u32[]{:S(2)}, u32[]{:S(2)}) collective-permute-start(bf16[256,256]{1,0:T(8,128)(2,1)S(1)} %and_select_fusion), channel_id=1, source_target_pairs={{0,12},{4,0},{8,4},{12,8},{1,13},{5,1},{9,5},{13,9},{2,14},{6,2},{... | collective-permute-start | bytes 393224 | tf_op jit(solution)/shard_map/ppermute | solution.py:198
  24.1 3.6 %collective-permute-start.1 = (bf16[256,256]{1,0:T(8,128)(2,1)S(1)}, bf16[256,256]{1,0:T(8,128)(2,1)S(1)}, u32[]{:S(2)}, u32[]{:S(2)}) collective-permute-start(bf16[256,256]{1,0:T(8,128)(2,1)S(1)} %and_select_fusion), channel_id=1, source_target_pairs={{0,8},{4,12},{8,0},{12,4},{1,9},{5,13},{9,1},{13,5},{2,10},{6,14},... | collective-permute-start | bytes 393224 | tf_op jit(solution)/shard_map/ppermute | solution.py:198
  28.8 3.3 %collective-permute-done.1 = bf16[256,256]{1,0:T(8,128)(2,1)S(1)} collective-permute-done((bf16[256,256]{1,0:T(8,128)(2,1)S(1)}, bf16[256,256]{1,0:T(8,128)(2,1)S(1)}, u32[]{:S(2)}, u32[]{:S(2)}) %collective-permute-start.1) | collective-permute-done | bytes 131104 | tf_op jit(solution)/shard_map/ppermute | solution.py:198
  35.1 7.1 %collective-permute-start.4 = (bf16[8,256,256]{2,1,0:T(8,128)(2,1)S(1)}, bf16[8,256,256]{2,1,0:T(8,128)(2,1)}, u32[]{:S(2)}, u32[]{:S(2)}) collective-permute-start(bf16[8,256,256]{2,1,0:T(8,128)(2,1)S(1)} %constant_dynamic-update-slice_fusion.own), channel_id=1, source_target_pairs={{0,1},{1,0},{2,3},{3,2},{4,5},{5,4},{6,7},{7,6},{8,9},{9,8},{10,11... | collective-permute-start | bytes 3145736 | tf_op jit(solution)/shard_map/ppermute | solution.py:247
  44.6 3.4 %shard_map.69 = (bf16[256,256]{1,0:T(8,128)(2,1)}, bf16[264,256]{1,0:T(8,128)(2,1)S(1)}) custom-call(s32[4]{0:T(128)S(1)} %pad_add_fusion.meta, s32[16]{0:T(128)S(1)} %bitcast.24, bf16[8,256,256]{2,1,0:T(8,128)(2,1)S(1)} %constant_dynamic-update-slice_fusion.own, bf16[8,256,256]{2,1,0:T(8,128)(2,1)} %collective-permute-done.4.across, ...), custom_call_target="tpu_custom_call" | custom-call | flops 1073741824 | bytes 8388608 | tf_op jit(solution)/shard_map/pallas_call | solution.py:251
  48.0 4.7 %collective-permute-start.15 = (bf16[264,256]{1,0:T(8,128)(2,1)S(1)}, bf16[264,256]{1,0:T(8,128)(2,1)S(1)}, u32[]{:S(2)}, u32[]{:S(2)}) collective-permute-start(bf16[264,256]{1,0:T(8,128)(2,1)S(1)} %get-tuple-element.16.message.refs_0_), channel_id=1, source_target_pairs={{0,2},{2,0},{1,3},{3,1},{4,6},{6,4},{5,7},{7,5},{8,10},{10,8},{9,1... | collective-permute-start | bytes 405512 | tf_op jit(solution)/shard_map/ppermute | solution.py:258
  52.7 5.8 %collective-permute-done.15 = bf16[264,256]{1,0:T(8,128)(2,1)S(1)} collective-permute-done((bf16[264,256]{1,0:T(8,128)(2,1)S(1)}, bf16[264,256]{1,0:T(8,128)(2,1)S(1)}, u32[]{:S(2)}, u32[]{:S(2)}) %collective-permute-start.15) | collective-permute-done | bytes 135200 | tf_op jit(solution)/shard_map/ppermute | solution.py:258
  58.6 3.6 %collective-permute-start.16 = (bf16[528,256]{1,0:T(8,128)(2,1)S(1)}, bf16[528,256]{1,0:T(8,128)(2,1)S(1)}, u32[]{:S(2)}, u32[]{:S(2)}) collective-permute-start(bf16[528,256]{1,0:T(8,128)(2,1)S(1)} %get-tuple-element.32), channel_id=1, source_target_pairs={{0,12},{4,0},{8,4},{12,8},{1,13},{5,1},{9,5},{13,9},{2,14},{6,2},{... | collective-permute-start | bytes 811016 | tf_op jit(solution)/shard_map/ppermute | solution.py:198
  62.2 3.5 %collective-permute-start.6 = (bf16[16,256,256]{2,1,0:T(8,128)(2,1)S(1)}, bf16[16,256,256]{2,1,0:T(8,128)(2,1)S(1)}, u32[]{:S(2)}, u32[]{:S(2)}) collective-permute-start(bf16[16,256,256]{2,1,0:T(8,128)(2,1)S(1)} %bitcast.20), channel_id=1, source_target_pairs={{0,1},{1,0},{2,3},{3,2},{4,5},{5,4},{6,7},{7,6},{8,9},{9,8},{10,11... | collective-permute-start | bytes 6291464 | tf_op jit(solution)/shard_map/ppermute | solution.py:249
  68.2 2.5 %collective-permute-start.18 = (bf16[528,256]{1,0:T(8,128)(2,1)S(1)}, bf16[528,256]{1,0:T(8,128)(2,1)S(1)}, u32[]{:S(2)}, u32[]{:S(2)}) collective-permute-start(bf16[528,256]{1,0:T(8,128)(2,1)S(1)} %get-tuple-element.32), channel_id=1, source_target_pairs={{0,4},{4,8},{8,12},{12,0},{1,5},{5,9},{9,13},{13,1},{2,6},{6,10},{... | collective-permute-start | bytes 811016 | tf_op jit(solution)/shard_map/ppermute | solution.py:198
  70.8 6.4 %collective-permute-done.17 = bf16[528,256]{1,0:T(8,128)(2,1)S(1)} collective-permute-done((bf16[528,256]{1,0:T(8,128)(2,1)S(1)}, bf16[528,256]{1,0:T(8,128)(2,1)S(1)}, u32[]{:S(2)}, u32[]{:S(2)}) %collective-permute-start.17) | collective-permute-done | bytes 270368 | tf_op jit(solution)/shard_map/ppermute | solution.py:198
  77.2 6.1 %collective-permute-done.18 = bf16[528,256]{1,0:T(8,128)(2,1)S(1)} collective-permute-done((bf16[528,256]{1,0:T(8,128)(2,1)S(1)}, bf16[528,256]{1,0:T(8,128)(2,1)S(1)}, u32[]{:S(2)}, u32[]{:S(2)}) %collective-permute-start.18) | collective-permute-done | bytes 270368 | tf_op jit(solution)/shard_map/ppermute | solution.py:198
  99.6 4.3 %collective-permute-start.9 = (bf16[520,256]{1,0:T(8,128)(2,1)S(1)}, bf16[520,256]{1,0:T(8,128)(2,1)S(1)}, u32[]{:S(2)}, u32[]{:S(2)}) collective-permute-start(bf16[520,256]{1,0:T(8,128)(2,1)S(1)} %get-tuple-element.20), channel_id=1, source_target_pairs={{0,12},{4,0},{8,4},{12,8},{1,13},{5,1},{9,5},{13,9},{2,14},{6,2},{... | collective-permute-start | bytes 798728 | tf_op jit(solution)/shard_map/ppermute | solution.py:198
  106.2 6.1 %collective-permute-done.8.c = bf16[520,256]{1,0:T(8,128)(2,1)S(1)} collective-permute-done((bf16[520,256]{1,0:T(8,128)(2,1)S(1)}, bf16[520,256]{1,0:T(8,128)(2,1)S(1)}, u32[]{:S(2)}, u32[]{:S(2)}) %collective-permute-start.8) | collective-permute-done | bytes 266272 | tf_op jit(solution)/shard_map/ppermute | solution.py:198
  112.4 10.5 %collective-permute-start.10 = (bf16[520,256]{1,0:T(8,128)(2,1)S(1)}, bf16[520,256]{1,0:T(8,128)(2,1)S(1)}, u32[]{:S(2)}, u32[]{:S(2)}) collective-permute-start(bf16[520,256]{1,0:T(8,128)(2,1)S(1)} %shard_map.72), channel_id=1, source_target_pairs={{0,16},{2,18},{16,32},{18,34},{32,48},{34,50},{48,66},{50,64},{64,... | collective-permute-start | bytes 798728 | tf_op jit(solution)/shard_map/ppermute | solution.py:271
  124.9 3.3 %collective-permute-done.10.refs_0_ = bf16[520,256]{1,0:T(8,128)(2,1)S(1)} collective-permute-done((bf16[520,256]{1,0:T(8,128)(2,1)S(1)}, bf16[520,256]{1,0:T(8,128)(2,1)S(1)}, u32[]{:S(2)}, u32[]{:S(2)}) %collective-permute-start.10) | collective-permute-done | bytes 266272 | tf_op jit(solution)/shard_map/ppermute | solution.py:271
  128.2 20.7 %collective-permute-done.11.refs_1_ = bf16[520,256]{1,0:T(8,128)(2,1)S(1)} collective-permute-done((bf16[520,256]{1,0:T(8,128)(2,1)S(1)}, bf16[520,256]{1,0:T(8,128)(2,1)S(1)}, u32[]{:S(2)}, u32[]{:S(2)}) %collective-permute-start.11) | collective-permute-done | bytes 266272 | tf_op jit(solution)/shard_map/ppermute | solution.py:270
  153.4 2.8 %collective-permute-start.14 = (bf16[512,256]{1,0:T(8,128)(2,1)S(1)}, bf16[512,256]{1,0:T(8,128)(2,1)S(1)}, u32[]{:S(2)}, u32[]{:S(2)}) collective-permute-start(bf16[512,256]{1,0:T(8,128)(2,1)S(1)} %shard_map.73), channel_id=1, source_target_pairs={{0,4},{4,8},{8,12},{12,0},{1,5},{5,9},{9,13},{13,1},{2,6},{6,10},{... | collective-permute-start | bytes 786440 | tf_op jit(solution)/shard_map/ppermute | solution.py:198
  158.3 3.3 %collective-permute-done.13 = bf16[512,256]{1,0:T(8,128)(2,1)S(1)} collective-permute-done((bf16[512,256]{1,0:T(8,128)(2,1)S(1)}, bf16[512,256]{1,0:T(8,128)(2,1)S(1)}, u32[]{:S(2)}, u32[]{:S(2)}) %collective-permute-start.13) | collective-permute-done | bytes 262176 | tf_op jit(solution)/shard_map/ppermute | solution.py:198
  161.5 6.7 %collective-permute-done.14 = bf16[512,256]{1,0:T(8,128)(2,1)S(1)} collective-permute-done((bf16[512,256]{1,0:T(8,128)(2,1)S(1)}, bf16[512,256]{1,0:T(8,128)(2,1)S(1)}, u32[]{:S(2)}, u32[]{:S(2)}) %collective-permute-start.14) | collective-permute-done | bytes 262176 | tf_op jit(solution)/shard_map/ppermute | solution.py:198
  (53 shorter events, 43.2 us)
Async XLA Ops:
  2.3 10.2 %collective-permute-start.3 = (bf16[256,256]{1,0:T(8,128)(2,1)S(1)}, bf16[256,256]{1,0:T(8,128)(2,1)S(1)}, u32[]{:S(2)}, u32[]{:S(2)}) collective-permute-start(bf16[256,256]{1,0:T(8,128)(2,1)S(1)} %and_select_fusion), channel_id=1, source_target_pairs={{0,2},{2,0},{1,3},{3,1},{4,6},{6,4},{5,7},{7,5},{8,10},{10,8},{9,1... | collective-permute-start | bytes 393224 | tf_op jit(solution)/shard_map/ppermute | solution.py:242
  13.3 28.9 %copy-start.1 = (bf16[1,1,16,256,256]{4,3,2,1,0:T(8,128)(2,1)S(1)}, bf16[1,1,16,256,256]{4,3,2,1,0:T(8,128)(2,1)}, u32[]{:S(2)}) copy-start(bf16[1,1,16,256,256]{4,3,2,1,0:T(8,128)(2,1)} %param.7) | copy-start | bytes 6291460
  13.3 19.6 %all-to-all-start = ((bf16[4,256,256]{2,1,0:T(8,128)(2,1)}), bf16[4,256,256]{2,1,0:T(8,128)(2,1)}, u32[]{:S(2)}, u32[]{:S(2)}) async-start(bf16[4,256,256]{2,1,0:T(8,128)(2,1)} %broadcast_in_dim.20), calls=%async_computation | async-start | bytes 1048576 | tf_op jit(solution)/shard_map/all_to_all | solution.py:208
  17.6 11.1 %collective-permute-start.2 = (bf16[256,256]{1,0:T(8,128)(2,1)S(1)}, bf16[256,256]{1,0:T(8,128)(2,1)S(1)}, u32[]{:S(2)}, u32[]{:S(2)}) collective-permute-start(bf16[256,256]{1,0:T(8,128)(2,1)S(1)} %and_select_fusion), channel_id=1, source_target_pairs={{0,4},{4,8},{8,12},{12,0},{1,5},{5,9},{9,13},{13,1},{2,6},{6,10},{... | collective-permute-start | bytes 393224 | tf_op jit(solution)/shard_map/ppermute | solution.py:198
  20.9 7.8 %collective-permute-start = (bf16[256,256]{1,0:T(8,128)(2,1)S(1)}, bf16[256,256]{1,0:T(8,128)(2,1)S(1)}, u32[]{:S(2)}, u32[]{:S(2)}) collective-permute-start(bf16[256,256]{1,0:T(8,128)(2,1)S(1)} %and_select_fusion), channel_id=1, source_target_pairs={{0,12},{4,0},{8,4},{12,8},{1,13},{5,1},{9,5},{13,9},{2,14},{6,2},{... | collective-permute-start | bytes 393224 | tf_op jit(solution)/shard_map/ppermute | solution.py:198
  24.1 7.9 %collective-permute-start.1 = (bf16[256,256]{1,0:T(8,128)(2,1)S(1)}, bf16[256,256]{1,0:T(8,128)(2,1)S(1)}, u32[]{:S(2)}, u32[]{:S(2)}) collective-permute-start(bf16[256,256]{1,0:T(8,128)(2,1)S(1)} %and_select_fusion), channel_id=1, source_target_pairs={{0,8},{4,12},{8,0},{12,4},{1,9},{5,13},{9,1},{13,5},{2,10},{6,14},... | collective-permute-start | bytes 393224 | tf_op jit(solution)/shard_map/ppermute | solution.py:198
  35.1 9.5 %collective-permute-start.4 = (bf16[8,256,256]{2,1,0:T(8,128)(2,1)S(1)}, bf16[8,256,256]{2,1,0:T(8,128)(2,1)}, u32[]{:S(2)}, u32[]{:S(2)}) collective-permute-start(bf16[8,256,256]{2,1,0:T(8,128)(2,1)S(1)} %constant_dynamic-update-slice_fusion.own), channel_id=1, source_target_pairs={{0,1},{1,0},{2,3},{3,2},{4,5},{5,4},{6,7},{7,6},{8,9},{9,8},{10,11... | collective-permute-start | bytes 3145736 | tf_op jit(solution)/shard_map/ppermute | solution.py:247
  48.0 10.6 %collective-permute-start.15 = (bf16[264,256]{1,0:T(8,128)(2,1)S(1)}, bf16[264,256]{1,0:T(8,128)(2,1)S(1)}, u32[]{:S(2)}, u32[]{:S(2)}) collective-permute-start(bf16[264,256]{1,0:T(8,128)(2,1)S(1)} %get-tuple-element.16.message.refs_0_), channel_id=1, source_target_pairs={{0,2},{2,0},{1,3},{3,1},{4,6},{6,4},{5,7},{7,5},{8,10},{10,8},{9,1... | collective-permute-start | bytes 405512 | tf_op jit(solution)/shard_map/ppermute | solution.py:258
  58.6 12.2 %collective-permute-start.16 = (bf16[528,256]{1,0:T(8,128)(2,1)S(1)}, bf16[528,256]{1,0:T(8,128)(2,1)S(1)}, u32[]{:S(2)}, u32[]{:S(2)}) collective-permute-start(bf16[528,256]{1,0:T(8,128)(2,1)S(1)} %get-tuple-element.32), channel_id=1, source_target_pairs={{0,12},{4,0},{8,4},{12,8},{1,13},{5,1},{9,5},{13,9},{2,14},{6,2},{... | collective-permute-start | bytes 811016 | tf_op jit(solution)/shard_map/ppermute | solution.py:198
  62.2 31.3 %collective-permute-start.6 = (bf16[16,256,256]{2,1,0:T(8,128)(2,1)S(1)}, bf16[16,256,256]{2,1,0:T(8,128)(2,1)S(1)}, u32[]{:S(2)}, u32[]{:S(2)}) collective-permute-start(bf16[16,256,256]{2,1,0:T(8,128)(2,1)S(1)} %bitcast.20), channel_id=1, source_target_pairs={{0,1},{1,0},{2,3},{3,2},{4,5},{5,4},{6,7},{7,6},{8,9},{9,8},{10,11... | collective-permute-start | bytes 6291464 | tf_op jit(solution)/shard_map/ppermute | solution.py:249
  65.7 11.5 %collective-permute-start.17 = (bf16[528,256]{1,0:T(8,128)(2,1)S(1)}, bf16[528,256]{1,0:T(8,128)(2,1)S(1)}, u32[]{:S(2)}, u32[]{:S(2)}) collective-permute-start(bf16[528,256]{1,0:T(8,128)(2,1)S(1)} %get-tuple-element.32), channel_id=1, source_target_pairs={{0,8},{4,12},{8,0},{12,4},{1,9},{5,13},{9,1},{13,5},{2,10},{6,14},... | collective-permute-start | bytes 811016 | tf_op jit(solution)/shard_map/ppermute | solution.py:198
  68.2 15.1 %collective-permute-start.18 = (bf16[528,256]{1,0:T(8,128)(2,1)S(1)}, bf16[528,256]{1,0:T(8,128)(2,1)S(1)}, u32[]{:S(2)}, u32[]{:S(2)}) collective-permute-start(bf16[528,256]{1,0:T(8,128)(2,1)S(1)} %get-tuple-element.32), channel_id=1, source_target_pairs={{0,4},{4,8},{8,12},{12,0},{1,5},{5,9},{9,13},{13,1},{2,6},{6,10},{... | collective-permute-start | bytes 811016 | tf_op jit(solution)/shard_map/ppermute | solution.py:198
  83.4 5.6 %collective-permute-start.19 = (bf16[2112,256]{1,0:T(8,128)(2,1)S(1)}, bf16[2112,256]{1,0:T(8,128)(2,1)S(1)}, u32[]{:S(2)}, u32[]{:S(2)}) collective-permute-start(bf16[2112,256]{1,0:T(8,128)(2,1)S(1)} %get-tuple-element.24), channel_id=1, source_target_pairs={{0,1},{1,0},{2,3},{3,2},{4,5},{5,4},{6,7},{7,6},{8,9},{9,8},{10,11... | collective-permute-start | bytes 3244040 | tf_op jit(solution)/shard_map/ppermute | solution.py:275
  85.8 7.8 %collective-permute-start.5 = (bf16[264,256]{1,0:T(8,128)(2,1)S(1)}, bf16[264,256]{1,0:T(8,128)(2,1)S(1)}, u32[]{:S(2)}, u32[]{:S(2)}) collective-permute-start(bf16[264,256]{1,0:T(8,128)(2,1)S(1)} %get-tuple-element.16.message.refs_0_), channel_id=1, source_target_pairs={{0,1},{1,0},{2,3},{3,2},{4,5},{5,4},{6,7},{7,6},{8,9},{9,8},{10,11... | collective-permute-start | bytes 405512 | tf_op jit(solution)/shard_map/ppermute | solution.py:257
  91.1 77.2 %collective-permute-start.20 = (bf16[8,256,256]{2,1,0:T(8,128)(2,1)S(1)}, bf16[8,256,256]{2,1,0:T(8,128)(2,1)S(1)}, u32[]{:S(2)}, u32[]{:S(2)}) collective-permute-start(bf16[8,256,256]{2,1,0:T(8,128)(2,1)S(1)} %get-tuple-element.23), channel_id=1, source_target_pairs={{0,1},{1,0},{2,3},{3,2},{4,5},{5,4},{6,7},{7,6},{8,9},{9,8},{10,11... | collective-permute-start | bytes 3145736 | tf_op jit(solution)/shard_map/ppermute | solution.py:284
  94.8 11.4 %collective-permute-start.7 = (bf16[520,256]{1,0:T(8,128)(2,1)S(1)}, bf16[520,256]{1,0:T(8,128)(2,1)S(1)}, u32[]{:S(2)}, u32[]{:S(2)}) collective-permute-start(bf16[520,256]{1,0:T(8,128)(2,1)S(1)} %get-tuple-element.18), channel_id=1, source_target_pairs={{0,8},{4,12},{8,0},{12,4},{1,9},{5,13},{9,1},{13,5},{2,10},{6,14},... | collective-permute-start | bytes 798728 | tf_op jit(solution)/shard_map/ppermute | solution.py:198
  97.3 15.0 %collective-permute-start.8 = (bf16[520,256]{1,0:T(8,128)(2,1)S(1)}, bf16[520,256]{1,0:T(8,128)(2,1)S(1)}, u32[]{:S(2)}, u32[]{:S(2)}) collective-permute-start(bf16[520,256]{1,0:T(8,128)(2,1)S(1)} %get-tuple-element.19), channel_id=1, source_target_pairs={{0,4},{4,8},{8,12},{12,0},{1,5},{5,9},{9,13},{13,1},{2,6},{6,10},{... | collective-permute-start | bytes 798728 | tf_op jit(solution)/shard_map/ppermute | solution.py:198
  99.6 12.7 %collective-permute-start.9 = (bf16[520,256]{1,0:T(8,128)(2,1)S(1)}, bf16[520,256]{1,0:T(8,128)(2,1)S(1)}, u32[]{:S(2)}, u32[]{:S(2)}) collective-permute-start(bf16[520,256]{1,0:T(8,128)(2,1)S(1)} %get-tuple-element.20), channel_id=1, source_target_pairs={{0,12},{4,0},{8,4},{12,8},{1,13},{5,1},{9,5},{13,9},{2,14},{6,2},{... | collective-permute-start | bytes 798728 | tf_op jit(solution)/shard_map/ppermute | solution.py:198
  112.4 15.8 %collective-permute-start.10 = (bf16[520,256]{1,0:T(8,128)(2,1)S(1)}, bf16[520,256]{1,0:T(8,128)(2,1)S(1)}, u32[]{:S(2)}, u32[]{:S(2)}) collective-permute-start(bf16[520,256]{1,0:T(8,128)(2,1)S(1)} %shard_map.72), channel_id=1, source_target_pairs={{0,16},{2,18},{16,32},{18,34},{32,48},{34,50},{48,66},{50,64},{64,... | collective-permute-start | bytes 798728 | tf_op jit(solution)/shard_map/ppermute | solution.py:271
  122.9 26.0 %collective-permute-start.11 = (bf16[520,256]{1,0:T(8,128)(2,1)S(1)}, bf16[520,256]{1,0:T(8,128)(2,1)S(1)}, u32[]{:S(2)}, u32[]{:S(2)}) collective-permute-start(bf16[520,256]{1,0:T(8,128)(2,1)S(1)} %shard_map.72), channel_id=1, source_target_pairs={{0,18},{2,16},{16,34},{18,32},{32,50},{34,48},{48,64},{50,66},{64,... | collective-permute-start | bytes 798728 | tf_op jit(solution)/shard_map/ppermute | solution.py:270
  149.0 9.3 %collective-permute-start.12 = (bf16[512,256]{1,0:T(8,128)(2,1)S(1)}, bf16[512,256]{1,0:T(8,128)(2,1)S(1)}, u32[]{:S(2)}, u32[]{:S(2)}) collective-permute-start(bf16[512,256]{1,0:T(8,128)(2,1)S(1)} %shard_map.73), channel_id=1, source_target_pairs={{0,12},{4,0},{8,4},{12,8},{1,13},{5,1},{9,5},{13,9},{2,14},{6,2},{... | collective-permute-start | bytes 786440 | tf_op jit(solution)/shard_map/ppermute | solution.py:198
  151.0 10.5 %collective-permute-start.13 = (bf16[512,256]{1,0:T(8,128)(2,1)S(1)}, bf16[512,256]{1,0:T(8,128)(2,1)S(1)}, u32[]{:S(2)}, u32[]{:S(2)}) collective-permute-start(bf16[512,256]{1,0:T(8,128)(2,1)S(1)} %shard_map.73), channel_id=1, source_target_pairs={{0,8},{4,12},{8,0},{12,4},{1,9},{5,13},{9,1},{13,5},{2,10},{6,14},... | collective-permute-start | bytes 786440 | tf_op jit(solution)/shard_map/ppermute | solution.py:198
  153.4 14.8 %collective-permute-start.14 = (bf16[512,256]{1,0:T(8,128)(2,1)S(1)}, bf16[512,256]{1,0:T(8,128)(2,1)S(1)}, u32[]{:S(2)}, u32[]{:S(2)}) collective-permute-start(bf16[512,256]{1,0:T(8,128)(2,1)S(1)} %shard_map.73), channel_id=1, source_target_pairs={{0,4},{4,8},{8,12},{12,0},{1,5},{5,9},{9,13},{13,1},{2,6},{6,10},{... | collective-permute-start | bytes 786440 | tf_op jit(solution)/shard_map/ppermute | solution.py:198
  168.8 3.5 %collective-permute-start.21 = (f32[256,256]{1,0:T(8,128)S(1)}, f32[256,256]{1,0:T(8,128)S(1)}, u32[]{:S(2)}, u32[]{:S(2)}) collective-permute-start(f32[256,256]{1,0:T(8,128)S(1)} %shard_map.76), channel_id=1, source_target_pairs={{0,1},{1,0},{2,3},{3,2},{4,5},{5,4},{6,7},{7,6},{8,9},{9,8},{10,11... | collective-permute-start | bytes 786440 | tf_op jit(solution)/shard_map/ppermute | solution.py:294
  (2 other events, 4.8 us)

commit v10 on v9

--- a/solution.py
+++ b/solution.py
@@ -131,27 +131,33 @@
     out[...] = (total * weight).astype(BF)
 
 
-def pool_two_kernel(meta, picks, pool, left, right, g_own, g_send, base, g):
-    channels, width = left.shape[0], left.shape[1]
-    half = channels // 2
+def vector_terms(meta, picks, pool, right, side, g_out):
+    half, width = g_out.shape[0], g_out.shape[1]
     span = width + TILE
     squares = count = jnp.zeros((1, width), F32)
     for at in range(16):
         q, c = unpack(pool[at * span + width:(at + 1) * span, :])
         squares, count = squares + q, count + c
     scale = lax.rsqrt(squares / count + 1e-6)
-    for j in range(channels):
-        t = channel(meta, lax.rem(meta[1] + j // half, 2), j % half)
+    for j in range(half):
+        t = channel(meta, side, j)
         c, yh, step = place(picks[t], meta)
         start = pl.multiple_of(((c * 4 + step) * 2 + yh) * span, TILE)
-        block = (dot(pool[pl.ds(start, width), :], right[t]) * scale).astype(BF)
-        (g_own if j < half else g_send)[j % half] = block
-        g[j] = left[t]
-    total = dot(g[0], g_own[0])
+        g_out[j] = (dot(pool[pl.ds(start, width), :], right[t]) * scale).astype(BF)
+
+
+def send_kernel(meta, picks, pool, right, g_send):
+    vector_terms(meta, picks, pool, right, 1 - meta[1], g_send)
+
+
+def pool_two_kernel(meta, picks, pool, left, right, g_send, g_own, base):
+    half = g_own.shape[0]
+    vector_terms(meta, picks, pool, right, meta[1], g_own)
+    total = dot(left[channel(meta, meta[1], 0)], g_own[0])
     for j in range(1, half):
-        total = total + dot(g[j], g_own[j])
+        total = total + dot(left[channel(meta, meta[1], j)], g_own[j])
     for j in range(half):
-        total = total + dot(g[half + j], g_send[j])
+        total = total + dot(left[channel(meta, 1 - meta[1], j)], g_send[j])
     base[...] = total
 
 
@@ -274,14 +280,14 @@
     two_own = jnp.concatenate(round_x(both))
     two_other = lax.ppermute(two_own, "c", SWAP)
     pool_two = jnp.concatenate([two_own, two_other])
-    g_own, g_send, base = call(
-        pool_two_kernel,
-        [((half, width, width), BF), ((half, width, width), BF), ((width, width), F32)],
-        [SMEM, SMEM, VMEM, VMEM, VMEM],
-        [pltpu.VMEM((channels, width, width), BF)],
-        2 * unit, 4 * channels * block_bytes,
-    )(meta, picks, pool_two, left, right_here)
+    g_send = call(
+        send_kernel, one((half, width, width), BF), [SMEM, SMEM, VMEM, VMEM], [], unit // 2, channels * block_bytes
+    )(meta, picks, pool_two, right_here)
     g_other = lax.ppermute(g_send, "c", SWAP)
+    g_own, base = call(
+        pool_two_kernel, [((half, width, width), BF), ((width, width), F32)], [SMEM, SMEM] + [VMEM] * 4, [],
+        3 * unit // 2, 4 * channels * block_bytes,
+    )(meta, picks, pool_two, left, right_here, g_send)
 
     factor = 1.0 / (width * math.sqrt(channels_of(sector_size)))
     edge = call(

time: 175 us -> 176 us (level)
  starting transfers between devices: 80.7 us -> 85.5 us
  waiting for transfers between devices: 74.4 us -> 69.8 us
    ppermute x12, waiting for transfers between devices: 36.3 us -> 32.4 us  [along_x(): lax.ppermute(value, 'x', [(i, (i + step) % count) for i in range(count)])]
    ppermute x12, starting transfers between devices: 34.9 us -> 38.3 us  [along_x(): lax.ppermute(value, 'x', [(i, (i + step) % count) for i in range(count)])]
  transfers between devices with their start and end apart: 23 -> 23, of which waited for: 14 -> 13; matrix products, arithmetic and copies ran while one was open for 1% -> 1% of each run, Pallas kernels for 3% -> 4%
where the time goes in v10:
time: 176 us; the launch traced here: 175 us
  starting transfers between devices  85.5 us (49%)
  waiting for transfers between devices  69.8 us (40%)
  Pallas kernels  11.4 us (6%)
  local copies, waits for them, and re-layouts  3.24 us (2%)
  other arithmetic  3.04 us (2%)
    ppermute x12, starting transfers between devices, along_x(): lax.ppermute(value, 'x', [(i, (i + step) % count) for i in range(count)])  38.3 us
    ppermute x12, waiting for transfers between devices, along_x(): lax.ppermute(value, 'x', [(i, (i + step) % count) for i in range(count)])  32.4 us
    ppermute x1, waiting for transfers between devices, body(): from_far = lax.ppermute(row, YROW, far)  20.7 us
    ppermute x1, starting transfers between devices, body(): from_near = lax.ppermute(row, YROW, near)  10.5 us
    ppermute x1, starting transfers between devices, body(): across = lax.ppermute(own, 'c', SWAP)  7.43 us
    ppermute x1, waiting for transfers between devices, body(): message_other = lax.ppermute(message, 'yh', SWAP)  5.83 us
    ppermute x1, waiting for transfers between devices, body(): masked_other = lax.ppermute(masked, 'yh', SWAP)  5.42 us
    ppermute x1, starting transfers between devices, body(): masked_other = lax.ppermute(masked, 'yh', SWAP)  4.76 us
  transfers between devices with their start and end apart: 23, of which 13 were waited for; matrix products, arithmetic and copies ran while one was open for 1% of the time, Pallas kernels for 4%

profile of v10, /device:TPU:217, one launch (start us, length us, event | category | flops | bytes accessed | tf_op | source)
XLA Modules:
  0.0 174.7 jit_solution(27535817550078604)
XLA Ops:
  2.3 4.8 %collective-permute-start.3 = (bf16[256,256]{1,0:T(8,128)(2,1)S(1)}, bf16[256,256]{1,0:T(8,128)(2,1)S(1)}, u32[]{:S(2)}, u32[]{:S(2)}) collective-permute-start(bf16[256,256]{1,0:T(8,128)(2,1)S(1)} %and_select_fusion), channel_id=1, source_target_pairs={{0,2},{2,0},{1,3},{3,1},{4,6},{6,4},{5,7},{7,5},{8,10},{10,8},{9,1... | collective-permute-start | bytes 393224 | tf_op jit(solution)/shard_map/ppermute | solution.py:248
  7.1 5.4 %collective-permute-done.3 = bf16[256,256]{1,0:T(8,128)(2,1)S(1)} collective-permute-done((bf16[256,256]{1,0:T(8,128)(2,1)S(1)}, bf16[256,256]{1,0:T(8,128)(2,1)S(1)}, u32[]{:S(2)}, u32[]{:S(2)}) %collective-permute-start.3) | collective-permute-done | bytes 131104 | tf_op jit(solution)/shard_map/ppermute | solution.py:248
  13.3 4.3 %all-to-all-start = ((bf16[4,256,256]{2,1,0:T(8,128)(2,1)}), bf16[4,256,256]{2,1,0:T(8,128)(2,1)}, u32[]{:S(2)}, u32[]{:S(2)}) async-start(bf16[4,256,256]{2,1,0:T(8,128)(2,1)} %broadcast_in_dim.20), calls=%async_computation | async-start | bytes 1048576 | tf_op jit(solution)/shard_map/all_to_all | solution.py:214
  17.6 3.3 %collective-permute-start.2 = (bf16[256,256]{1,0:T(8,128)(2,1)S(1)}, bf16[256,256]{1,0:T(8,128)(2,1)S(1)}, u32[]{:S(2)}, u32[]{:S(2)}) collective-permute-start(bf16[256,256]{1,0:T(8,128)(2,1)S(1)} %and_select_fusion), channel_id=1, source_target_pairs={{0,4},{4,8},{8,12},{12,0},{1,5},{5,9},{9,13},{13,1},{2,6},{6,10},{... | collective-permute-start | bytes 393224 | tf_op jit(solution)/shard_map/ppermute | solution.py:204
  20.9 4.3 %collective-permute-start.1 = (bf16[256,256]{1,0:T(8,128)(2,1)S(1)}, bf16[256,256]{1,0:T(8,128)(2,1)S(1)}, u32[]{:S(2)}, u32[]{:S(2)}) collective-permute-start(bf16[256,256]{1,0:T(8,128)(2,1)S(1)} %and_select_fusion), channel_id=1, source_target_pairs={{0,8},{4,12},{8,0},{12,4},{1,9},{5,13},{9,1},{13,5},{2,10},{6,14},... | collective-permute-start | bytes 393224 | tf_op jit(solution)/shard_map/ppermute | solution.py:204
  25.2 3.1 %collective-permute-start = (bf16[256,256]{1,0:T(8,128)(2,1)S(1)}, bf16[256,256]{1,0:T(8,128)(2,1)S(1)}, u32[]{:S(2)}, u32[]{:S(2)}) collective-permute-start(bf16[256,256]{1,0:T(8,128)(2,1)S(1)} %and_select_fusion), channel_id=1, source_target_pairs={{0,12},{4,0},{8,4},{12,8},{1,13},{5,1},{9,5},{13,9},{2,14},{6,2},{... | collective-permute-start | bytes 393224 | tf_op jit(solution)/shard_map/ppermute | solution.py:204
  34.7 7.4 %collective-permute-start.4 = (bf16[8,256,256]{2,1,0:T(8,128)(2,1)S(1)}, bf16[8,256,256]{2,1,0:T(8,128)(2,1)}, u32[]{:S(2)}, u32[]{:S(2)}) collective-permute-start(bf16[8,256,256]{2,1,0:T(8,128)(2,1)S(1)} %constant_dynamic-update-slice_fusion.own), channel_id=1, source_target_pairs={{0,1},{1,0},{2,3},{3,2},{4,5},{5,4},{6,7},{7,6},{8,9},{9,8},{10,11... | collective-permute-start | bytes 3145736 | tf_op jit(solution)/shard_map/ppermute | solution.py:253
  44.5 3.4 %shard_map.69 = (bf16[256,256]{1,0:T(8,128)(2,1)}, bf16[264,256]{1,0:T(8,128)(2,1)S(1)}) custom-call(s32[4]{0:T(128)S(1)} %pad_add_fusion.meta, s32[16]{0:T(128)S(1)} %bitcast.24, bf16[8,256,256]{2,1,0:T(8,128)(2,1)S(1)} %constant_dynamic-update-slice_fusion.own, bf16[8,256,256]{2,1,0:T(8,128)(2,1)} %collective-permute-done.4.across, ...), custom_call_target="tpu_custom_call" | custom-call | flops 1073741824 | bytes 8388608 | tf_op jit(solution)/shard_map/pallas_call | solution.py:257
  47.9 4.7 %collective-permute-start.15 = (bf16[264,256]{1,0:T(8,128)(2,1)S(1)}, bf16[264,256]{1,0:T(8,128)(2,1)S(1)}, u32[]{:S(2)}, u32[]{:S(2)}) collective-permute-start(bf16[264,256]{1,0:T(8,128)(2,1)S(1)} %get-tuple-element.15.message.refs_0_), channel_id=1, source_target_pairs={{0,2},{2,0},{1,3},{3,1},{4,6},{6,4},{5,7},{7,5},{8,10},{10,8},{9,1... | collective-permute-start | bytes 405512 | tf_op jit(solution)/shard_map/ppermute | solution.py:264
  52.6 5.8 %collective-permute-done.15 = bf16[264,256]{1,0:T(8,128)(2,1)S(1)} collective-permute-done((bf16[264,256]{1,0:T(8,128)(2,1)S(1)}, bf16[264,256]{1,0:T(8,128)(2,1)S(1)}, u32[]{:S(2)}, u32[]{:S(2)}) %collective-permute-start.15) | collective-permute-done | bytes 135200 | tf_op jit(solution)/shard_map/ppermute | solution.py:264
  58.5 4.3 %collective-permute-start.16 = (bf16[528,256]{1,0:T(8,128)(2,1)S(1)}, bf16[528,256]{1,0:T(8,128)(2,1)S(1)}, u32[]{:S(2)}, u32[]{:S(2)}) collective-permute-start(bf16[528,256]{1,0:T(8,128)(2,1)S(1)} %get-tuple-element.30), channel_id=1, source_target_pairs={{0,12},{4,0},{8,4},{12,8},{1,13},{5,1},{9,5},{13,9},{2,14},{6,2},{... | collective-permute-start | bytes 811016 | tf_op jit(solution)/shard_map/ppermute | solution.py:204
  62.8 3.5 %collective-permute-start.6 = (bf16[16,256,256]{2,1,0:T(8,128)(2,1)S(1)}, bf16[16,256,256]{2,1,0:T(8,128)(2,1)S(1)}, u32[]{:S(2)}, u32[]{:S(2)}) collective-permute-start(bf16[16,256,256]{2,1,0:T(8,128)(2,1)S(1)} %bitcast.20), channel_id=1, source_target_pairs={{0,1},{1,0},{2,3},{3,2},{4,5},{5,4},{6,7},{7,6},{8,9},{9,8},{10,11... | collective-permute-start | bytes 6291464 | tf_op jit(solution)/shard_map/ppermute | solution.py:255
  66.3 3.1 %collective-permute-start.17 = (bf16[528,256]{1,0:T(8,128)(2,1)S(1)}, bf16[528,256]{1,0:T(8,128)(2,1)S(1)}, u32[]{:S(2)}, u32[]{:S(2)}) collective-permute-start(bf16[528,256]{1,0:T(8,128)(2,1)S(1)} %get-tuple-element.30), channel_id=1, source_target_pairs={{0,8},{4,12},{8,0},{12,4},{1,9},{5,13},{9,1},{13,5},{2,10},{6,14},... | collective-permute-start | bytes 811016 | tf_op jit(solution)/shard_map/ppermute | solution.py:204
  71.6 6.2 %collective-permute-done.17 = bf16[528,256]{1,0:T(8,128)(2,1)S(1)} collective-permute-done((bf16[528,256]{1,0:T(8,128)(2,1)S(1)}, bf16[528,256]{1,0:T(8,128)(2,1)S(1)}, u32[]{:S(2)}, u32[]{:S(2)}) %collective-permute-start.17) | collective-permute-done | bytes 270368 | tf_op jit(solution)/shard_map/ppermute | solution.py:204
  77.8 6.1 %collective-permute-done.18 = bf16[528,256]{1,0:T(8,128)(2,1)S(1)} collective-permute-done((bf16[528,256]{1,0:T(8,128)(2,1)S(1)}, bf16[528,256]{1,0:T(8,128)(2,1)S(1)}, u32[]{:S(2)}, u32[]{:S(2)}) %collective-permute-start.18) | collective-permute-done | bytes 270368 | tf_op jit(solution)/shard_map/ppermute | solution.py:204
  94.4 3.1 %collective-permute-start.7 = (bf16[520,256]{1,0:T(8,128)(2,1)S(1)}, bf16[520,256]{1,0:T(8,128)(2,1)S(1)}, u32[]{:S(2)}, u32[]{:S(2)}) collective-permute-start(bf16[520,256]{1,0:T(8,128)(2,1)S(1)} %get-tuple-element.17), channel_id=1, source_target_pairs={{0,8},{4,12},{8,0},{12,4},{1,9},{5,13},{9,1},{13,5},{2,10},{6,14},... | collective-permute-start | bytes 798728 | tf_op jit(solution)/shard_map/ppermute | solution.py:204
  99.5 4.6 %collective-permute-start.9 = (bf16[520,256]{1,0:T(8,128)(2,1)S(1)}, bf16[520,256]{1,0:T(8,128)(2,1)S(1)}, u32[]{:S(2)}, u32[]{:S(2)}) collective-permute-start(bf16[520,256]{1,0:T(8,128)(2,1)S(1)} %get-tuple-element.19), channel_id=1, source_target_pairs={{0,12},{4,0},{8,4},{12,8},{1,13},{5,1},{9,5},{13,9},{2,14},{6,2},{... | collective-permute-start | bytes 798728 | tf_op jit(solution)/shard_map/ppermute | solution.py:204
  105.8 6.1 %collective-permute-done.8.c = bf16[520,256]{1,0:T(8,128)(2,1)S(1)} collective-permute-done((bf16[520,256]{1,0:T(8,128)(2,1)S(1)}, bf16[520,256]{1,0:T(8,128)(2,1)S(1)}, u32[]{:S(2)}, u32[]{:S(2)}) %collective-permute-start.8) | collective-permute-done | bytes 266272 | tf_op jit(solution)/shard_map/ppermute | solution.py:204
  112.0 10.5 %collective-permute-start.10 = (bf16[520,256]{1,0:T(8,128)(2,1)S(1)}, bf16[520,256]{1,0:T(8,128)(2,1)S(1)}, u32[]{:S(2)}, u32[]{:S(2)}) collective-permute-start(bf16[520,256]{1,0:T(8,128)(2,1)S(1)} %shard_map.72), channel_id=1, source_target_pairs={{0,16},{2,18},{16,32},{18,34},{32,48},{34,50},{48,66},{50,64},{64,... | collective-permute-start | bytes 798728 | tf_op jit(solution)/shard_map/ppermute | solution.py:277
  124.4 3.3 %collective-permute-done.10.refs_0_ = bf16[520,256]{1,0:T(8,128)(2,1)S(1)} collective-permute-done((bf16[520,256]{1,0:T(8,128)(2,1)S(1)}, bf16[520,256]{1,0:T(8,128)(2,1)S(1)}, u32[]{:S(2)}, u32[]{:S(2)}) %collective-permute-start.10) | collective-permute-done | bytes 266272 | tf_op jit(solution)/shard_map/ppermute | solution.py:277
  127.8 20.7 %collective-permute-done.11.refs_1_ = bf16[520,256]{1,0:T(8,128)(2,1)S(1)} collective-permute-done((bf16[520,256]{1,0:T(8,128)(2,1)S(1)}, bf16[520,256]{1,0:T(8,128)(2,1)S(1)}, u32[]{:S(2)}, u32[]{:S(2)}) %collective-permute-start.11) | collective-permute-done | bytes 266272 | tf_op jit(solution)/shard_map/ppermute | solution.py:276
  153.5 3.5 %collective-permute-start.12 = (bf16[512,256]{1,0:T(8,128)(2,1)S(1)}, bf16[512,256]{1,0:T(8,128)(2,1)S(1)}, u32[]{:S(2)}, u32[]{:S(2)}) collective-permute-start(bf16[512,256]{1,0:T(8,128)(2,1)S(1)} %shard_map.73), channel_id=1, source_target_pairs={{0,12},{4,0},{8,4},{12,8},{1,13},{5,1},{9,5},{13,9},{2,14},{6,2},{... | collective-permute-start | bytes 786440 | tf_op jit(solution)/shard_map/ppermute | solution.py:204
  157.0 7.7 %collective-permute-done.14 = bf16[512,256]{1,0:T(8,128)(2,1)S(1)} collective-permute-done((bf16[512,256]{1,0:T(8,128)(2,1)S(1)}, bf16[512,256]{1,0:T(8,128)(2,1)S(1)}, u32[]{:S(2)}, u32[]{:S(2)}) %collective-permute-start.14) | collective-permute-done | bytes 262176 | tf_op jit(solution)/shard_map/ppermute | solution.py:204
  167.5 3.5 %collective-permute-start.21 = (f32[256,256]{1,0:T(8,128)S(1)}, f32[256,256]{1,0:T(8,128)S(1)}, u32[]{:S(2)}, u32[]{:S(2)}) collective-permute-start(f32[256,256]{1,0:T(8,128)S(1)} %shard_map.77), channel_id=1, source_target_pairs={{0,1},{1,0},{2,3},{3,2},{4,5},{5,4},{6,7},{7,6},{8,9},{9,8},{10,11... | collective-permute-start | bytes 786440 | tf_op jit(solution)/shard_map/ppermute | solution.py:300
  (54 shorter events, 40.3 us)
Async XLA Ops:
  2.3 10.2 %collective-permute-start.3 = (bf16[256,256]{1,0:T(8,128)(2,1)S(1)}, bf16[256,256]{1,0:T(8,128)(2,1)S(1)}, u32[]{:S(2)}, u32[]{:S(2)}) collective-permute-start(bf16[256,256]{1,0:T(8,128)(2,1)S(1)} %and_select_fusion), channel_id=1, source_target_pairs={{0,2},{2,0},{1,3},{3,1},{4,6},{6,4},{5,7},{7,5},{8,10},{10,8},{9,1... | collective-permute-start | bytes 393224 | tf_op jit(solution)/shard_map/ppermute | solution.py:248
  13.3 28.8 %copy-start.1 = (bf16[1,1,16,256,256]{4,3,2,1,0:T(8,128)(2,1)S(1)}, bf16[1,1,16,256,256]{4,3,2,1,0:T(8,128)(2,1)}, u32[]{:S(2)}) copy-start(bf16[1,1,16,256,256]{4,3,2,1,0:T(8,128)(2,1)} %param.7) | copy-start | bytes 6291460
  13.3 19.2 %all-to-all-start = ((bf16[4,256,256]{2,1,0:T(8,128)(2,1)}), bf16[4,256,256]{2,1,0:T(8,128)(2,1)}, u32[]{:S(2)}, u32[]{:S(2)}) async-start(bf16[4,256,256]{2,1,0:T(8,128)(2,1)} %broadcast_in_dim.20), calls=%async_computation | async-start | bytes 1048576 | tf_op jit(solution)/shard_map/all_to_all | solution.py:214
  17.6 11.7 %collective-permute-start.2 = (bf16[256,256]{1,0:T(8,128)(2,1)S(1)}, bf16[256,256]{1,0:T(8,128)(2,1)S(1)}, u32[]{:S(2)}, u32[]{:S(2)}) collective-permute-start(bf16[256,256]{1,0:T(8,128)(2,1)S(1)} %and_select_fusion), channel_id=1, source_target_pairs={{0,4},{4,8},{8,12},{12,0},{1,5},{5,9},{9,13},{13,1},{2,6},{6,10},{... | collective-permute-start | bytes 393224 | tf_op jit(solution)/shard_map/ppermute | solution.py:204
  20.9 9.0 %collective-permute-start.1 = (bf16[256,256]{1,0:T(8,128)(2,1)S(1)}, bf16[256,256]{1,0:T(8,128)(2,1)S(1)}, u32[]{:S(2)}, u32[]{:S(2)}) collective-permute-start(bf16[256,256]{1,0:T(8,128)(2,1)S(1)} %and_select_fusion), channel_id=1, source_target_pairs={{0,8},{4,12},{8,0},{12,4},{1,9},{5,13},{9,1},{13,5},{2,10},{6,14},... | collective-permute-start | bytes 393224 | tf_op jit(solution)/shard_map/ppermute | solution.py:204
  25.2 6.4 %collective-permute-start = (bf16[256,256]{1,0:T(8,128)(2,1)S(1)}, bf16[256,256]{1,0:T(8,128)(2,1)S(1)}, u32[]{:S(2)}, u32[]{:S(2)}) collective-permute-start(bf16[256,256]{1,0:T(8,128)(2,1)S(1)} %and_select_fusion), channel_id=1, source_target_pairs={{0,12},{4,0},{8,4},{12,8},{1,13},{5,1},{9,5},{13,9},{2,14},{6,2},{... | collective-permute-start | bytes 393224 | tf_op jit(solution)/shard_map/ppermute | solution.py:204
  34.7 9.8 %collective-permute-start.4 = (bf16[8,256,256]{2,1,0:T(8,128)(2,1)S(1)}, bf16[8,256,256]{2,1,0:T(8,128)(2,1)}, u32[]{:S(2)}, u32[]{:S(2)}) collective-permute-start(bf16[8,256,256]{2,1,0:T(8,128)(2,1)S(1)} %constant_dynamic-update-slice_fusion.own), channel_id=1, source_target_pairs={{0,1},{1,0},{2,3},{3,2},{4,5},{5,4},{6,7},{7,6},{8,9},{9,8},{10,11... | collective-permute-start | bytes 3145736 | tf_op jit(solution)/shard_map/ppermute | solution.py:253
  47.9 10.6 %collective-permute-start.15 = (bf16[264,256]{1,0:T(8,128)(2,1)S(1)}, bf16[264,256]{1,0:T(8,128)(2,1)S(1)}, u32[]{:S(2)}, u32[]{:S(2)}) collective-permute-start(bf16[264,256]{1,0:T(8,128)(2,1)S(1)} %get-tuple-element.15.message.refs_0_), channel_id=1, source_target_pairs={{0,2},{2,0},{1,3},{3,1},{4,6},{6,4},{5,7},{7,5},{8,10},{10,8},{9,1... | collective-permute-start | bytes 405512 | tf_op jit(solution)/shard_map/ppermute | solution.py:264
  58.5 13.1 %collective-permute-start.16 = (bf16[528,256]{1,0:T(8,128)(2,1)S(1)}, bf16[528,256]{1,0:T(8,128)(2,1)S(1)}, u32[]{:S(2)}, u32[]{:S(2)}) collective-permute-start(bf16[528,256]{1,0:T(8,128)(2,1)S(1)} %get-tuple-element.30), channel_id=1, source_target_pairs={{0,12},{4,0},{8,4},{12,8},{1,13},{5,1},{9,5},{13,9},{2,14},{6,2},{... | collective-permute-start | bytes 811016 | tf_op jit(solution)/shard_map/ppermute | solution.py:204
  62.8 30.3 %collective-permute-start.6 = (bf16[16,256,256]{2,1,0:T(8,128)(2,1)S(1)}, bf16[16,256,256]{2,1,0:T(8,128)(2,1)S(1)}, u32[]{:S(2)}, u32[]{:S(2)}) collective-permute-start(bf16[16,256,256]{2,1,0:T(8,128)(2,1)S(1)} %bitcast.20), channel_id=1, source_target_pairs={{0,1},{1,0},{2,3},{3,2},{4,5},{5,4},{6,7},{7,6},{8,9},{9,8},{10,11... | collective-permute-start | bytes 6291464 | tf_op jit(solution)/shard_map/ppermute | solution.py:255
  66.3 11.5 %collective-permute-start.17 = (bf16[528,256]{1,0:T(8,128)(2,1)S(1)}, bf16[528,256]{1,0:T(8,128)(2,1)S(1)}, u32[]{:S(2)}, u32[]{:S(2)}) collective-permute-start(bf16[528,256]{1,0:T(8,128)(2,1)S(1)} %get-tuple-element.30), channel_id=1, source_target_pairs={{0,8},{4,12},{8,0},{12,4},{1,9},{5,13},{9,1},{13,5},{2,10},{6,14},... | collective-permute-start | bytes 811016 | tf_op jit(solution)/shard_map/ppermute | solution.py:204
  69.5 14.5 %collective-permute-start.18 = (bf16[528,256]{1,0:T(8,128)(2,1)S(1)}, bf16[528,256]{1,0:T(8,128)(2,1)S(1)}, u32[]{:S(2)}, u32[]{:S(2)}) collective-permute-start(bf16[528,256]{1,0:T(8,128)(2,1)S(1)} %get-tuple-element.30), channel_id=1, source_target_pairs={{0,4},{4,8},{8,12},{12,0},{1,5},{5,9},{9,13},{13,1},{2,6},{6,10},{... | collective-permute-start | bytes 811016 | tf_op jit(solution)/shard_map/ppermute | solution.py:204
  84.0 5.6 %collective-permute-start.19 = (bf16[2112,256]{1,0:T(8,128)(2,1)S(1)}, bf16[2112,256]{1,0:T(8,128)(2,1)S(1)}, u32[]{:S(2)}, u32[]{:S(2)}) collective-permute-start(bf16[2112,256]{1,0:T(8,128)(2,1)S(1)} %get-tuple-element.22), channel_id=1, source_target_pairs={{0,1},{1,0},{2,3},{3,2},{4,5},{5,4},{6,7},{7,6},{8,9},{9,8},{10,11... | collective-permute-start | bytes 3244040 | tf_op jit(solution)/shard_map/ppermute | solution.py:281
  86.4 6.7 %collective-permute-start.5 = (bf16[264,256]{1,0:T(8,128)(2,1)S(1)}, bf16[264,256]{1,0:T(8,128)(2,1)S(1)}, u32[]{:S(2)}, u32[]{:S(2)}) collective-permute-start(bf16[264,256]{1,0:T(8,128)(2,1)S(1)} %get-tuple-element.15.message.refs_0_), channel_id=1, source_target_pairs={{0,1},{1,0},{2,3},{3,2},{4,5},{5,4},{6,7},{7,6},{8,9},{9,8},{10,11... | collective-permute-start | bytes 405512 | tf_op jit(solution)/shard_map/ppermute | solution.py:263
  90.7 76.4 %collective-permute-start.20 = (bf16[8,256,256]{2,1,0:T(8,128)(2,1)S(1)}, bf16[8,256,256]{2,1,0:T(8,128)(2,1)S(1)}, u32[]{:S(2)}, u32[]{:S(2)}) collective-permute-start(bf16[8,256,256]{2,1,0:T(8,128)(2,1)S(1)} %shard_map.74.g_send), channel_id=1, source_target_pairs={{0,1},{1,0},{2,3},{3,2},{4,5},{5,4},{6,7},{7,6},{8,9},{9,8},{10,11... | collective-permute-start | bytes 3145736 | tf_op jit(solution)/shard_map/ppermute | solution.py:286
  94.4 11.4 %collective-permute-start.7 = (bf16[520,256]{1,0:T(8,128)(2,1)S(1)}, bf16[520,256]{1,0:T(8,128)(2,1)S(1)}, u32[]{:S(2)}, u32[]{:S(2)}) collective-permute-start(bf16[520,256]{1,0:T(8,128)(2,1)S(1)} %get-tuple-element.17), channel_id=1, source_target_pairs={{0,8},{4,12},{8,0},{12,4},{1,9},{5,13},{9,1},{13,5},{2,10},{6,14},... | collective-permute-start | bytes 798728 | tf_op jit(solution)/shard_map/ppermute | solution.py:204
  97.5 14.3 %collective-permute-start.8 = (bf16[520,256]{1,0:T(8,128)(2,1)S(1)}, bf16[520,256]{1,0:T(8,128)(2,1)S(1)}, u32[]{:S(2)}, u32[]{:S(2)}) collective-permute-start(bf16[520,256]{1,0:T(8,128)(2,1)S(1)} %get-tuple-element.18), channel_id=1, source_target_pairs={{0,4},{4,8},{8,12},{12,0},{1,5},{5,9},{9,13},{13,1},{2,6},{6,10},{... | collective-permute-start | bytes 798728 | tf_op jit(solution)/shard_map/ppermute | solution.py:204
  99.5 12.4 %collective-permute-start.9 = (bf16[520,256]{1,0:T(8,128)(2,1)S(1)}, bf16[520,256]{1,0:T(8,128)(2,1)S(1)}, u32[]{:S(2)}, u32[]{:S(2)}) collective-permute-start(bf16[520,256]{1,0:T(8,128)(2,1)S(1)} %get-tuple-element.19), channel_id=1, source_target_pairs={{0,12},{4,0},{8,4},{12,8},{1,13},{5,1},{9,5},{13,9},{2,14},{6,2},{... | collective-permute-start | bytes 798728 | tf_op jit(solution)/shard_map/ppermute | solution.py:204
  112.0 15.8 %collective-permute-start.10 = (bf16[520,256]{1,0:T(8,128)(2,1)S(1)}, bf16[520,256]{1,0:T(8,128)(2,1)S(1)}, u32[]{:S(2)}, u32[]{:S(2)}) collective-permute-start(bf16[520,256]{1,0:T(8,128)(2,1)S(1)} %shard_map.72), channel_id=1, source_target_pairs={{0,16},{2,18},{16,32},{18,34},{32,48},{34,50},{48,66},{50,64},{64,... | collective-permute-start | bytes 798728 | tf_op jit(solution)/shard_map/ppermute | solution.py:277
  122.5 26.0 %collective-permute-start.11 = (bf16[520,256]{1,0:T(8,128)(2,1)S(1)}, bf16[520,256]{1,0:T(8,128)(2,1)S(1)}, u32[]{:S(2)}, u32[]{:S(2)}) collective-permute-start(bf16[520,256]{1,0:T(8,128)(2,1)S(1)} %shard_map.72), channel_id=1, source_target_pairs={{0,18},{2,16},{16,34},{18,32},{32,50},{34,48},{48,64},{50,66},{64,... | collective-permute-start | bytes 798728 | tf_op jit(solution)/shard_map/ppermute | solution.py:276
  148.6 16.1 %collective-permute-start.14 = (bf16[512,256]{1,0:T(8,128)(2,1)S(1)}, bf16[512,256]{1,0:T(8,128)(2,1)S(1)}, u32[]{:S(2)}, u32[]{:S(2)}) collective-permute-start(bf16[512,256]{1,0:T(8,128)(2,1)S(1)} %shard_map.73), channel_id=1, source_target_pairs={{0,4},{4,8},{8,12},{12,0},{1,5},{5,9},{9,13},{13,1},{2,6},{6,10},{... | collective-permute-start | bytes 786440 | tf_op jit(solution)/shard_map/ppermute | solution.py:204
  150.5 14.2 %collective-permute-start.13 = (bf16[512,256]{1,0:T(8,128)(2,1)S(1)}, bf16[512,256]{1,0:T(8,128)(2,1)S(1)}, u32[]{:S(2)}, u32[]{:S(2)}) collective-permute-start(bf16[512,256]{1,0:T(8,128)(2,1)S(1)} %shard_map.73), channel_id=1, source_target_pairs={{0,8},{4,12},{8,0},{12,4},{1,9},{5,13},{9,1},{13,5},{2,10},{6,14},... | collective-permute-start | bytes 786440 | tf_op jit(solution)/shard_map/ppermute | solution.py:204
  153.5 13.5 %collective-permute-start.12 = (bf16[512,256]{1,0:T(8,128)(2,1)S(1)}, bf16[512,256]{1,0:T(8,128)(2,1)S(1)}, u32[]{:S(2)}, u32[]{:S(2)}) collective-permute-start(bf16[512,256]{1,0:T(8,128)(2,1)S(1)} %shard_map.73), channel_id=1, source_target_pairs={{0,12},{4,0},{8,4},{12,8},{1,13},{5,1},{9,5},{13,9},{2,14},{6,2},{... | collective-permute-start | bytes 786440 | tf_op jit(solution)/shard_map/ppermute | solution.py:204
  167.5 5.9 %collective-permute-start.21 = (f32[256,256]{1,0:T(8,128)S(1)}, f32[256,256]{1,0:T(8,128)S(1)}, u32[]{:S(2)}, u32[]{:S(2)}) collective-permute-start(f32[256,256]{1,0:T(8,128)S(1)} %shard_map.77), channel_id=1, source_target_pairs={{0,1},{1,0},{2,3},{3,2},{4,5},{5,4},{6,7},{7,6},{8,9},{9,8},{10,11... | collective-permute-start | bytes 786440 | tf_op jit(solution)/shard_map/ppermute | solution.py:300
  (2 other events, 4.8 us)

commit v11 on v10

--- a/solution.py
+++ b/solution.py
@@ -151,12 +151,9 @@
 
 
 def pool_two_kernel(meta, picks, pool, left, right, g_send, g_own, base):
-    half = g_own.shape[0]
     vector_terms(meta, picks, pool, right, meta[1], g_own)
-    total = dot(left[channel(meta, meta[1], 0)], g_own[0])
-    for j in range(1, half):
-        total = total + dot(left[channel(meta, meta[1], j)], g_own[j])
-    for j in range(half):
+    total = dot(left[channel(meta, 1 - meta[1], 0)], g_send[0])
+    for j in range(1, g_send.shape[0]):
         total = total + dot(left[channel(meta, 1 - meta[1], j)], g_send[j])
     base[...] = total
 
@@ -169,11 +166,12 @@
     out[...] = total
 
 
-def own_kernel(edges, g, base, out):
+def own_kernel(meta, edges, left, g, base, out):
     width = g.shape[1]
     total = base[...]
     for j in range(g.shape[0]):
-        total = total + dot(edges[j * width:(j + 1) * width, :], g[j])
+        updated = left[channel(meta, meta[1], j)].astype(F32) + edges[j * width:(j + 1) * width, :].astype(F32)
+        total = total + dot(updated.astype(BF), g[j])
     out[...] = total
 
 
@@ -298,9 +296,9 @@
         edges_own, g_other
     )
     from_other = lax.ppermute(for_other, "c", SWAP)
-    from_own = call(own_kernel, one((width, width), F32), [VMEM] * 3, [], unit // 2, 3 * half * block_bytes)(
-        edges_own, g_own, base
-    )
+    from_own = call(
+        own_kernel, one((width, width), F32), [SMEM] + [VMEM] * 4, [], unit // 2, 4 * half * block_bytes
+    )(meta, edges_own, left, g_own, base)
     second = call(second_kernel, one((width, width), BF), [SMEM, VMEM, VMEM], [], 1 << 18, 3 * block_bytes)(
         meta, from_own, from_other
     )

time: 176 us -> 175 us (level)
  no operation moved by 1% of the time
where the time goes in v11:
time: 175 us
  starting transfers between devices  85.5 us (49%)
  waiting for transfers between devices  69.8 us (40%)
  Pallas kernels  11.3 us (6%)
  local copies, waits for them, and re-layouts  3.24 us (2%)
  other arithmetic  3.04 us (2%)
    ppermute x12, starting transfers between devices, along_x(): lax.ppermute(value, 'x', [(i, (i + step) % count) for i in range(count)])  38.3 us
    ppermute x12, waiting for transfers between devices, along_x(): lax.ppermute(value, 'x', [(i, (i + step) % count) for i in range(count)])  32.4 us
    ppermute x1, waiting for transfers between devices, body(): from_far = lax.ppermute(row, YROW, far)  20.7 us
    ppermute x1, starting transfers between devices, body(): from_near = lax.ppermute(row, YROW, near)  10.5 us
    ppermute x1, starting transfers between devices, body(): across = lax.ppermute(own, 'c', SWAP)  7.43 us
    ppermute x1, waiting for transfers between devices, body(): message_other = lax.ppermute(message, 'yh', SWAP)  5.83 us
    ppermute x1, waiting for transfers between devices, body(): masked_other = lax.ppermute(masked, 'yh', SWAP)  5.42 us
    ppermute x1, starting transfers between devices, body(): masked_other = lax.ppermute(masked, 'yh', SWAP)  4.76 us
  transfers between devices with their start and end apart: 23, of which 13 were waited for; matrix products, arithmetic and copies ran while one was open for 1% of the time, Pallas kernels for 4%

profile of v11, /device:TPU:217, one launch (start us, length us, event | category | flops | bytes accessed | tf_op | source)
XLA Modules:
  0.0 174.6 jit_solution(9071732109337657309)
XLA Ops:
  2.3 4.8 %collective-permute-start.3 = (bf16[256,256]{1,0:T(8,128)(2,1)S(1)}, bf16[256,256]{1,0:T(8,128)(2,1)S(1)}, u32[]{:S(2)}, u32[]{:S(2)}) collective-permute-start(bf16[256,256]{1,0:T(8,128)(2,1)S(1)} %and_select_fusion), channel_id=1, source_target_pairs={{0,2},{2,0},{1,3},{3,1},{4,6},{6,4},{5,7},{7,5},{8,10},{10,8},{9,1... | collective-permute-start | bytes 393224 | tf_op jit(solution)/shard_map/ppermute | solution.py:246
  7.1 5.4 %collective-permute-done.3 = bf16[256,256]{1,0:T(8,128)(2,1)S(1)} collective-permute-done((bf16[256,256]{1,0:T(8,128)(2,1)S(1)}, bf16[256,256]{1,0:T(8,128)(2,1)S(1)}, u32[]{:S(2)}, u32[]{:S(2)}) %collective-permute-start.3) | collective-permute-done | bytes 131104 | tf_op jit(solution)/shard_map/ppermute | solution.py:246
  13.3 4.3 %all-to-all-start = ((bf16[4,256,256]{2,1,0:T(8,128)(2,1)}), bf16[4,256,256]{2,1,0:T(8,128)(2,1)}, u32[]{:S(2)}, u32[]{:S(2)}) async-start(bf16[4,256,256]{2,1,0:T(8,128)(2,1)} %broadcast_in_dim.20), calls=%async_computation | async-start | bytes 1048576 | tf_op jit(solution)/shard_map/all_to_all | solution.py:212
  17.6 3.3 %collective-permute-start.2 = (bf16[256,256]{1,0:T(8,128)(2,1)S(1)}, bf16[256,256]{1,0:T(8,128)(2,1)S(1)}, u32[]{:S(2)}, u32[]{:S(2)}) collective-permute-start(bf16[256,256]{1,0:T(8,128)(2,1)S(1)} %and_select_fusion), channel_id=1, source_target_pairs={{0,4},{4,8},{8,12},{12,0},{1,5},{5,9},{9,13},{13,1},{2,6},{6,10},{... | collective-permute-start | bytes 393224 | tf_op jit(solution)/shard_map/ppermute | solution.py:202
  20.9 4.3 %collective-permute-start.1 = (bf16[256,256]{1,0:T(8,128)(2,1)S(1)}, bf16[256,256]{1,0:T(8,128)(2,1)S(1)}, u32[]{:S(2)}, u32[]{:S(2)}) collective-permute-start(bf16[256,256]{1,0:T(8,128)(2,1)S(1)} %and_select_fusion), channel_id=1, source_target_pairs={{0,8},{4,12},{8,0},{12,4},{1,9},{5,13},{9,1},{13,5},{2,10},{6,14},... | collective-permute-start | bytes 393224 | tf_op jit(solution)/shard_map/ppermute | solution.py:202
  25.2 3.1 %collective-permute-start = (bf16[256,256]{1,0:T(8,128)(2,1)S(1)}, bf16[256,256]{1,0:T(8,128)(2,1)S(1)}, u32[]{:S(2)}, u32[]{:S(2)}) collective-permute-start(bf16[256,256]{1,0:T(8,128)(2,1)S(1)} %and_select_fusion), channel_id=1, source_target_pairs={{0,12},{4,0},{8,4},{12,8},{1,13},{5,1},{9,5},{13,9},{2,14},{6,2},{... | collective-permute-start | bytes 393224 | tf_op jit(solution)/shard_map/ppermute | solution.py:202
  34.7 7.4 %collective-permute-start.4 = (bf16[8,256,256]{2,1,0:T(8,128)(2,1)S(1)}, bf16[8,256,256]{2,1,0:T(8,128)(2,1)}, u32[]{:S(2)}, u32[]{:S(2)}) collective-permute-start(bf16[8,256,256]{2,1,0:T(8,128)(2,1)S(1)} %constant_dynamic-update-slice_fusion.own), channel_id=1, source_target_pairs={{0,1},{1,0},{2,3},{3,2},{4,5},{5,4},{6,7},{7,6},{8,9},{9,8},{10,11... | collective-permute-start | bytes 3145736 | tf_op jit(solution)/shard_map/ppermute | solution.py:251
  44.5 3.4 %shard_map.69 = (bf16[256,256]{1,0:T(8,128)(2,1)}, bf16[264,256]{1,0:T(8,128)(2,1)S(1)}) custom-call(s32[4]{0:T(128)S(1)} %pad_add_fusion.meta, s32[16]{0:T(128)S(1)} %bitcast.25, bf16[8,256,256]{2,1,0:T(8,128)(2,1)S(1)} %constant_dynamic-update-slice_fusion.own, bf16[8,256,256]{2,1,0:T(8,128)(2,1)} %collective-permute-done.4.across, ...), custom_call_target="tpu_custom_call" | custom-call | flops 1073741824 | bytes 8388608 | tf_op jit(solution)/shard_map/pallas_call | solution.py:255
  47.9 4.7 %collective-permute-start.15 = (bf16[264,256]{1,0:T(8,128)(2,1)S(1)}, bf16[264,256]{1,0:T(8,128)(2,1)S(1)}, u32[]{:S(2)}, u32[]{:S(2)}) collective-permute-start(bf16[264,256]{1,0:T(8,128)(2,1)S(1)} %get-tuple-element.15.message.refs_0_), channel_id=1, source_target_pairs={{0,2},{2,0},{1,3},{3,1},{4,6},{6,4},{5,7},{7,5},{8,10},{10,8},{9,1... | collective-permute-start | bytes 405512 | tf_op jit(solution)/shard_map/ppermute | solution.py:262
  52.6 5.8 %collective-permute-done.15 = bf16[264,256]{1,0:T(8,128)(2,1)S(1)} collective-permute-done((bf16[264,256]{1,0:T(8,128)(2,1)S(1)}, bf16[264,256]{1,0:T(8,128)(2,1)S(1)}, u32[]{:S(2)}, u32[]{:S(2)}) %collective-permute-start.15) | collective-permute-done | bytes 135200 | tf_op jit(solution)/shard_map/ppermute | solution.py:262
  58.5 4.3 %collective-permute-start.16 = (bf16[528,256]{1,0:T(8,128)(2,1)S(1)}, bf16[528,256]{1,0:T(8,128)(2,1)S(1)}, u32[]{:S(2)}, u32[]{:S(2)}) collective-permute-start(bf16[528,256]{1,0:T(8,128)(2,1)S(1)} %get-tuple-element.30), channel_id=1, source_target_pairs={{0,12},{4,0},{8,4},{12,8},{1,13},{5,1},{9,5},{13,9},{2,14},{6,2},{... | collective-permute-start | bytes 811016 | tf_op jit(solution)/shard_map/ppermute | solution.py:202
  62.8 3.5 %collective-permute-start.6 = (bf16[16,256,256]{2,1,0:T(8,128)(2,1)S(1)}, bf16[16,256,256]{2,1,0:T(8,128)(2,1)S(1)}, u32[]{:S(2)}, u32[]{:S(2)}) collective-permute-start(bf16[16,256,256]{2,1,0:T(8,128)(2,1)S(1)} %bitcast.20), channel_id=1, source_target_pairs={{0,1},{1,0},{2,3},{3,2},{4,5},{5,4},{6,7},{7,6},{8,9},{9,8},{10,11... | collective-permute-start | bytes 6291464 | tf_op jit(solution)/shard_map/ppermute | solution.py:253
  66.3 3.1 %collective-permute-start.17 = (bf16[528,256]{1,0:T(8,128)(2,1)S(1)}, bf16[528,256]{1,0:T(8,128)(2,1)S(1)}, u32[]{:S(2)}, u32[]{:S(2)}) collective-permute-start(bf16[528,256]{1,0:T(8,128)(2,1)S(1)} %get-tuple-element.30), channel_id=1, source_target_pairs={{0,8},{4,12},{8,0},{12,4},{1,9},{5,13},{9,1},{13,5},{2,10},{6,14},... | collective-permute-start | bytes 811016 | tf_op jit(solution)/shard_map/ppermute | solution.py:202
  71.6 6.2 %collective-permute-done.17 = bf16[528,256]{1,0:T(8,128)(2,1)S(1)} collective-permute-done((bf16[528,256]{1,0:T(8,128)(2,1)S(1)}, bf16[528,256]{1,0:T(8,128)(2,1)S(1)}, u32[]{:S(2)}, u32[]{:S(2)}) %collective-permute-start.17) | collective-permute-done | bytes 270368 | tf_op jit(solution)/shard_map/ppermute | solution.py:202
  77.8 6.1 %collective-permute-done.18 = bf16[528,256]{1,0:T(8,128)(2,1)S(1)} collective-permute-done((bf16[528,256]{1,0:T(8,128)(2,1)S(1)}, bf16[528,256]{1,0:T(8,128)(2,1)S(1)}, u32[]{:S(2)}, u32[]{:S(2)}) %collective-permute-start.18) | collective-permute-done | bytes 270368 | tf_op jit(solution)/shard_map/ppermute | solution.py:202
  94.4 3.1 %collective-permute-start.7 = (bf16[520,256]{1,0:T(8,128)(2,1)S(1)}, bf16[520,256]{1,0:T(8,128)(2,1)S(1)}, u32[]{:S(2)}, u32[]{:S(2)}) collective-permute-start(bf16[520,256]{1,0:T(8,128)(2,1)S(1)} %get-tuple-element.17), channel_id=1, source_target_pairs={{0,8},{4,12},{8,0},{12,4},{1,9},{5,13},{9,1},{13,5},{2,10},{6,14},... | collective-permute-start | bytes 798728 | tf_op jit(solution)/shard_map/ppermute | solution.py:202
  99.5 4.6 %collective-permute-start.9 = (bf16[520,256]{1,0:T(8,128)(2,1)S(1)}, bf16[520,256]{1,0:T(8,128)(2,1)S(1)}, u32[]{:S(2)}, u32[]{:S(2)}) collective-permute-start(bf16[520,256]{1,0:T(8,128)(2,1)S(1)} %get-tuple-element.19), channel_id=1, source_target_pairs={{0,12},{4,0},{8,4},{12,8},{1,13},{5,1},{9,5},{13,9},{2,14},{6,2},{... | collective-permute-start | bytes 798728 | tf_op jit(solution)/shard_map/ppermute | solution.py:202
  105.8 6.1 %collective-permute-done.8.c = bf16[520,256]{1,0:T(8,128)(2,1)S(1)} collective-permute-done((bf16[520,256]{1,0:T(8,128)(2,1)S(1)}, bf16[520,256]{1,0:T(8,128)(2,1)S(1)}, u32[]{:S(2)}, u32[]{:S(2)}) %collective-permute-start.8) | collective-permute-done | bytes 266272 | tf_op jit(solution)/shard_map/ppermute | solution.py:202
  112.0 10.5 %collective-permute-start.10 = (bf16[520,256]{1,0:T(8,128)(2,1)S(1)}, bf16[520,256]{1,0:T(8,128)(2,1)S(1)}, u32[]{:S(2)}, u32[]{:S(2)}) collective-permute-start(bf16[520,256]{1,0:T(8,128)(2,1)S(1)} %shard_map.72), channel_id=1, source_target_pairs={{0,16},{2,18},{16,32},{18,34},{32,48},{34,50},{48,66},{50,64},{64,... | collective-permute-start | bytes 798728 | tf_op jit(solution)/shard_map/ppermute | solution.py:275
  124.4 3.3 %collective-permute-done.10.refs_0_ = bf16[520,256]{1,0:T(8,128)(2,1)S(1)} collective-permute-done((bf16[520,256]{1,0:T(8,128)(2,1)S(1)}, bf16[520,256]{1,0:T(8,128)(2,1)S(1)}, u32[]{:S(2)}, u32[]{:S(2)}) %collective-permute-start.10) | collective-permute-done | bytes 266272 | tf_op jit(solution)/shard_map/ppermute | solution.py:275
  127.8 20.7 %collective-permute-done.11.refs_1_ = bf16[520,256]{1,0:T(8,128)(2,1)S(1)} collective-permute-done((bf16[520,256]{1,0:T(8,128)(2,1)S(1)}, bf16[520,256]{1,0:T(8,128)(2,1)S(1)}, u32[]{:S(2)}, u32[]{:S(2)}) %collective-permute-start.11) | collective-permute-done | bytes 266272 | tf_op jit(solution)/shard_map/ppermute | solution.py:274
  153.5 3.5 %collective-permute-start.12 = (bf16[512,256]{1,0:T(8,128)(2,1)S(1)}, bf16[512,256]{1,0:T(8,128)(2,1)S(1)}, u32[]{:S(2)}, u32[]{:S(2)}) collective-permute-start(bf16[512,256]{1,0:T(8,128)(2,1)S(1)} %shard_map.73), channel_id=1, source_target_pairs={{0,12},{4,0},{8,4},{12,8},{1,13},{5,1},{9,5},{13,9},{2,14},{6,2},{... | collective-permute-start | bytes 786440 | tf_op jit(solution)/shard_map/ppermute | solution.py:202
  157.0 7.7 %collective-permute-done.14 = bf16[512,256]{1,0:T(8,128)(2,1)S(1)} collective-permute-done((bf16[512,256]{1,0:T(8,128)(2,1)S(1)}, bf16[512,256]{1,0:T(8,128)(2,1)S(1)}, u32[]{:S(2)}, u32[]{:S(2)}) %collective-permute-start.14) | collective-permute-done | bytes 262176 | tf_op jit(solution)/shard_map/ppermute | solution.py:202
  167.5 3.5 %collective-permute-start.21 = (f32[256,256]{1,0:T(8,128)S(1)}, f32[256,256]{1,0:T(8,128)S(1)}, u32[]{:S(2)}, u32[]{:S(2)}) collective-permute-start(f32[256,256]{1,0:T(8,128)S(1)} %shard_map.77), channel_id=1, source_target_pairs={{0,1},{1,0},{2,3},{3,2},{4,5},{5,4},{6,7},{7,6},{8,9},{9,8},{10,11... | collective-permute-start | bytes 786440 | tf_op jit(solution)/shard_map/ppermute | solution.py:298
  (54 shorter events, 40.2 us)
Async XLA Ops:
  2.3 10.2 %collective-permute-start.3 = (bf16[256,256]{1,0:T(8,128)(2,1)S(1)}, bf16[256,256]{1,0:T(8,128)(2,1)S(1)}, u32[]{:S(2)}, u32[]{:S(2)}) collective-permute-start(bf16[256,256]{1,0:T(8,128)(2,1)S(1)} %and_select_fusion), channel_id=1, source_target_pairs={{0,2},{2,0},{1,3},{3,1},{4,6},{6,4},{5,7},{7,5},{8,10},{10,8},{9,1... | collective-permute-start | bytes 393224 | tf_op jit(solution)/shard_map/ppermute | solution.py:246
  13.3 28.8 %copy-start.1 = (bf16[1,1,16,256,256]{4,3,2,1,0:T(8,128)(2,1)S(1)}, bf16[1,1,16,256,256]{4,3,2,1,0:T(8,128)(2,1)}, u32[]{:S(2)}) copy-start(bf16[1,1,16,256,256]{4,3,2,1,0:T(8,128)(2,1)} %param.7) | copy-start | bytes 6291460
  13.3 19.2 %all-to-all-start = ((bf16[4,256,256]{2,1,0:T(8,128)(2,1)}), bf16[4,256,256]{2,1,0:T(8,128)(2,1)}, u32[]{:S(2)}, u32[]{:S(2)}) async-start(bf16[4,256,256]{2,1,0:T(8,128)(2,1)} %broadcast_in_dim.20), calls=%async_computation | async-start | bytes 1048576 | tf_op jit(solution)/shard_map/all_to_all | solution.py:212
  17.6 11.7 %collective-permute-start.2 = (bf16[256,256]{1,0:T(8,128)(2,1)S(1)}, bf16[256,256]{1,0:T(8,128)(2,1)S(1)}, u32[]{:S(2)}, u32[]{:S(2)}) collective-permute-start(bf16[256,256]{1,0:T(8,128)(2,1)S(1)} %and_select_fusion), channel_id=1, source_target_pairs={{0,4},{4,8},{8,12},{12,0},{1,5},{5,9},{9,13},{13,1},{2,6},{6,10},{... | collective-permute-start | bytes 393224 | tf_op jit(solution)/shard_map/ppermute | solution.py:202
  20.9 9.0 %collective-permute-start.1 = (bf16[256,256]{1,0:T(8,128)(2,1)S(1)}, bf16[256,256]{1,0:T(8,128)(2,1)S(1)}, u32[]{:S(2)}, u32[]{:S(2)}) collective-permute-start(bf16[256,256]{1,0:T(8,128)(2,1)S(1)} %and_select_fusion), channel_id=1, source_target_pairs={{0,8},{4,12},{8,0},{12,4},{1,9},{5,13},{9,1},{13,5},{2,10},{6,14},... | collective-permute-start | bytes 393224 | tf_op jit(solution)/shard_map/ppermute | solution.py:202
  25.2 6.4 %collective-permute-start = (bf16[256,256]{1,0:T(8,128)(2,1)S(1)}, bf16[256,256]{1,0:T(8,128)(2,1)S(1)}, u32[]{:S(2)}, u32[]{:S(2)}) collective-permute-start(bf16[256,256]{1,0:T(8,128)(2,1)S(1)} %and_select_fusion), channel_id=1, source_target_pairs={{0,12},{4,0},{8,4},{12,8},{1,13},{5,1},{9,5},{13,9},{2,14},{6,2},{... | collective-permute-start | bytes 393224 | tf_op jit(solution)/shard_map/ppermute | solution.py:202
  34.7 9.8 %collective-permute-start.4 = (bf16[8,256,256]{2,1,0:T(8,128)(2,1)S(1)}, bf16[8,256,256]{2,1,0:T(8,128)(2,1)}, u32[]{:S(2)}, u32[]{:S(2)}) collective-permute-start(bf16[8,256,256]{2,1,0:T(8,128)(2,1)S(1)} %constant_dynamic-update-slice_fusion.own), channel_id=1, source_target_pairs={{0,1},{1,0},{2,3},{3,2},{4,5},{5,4},{6,7},{7,6},{8,9},{9,8},{10,11... | collective-permute-start | bytes 3145736 | tf_op jit(solution)/shard_map/ppermute | solution.py:251
  47.9 10.6 %collective-permute-start.15 = (bf16[264,256]{1,0:T(8,128)(2,1)S(1)}, bf16[264,256]{1,0:T(8,128)(2,1)S(1)}, u32[]{:S(2)}, u32[]{:S(2)}) collective-permute-start(bf16[264,256]{1,0:T(8,128)(2,1)S(1)} %get-tuple-element.15.message.refs_0_), channel_id=1, source_target_pairs={{0,2},{2,0},{1,3},{3,1},{4,6},{6,4},{5,7},{7,5},{8,10},{10,8},{9,1... | collective-permute-start | bytes 405512 | tf_op jit(solution)/shard_map/ppermute | solution.py:262
  58.5 13.1 %collective-permute-start.16 = (bf16[528,256]{1,0:T(8,128)(2,1)S(1)}, bf16[528,256]{1,0:T(8,128)(2,1)S(1)}, u32[]{:S(2)}, u32[]{:S(2)}) collective-permute-start(bf16[528,256]{1,0:T(8,128)(2,1)S(1)} %get-tuple-element.30), channel_id=1, source_target_pairs={{0,12},{4,0},{8,4},{12,8},{1,13},{5,1},{9,5},{13,9},{2,14},{6,2},{... | collective-permute-start | bytes 811016 | tf_op jit(solution)/shard_map/ppermute | solution.py:202
  62.8 30.3 %collective-permute-start.6 = (bf16[16,256,256]{2,1,0:T(8,128)(2,1)S(1)}, bf16[16,256,256]{2,1,0:T(8,128)(2,1)S(1)}, u32[]{:S(2)}, u32[]{:S(2)}) collective-permute-start(bf16[16,256,256]{2,1,0:T(8,128)(2,1)S(1)} %bitcast.20), channel_id=1, source_target_pairs={{0,1},{1,0},{2,3},{3,2},{4,5},{5,4},{6,7},{7,6},{8,9},{9,8},{10,11... | collective-permute-start | bytes 6291464 | tf_op jit(solution)/shard_map/ppermute | solution.py:253
  66.3 11.5 %collective-permute-start.17 = (bf16[528,256]{1,0:T(8,128)(2,1)S(1)}, bf16[528,256]{1,0:T(8,128)(2,1)S(1)}, u32[]{:S(2)}, u32[]{:S(2)}) collective-permute-start(bf16[528,256]{1,0:T(8,128)(2,1)S(1)} %get-tuple-element.30), channel_id=1, source_target_pairs={{0,8},{4,12},{8,0},{12,4},{1,9},{5,13},{9,1},{13,5},{2,10},{6,14},... | collective-permute-start | bytes 811016 | tf_op jit(solution)/shard_map/ppermute | solution.py:202
  69.5 14.5 %collective-permute-start.18 = (bf16[528,256]{1,0:T(8,128)(2,1)S(1)}, bf16[528,256]{1,0:T(8,128)(2,1)S(1)}, u32[]{:S(2)}, u32[]{:S(2)}) collective-permute-start(bf16[528,256]{1,0:T(8,128)(2,1)S(1)} %get-tuple-element.30), channel_id=1, source_target_pairs={{0,4},{4,8},{8,12},{12,0},{1,5},{5,9},{9,13},{13,1},{2,6},{6,10},{... | collective-permute-start | bytes 811016 | tf_op jit(solution)/shard_map/ppermute | solution.py:202
  84.0 5.6 %collective-permute-start.19 = (bf16[2112,256]{1,0:T(8,128)(2,1)S(1)}, bf16[2112,256]{1,0:T(8,128)(2,1)S(1)}, u32[]{:S(2)}, u32[]{:S(2)}) collective-permute-start(bf16[2112,256]{1,0:T(8,128)(2,1)S(1)} %get-tuple-element.22), channel_id=1, source_target_pairs={{0,1},{1,0},{2,3},{3,2},{4,5},{5,4},{6,7},{7,6},{8,9},{9,8},{10,11... | collective-permute-start | bytes 3244040 | tf_op jit(solution)/shard_map/ppermute | solution.py:279
  86.4 6.7 %collective-permute-start.5 = (bf16[264,256]{1,0:T(8,128)(2,1)S(1)}, bf16[264,256]{1,0:T(8,128)(2,1)S(1)}, u32[]{:S(2)}, u32[]{:S(2)}) collective-permute-start(bf16[264,256]{1,0:T(8,128)(2,1)S(1)} %get-tuple-element.15.message.refs_0_), channel_id=1, source_target_pairs={{0,1},{1,0},{2,3},{3,2},{4,5},{5,4},{6,7},{7,6},{8,9},{9,8},{10,11... | collective-permute-start | bytes 405512 | tf_op jit(solution)/shard_map/ppermute | solution.py:261
  90.7 76.4 %collective-permute-start.20 = (bf16[8,256,256]{2,1,0:T(8,128)(2,1)S(1)}, bf16[8,256,256]{2,1,0:T(8,128)(2,1)S(1)}, u32[]{:S(2)}, u32[]{:S(2)}) collective-permute-start(bf16[8,256,256]{2,1,0:T(8,128)(2,1)S(1)} %shard_map.74.g_send), channel_id=1, source_target_pairs={{0,1},{1,0},{2,3},{3,2},{4,5},{5,4},{6,7},{7,6},{8,9},{9,8},{10,11... | collective-permute-start | bytes 3145736 | tf_op jit(solution)/shard_map/ppermute | solution.py:284
  94.4 11.4 %collective-permute-start.7 = (bf16[520,256]{1,0:T(8,128)(2,1)S(1)}, bf16[520,256]{1,0:T(8,128)(2,1)S(1)}, u32[]{:S(2)}, u32[]{:S(2)}) collective-permute-start(bf16[520,256]{1,0:T(8,128)(2,1)S(1)} %get-tuple-element.17), channel_id=1, source_target_pairs={{0,8},{4,12},{8,0},{12,4},{1,9},{5,13},{9,1},{13,5},{2,10},{6,14},... | collective-permute-start | bytes 798728 | tf_op jit(solution)/shard_map/ppermute | solution.py:202
  97.5 14.3 %collective-permute-start.8 = (bf16[520,256]{1,0:T(8,128)(2,1)S(1)}, bf16[520,256]{1,0:T(8,128)(2,1)S(1)}, u32[]{:S(2)}, u32[]{:S(2)}) collective-permute-start(bf16[520,256]{1,0:T(8,128)(2,1)S(1)} %get-tuple-element.18), channel_id=1, source_target_pairs={{0,4},{4,8},{8,12},{12,0},{1,5},{5,9},{9,13},{13,1},{2,6},{6,10},{... | collective-permute-start | bytes 798728 | tf_op jit(solution)/shard_map/ppermute | solution.py:202
  99.5 12.4 %collective-permute-start.9 = (bf16[520,256]{1,0:T(8,128)(2,1)S(1)}, bf16[520,256]{1,0:T(8,128)(2,1)S(1)}, u32[]{:S(2)}, u32[]{:S(2)}) collective-permute-start(bf16[520,256]{1,0:T(8,128)(2,1)S(1)} %get-tuple-element.19), channel_id=1, source_target_pairs={{0,12},{4,0},{8,4},{12,8},{1,13},{5,1},{9,5},{13,9},{2,14},{6,2},{... | collective-permute-start | bytes 798728 | tf_op jit(solution)/shard_map/ppermute | solution.py:202
  112.0 15.8 %collective-permute-start.10 = (bf16[520,256]{1,0:T(8,128)(2,1)S(1)}, bf16[520,256]{1,0:T(8,128)(2,1)S(1)}, u32[]{:S(2)}, u32[]{:S(2)}) collective-permute-start(bf16[520,256]{1,0:T(8,128)(2,1)S(1)} %shard_map.72), channel_id=1, source_target_pairs={{0,16},{2,18},{16,32},{18,34},{32,48},{34,50},{48,66},{50,64},{64,... | collective-permute-start | bytes 798728 | tf_op jit(solution)/shard_map/ppermute | solution.py:275
  122.5 26.0 %collective-permute-start.11 = (bf16[520,256]{1,0:T(8,128)(2,1)S(1)}, bf16[520,256]{1,0:T(8,128)(2,1)S(1)}, u32[]{:S(2)}, u32[]{:S(2)}) collective-permute-start(bf16[520,256]{1,0:T(8,128)(2,1)S(1)} %shard_map.72), channel_id=1, source_target_pairs={{0,18},{2,16},{16,34},{18,32},{32,50},{34,48},{48,64},{50,66},{64,... | collective-permute-start | bytes 798728 | tf_op jit(solution)/shard_map/ppermute | solution.py:274
  148.6 16.1 %collective-permute-start.14 = (bf16[512,256]{1,0:T(8,128)(2,1)S(1)}, bf16[512,256]{1,0:T(8,128)(2,1)S(1)}, u32[]{:S(2)}, u32[]{:S(2)}) collective-permute-start(bf16[512,256]{1,0:T(8,128)(2,1)S(1)} %shard_map.73), channel_id=1, source_target_pairs={{0,4},{4,8},{8,12},{12,0},{1,5},{5,9},{9,13},{13,1},{2,6},{6,10},{... | collective-permute-start | bytes 786440 | tf_op jit(solution)/shard_map/ppermute | solution.py:202
  150.5 14.2 %collective-permute-start.13 = (bf16[512,256]{1,0:T(8,128)(2,1)S(1)}, bf16[512,256]{1,0:T(8,128)(2,1)S(1)}, u32[]{:S(2)}, u32[]{:S(2)}) collective-permute-start(bf16[512,256]{1,0:T(8,128)(2,1)S(1)} %shard_map.73), channel_id=1, source_target_pairs={{0,8},{4,12},{8,0},{12,4},{1,9},{5,13},{9,1},{13,5},{2,10},{6,14},... | collective-permute-start | bytes 786440 | tf_op jit(solution)/shard_map/ppermute | solution.py:202
  153.5 13.5 %collective-permute-start.12 = (bf16[512,256]{1,0:T(8,128)(2,1)S(1)}, bf16[512,256]{1,0:T(8,128)(2,1)S(1)}, u32[]{:S(2)}, u32[]{:S(2)}) collective-permute-start(bf16[512,256]{1,0:T(8,128)(2,1)S(1)} %shard_map.73), channel_id=1, source_target_pairs={{0,12},{4,0},{8,4},{12,8},{1,13},{5,1},{9,5},{13,9},{2,14},{6,2},{... | collective-permute-start | bytes 786440 | tf_op jit(solution)/shard_map/ppermute | solution.py:202
  167.5 5.8 %collective-permute-start.21 = (f32[256,256]{1,0:T(8,128)S(1)}, f32[256,256]{1,0:T(8,128)S(1)}, u32[]{:S(2)}, u32[]{:S(2)}) collective-permute-start(f32[256,256]{1,0:T(8,128)S(1)} %shard_map.77), channel_id=1, source_target_pairs={{0,1},{1,0},{2,3},{3,2},{4,5},{5,4},{6,7},{7,6},{8,9},{9,8},{10,11... | collective-permute-start | bytes 786440 | tf_op jit(solution)/shard_map/ppermute | solution.py:298
  (2 other events, 4.8 us)
